TPU v7x, 32 devices: a whole 2x2x4 slice. The times are simulated.
32 devices in a mesh: dev: 32 (over z, y, x, core).
Axes of the slice: x: 2, y: 2, z: 4, core: 2. Of those that a mesh axis runs over, the one named last changes fastest.
Arguments:
- inputs: bfloat16 [65536, 227], P('dev'), may hold values from -6 to 6
- targets: float32 [65536, 227], P('dev'), may hold values from -6 to 6
- geometry: bfloat16 [8192, 4], P('dev'), may hold values from -6 to 6
- land_sea: int32 [65536], P('dev'), may hold values 0 or 1
- level_mask: int32 [65536, 227], P('dev'), may hold values from 0 to 1
- edge_owners: int32 [8192, 2], P('dev'), may hold values from 0 to 31, all different within a row; in each aligned block of 256 rows (0 to 255, 256 to 511, ...) at most 20 rows name the same one
- edge_local: int32 [8192, 2], P('dev'), may hold values from 0 to 2047
- step_count: int32 [1], replicated, may hold values from 1 to 20
- master: float32 [6545408], P('dev'), as said below
- first_moment: float32 [6545408], P('dev'), as said below
- second_moment: float32 [6545408], P('dev'), as said below
- ema: float32 [6545408], P('dev'), as said below
Outputs:
- new_master: float32 [6545408], P('dev')
- new_first: float32 [6545408], P('dev')
- new_second: float32 [6545408], P('dev')
- new_ema: float32 [6545408], P('dev')
- loss: float32 [], replicated
- grad_norm: float32 [], replicated
Inputs may be any that keep to these rules, and one draw needn't show every extreme that they name: `edge_owners`: the two columns of a row differ; within the rows of one device no device is named more than 20 times, and some device is named exactly 20 times. `master`: Finite, of the size of fan-in scaled weights, gains near 1. `first_moment`: Finite, both signs. `second_moment`: Positive. `ema`: Finite, of the size of fan-in scaled weights, gains near 1.
All inputs are finite; a program needn't handle non-finite values. No bound on the sum of `land_sea` on one device may be relied on, other than what follows from the above.
Results may differ from a plain program's by a relative error of at most 0.00045.
The roundings to bfloat16 on the way count: a program that leaves them out, or rounds other values in their place, can miss the bound.
Values may be sent and summed in bfloat16 or wider, within the bound.
A program may use at most 192 MiB of HBM per device.

v0:
```python
import jax
import jax.numpy as jnp
import numpy as np
from jax import lax
from jax.sharding import PartitionSpec as P

LATENT = 512
VARS = 227
GEO = 4
SEA_VARS = 4
LAYERS = 3
PARAMS = 6545408


norm_eps = 1e-05
clip_limit = 0.01
beta_one = 0.9
beta_two = 0.999
adam_eps = 1e-08
learn_rate = 0.03
decay_rate = 0.1
ema_keep = 0.9


def layout(width, variables, geometry, layers):
    shapes = [(variables, width, True), (geometry, width, True)]
    for k in range(layers):
        shapes.append((3 * width, width, True))
        shapes.append((2 * width, width, True))
    shapes.append((width, variables, False))
    segments = []
    offset = 0
    for block_id, (fan_in, fan_out, normed) in enumerate(shapes):
        members = [
            ("w_in", (fan_in, width)),
            ("b_in", (width,)),
            ("w_out", (width, fan_out)),
            ("b_out", (fan_out,)),
        ]
        if normed:
            members = members + [("gain", (fan_out,)), ("shift", (fan_out,))]
        for part_name, part_shape in members:
            entries = int(np.prod(part_shape))
            segments.append((block_id, part_name, part_shape, offset, entries))
            offset += entries
    return (segments, offset)


def unpack(flat, segments):
    blocks = [dict() for k in range(segments[-1][0] + 1)]
    for block_id, part_name, part_shape, offset, entries in segments:
        blocks[block_id][part_name] = flat[offset : offset + entries].reshape(part_shape)
    return blocks


def mlp_forward(params, source):
    pre = jnp.dot(source, params["w_in"], preferred_element_type=jnp.float32) + params[
        "b_in"
    ].astype(jnp.float32)
    act = jax.nn.silu(pre).astype(jnp.bfloat16)
    post = jnp.dot(act, params["w_out"], preferred_element_type=jnp.float32) + params[
        "b_out"
    ].astype(jnp.float32)
    if "gain" in params:
        centred = post - jnp.mean(post, axis=-1, keepdims=True)
        inv_std = lax.rsqrt(jnp.mean(centred * centred, axis=-1, keepdims=True) + norm_eps)
        scaled = centred * inv_std
        result = scaled * params["gain"].astype(jnp.float32) + params["shift"].astype(jnp.float32)
        return (result, (source, pre, act, scaled, inv_std))
    return (post, (source, pre, act, None, None))


def mlp_backward(params, kept, grad_out, need_input):
    source, pre, act, scaled, inv_std = kept
    grads = {}
    if scaled is not None:
        grads["gain"] = jnp.sum(grad_out * scaled, axis=0)
        grads["shift"] = jnp.sum(grad_out, axis=0)
        grad_scaled = grad_out * params["gain"].astype(jnp.float32)
        grad_post = inv_std * (
            grad_scaled
            - jnp.mean(grad_scaled, axis=-1, keepdims=True)
            - scaled * jnp.mean(grad_scaled * scaled, axis=-1, keepdims=True)
        )
    else:
        grad_post = grad_out
    post_low = grad_post.astype(jnp.bfloat16)
    grads["w_out"] = jnp.einsum("ni,nj->ij", act, post_low, preferred_element_type=jnp.float32)
    grads["b_out"] = jnp.sum(post_low.astype(jnp.float32), axis=0)
    grad_act = jnp.einsum(
        "nj,ij->ni", post_low, params["w_out"], preferred_element_type=jnp.float32
    )
    sigma = jax.nn.sigmoid(pre)
    pre_low = (grad_act * sigma * (1.0 + pre * (1.0 - sigma))).astype(jnp.bfloat16)
    grads["w_in"] = jnp.einsum("ni,nj->ij", source, pre_low, preferred_element_type=jnp.float32)
    grads["b_in"] = jnp.sum(pre_low.astype(jnp.float32), axis=0)
    grad_source = None
    if need_input:
        grad_source = jnp.einsum(
            "nj,ij->ni", pre_low, params["w_in"], preferred_element_type=jnp.float32
        )
    return (grad_source, grads)


def make_routes(edge_owners, edge_local):
    devices = lax.axis_size("dev")
    edges_here = edge_owners.shape[0]
    capacity = 5 * edges_here // (2 * devices)
    wanted_owner = edge_owners.reshape(-1)
    wanted_local = edge_local.reshape(-1)
    one_hot = (wanted_owner[:, None] == jnp.arange(devices, dtype=jnp.int32)[None, :]).astype(
        jnp.int32
    )
    ranking = jnp.sum((jnp.cumsum(one_hot, axis=0) - 1) * one_hot, axis=1)
    position = wanted_owner * capacity + ranking
    asking = jnp.zeros((devices * capacity,), jnp.int32).at[position].set(wanted_local + 1)
    served = lax.all_to_all(
        asking.reshape(devices, capacity), "dev", split_axis=0, concat_axis=0, tiled=True
    ).reshape(-1)
    valid = served > 0
    served_rows = jnp.maximum(served - 1, 0)
    return (served_rows, valid, position, position[1::2], devices, capacity)


def layer_forward(edge_params, node_params, node, edge, routes):
    served_rows, valid, position, recv_pos, devices, capacity = routes
    node_low = node.astype(jnp.bfloat16)
    outgoing = jnp.where(valid[:, None], node_low[served_rows], jnp.zeros((), jnp.bfloat16))
    arrived = lax.all_to_all(
        outgoing.reshape(devices, capacity, LATENT), "dev", split_axis=0, concat_axis=0, tiled=True
    ).reshape(-1, LATENT)
    gathered = arrived[position].reshape(edge.shape[0], 2 * LATENT)
    edge_in = jnp.concatenate([edge.astype(jnp.bfloat16), gathered], axis=1)
    edge_out, edge_kept = mlp_forward(edge_params, edge_in)
    edge_new = edge + edge_out
    buffer = (
        jnp.zeros((devices * capacity, LATENT), jnp.bfloat16)
        .at[recv_pos]
        .set(edge_new.astype(jnp.bfloat16))
    )
    landed = lax.all_to_all(
        buffer.reshape(devices, capacity, LATENT), "dev", split_axis=0, concat_axis=0, tiled=True
    ).reshape(-1, LATENT)
    landed = jnp.where(valid[:, None], landed.astype(jnp.float32), 0.0)
    summed = jnp.zeros(node.shape, jnp.float32).at[served_rows].add(landed)
    node_in = jnp.concatenate([node_low, summed.astype(jnp.bfloat16)], axis=1)
    node_out, node_kept = mlp_forward(node_params, node_in)
    return (node + node_out, edge_new, (edge_kept, node_kept))


def layer_backward(edge_params, node_params, kept, grad_node, grad_edge, routes):
    served_rows, valid, position, recv_pos, devices, capacity = routes
    edge_kept, node_kept = kept
    node_source, node_grads = mlp_backward(node_params, node_kept, grad_node, True)
    grad_total = grad_node + node_source[:, :LATENT]
    summed_low = node_source[:, LATENT:].astype(jnp.bfloat16)
    outgoing = jnp.where(valid[:, None], summed_low[served_rows], jnp.zeros((), jnp.bfloat16))
    returned = lax.all_to_all(
        outgoing.reshape(devices, capacity, LATENT), "dev", split_axis=0, concat_axis=0, tiled=True
    ).reshape(-1, LATENT)
    edge_total = grad_edge + returned[recv_pos].astype(jnp.float32)
    edge_source, edge_grads = mlp_backward(edge_params, edge_kept, edge_total, True)
    edge_prev = edge_total + edge_source[:, :LATENT]
    gathered_low = edge_source[:, LATENT:].reshape(-1, LATENT).astype(jnp.bfloat16)
    buffer = jnp.zeros((devices * capacity, LATENT), jnp.bfloat16).at[position].set(gathered_low)
    landed = lax.all_to_all(
        buffer.reshape(devices, capacity, LATENT), "dev", split_axis=0, concat_axis=0, tiled=True
    ).reshape(-1, LATENT)
    landed = jnp.where(valid[:, None], landed.astype(jnp.float32), 0.0)
    grad_total = grad_total.at[served_rows].add(landed)
    return (grad_total, edge_prev, edge_grads, node_grads)


def local(
    inputs,
    targets,
    geometry,
    land_sea,
    level_mask,
    edge_owners,
    edge_local,
    step_count,
    master,
    first_moment,
    second_moment,
    ema,
):
    segments, total = layout(LATENT, VARS, GEO, LAYERS)
    full_weights = lax.all_gather(master.astype(jnp.bfloat16), "dev", axis=0, tiled=True)
    blocks = unpack(full_weights, segments)
    routes = make_routes(edge_owners, edge_local)
    node, enc_kept = mlp_forward(blocks[0], inputs)
    edge, geo_kept = mlp_forward(blocks[1], geometry)
    layer_kept = []
    for k in range(LAYERS):
        node, edge, kept = layer_forward(blocks[2 + 2 * k], blocks[3 + 2 * k], node, edge, routes)
        layer_kept.append(kept)
    decoded, dec_kept = mlp_forward(blocks[2 + 2 * LAYERS], node.astype(jnp.bfloat16))
    pred = inputs.astype(jnp.float32) + decoded
    ocean = (jnp.arange(VARS) < SEA_VARS).astype(jnp.float32)
    mask = level_mask.astype(jnp.float32) * (
        1.0 - land_sea.astype(jnp.float32)[:, None] * ocean[None, :]
    )
    residual = pred - targets
    error_sum, count = lax.psum((jnp.sum(mask * residual * residual), jnp.sum(mask)), "dev")
    divisor = jnp.maximum(count, 1.0)
    loss = error_sum / divisor
    grad_pred = 2.0 * mask * residual / divisor
    grads = [None] * (3 + 2 * LAYERS)
    dec_source, grads[2 + 2 * LAYERS] = mlp_backward(
        blocks[2 + 2 * LAYERS], dec_kept, grad_pred, True
    )
    grad_node = dec_source
    grad_edge = jnp.zeros(edge.shape, jnp.float32)
    for k in reversed(range(LAYERS)):
        grad_node, grad_edge, grads[2 + 2 * k], grads[3 + 2 * k] = layer_backward(
            blocks[2 + 2 * k], blocks[3 + 2 * k], layer_kept[k], grad_node, grad_edge, routes
        )
    unused, grads[1] = mlp_backward(blocks[1], geo_kept, grad_edge, False)
    unused, grads[0] = mlp_backward(blocks[0], enc_kept, grad_node, False)
    pieces = [
        grads[block_id][part_name].reshape(-1)
        for block_id, part_name, part_shape, offset, entries in segments
    ]
    pieces.append(jnp.zeros((PARAMS - total,), jnp.float32))
    flat_grad = jnp.concatenate(pieces)
    summed_grad = lax.psum(flat_grad, "dev")
    share = master.shape[0]
    own_grad = lax.dynamic_slice_in_dim(summed_grad, lax.axis_index("dev") * share, share)
    squares = jnp.sum(summed_grad * summed_grad)
    grad_norm = jnp.sqrt(squares)
    clipped = own_grad * jnp.minimum(1.0, clip_limit / grad_norm)
    step = step_count[0].astype(jnp.float32)
    new_first = beta_one * first_moment + (1.0 - beta_one) * clipped
    new_second = beta_two * second_moment + (1.0 - beta_two) * clipped * clipped
    first_hat = new_first / (1.0 - beta_one**step)
    second_hat = new_second / (1.0 - beta_two**step)
    new_master = master - learn_rate * (
        first_hat / (jnp.sqrt(second_hat) + adam_eps) + decay_rate * master
    )
    new_ema = ema_keep * ema + (1.0 - ema_keep) * new_master
    return (new_master, new_first, new_second, new_ema, loss, grad_norm)


def solution(mesh):
    in_specs = (
        P("dev", None),
        P("dev", None),
        P("dev", None),
        P("dev"),
        P("dev", None),
        P("dev", None),
        P("dev", None),
        P(),
        P("dev"),
        P("dev"),
        P("dev"),
        P("dev"),
    )
    out_specs = (P("dev"), P("dev"), P("dev"), P("dev"), P(), P())
    return jax.shard_map(local, mesh=mesh, in_specs=in_specs, out_specs=out_specs, check_vma=False)
```

profile of v0, /device:TPU:27, one launch (start us, length us, event | category | flops | bytes accessed | tf_op | source)
XLA Modules:
  0.0 1847.2 jit_solution(10392052022695157452)
XLA Ops:
  8.4 5.4 reshape.886
  21.7 6.8 all-to-all-start
  32.9 140.3 %all-gather.3.cloned.1.call-done = bf16[32,1,204544]{2,1,0:T(2,128)(2,1)} async-done(((bf16[1,1,204544]{2,1,0:T(2,128)(2,1)}), bf16[32,1,204544]{2,1,0:T(2,128)(2,1)}) %all-gather.3.cloned.1.call-update) | async-done | bytes 13090832 | tf_op jit(solution)/shard_map/all_gather | solution.py:189
  173.1 277.2 %reduce = bf16[32,204544]{1,0:T(8,128)(2,1)} reduce(bf16[32,1,204544]{2,1,0:T(2,128)(2,1)} %all-gather.3.cloned.1.call-done, bf16[]{:T(256)} %constant.119), dimensions={1}, to_apply=%all-gather.reduce_sub_computation | reduce | bytes 26181634 | tf_op jit(solution)/shard_map/all_gather | solution.py:189
  450.3 23.4 %reshape.887 = bf16[6545408]{0:T(1024)(128)(2,1)} reshape(bf16[32,204544]{1,0:T(8,128)(2,1)} %reduce) | data formatting | bytes 26181632
  477.7 5.1 fusion.104
  510.1 5.0 all-to-all-start.1
  518.9 14.0 all-to-all-done.1
  542.8 6.7 all-to-all-start.2
  557.5 9.7 all-to-all-done.2
  567.3 10.2 scatter_custom_fusion.2
  582.3 6.6 multiply_convert_fusion.12
  606.6 6.5 all-to-all-start.3
  616.6 14.3 all-to-all-done.3
  642.8 6.4 all-to-all-start.4
  651.8 15.2 all-to-all-done.4
  667.1 10.1 scatter_custom_fusion.4
  682.0 6.8 multiply_convert_fusion.11
  705.1 6.4 all-to-all-start.5
  714.8 14.5 all-to-all-done.5
  740.8 6.5 all-to-all-start.6
  753.2 11.9 all-to-all-done.6
  766.4 10.3 scatter_custom_fusion.6
  781.5 6.9 multiply_convert_fusion.10
  804.6 39.8 %all-reduce = (f32[]{:T(128)}, f32[]{:T(128)}) all-reduce(f32[]{:T(128)} %get-tuple-element.19, f32[]{:T(128)} %get-tuple-element.18), channel_id=1, replica_groups=mesh['dev'=32] {'dev'}, use_global_device_ids=true, to_apply=%region_27.28 | all-reduce | flops 2 | bytes 16 | tf_op jit(solution)/shard_map/psum | solution.py:205
  855.5 5.4 copy.85
  860.9 5.5 multiply_reduce_fusion.1
  886.5 7.3 all-to-all-start.7
  897.7 13.8 all-to-all-done.7
  921.4 6.5 all-to-all-start.8
  947.0 12.2 scatter_custom_fusion.8
  959.3 5.4 copy.86
  964.7 5.0 multiply_reduce_fusion.2
  987.4 6.9 all-to-all-start.9
  1022.4 6.7 all-to-all-start.10
  1034.0 5.0 fusion.107
  1046.9 12.2 scatter_custom_fusion.10
  1059.2 5.4 copy.87
  1089.4 6.9 all-to-all-start.11
  1106.5 5.0 fusion.108
  1124.9 6.4 all-to-all-start.12
  1140.2 9.0 all-to-all-done.12
  1149.3 12.2 scatter_custom_fusion.12
  1164.0 5.4 copy.88
  1169.5 5.0 multiply_reduce_fusion.4
  1187.2 231.7 %concatenate.27 = f32[6545408]{0:T(1024)} concatenate(f32[116224]{0:T(1024)} %reshape.644, f32[512]{0:T(512)S(1)} %get-tuple-element.150, f32[262144]{0:T(1024)} %bitcast.184, f32[512]{0:T(512)S(1)} %get-tuple-element.59, f32[512]{0:T(512)S(1)} %get-tuple-element.12, f32[512]{0:T(512)S(1)} %reduce_sum.668, f32[2048]{0:T(1024)S(1)} %bitcast.185, f32[512]{0:T(512)S(1)} %get-tuple-element.152, ...), dimensions={0} | concatenate | bytes 52363264 | tf_op jit(solution)/shard_map/concatenate | solution.py:226
  1420.3 402.8 %all-reduce.3.cloned.1.call-done = f32[6545408]{0:T(1024)} async-done(((f32[6545408]{0:T(1024)}), f32[6545408]{0:T(1024)}) %all-reduce.3.cloned.1.call-update) | async-done | bytes 26181648 | tf_op jit(solution)/shard_map/psum | solution.py:227
  1823.1 10.4 multiply_reduce_fusion
  (700 shorter events, 366.5 us)
Async XLA Ops:
  7.2 507.9 %copy-start = (bf16[256,4]{0,1:T(4,128)(2,1)S(1)}, bf16[256,4]{0,1:T(4,128)(2,1)}, u32[]{:S(2)}) copy-start(bf16[256,4]{0,1:T(4,128)(2,1)} %param.14) | copy-start | bytes 6148
  7.2 166.0 %all-gather.3.cloned.1.call-start = ((), (), s32[]{:S(2)}) async-start(), calls=%async_computation.14 | async-start | bytes 26999808 | tf_op jit(solution)/shard_map/all_gather | solution.py:189
  21.7 10.0 all-to-all-start
  32.8 417.5 %copy-start.169 = (s32[640]{0:T(1024)}, s32[640]{0:T(1024)S(1)}, u32[]{:S(2)}) copy-start(s32[640]{0:T(1024)S(1)} %reshape.782) | copy-start | bytes 7684
  32.9 473.2 %copy-start.118 = (s32[1024]{0:T(1024)}, s32[1024]{0:T(1024)S(1)}, u32[]{:S(2)}) copy-start(s32[1024]{0:T(1024)S(1)} %pad_clamp_fusion.2) | copy-start | bytes 12292
  475.8 18.4 copy-start.187
  475.8 23.8 %copy-start.122 = (f32[512]{0:T(512)}, f32[512]{0:T(512)S(1)}, u32[]{:S(2)}) copy-start(f32[512]{0:T(512)S(1)} %get-tuple-element.115) | copy-start | bytes 6148
  475.9 23.8 %copy-start.130 = (f32[512]{0:T(512)}, f32[512]{0:T(512)S(1)}, u32[]{:S(2)}) copy-start(f32[512]{0:T(512)S(1)} %get-tuple-element.114) | copy-start | bytes 6148
  475.9 23.8 %copy-start.163 = (f32[512]{0:T(512)}, f32[512]{0:T(512)S(1)}, u32[]{:S(2)}) copy-start(f32[512]{0:T(512)S(1)} %get-tuple-element.113) | copy-start | bytes 6148
  499.0 93.4 %copy-start.106 = (f32[2048]{0:T(1024)}, f32[2048]{0:T(1024)S(1)}, u32[]{:S(2)}) copy-start(f32[2048]{0:T(1024)S(1)} %broadcast_multiply_fusion.11) | copy-start | bytes 24580
  510.1 22.8 %all-to-all-start.1 = ((bf16[32,20,512]{2,1,0:T(8,128)(2,1)}), bf16[32,20,512]{2,1,0:T(8,128)(2,1)S(1)}, u32[]{:S(2)}, u32[]{:S(2)}) async-start(bf16[32,20,512]{2,1,0:T(8,128)(2,1)} %broadcast_select_fusion.5), calls=%async_computation.1 | async-start | bytes 1572864 | tf_op jit(solution)/shard_map/all_to_all | solution.py:129
  516.5 22.3 %copy-start.20 = (f32[256,512]{1,0:T(8,128)}, f32[256,512]{1,0:T(8,128)S(1)}, u32[]{:S(2)}) copy-start(f32[256,512]{1,0:T(8,128)S(1)} %get-tuple-element.128) | copy-start | bytes 1572868
  516.5 19.0 %copy-start.34 = (bf16[1536,512]{1,0:T(8,128)(2,1)S(1)}, bf16[1536,512]{1,0:T(8,128)(2,1)}, u32[]{:S(2)}) copy-start(bf16[1536,512]{1,0:T(8,128)(2,1)} %slice.397) | copy-start | bytes 4718596
  539.9 95.3 %copy-start.73 = (bf16[256,512]{1,0:T(8,128)(2,1)}, bf16[256,512]{1,0:T(8,128)(2,1)S(1)}, u32[]{:S(2)}) copy-start(bf16[256,512]{1,0:T(8,128)(2,1)S(1)} %get-tuple-element.65) | copy-start | bytes 786436
  542.8 24.4 %all-to-all-start.2 = ((bf16[32,20,512]{2,1,0:T(8,128)(2,1)}), bf16[32,20,512]{2,1,0:T(8,128)(2,1)S(1)}, u32[]{:S(2)}, u32[]{:S(2)}) async-start(bf16[32,20,512]{2,1,0:T(8,128)(2,1)} %reshape.630), calls=%async_computation.2 | async-start | bytes 1572864 | tf_op jit(solution)/shard_map/all_to_all | solution.py:141
  553.4 13.9 copy-start.137
  557.5 35.0 %copy-start.148 = (f32[512]{0:T(512)}, f32[512]{0:T(512)S(1)}, u32[]{:S(2)}) copy-start(f32[512]{0:T(512)S(1)} %get-tuple-element.87) | copy-start | bytes 6148
  605.5 26.7 %copy-start.158 = (s32[1024]{0:T(1024)S(1)}, s32[1024]{0:T(1024)}, u32[]{:S(2)}) copy-start(s32[1024]{0:T(1024)} %pad_clamp_fusion.1) | copy-start | bytes 12292
  606.6 24.4 %all-to-all-start.3 = ((bf16[32,20,512]{2,1,0:T(8,128)(2,1)}), bf16[32,20,512]{2,1,0:T(8,128)(2,1)}, u32[]{:S(2)}, u32[]{:S(2)}) async-start(bf16[32,20,512]{2,1,0:T(8,128)(2,1)} %broadcast_select_fusion.4), calls=%async_computation.3 | async-start | bytes 1572864 | tf_op jit(solution)/shard_map/all_to_all | solution.py:129
  614.1 22.7 %copy-start.36 = (bf16[1536,512]{1,0:T(8,128)(2,1)}, bf16[1536,512]{1,0:T(8,128)(2,1)S(1)}, u32[]{:S(2)}) copy-start(bf16[1536,512]{1,0:T(8,128)(2,1)S(1)} %slice.413) | copy-start | bytes 4718596
  636.8 12.4 copy-start.49
  638.5 12.2 copy-start.56
  641.7 25.4 %copy-start.138 = (pred[640]{0:T(1024)(128)(4,1)S(1)}, pred[640]{0:T(1024)(128)(4,1)}, u32[]{:S(2)}) copy-start(pred[640]{0:T(1024)(128)(4,1)} %gt.15) | copy-start | bytes 1924
  642.8 24.2 %all-to-all-start.4 = ((bf16[32,20,512]{2,1,0:T(8,128)(2,1)}), bf16[32,20,512]{2,1,0:T(8,128)(2,1)S(1)}, u32[]{:S(2)}, u32[]{:S(2)}) async-start(bf16[32,20,512]{2,1,0:T(8,128)(2,1)} %reshape.633), calls=%async_computation.4 | async-start | bytes 1572864 | tf_op jit(solution)/shard_map/all_to_all | solution.py:141
  704.0 25.4 %copy-start.159 = (s32[1024]{0:T(1024)S(1)}, s32[1024]{0:T(1024)}, u32[]{:S(2)}) copy-start(s32[1024]{0:T(1024)} %pad_clamp_fusion.1) | copy-start | bytes 12292
  705.1 24.2 %all-to-all-start.5 = ((bf16[32,20,512]{2,1,0:T(8,128)(2,1)}), bf16[32,20,512]{2,1,0:T(8,128)(2,1)S(1)}, u32[]{:S(2)}, u32[]{:S(2)}) async-start(bf16[32,20,512]{2,1,0:T(8,128)(2,1)} %broadcast_select_fusion.3), calls=%async_computation.5 | async-start | bytes 1572864 | tf_op jit(solution)/shard_map/all_to_all | solution.py:129
  714.8 16.9 copy-start.76
  714.8 16.9 copy-start.186
  733.9 13.3 copy-start.175
  733.9 15.0 copy-start.48
  735.9 15.5 copy-start.53
  740.8 25.6 %copy-start.139 = (pred[640]{0:T(1024)(128)(4,1)S(1)}, pred[640]{0:T(1024)(128)(4,1)}, u32[]{:S(2)}) copy-start(pred[640]{0:T(1024)(128)(4,1)} %gt.15) | copy-start | bytes 1924
  740.8 24.4 %all-to-all-start.6 = ((bf16[32,20,512]{2,1,0:T(8,128)(2,1)}), bf16[32,20,512]{2,1,0:T(8,128)(2,1)}, u32[]{:S(2)}, u32[]{:S(2)}) async-start(bf16[32,20,512]{2,1,0:T(8,128)(2,1)} %reshape.636), calls=%async_computation.6 | async-start | bytes 1572864 | tf_op jit(solution)/shard_map/all_to_all | solution.py:141
  882.1 11.7 copy-start.40
  886.5 25.0 %all-to-all-start.7 = ((bf16[32,20,512]{2,1,0:T(8,128)(2,1)}), bf16[32,20,512]{2,1,0:T(8,128)(2,1)}, u32[]{:S(2)}, u32[]{:S(2)}) async-start(bf16[32,20,512]{2,1,0:T(8,128)(2,1)} %broadcast_select_fusion.2), calls=%async_computation.7 | async-start | bytes 1572864 | tf_op jit(solution)/shard_map/all_to_all | solution.py:158
  897.7 16.8 copy-start.103
  897.7 16.8 copy-start.201
  921.4 13.0 copy-start.28
  921.4 24.4 %all-to-all-start.8 = ((bf16[32,20,512]{2,1,0:T(8,128)(2,1)}), bf16[32,20,512]{2,1,0:T(8,128)(2,1)}, u32[]{:S(2)}, u32[]{:S(2)}) async-start(bf16[32,20,512]{2,1,0:T(8,128)(2,1)} %reshape.639), calls=%async_computation.8 | async-start | bytes 1572864 | tf_op jit(solution)/shard_map/all_to_all | solution.py:166
  987.4 24.6 %all-to-all-start.9 = ((bf16[32,20,512]{2,1,0:T(8,128)(2,1)}), bf16[32,20,512]{2,1,0:T(8,128)(2,1)S(1)}, u32[]{:S(2)}, u32[]{:S(2)}) async-start(bf16[32,20,512]{2,1,0:T(8,128)(2,1)} %broadcast_select_fusion.1), calls=%async_computation.9 | async-start | bytes 1572864 | tf_op jit(solution)/shard_map/all_to_all | solution.py:158
  1022.4 24.4 %all-to-all-start.10 = ((bf16[32,20,512]{2,1,0:T(8,128)(2,1)}), bf16[32,20,512]{2,1,0:T(8,128)(2,1)S(1)}, u32[]{:S(2)}, u32[]{:S(2)}) async-start(bf16[32,20,512]{2,1,0:T(8,128)(2,1)} %reshape.641), calls=%async_computation.10 | async-start | bytes 1572864 | tf_op jit(solution)/shard_map/all_to_all | solution.py:166
  1089.4 24.6 %all-to-all-start.11 = ((bf16[32,20,512]{2,1,0:T(8,128)(2,1)}), bf16[32,20,512]{2,1,0:T(8,128)(2,1)}, u32[]{:S(2)}, u32[]{:S(2)}) async-start(bf16[32,20,512]{2,1,0:T(8,128)(2,1)} %broadcast_select_fusion), calls=%async_computation.11 | async-start | bytes 1572864 | tf_op jit(solution)/shard_map/all_to_all | solution.py:158
  1124.9 24.2 %all-to-all-start.12 = ((bf16[32,20,512]{2,1,0:T(8,128)(2,1)}), bf16[32,20,512]{2,1,0:T(8,128)(2,1)S(1)}, u32[]{:S(2)}, u32[]{:S(2)}) async-start(bf16[32,20,512]{2,1,0:T(8,128)(2,1)} %reshape.643), calls=%async_computation.12 | async-start | bytes 1572864 | tf_op jit(solution)/shard_map/all_to_all | solution.py:166
  1131.3 691.7 %all-reduce.3.cloned.1.call-start = ((), (), s32[]{:S(2)}) async-start(), calls=%async_computation.13 | async-start | bytes 52363264 | tf_op jit(solution)/shard_map/psum | solution.py:227
  1420.3 413.9 %copy-start.50 = (f32[204544]{0:T(1024)S(1)}, f32[204544]{0:T(1024)}, u32[]{:S(2)}) copy-start(f32[204544]{0:T(1024)} %param.20) | copy-start | bytes 2454532
  1420.3 413.9 %copy-start.88 = (f32[204544]{0:T(1024)S(1)}, f32[204544]{0:T(1024)}, u32[]{:S(2)}) copy-start(f32[204544]{0:T(1024)} %param.23) | copy-start | bytes 2454532
  1420.3 413.9 %copy-start.89 = (f32[204544]{0:T(1024)S(1)}, f32[204544]{0:T(1024)}, u32[]{:S(2)}) copy-start(f32[204544]{0:T(1024)} %param.22) | copy-start | bytes 2454532
  1420.3 413.9 %copy-start.90 = (f32[204544]{0:T(1024)S(1)}, f32[204544]{0:T(1024)}, u32[]{:S(2)}) copy-start(f32[204544]{0:T(1024)} %param.21) | copy-start | bytes 2454532
  (183 other events, 762.5 us)
Sparse Core Ops, SparseCore 0:
  14.0 159.1 all-gather.2
  1419.0 404.0 all-reduce.2
where the time goes:
time: 1870 us; the launch traced here: 1850 us
  waiting for transfers between devices  657 us (35%)
  local copies, waits for them, and re-layouts  482 us (26%)
  other arithmetic  448 us (24%)
  matrix products  112 us (6%)
  starting transfers between devices  85.5 us (5%)
  blocking collectives  39.8 us (2%)
  between operations  22.5 us (1%)
    psum x1, waiting for transfers between devices, local(): summed_grad = lax.psum(flat_grad, 'dev')  403 us
    all_gather x1, other arithmetic, local(): lax.all_gather(master.astype(jnp.bfloat16), 'dev', axis=0, tiled=True)  277 us
    concatenate x1, local copies, waits for them, and re-layouts, local(): flat_grad = jnp.concatenate(pieces)  232 us
    all_gather x1, waiting for transfers between devices, local(): lax.all_gather(master.astype(jnp.bfloat16), 'dev', axis=0, tiled=True)  140 us
    unnamed x451, local copies, waits for them, and re-layouts  92.2 us
    all_to_all x3, waiting for transfers between devices, layer_forward(): lax.all_to_all(outgoing.reshape(devices, capacity, LATENT), 'dev', split_...  42.8 us
    psum x1, blocking collectives, local(): lax.psum((jnp.sum(mask * residual * residual), jnp.sum(mask)), 'dev')  39.8 us
    slice x22, local copies, waits for them, and re-layouts, unpack(): flat[offset:offset + entries].reshape(part_shape)  38.7 us
  transfers between devices with their start and end apart: 15, of which 15 were waited for; matrix products, arithmetic and copies ran while one was open for 6% of the time, Pallas kernels for 0%

commit v1 on v0

v1 whole, which is shorter than its diff:
```python
import functools

import jax
import jax.numpy as jnp
import numpy as np
from jax import lax
from jax.experimental import pallas as pl
from jax.experimental.pallas import tpu as pltpu
from jax.sharding import PartitionSpec as P

LATENT = 512
VARS = 227
GEO = 4
SEA_VARS = 4
LAYERS = 3
PARAMS = 6545408


norm_eps = 1e-05
clip_limit = 0.01
beta_one = 0.9
beta_two = 0.999
adam_eps = 1e-08
learn_rate = 0.03
decay_rate = 0.1
ema_keep = 0.9


def layout(width, variables, geometry, layers):
    shapes = [(variables, width, True), (geometry, width, True)]
    for k in range(layers):
        shapes.append((3 * width, width, True))
        shapes.append((2 * width, width, True))
    shapes.append((width, variables, False))
    segments = []
    offset = 0
    for block_id, (fan_in, fan_out, normed) in enumerate(shapes):
        members = [
            ("w_in", (fan_in, width)),
            ("b_in", (width,)),
            ("w_out", (width, fan_out)),
            ("b_out", (fan_out,)),
        ]
        if normed:
            members = members + [("gain", (fan_out,)), ("shift", (fan_out,))]
        for part_name, part_shape in members:
            entries = int(np.prod(part_shape))
            segments.append((block_id, part_name, part_shape, offset, entries))
            offset += entries
    return (segments, offset)


def unpack(flat, segments):
    blocks = [dict() for k in range(segments[-1][0] + 1)]
    for block_id, part_name, part_shape, offset, entries in segments:
        blocks[block_id][part_name] = flat[offset : offset + entries].reshape(part_shape)
    return blocks


MESH = pl.DeviceIdType.MESH

def remote(src, dst, send, recv, target):
    return pltpu.make_async_remote_copy(src, dst, send, recv, device_id=(target,), device_id_type=MESH)

def greet(n, me):
    barrier = pltpu.get_barrier_semaphore()
    def hello(j, c):
        pl.semaphore_signal(barrier, inc=1, device_id=(lax.rem(me + j, n),), device_id_type=MESH)
        return c
    lax.fori_loop(1, n, hello, 0)
    pl.semaphore_wait(barrier, n - 1)

def a2a_kernel(n, a_ref, o_ref, own, ssem, rsem):
    me = lax.axis_index('dev')
    greet(n, me)
    here = pltpu.make_async_copy(a_ref.at[me], o_ref.at[me], own)
    here.start()
    def go(j, c):
        t = lax.rem(me + j, n)
        remote(a_ref.at[t], o_ref.at[me], ssem.at[j], rsem.at[j], t).start()
        return c
    lax.fori_loop(1, n, go, 0)
    def end(j, c):
        t = lax.rem(me + j, n)
        remote(a_ref.at[t], o_ref.at[me], ssem.at[j], rsem.at[j], t).wait()
        return c
    lax.fori_loop(1, n, end, 0)
    here.wait()

def a2a(x, cid, space=pl.ANY):
    n = x.shape[0]
    return pl.pallas_call(
        functools.partial(a2a_kernel, n),
        out_shape=jax.ShapeDtypeStruct(x.shape, x.dtype),
        in_specs=[pl.BlockSpec(memory_space=space)],
        out_specs=pl.BlockSpec(memory_space=space),
        scratch_shapes=[pltpu.SemaphoreType.DMA, pltpu.SemaphoreType.DMA((n,)), pltpu.SemaphoreType.DMA((n,))],
        compiler_params=pltpu.CompilerParams(collective_id=cid, has_side_effects=True),
    )(x)

def gather_kernel(w_ref, ask_ref, num_ref, o_ref, served_ref, nums_ref, own, small_s, small_r, zs, zr, hs, hr, cs, cr, ds, dr, bs, br):
    n = 32
    me = lax.axis_index('dev')
    c, x, y, z = lax.rem(me, 2), lax.rem(me // 2, 2), lax.rem(me // 4, 2), me // 8
    rows = w_ref.shape[0]
    half = rows // 2
    A, B = pl.ds(0, half), pl.ds(half, half)
    def dev(z, y, x, c):
        return ((z * 2 + y) * 2 + x) * 2 + c
    greet(n, me)
    tx, ty, tc = dev(z, y, 1 - x, c), dev(z, 1 - y, x, c), dev(z, y, x, 1 - c)
    pend = []
    def start(cp):
        cp.start(); pend.append(cp)
    mine = pltpu.make_async_copy(w_ref, o_ref.at[me], own.at[0])
    mine.start()
    start(remote(w_ref.at[A], o_ref.at[me, A], hs.at[0, 0], hr.at[0, 0], tx))
    start(remote(w_ref.at[B], o_ref.at[me, B], hs.at[0, 1], hr.at[0, 1], ty))
    for j in (1, 3, 2):
        start(remote(w_ref, o_ref.at[me], zs.at[j], zr.at[4 - j], dev(lax.rem(z + j, 4), y, x, c)))
    start(remote(w_ref, o_ref.at[me], bs.at[0], br.at[0], tc))
    mine2 = pltpu.make_async_copy(ask_ref.at[me], served_ref.at[me], own.at[1])
    mine2.start()
    mine3 = pltpu.make_async_copy(num_ref, nums_ref.at[me], own.at[2])
    mine3.start()
    def go(j, carry):
        t = lax.rem(me + j, n)
        remote(ask_ref.at[t], served_ref.at[me], small_s.at[0, j], small_r.at[0, j], t).start()
        remote(num_ref, nums_ref.at[me], small_s.at[1, j], small_r.at[1, j], t).start()
        return carry
    lax.fori_loop(1, n, go, 0)
    nb = [1]
    def sib(slot, part):
        i = nb[0]; nb[0] += 1
        ref = o_ref.at[slot] if part is None else o_ref.at[slot, part]
        start(remote(ref, ref, bs.at[i], br.at[i], tc))
    def second(k, zz):
        s = dev(zz, y, x, c)
        sx, sy = dev(zz, y, 1 - x, c), dev(zz, 1 - y, x, c)
        own_a = w_ref.at[A] if k == 0 else o_ref.at[s, A]
        own_b = w_ref.at[B] if k == 0 else o_ref.at[s, B]
        remote(own_a, o_ref.at[sx, A], hs.at[k, 0], hr.at[k, 0], tx).wait_recv()
        start(remote(own_a, o_ref.at[s, A], cs.at[k, 0], cr.at[k, 0], ty))
        start(remote(o_ref.at[sx, A], o_ref.at[sx, A], cs.at[k, 1], cr.at[k, 1], ty))
        remote(own_b, o_ref.at[sy, B], hs.at[k, 1], hr.at[k, 1], ty).wait_recv()
        start(remote(own_b, o_ref.at[s, B], ds.at[k, 0], dr.at[k, 0], tx))
        start(remote(o_ref.at[sy, B], o_ref.at[sy, B], ds.at[k, 1], dr.at[k, 1], tx))
        sib(sx, A)
        sib(sy, B)
    def third(k, zz):
        sx, sy, sd = dev(zz, y, 1 - x, c), dev(zz, 1 - y, x, c), dev(zz, 1 - y, 1 - x, c)
        w = w_ref.at[A]
        remote(w, o_ref.at[sy, A], cs.at[k, 0], cr.at[k, 0], ty).wait_recv()
        sib(sy, A)
        remote(w, o_ref.at[sx, B], ds.at[k, 0], dr.at[k, 0], tx).wait_recv()
        sib(sx, B)
        remote(w, o_ref.at[sd, A], cs.at[k, 1], cr.at[k, 1], ty).wait_recv()
        sib(sd, A)
        remote(w, o_ref.at[sd, B], ds.at[k, 1], dr.at[k, 1], tx).wait_recv()
        sib(sd, B)
    def first(k, zz):
        s = dev(zz, y, x, c)
        remote(w_ref, o_ref.at[s], zs.at[k], zr.at[k], tc).wait_recv()
        start(remote(o_ref.at[s, A], o_ref.at[s, A], hs.at[k, 0], hr.at[k, 0], tx))
        start(remote(o_ref.at[s, B], o_ref.at[s, B], hs.at[k, 1], hr.at[k, 1], ty))
        sib(s, None)
    order = [0, 1, 3, 2]
    zz = [lax.rem(z + k, 4) for k in range(4)]
    second(0, zz[0])
    first(1, zz[1])
    second(1, zz[1])
    first(3, zz[3])
    third(0, zz[0])
    second(3, zz[3])
    first(2, zz[2])
    third(1, zz[1])
    second(2, zz[2])
    third(3, zz[3])
    third(2, zz[2])
    nb2 = [0]
    def got(part):
        i = nb2[0]; nb2[0] += 1
        ref = w_ref if part is None else w_ref.at[part]
        o = o_ref.at[me] if part is None else o_ref.at[me, part]
        remote(ref, o, bs.at[i], br.at[i], tc).wait_recv()
    got(None)
    def g2(): got(A); got(B)
    def g3(): got(A); got(B); got(A); got(B)
    def g1(): got(None)
    g2(); g1(); g2(); g1(); g3(); g2(); g1(); g3(); g2(); g3(); g3()
    def end(j, carry):
        t = lax.rem(me + j, n)
        remote(ask_ref.at[t], served_ref.at[me], small_s.at[0, j], small_r.at[0, j], t).wait()
        remote(num_ref, nums_ref.at[me], small_s.at[1, j], small_r.at[1, j], t).wait()
        return carry
    lax.fori_loop(1, n, end, 0)
    for cp in pend:
        cp.wait_send()
    mine.wait(); mine2.wait(); mine3.wait()

def gather_weights(w, ask, num, cid):
    n = 32
    rows = w.shape[0]
    D = pltpu.SemaphoreType.DMA
    sib = 1 + 4 * 2 + 3 + 4 * 4
    anyspec = pl.BlockSpec(memory_space=pl.ANY)
    return pl.pallas_call(
        gather_kernel,
        out_shape=(jax.ShapeDtypeStruct((n, rows, 128), w.dtype), jax.ShapeDtypeStruct(ask.shape, ask.dtype), jax.ShapeDtypeStruct((n,) + num.shape, num.dtype)),
        in_specs=[anyspec] * 3, out_specs=(anyspec,) * 3,
        scratch_shapes=[D((3,)), D((2, n)), D((2, n)), D((4,)), D((4,)), D((4, 2)), D((4, 2)), D((4, 2)), D((4, 2)), D((4, 2)), D((4, 2)), D((sib,)), D((sib,))],
        compiler_params=pltpu.CompilerParams(collective_id=cid, has_side_effects=True),
    )(w, ask, num)


def accumulate(dst, src, rows):
    step = 80
    whole = rows // step
    def body(i, carry):
        at = pl.ds(pl.multiple_of(i * step, 8), step)
        dst[at] = dst[at] + src[at]
        return carry
    lax.fori_loop(0, whole, body, 0)
    if rows % step:
        at = pl.ds(whole * step, rows % step)
        dst[at] = dst[at] + src[at]

def reduce_kernel(share_rows, lead, g_ref, err_ref, o_ref, sq_ref, errs_ref, L, R, YA, XA, XB, YB, Z, sq, own, ls, rs0_s, rs0_r, as1, ar1, as2, ar2, bs1, br1, bs2, br2, zs, zr, es, er, qs, qr):
    n = 32
    me = lax.axis_index('dev')
    c, x, y, z = lax.rem(me, 2), lax.rem(me // 2, 2), lax.rem(me // 4, 2), me // 8
    rows = L.shape[2]
    half = rows // 2
    A, B = pl.ds(0, half), pl.ds(half, half)
    def dev(z, y, x, c):
        return ((z * 2 + y) * 2 + x) * 2 + c
    def begin(d):
        return pl.multiple_of((lead + share_rows * d) // 8 * 8, 8)
    greet(n, me)
    tx, ty, tc = dev(z, y, 1 - x, c), dev(z, 1 - y, x, c), dev(z, y, x, 1 - c)
    pend = []
    def start(cp):
        cp.start(); pend.append(cp)
    order = [1, 2, 3, 0]
    zz = [lax.rem(z + k, 4) for k in range(4)]
    for k in order:
        for i in range(4):
            ys, xs = i // 2, i % 2
            start(remote(g_ref.at[pl.ds(begin(dev(zz[k], ys, xs, 1 - c)), rows)], R.at[k, i], rs0_s.at[k, i], rs0_r.at[k, i], tc))
            pltpu.make_async_copy(g_ref.at[pl.ds(begin(dev(zz[k], ys, xs, c)), rows)], L.at[k, i], ls.at[k, i]).start()
    e_own = pltpu.make_async_copy(err_ref, errs_ref.at[me], own.at[0])
    e_own.start()
    def go(j, carry):
        t = lax.rem(me + j, n)
        remote(err_ref, errs_ref.at[me], es.at[j], er.at[j], t).start()
        return carry
    lax.fori_loop(1, n, go, 0)
    i_own, i_x, i_y = y * 2 + x, y * 2 + 1 - x, (1 - y) * 2 + x
    def s0(k):
        for i in range(4):
            pltpu.make_async_copy(g_ref.at[pl.ds(0, rows)], L.at[k, i], ls.at[k, i]).wait()
            remote(L.at[k, i], R.at[k, i], rs0_s.at[k, i], rs0_r.at[k, i], tc).wait_recv()
            accumulate(L.at[k, i], R.at[k, i], rows)
        for j in range(2):
            start(remote(L.at[k, (1 - y) * 2 + j, A], YA.at[k, j], as1.at[k, j], ar1.at[k, j], ty))
            start(remote(L.at[k, j * 2 + 1 - x, B], XB.at[k, j], bs1.at[k, j], br1.at[k, j], tx))
    def mid(k):
        for j in range(2):
            remote(L.at[k, 0, A], YA.at[k, j], as1.at[k, j], ar1.at[k, j], ty).wait_recv()
            accumulate(L.at[k, y * 2 + j, A], YA.at[k, j], half)
        start(remote(L.at[k, i_x, A], XA.at[k], as2.at[k], ar2.at[k], tx))
        for j in range(2):
            remote(L.at[k, 0, B], XB.at[k, j], bs1.at[k, j], br1.at[k, j], tx).wait_recv()
            accumulate(L.at[k, j * 2 + x, B], XB.at[k, j], half)
        start(remote(L.at[k, i_y, B], YB.at[k], bs2.at[k], br2.at[k], ty))
    def fin(k):
        remote(L.at[k, 0, A], XA.at[k], as2.at[k], ar2.at[k], tx).wait_recv()
        accumulate(L.at[k, i_own, A], XA.at[k], half)
        remote(L.at[k, 0, B], YB.at[k], bs2.at[k], br2.at[k], ty).wait_recv()
        accumulate(L.at[k, i_own, B], YB.at[k], half)
        if k:
            start(remote(L.at[k, i_own], Z.at[k - 1], zs.at[k - 1], zr.at[k - 1], dev(zz[k], y, x, c)))
    s0(1)
    s0(2)
    mid(1)
    s0(3)
    mid(2)
    fin(1)
    s0(0)
    mid(3)
    fin(2)
    mid(0)
    fin(3)
    fin(0)
    for k in range(3):
        remote(L.at[0, 0], Z.at[k], zs.at[k], zr.at[k], tc).wait_recv()
    first = lax.rem(lead + share_rows * me, 8)
    sq[...] = jnp.zeros_like(sq)
    mine = L.at[0, i_own]
    def total(i, carry):
        r = pl.multiple_of(i * 8, 8)
        at = pl.ds(r, 8)
        v = mine[at] + Z[0, at] + (Z[1, at] + Z[2, at])
        o_ref[at] = v
        row = r + lax.broadcasted_iota(jnp.int32, (8, 128), 0)
        inside = (row >= first) & (row < first + share_rows)
        v = jnp.where(inside, v, 0.0)
        sq[...] += v * v
        return carry
    lax.fori_loop(0, rows // 8, total, 0)
    q_own = pltpu.make_async_copy(sq, sq_ref.at[me], own.at[1])
    q_own.start()
    def go2(j, carry):
        t = lax.rem(me + j, n)
        remote(sq, sq_ref.at[me], qs.at[j], qr.at[j], t).start()
        return carry
    lax.fori_loop(1, n, go2, 0)
    for cp in pend:
        cp.wait_send()
    def end(j, carry):
        t = lax.rem(me + j, n)
        remote(err_ref, errs_ref.at[me], es.at[j], er.at[j], t).wait()
        remote(sq, sq_ref.at[me], qs.at[j], qr.at[j], t).wait()
        return carry
    lax.fori_loop(1, n, end, 0)
    e_own.wait()
    q_own.wait()

def reduce_gradient(g, err, share_rows, lead, rows, cid):
    n = 32
    D = pltpu.SemaphoreType.DMA
    anyspec = pl.BlockSpec(memory_space=pl.ANY)
    vm = pl.BlockSpec(memory_space=pltpu.VMEM)
    half = rows // 2
    F = lambda *s: pltpu.VMEM(s + (128,), jnp.float32)
    return pl.pallas_call(
        functools.partial(reduce_kernel, share_rows, lead),
        out_shape=(jax.ShapeDtypeStruct((rows, 128), jnp.float32), jax.ShapeDtypeStruct((n, 8, 128), jnp.float32), jax.ShapeDtypeStruct((n, 8, 128), jnp.float32)),
        in_specs=[anyspec, vm], out_specs=(vm, vm, vm),
        scratch_shapes=[F(4, 4, rows), F(4, 4, rows), F(4, 2, half), F(4, half), F(4, 2, half), F(4, half), F(3, rows), F(8),
            D((2,)), D((4, 4)), D((4, 4)), D((4, 4)), D((4, 2)), D((4, 2)), D((4,)), D((4,)), D((4, 2)), D((4, 2)), D((4,)), D((4,)), D((3,)), D((3,)), D((n,)), D((n,)), D((n,)), D((n,))],
        compiler_params=pltpu.CompilerParams(collective_id=cid, has_side_effects=True, vmem_limit_bytes=48 << 20),
    )(g, err)


F32, BF16 = jnp.float32, jnp.bfloat16
VMEM_LIMIT = 56 << 20


def mm(a, b):
    return jnp.dot(a, b, preferred_element_type=F32)


def mm_nt(a, b):
    return lax.dot_general(a, b, (((1,), (1,)), ((), ())), preferred_element_type=F32)


def mm_tn(a, b):
    return lax.dot_general(a, b, (((0,), (0,)), ((), ())), preferred_element_type=F32)


def col(v):
    return jnp.sum(v, axis=0, keepdims=True)


def pick(slots, first, rows):
    r = first + lax.broadcasted_iota(jnp.int32, (slots.shape[0], rows), 1)
    return jnp.where(slots == r, 1.0, 0.0).astype(BF16)


def place(slots, first, rows):
    r = first + lax.broadcasted_iota(jnp.int32, (rows, slots.shape[1]), 0)
    return jnp.where(slots == r, 1.0, 0.0).astype(BF16)


def activate(pre):
    sigma = jax.nn.sigmoid(pre)
    return sigma, (pre * sigma).astype(BF16)


def normalize(post):
    centred = post - jnp.mean(post, axis=-1, keepdims=True)
    inv = lax.rsqrt(jnp.mean(centred * centred, axis=-1, keepdims=True) + norm_eps)
    return centred * inv, inv


def forward(us, w_in, w_out, vec):
    pre = vec[0:1, :]
    at = 0
    for u in us:
        pre = pre + mm(u, w_in[at : at + u.shape[1], :])
        at += u.shape[1]
    _, act = activate(pre)
    post = mm(act, w_out[...]) + vec[1:2, :]
    hat, inv = normalize(post)
    return hat * vec[2:3, :] + vec[3:4, :], pre, hat, inv


def norm_back(g, hat, inv, gain):
    s = g * gain
    return inv * (
        s - jnp.mean(s, axis=-1, keepdims=True) - hat * jnp.mean(s * hat, axis=-1, keepdims=True)
    )


def back(us, g_post, pre, w_out, d_in, d_out, d_vec):
    low = g_post.astype(BF16)
    sigma, act = activate(pre)
    d_out[...] += mm_tn(act, low)
    d_vec[1:2, : low.shape[1]] += col(low.astype(F32))
    g_act = mm_nt(low, w_out[...])
    g_pre = (g_act * sigma * (1.0 + pre * (1.0 - sigma))).astype(BF16)
    d_vec[0:1, :] += col(g_pre.astype(F32))
    at = 0
    for u in us:
        d_in[at : at + u.shape[1], :] += mm_tn(u, g_pre)
        at += u.shape[1]
    return g_pre


def pack(packed, lead, rows_in, d_in, d_out, d_vec):
    at = lead
    def matrix(ref, rows, at):
        for j in range(4):
            packed[pl.ds(at + j, rows, stride=4), :] = ref[:rows, 128 * j : 128 * (j + 1)]
        return at + 4 * rows
    def vector(i, at):
        for j in range(4):
            packed[at + j : at + j + 1, :] = d_vec[i : i + 1, 128 * j : 128 * (j + 1)]
        return at + 4
    at = matrix(d_in, rows_in, at)
    at = vector(0, at)
    if d_out is not None:
        at = matrix(d_out, d_out.shape[0], at)
        for i in (1, 2, 3):
            at = vector(i, at)
    return at


def clear(*refs):
    for ref in refs:
        ref[...] = jnp.zeros_like(ref)


def spec(shape, fixed=True):
    if fixed:
        return pl.BlockSpec(shape, lambda i: (0,) * len(shape))
    return pl.BlockSpec(shape, lambda i: (i,) + (0,) * (len(shape) - 1))


def params(**more):
    return pltpu.CompilerParams(vmem_limit_bytes=VMEM_LIMIT, **more)


def shaped(*shape, dtype=F32):
    return jax.ShapeDtypeStruct(shape, dtype)


ANY = pl.BlockSpec(memory_space=pl.ANY)


def encode_kernel(bm, x, w_in, w_out, vec, want, node, low, pre, hat, inv, out, acc):
    i = pl.program_id(0)
    r, p, h, v = forward([x[...]], w_in, w_out, vec)
    node[...] = r
    low[...] = r.astype(BF16)
    pre[...], hat[...], inv[...] = p, h, v
    send_rows(i, bm, low[...], want, out, acc)


def send_rows(i, bm, low, want, out, acc):
    @pl.when(i == 0)
    def _():
        clear(acc)
    acc[...] += mm(pick(want[...], i * bm, bm), low)
    @pl.when(i == pl.num_programs(0) - 1)
    def _():
        out[...] = acc[...].astype(BF16)


def kept_shapes(rows):
    return (shaped(rows, LATENT), shaped(rows, LATENT), shaped(rows, 1))


def kept_specs(bm):
    return (spec((bm, LATENT), False), spec((bm, LATENT), False), spec((bm, 1), False))


def encode(x, block, want, bm=256):
    rows, k = x.shape
    slots = want.shape[0]
    w_in, w_out, vec = block
    return pl.pallas_call(
        functools.partial(encode_kernel, bm),
        grid=(rows // bm,),
        out_shape=(shaped(rows, LATENT), shaped(rows, LATENT, dtype=BF16)) + kept_shapes(rows) + (shaped(slots, LATENT, dtype=BF16),),
        in_specs=[spec((bm, k), False), spec(w_in.shape), spec(w_out.shape), spec(vec.shape), spec((slots, 1))],
        out_specs=(spec((bm, LATENT), False), spec((bm, LATENT), False)) + kept_specs(bm) + (spec((slots, LATENT)),),
        scratch_shapes=[pltpu.VMEM((slots, LATENT), F32)],
        compiler_params=params(),
        name="encode",
    )(x, w_in, w_out, vec, want)


def node_kernel(bm, served, want, landed, node, low, w_in, w_out, vec, node_new, low_new, sums, pre, hat, inv, out, acc):
    i = pl.program_id(0)
    got = mm(place(served[...], i * bm, bm), landed[...]).astype(BF16)
    sums[...] = got
    r, p, h, v = forward([low[...], got], w_in, w_out, vec)
    r = node[...] + r
    node_new[...] = r
    low_new[...] = r.astype(BF16)
    pre[...], hat[...], inv[...] = p, h, v
    send_rows(i, bm, low_new[...], want, out, acc)


def node_forward(served, want, landed, node, low, block, bm=256):
    rows = node.shape[0]
    slots = want.shape[0]
    w_in, w_out, vec = block
    b = lambda: spec((bm, LATENT), False)
    return pl.pallas_call(
        functools.partial(node_kernel, bm),
        grid=(rows // bm,),
        out_shape=(shaped(rows, LATENT), shaped(rows, LATENT, dtype=BF16), shaped(rows, LATENT, dtype=BF16)) + kept_shapes(rows) + (shaped(slots, LATENT, dtype=BF16),),
        in_specs=[spec((1, slots)), spec((slots, 1)), spec((slots, LATENT)), b(), b(), spec(w_in.shape), spec(w_out.shape), spec(vec.shape)],
        out_specs=(b(), b(), b()) + kept_specs(bm) + (spec((slots, LATENT)),),
        scratch_shapes=[pltpu.VMEM((slots, LATENT), F32)],
        compiler_params=params(),
        name="node_forward",
    )(served, want, landed, node, low, w_in, w_out, vec)


def edge_kernel(first, pos, pos_r, arrived, source, w_in, w_out, vec, *rest):
    if first:
        g_in, g_out, g_vec, edge_new, buffer, edge_low, sent, recv, pre, hat, inv, g_pre, g_hat, g_inv = rest
        edge, p, h, v = forward([source[...]], g_in, g_out, g_vec)
        g_pre[...], g_hat[...], g_inv[...] = p, h, v
    else:
        edge_new, buffer, edge_low, sent, recv, pre, hat, inv = rest
        edge = source[...]
    slots = arrived.shape[0]
    e = edge.astype(BF16)
    s = mm(pick(pos[:, 0:1], 0, slots), arrived[...]).astype(BF16)
    r = mm(pick(pos[:, 1:2], 0, slots), arrived[...]).astype(BF16)
    edge_low[...], sent[...], recv[...] = e, s, r
    out, p, h, v = forward([e, s, r], w_in, w_out, vec)
    new = edge + out
    edge_new[...] = new
    pre[...], hat[...], inv[...] = p, h, v
    buffer[...] = mm(place(pos_r[...], 0, slots), new.astype(BF16)).astype(BF16)


def edge_forward(pos, pos_r, arrived, source, block, geo=None):
    rows = source.shape[0]
    slots = arrived.shape[0]
    kept = kept_shapes(rows)
    return pl.pallas_call(
        functools.partial(edge_kernel, geo is not None),
        out_shape=(shaped(rows, LATENT), shaped(slots, LATENT, dtype=BF16)) + (shaped(rows, LATENT, dtype=BF16),) * 3 + kept + (kept if geo is not None else ()),
        compiler_params=params(),
        name="edge_forward",
    )(pos, pos_r, arrived, source, *block, *(geo or ()))


def decode_kernel(bm, at, x, target, level, land, count, low, w_in, w_out, vec, flat, g_node, d_out_o, d_vec_o, err_o, packed, d_in, d_out, d_vec, err, sem):
    i = pl.program_id(0)
    @pl.when(i == 0)
    def _():
        clear(d_in, d_out, d_vec, err)
    u = low[...]
    pre = vec[0:1, :] + mm(u, w_in[...])
    _, act = activate(pre)
    wide = w_out.shape[1]
    post = mm(act, w_out[...]) + vec[1:2, :wide]
    sea = (lax.broadcasted_iota(jnp.int32, (1, VARS), 1) < SEA_VARS).astype(F32)
    mask = level[...].astype(F32) * (1.0 - land[...].astype(F32) * sea)
    residual = x[...].astype(F32) + post[:, :VARS] - target[...]
    divisor = jnp.maximum(count[...], 1.0)
    err[:, :VARS] += col(mask * residual * residual)
    g = 2.0 * mask * residual / divisor
    g_low = jnp.concatenate([g, jnp.zeros((bm, wide - VARS), F32)], axis=1)
    g_pre = back([u], g_low, pre, w_out, d_in, d_out, d_vec)
    g_node[...] = mm_nt(g_pre, w_in[...])
    @pl.when(i == pl.num_programs(0) - 1)
    def _():
        d_out_o[...] = d_out[...]
        d_vec_o[...] = d_vec[...]
        err_o[...] = err[...]
        for j in range(4):
            packed[pl.ds(j, LATENT, stride=4), :] = d_in[:, 128 * j : 128 * (j + 1)]
        cp = pltpu.make_async_copy(packed, flat.at[pl.ds(at, 4 * LATENT)], sem)
        cp.start()
        cp.wait()


def decode(x, target, level, land, count, low, block, flat_rows, at, bm=256):
    rows = low.shape[0]
    w_in, w_out, vec = block
    wide = w_out.shape[1]
    v = lambda: spec((bm, VARS), False)
    return pl.pallas_call(
        functools.partial(decode_kernel, bm, at),
        grid=(rows // bm,),
        out_shape=(shaped(flat_rows, 128), shaped(rows, LATENT), shaped(LATENT, wide), shaped(8, LATENT), shaped(1, wide)),
        in_specs=[v(), v(), v(), spec((bm, 1), False), spec((1, 1)), spec((bm, LATENT), False), spec(w_in.shape), spec(w_out.shape), spec(vec.shape)],
        out_specs=(ANY, spec((bm, LATENT), False), spec((LATENT, wide)), spec((8, LATENT)), spec((1, wide))),
        scratch_shapes=[pltpu.VMEM((4 * LATENT, 128), F32), pltpu.VMEM((LATENT, LATENT), F32), pltpu.VMEM((LATENT, wide), F32), pltpu.VMEM((8, LATENT), F32), pltpu.VMEM((1, wide), F32), pltpu.SemaphoreType.DMA],
        compiler_params=params(),
        name="decode",
    )(x, target, level, land, count, low, w_in, w_out, vec)


def layer_norm_back(g, hat, inv, vec, d_vec):
    d_vec[2:3, :] += col(g * hat)
    d_vec[3:4, :] += col(g)
    return norm_back(g, hat, inv, vec[2:3, :])


def node_back_kernel(bm, at, landed_given, tail_at, served, want, g_node, low, sums, pre, hat, inv, w_in, w_out, vec, flat_in, extra, flat, g_prev, out, packed, d_in, d_out, d_vec, acc, sem):
    i = pl.program_id(0)
    @pl.when(i == 0)
    def _():
        clear(d_in, d_out, d_vec, acc)
        if tail_at is not None:
            pltpu.make_async_copy(extra, flat.at[pl.ds(tail_at, extra.shape[0])], sem.at[0]).start()
    g = g_node[...]
    if landed_given:
        g = g + mm(place(served[...], i * bm, bm), extra[...])
    g_post = layer_norm_back(g, hat[...], inv[...], vec, d_vec)
    u, s = low[...], sums[...]
    g_pre = back([u, s], g_post, pre[...], w_out, d_in, d_out, d_vec)
    g_prev[...] = g + mm_nt(g_pre, w_in[:LATENT, :])
    g_sum = mm_nt(g_pre, w_in[LATENT:, :]).astype(BF16)
    send_rows(i, bm, g_sum, want, out, acc)
    @pl.when(i == pl.num_programs(0) - 1)
    def _():
        pack(packed, 0, 2 * LATENT, d_in, d_out, d_vec)
        cp = pltpu.make_async_copy(packed, flat.at[pl.ds(at, packed.shape[0])], sem.at[1])
        cp.start()
        if tail_at is not None:
            pltpu.make_async_copy(extra, flat.at[pl.ds(tail_at, extra.shape[0])], sem.at[0]).wait()
        cp.wait()


def node_backward(served, want, g_node, low, sums, kept, block, flat, at, landed=None, tail=None, tail_at=None, bm=256):
    rows = low.shape[0]
    slots = want.shape[0]
    w_in, w_out, vec = block
    b = lambda: spec((bm, LATENT), False)
    extra = landed if landed is not None else tail
    return pl.pallas_call(
        functools.partial(node_back_kernel, bm, at, landed is not None, tail_at),
        grid=(rows // bm,),
        out_shape=(shaped(*flat.shape), shaped(rows, LATENT), shaped(slots, LATENT, dtype=BF16)),
        in_specs=[spec((1, slots)), spec((slots, 1)), b(), b(), b()] + list(kept_specs(bm)) + [spec(w_in.shape), spec(w_out.shape), spec(vec.shape), ANY, spec(extra.shape)],
        out_specs=(ANY, b(), spec((slots, LATENT))),
        scratch_shapes=[pltpu.VMEM((8 * LATENT + 4 * LATENT + 16, 128), F32), pltpu.VMEM((2 * LATENT, LATENT), F32), pltpu.VMEM((LATENT, LATENT), F32), pltpu.VMEM((8, LATENT), F32), pltpu.VMEM((slots, LATENT), F32), pltpu.SemaphoreType.DMA((2,))],
        input_output_aliases={11: 0},
        compiler_params=params(),
        name="node_backward",
    )(served, want, g_node, low, sums, *kept, w_in, w_out, vec, flat, extra)


def edge_back_kernel(at, has_edge, geo_at, pos, pos_s, pos_r, returned, edge_low, sent, recv, pre, hat, inv, w_in, w_out, vec, flat_in, *rest):
    rest = list(rest)
    g_edge = rest.pop(0) if has_edge else None
    if geo_at is not None:
        geo, g_pre, g_hat, g_inv, g_out, g_vec = rest[:6]
        rest = rest[6:]
    flat, edge_prev, buffer, packed, d_in, d_out, d_vec, sem = rest[:8]
    slots = returned.shape[0]
    clear(d_in, d_out, d_vec)
    g = mm(pick(pos[:, 1:2], 0, slots), returned[...])
    if has_edge:
        g = g_edge[...] + g
    g_post = layer_norm_back(g, hat[...], inv[...], vec, d_vec)
    p = back([edge_low[...], sent[...], recv[...]], g_post, pre[...], w_out, d_in, d_out, d_vec)
    prev = g + mm_nt(p, w_in[:LATENT, :])
    edge_prev[...] = prev
    s = mm_nt(p, w_in[LATENT : 2 * LATENT, :]).astype(BF16)
    r = mm_nt(p, w_in[2 * LATENT :, :]).astype(BF16)
    buffer[...] = (mm(place(pos_s[...], 0, slots), s) + mm(place(pos_r[...], 0, slots), r)).astype(BF16)
    pack(packed, 0, 3 * LATENT, d_in, d_out, d_vec)
    cp = pltpu.make_async_copy(packed, flat.at[pl.ds(at, packed.shape[0])], sem.at[0])
    cp.start()
    if geo_at is not None:
        packed2, c_in, c_out, c_vec = rest[8:]
        clear(c_in, c_out, c_vec)
        g_post = layer_norm_back(prev, g_hat[...], g_inv[...], g_vec, c_vec)
        back([geo[...]], g_post, g_pre[...], g_out, c_in, c_out, c_vec)
        pack(packed2, 0, GEO, c_in, c_out, c_vec)
        cp2 = pltpu.make_async_copy(packed2, flat.at[pl.ds(geo_at, packed2.shape[0])], sem.at[1])
        cp2.start()
        cp2.wait()
    cp.wait()


def edge_backward(pos, pos_s, pos_r, returned, ins, kept, block, flat, at, g_edge=None, geo=None, geo_at=None):
    rows = pos.shape[0]
    slots = returned.shape[0]
    V = pl.BlockSpec(memory_space=pltpu.VMEM)
    args = [pos, pos_s, pos_r, returned, *ins, *kept, *block, flat]
    which = len(args) - 1
    if g_edge is not None:
        args.append(g_edge)
    scratch = [pltpu.VMEM((12 * LATENT + 4 * LATENT + 16, 128), F32), pltpu.VMEM((3 * LATENT, LATENT), F32), pltpu.VMEM((LATENT, LATENT), F32), pltpu.VMEM((8, LATENT), F32), pltpu.SemaphoreType.DMA((2,))]
    if geo is not None:
        args += geo
        wide = geo[0].shape[1]
        scratch += [pltpu.VMEM((4 * GEO + 4 * LATENT + 16, 128), F32), pltpu.VMEM((wide, LATENT), F32), pltpu.VMEM((LATENT, LATENT), F32), pltpu.VMEM((8, LATENT), F32)]
    return pl.pallas_call(
        functools.partial(edge_back_kernel, at, g_edge is not None, geo_at),
        out_shape=(shaped(*flat.shape), shaped(rows, LATENT), shaped(slots, LATENT, dtype=BF16)),
        in_specs=[ANY if i == which else V for i in range(len(args))],
        out_specs=(ANY, V, V),
        scratch_shapes=scratch,
        input_output_aliases={which: 0},
        compiler_params=params(),
        name="edge_backward",
    )(*args)


def encode_back_kernel(bm, served, landed, g_node, x, pre, hat, inv, w_out, vec, flat_in, flat, packed, d_in, d_out, d_vec, sem):
    i = pl.program_id(0)
    @pl.when(i == 0)
    def _():
        clear(d_in, d_out, d_vec)
    g = g_node[...] + mm(place(served[...], i * bm, bm), landed[...])
    g_post = layer_norm_back(g, hat[...], inv[...], vec, d_vec)
    back([x[...]], g_post, pre[...], w_out, d_in, d_out, d_vec)
    @pl.when(i == pl.num_programs(0) - 1)
    def _():
        packed[0:4, :] = jnp.zeros((4, 128), F32)
        pack(packed, 4, VARS, d_in, d_out, d_vec)
        cp = pltpu.make_async_copy(packed, flat.at[pl.ds(0, packed.shape[0])], sem)
        cp.start()
        cp.wait()


def encode_backward(served, landed, g_node, x, kept, block, flat, bm=256):
    rows, k = x.shape
    slots = landed.shape[0]
    w_in, w_out, vec = block
    return pl.pallas_call(
        functools.partial(encode_back_kernel, bm),
        grid=(rows // bm,),
        out_shape=shaped(*flat.shape),
        in_specs=[spec((1, slots)), spec((slots, LATENT)), spec((bm, LATENT), False), spec((bm, k), False)] + list(kept_specs(bm)) + [spec(w_out.shape), spec(vec.shape), ANY],
        out_specs=ANY,
        scratch_shapes=[pltpu.VMEM((4 + 4 * VARS + 4 * LATENT + 16, 128), F32), pltpu.VMEM((k, LATENT), F32), pltpu.VMEM((LATENT, LATENT), F32), pltpu.VMEM((8, LATENT), F32), pltpu.SemaphoreType.DMA],
        input_output_aliases={9: 0},
        compiler_params=params(),
        name="encode_backward",
    )(served, landed, g_node, x, *kept, w_out, vec, flat)


def make_asks(edge_owners, edge_local, devices):
    edges_here = edge_owners.shape[0]
    capacity = (5 * edges_here // (2 * devices) + 7) // 8 * 8
    owner = edge_owners.reshape(-1)
    local = edge_local.reshape(-1)
    wants = owner.shape[0]
    order = jnp.arange(wants, dtype=jnp.int32)
    before = (owner[:, None] == owner[None, :]) & (order[None, :] < order[:, None])
    ranking = jnp.sum(before.astype(jnp.int32), axis=1)
    position = owner * capacity + ranking
    slots = jnp.arange(devices * capacity, dtype=jnp.int32)
    asking = jnp.sum(jnp.where(slots[:, None] == position[None, :], local[None, :] + 1, 0), axis=1) - 1
    return (position, asking, capacity)


def widen(values, width):
    return jnp.pad(values, ((0, 0), (0, width - values.shape[1])))


def make_block(params):
    rows = params["w_in"].shape[0]
    w_in = jnp.pad(params["w_in"], ((0, -rows % 128), (0, 0)))
    w_out = widen(params["w_out"], (params["w_out"].shape[1] + 127) // 128 * 128)
    names = [name for name in ("b_in", "b_out", "gain", "shift") if name in params]
    vectors = [widen(params[name][None], LATENT) for name in names]
    vectors.append(jnp.zeros((8 - len(vectors), LATENT), jnp.bfloat16))
    return (w_in, w_out, jnp.concatenate(vectors).astype(jnp.float32))


def local(
    inputs,
    targets,
    geometry,
    land_sea,
    level_mask,
    edge_owners,
    edge_local,
    step_count,
    master,
    first_moment,
    second_moment,
    ema,
):
    segments, total = layout(LATENT, VARS, GEO, LAYERS)
    devices = lax.axis_size("dev")
    share = master.shape[0]
    mine = devices == 32 and share % 128 == 0
    ocean = (jnp.arange(VARS) < SEA_VARS).astype(jnp.float32)
    position, asking, capacity = make_asks(edge_owners, edge_local, devices)
    slots = devices * capacity
    counted = jnp.sum(level_mask * (1 - land_sea[:, None] * ocean.astype(jnp.int32)[None, :])).astype(jnp.float32)
    if mine:
        share_rows = share // 128
        pad_rows = (share_rows + 31) // 32 * 32
        low = jnp.pad(master.astype(jnp.bfloat16).reshape(share_rows, 128), ((0, pad_rows - share_rows), (0, 0)))
        ask = jnp.pad(asking.reshape(devices, 1, capacity), ((0, 0), (0, 0), (0, 128 - capacity)))
        number = jnp.zeros((8, 128), jnp.float32).at[0, 0].set(counted)
        gathered, served, numbers = gather_weights(low, ask, number, 1)
        full_weights = gathered[:, :share_rows].reshape(-1)
        served = served[:, 0, :capacity].reshape(-1)
        count = jnp.sum(numbers)
    else:
        full_weights = lax.all_gather(master.astype(jnp.bfloat16), "dev", axis=0, tiled=True)
        served = lax.all_to_all(asking.reshape(devices, capacity), "dev", 0, 0, tiled=True).reshape(-1)
        count = lax.psum(counted, "dev")
    blocks = [make_block(b) for b in unpack(full_weights, segments)]
    want = served[:, None]
    served = served[None, :]
    pos = position.reshape(-1, 2)
    pos_s, pos_r = pos[:, 0][None, :], pos[:, 1][None, :]

    def exchange(rows):
        return a2a(rows.reshape(devices, capacity, LATENT), 0).reshape(slots, LATENT)

    x = widen(inputs, 256)
    geo = widen(geometry, 128)
    node, low, *enc_kept, outgoing = encode(x, blocks[0], want)
    node_kept, edge_kept = [], []
    edge = geo
    for k in range(LAYERS):
        arrived = exchange(outgoing)
        edge, buffer, *kept = edge_forward(pos, pos_r, arrived, edge, blocks[2 + 2 * k], blocks[1] if k == 0 else None)
        edge_kept.append((kept[:3], kept[3:6]))
        if k == 0:
            geo_kept = kept[6:]
        landed = exchange(buffer)
        before = low
        node, low, sums, *kept, outgoing = node_forward(served, want, landed, node, low, blocks[3 + 2 * k])
        node_kept.append((before, sums, kept))
    pieces = [4 * s for s in (VARS + LATENT + 4, GEO + LATENT + 4) + (3 * LATENT + LATENT + 4, 2 * LATENT + LATENT + 4) * LAYERS]
    lead = 4
    places = [0] + [lead + sum(pieces[: i + 1]) for i in range(len(pieces))]
    flat_rows = (lead + PARAMS // 128 + 15) // 16 * 16 + 8
    dec_at = places[-1]
    tail_at = dec_at + 4 * LATENT
    flat, g_node, d_out, d_vec, errors = decode(
        inputs, targets, level_mask, land_sea[:, None], count.reshape(1, 1), low, blocks[-1], flat_rows, dec_at
    )
    error_here = jnp.sum(errors)
    tail = jnp.concatenate([d_vec[0], d_out[:, :VARS].reshape(-1), d_vec[1, :VARS]])
    tail_rows = flat_rows - tail_at
    tail = jnp.pad(tail, (0, tail_rows * 128 - tail.shape[0])).reshape(tail_rows, 128)
    landed, g_edge = None, None
    for k in reversed(range(LAYERS)):
        before, sums, kept = node_kept[k]
        more = dict(landed=landed) if landed is not None else dict(tail=tail, tail_at=tail_at)
        flat, g_node, outgoing = node_backward(served, want, g_node, before, sums, kept, blocks[3 + 2 * k], flat, places[3 + 2 * k], **more)
        returned = exchange(outgoing)
        ins, kept = edge_kept[k]
        more = dict(geo=[geo, *geo_kept, blocks[1][1], blocks[1][2]], geo_at=places[1]) if k == 0 else {}
        flat, g_edge, buffer = edge_backward(pos, pos_s, pos_r, returned, ins, kept, blocks[2 + 2 * k], flat, places[2 + 2 * k], g_edge=g_edge, **more)
        landed = exchange(buffer)
    flat = encode_backward(served, landed, g_node, x, enc_kept, blocks[0], flat)
    if mine:
        rows = (share_rows + 6 + 15) // 16 * 16
        error = jnp.zeros((8, 128), jnp.float32).at[0, 0].set(error_here)
        summed, squares, errors = reduce_gradient(flat, error, share_rows, lead, rows, 2)
        skip = lax.rem(lead + share_rows * lax.axis_index("dev"), 8)
        own_grad = lax.dynamic_slice_in_dim(summed, skip, share_rows).reshape(-1)
        grad_norm = jnp.sqrt(jnp.sum(squares))
        error_sum = jnp.sum(errors)
    else:
        own_grad = lax.psum_scatter(flat[lead : lead + PARAMS // 128].reshape(-1), "dev", scatter_dimension=0, tiled=True)
        error_sum, squares = lax.psum((error_here, jnp.sum(own_grad * own_grad)), "dev")
        grad_norm = jnp.sqrt(squares)
    loss = error_sum / jnp.maximum(count, 1.0)
    clipped = own_grad * jnp.minimum(1.0, clip_limit / grad_norm)
    step = step_count[0].astype(jnp.float32)
    new_first = beta_one * first_moment + (1.0 - beta_one) * clipped
    new_second = beta_two * second_moment + (1.0 - beta_two) * clipped * clipped
    first_hat = new_first / (1.0 - beta_one**step)
    second_hat = new_second / (1.0 - beta_two**step)
    new_master = master - learn_rate * (
        first_hat / (jnp.sqrt(second_hat) + adam_eps) + decay_rate * master
    )
    new_ema = ema_keep * ema + (1.0 - ema_keep) * new_master
    return (new_master, new_first, new_second, new_ema, loss, grad_norm)


def solution(mesh):
    in_specs = (
        P("dev", None),
        P("dev", None),
        P("dev", None),
        P("dev"),
        P("dev", None),
        P("dev", None),
        P("dev", None),
        P(),
        P("dev"),
        P("dev"),
        P("dev"),
        P("dev"),
    )
    out_specs = (P("dev"), P("dev"), P("dev"), P("dev"), P(), P())
    return jax.shard_map(local, mesh=mesh, in_specs=in_specs, out_specs=out_specs, check_vma=False)
```

time: 1870 us -> 810 us (0.43)
  Pallas kernels: 0 us -> 701 us
  waiting for transfers between devices: 657 us -> 0 us
  other arithmetic: 448 us -> 19.1 us
  local copies, waits for them, and re-layouts: 482 us -> 70.3 us
  matrix products: 112 us -> 0 us
  starting transfers between devices: 85.5 us -> 0 us
  blocking collectives: 39.8 us -> 0 us
    pallas_call x0 -> x29, Pallas kernels: none -> 701 us  [the longest x12 280 us: a2a(): pl.pallas_call(functools.partial(a2a_kernel, n), out_shape=jax.ShapeDtype...]
    psum x1 -> x0, waiting for transfers between devices: 403 us -> none  [local(): summed_grad = lax.psum(flat_grad, 'dev')]
    all_gather x1 -> x0, other arithmetic: 277 us -> none  [local(): lax.all_gather(master.astype(jnp.bfloat16), 'dev', axis=0, tiled=True)]
    concatenate x1 -> x9, local copies, waits for them, and re-layouts: 232 us -> 0.33 us  [make_block(): return (w_in, w_out, jnp.concatenate(vectors).astype(jnp.float32))]
    all_gather x1 -> x0, waiting for transfers between devices: 140 us -> none  [local(): lax.all_gather(master.astype(jnp.bfloat16), 'dev', axis=0, tiled=True)]
    all_to_all x13 -> x0, waiting for transfers between devices: 113 us -> none  [the longest x3 42.8 us: layer_forward(): lax.all_to_all(outgoing.reshape(devices, capacity, LATENT), 'dev', split_...]
    dot_general x52 -> x0, matrix products: 112 us -> none  [the longest x9 32.7 us: mlp_forward(): jnp.dot(source, params['w_in'], preferred_element_type=jnp.float32)]
    unnamed x451 -> x33, local copies, waits for them, and re-layouts: 92.2 us -> 6.18 us
  transfers between devices with their start and end apart: 15 -> 0, of which waited for: 15 -> 0; matrix products, arithmetic and copies ran while one was open for 6% -> 0% of each run, Pallas kernels for 0% -> 0%
where the time goes in v1:
time: 810 us; the launch traced here: 798 us
  Pallas kernels  701 us (87%)
  local copies, waits for them, and re-layouts  70.3 us (9%)
  other arithmetic  19.1 us (2%)
    pallas_call x12, Pallas kernels, a2a(): pl.pallas_call(functools.partial(a2a_kernel, n), out_shape=jax.ShapeDtype...  280 us
    pallas_call x1, Pallas kernels, reduce_gradient(): pl.pallas_call(functools.partial(reduce_kernel, share_rows, lead), out_sh...  149 us
    pallas_call x1, Pallas kernels, gather_weights(): pl.pallas_call(gather_kernel, out_shape=(jax.ShapeDtypeStruct((n, rows, 1...  72.3 us
    pallas_call x3, Pallas kernels, node_backward(): pl.pallas_call(functools.partial(node_back_kernel, bm, at, landed is not...  69.9 us
    pallas_call x3, Pallas kernels, node_forward(): pl.pallas_call(functools.partial(node_kernel, bm), grid=(rows // bm,), ou...  50.3 us
    slice x10, local copies, waits for them, and re-layouts, unpack(): flat[offset:offset + entries].reshape(part_shape)  36.6 us
    pallas_call x3, Pallas kernels, edge_backward(): pl.pallas_call(functools.partial(edge_back_kernel, at, g_edge is not None...  22.9 us

profile of v1, /device:TPU:27, one launch (start us, length us, event | category | flops | bytes accessed | tf_op | source)
XLA Modules:
  0.0 797.9 jit_solution(510485314119678330)
XLA Ops:
  0.6 0.8 copy.68
  3.8 1.2 convert_bitcast_fusion
  5.8 2.7 multiply_reduce_fusion
  9.7 72.3 %shard_map.163 = (bf16[32,1600,128]{2,1,0:T(8,128)(2,1)}, s32[32,1,128]{2,1,0:T(1,128)}, f32[32,8,128]{2,1,0:T(8,128)}) custom-call(bf16[1600,128]{1,0:T(8,128)(2,1)} %pad.47.w_ref, s32[32,1,128]{2,1,0:T(1,128)} %pad.48.ask_ref, f32[8,128]{1,0:T(8,128)} %scatter.6.num_ref), custom_call_target="tpu_custom_call" | custom-call | tf_op jit(solution)/shard_map/pallas_call | solution.py:207
  82.1 12.8 %reshape.270 = bf16[6545408]{0:T(1024)(128)(2,1)} reshape(bf16[32,1598,128]{2,1,0:T(8,128)(2,1)} %bitcast.49) | data formatting | bytes 26181632 | tf_op jit(solution)/shard_map/reshape | solution.py:816
  96.3 19.6 %slice.233 = bf16[12784,512]{1,0:T(8,128)(2,1)} reshape(bf16[32,1598,128]{2,1,0:T(8,128)(2,1)} %bitcast.50) | data formatting | bytes 26181632 | tf_op jit(solution)/shard_map/slice | solution.py:56
  116.0 4.7 fusion.13
  120.8 0.9 broadcast_in_dim_reshape_squeeze.8.want
  121.7 1.8 slice_select_fusion.w_in
  124.0 1.3 pad.49.x
  125.3 12.3 %encode.1 = (f32[2048,512]{1,0:T(8,128)}, bf16[2048,512]{1,0:T(8,128)(2,1)}, f32[2048,512]{1,0:T(8,128)}, f32[2048,512]{1,0:T(8,128)}, f32[2048,1]{1,0:T(8,128)}, /*index=5*/bf16[768,512]{1,0:T(8,128)(2,1)}) custom-call(bf16[2048,256]{1,0:T(8,128)(2,1)} %pad.49.x, bf16[256,512]{1,0:T(8,128)(2,1)} %slice_select_fusion.w_in, ...), custom_call_target="tpu_custom_call" | custom-call | tf_op jit(solution)/shard_map/encode/pallas_call | solution.py:493
  137.6 21.8 %shard_map.164 = bf16[32,24,512]{2,1,0:T(8,128)(2,1)} custom-call(bf16[32,24,512]{2,1,0:T(8,128)(2,1)} %bitcast.74), custom_call_target="tpu_custom_call" | custom-call | tf_op jit(solution)/shard_map/pallas_call | solution.py:92
  161.9 5.2 fusion.15
  169.3 5.3 edge_forward.3
  174.6 22.8 %shard_map.165 = bf16[32,24,512]{2,1,0:T(8,128)(2,1)} custom-call(bf16[32,24,512]{2,1,0:T(8,128)(2,1)} %bitcast.69), custom_call_target="tpu_custom_call" | custom-call | tf_op jit(solution)/shard_map/pallas_call | solution.py:92
  197.4 0.8 fusion.12
  198.9 3.9 fusion.14
  203.5 16.6 %node_forward.3 = (f32[2048,512]{1,0:T(8,128)}, bf16[2048,512]{1,0:T(8,128)(2,1)}, bf16[2048,512]{1,0:T(8,128)(2,1)}, f32[2048,512]{1,0:T(8,128)}, f32[2048,512]...) custom-call(s32[1,768]{1,0:T(1,128)} %broadcast_in_dim_reshape_squeeze.6.served, ...), custom_call_target="tpu_custom_call" | custom-call | tf_op jit(solution)/shard_map/node_forward/pallas_call | solution.py:522
  220.1 23.5 %shard_map.166 = bf16[32,24,512]{2,1,0:T(8,128)(2,1)} custom-call(bf16[32,24,512]{2,1,0:T(8,128)(2,1)} %bitcast.72), custom_call_target="tpu_custom_call" | custom-call | tf_op jit(solution)/shard_map/pallas_call | solution.py:92
  244.3 4.8 edge_forward.4
  249.1 23.5 %shard_map.167 = bf16[32,24,512]{2,1,0:T(8,128)(2,1)} custom-call(bf16[32,24,512]{2,1,0:T(8,128)(2,1)} %bitcast.70), custom_call_target="tpu_custom_call" | custom-call | tf_op jit(solution)/shard_map/pallas_call | solution.py:92
  273.3 16.6 %node_forward.4 = (f32[2048,512]{1,0:T(8,128)}, bf16[2048,512]{1,0:T(8,128)(2,1)}, bf16[2048,512]{1,0:T(8,128)(2,1)}, f32[2048,512]{1,0:T(8,128)}, f32[2048,512]...) custom-call(s32[1,768]{1,0:T(1,128)} %broadcast_in_dim_reshape_squeeze.6.served, ...), custom_call_target="tpu_custom_call" | custom-call | tf_op jit(solution)/shard_map/node_forward/pallas_call | solution.py:522
  289.9 23.5 %shard_map.168 = bf16[32,24,512]{2,1,0:T(8,128)(2,1)} custom-call(bf16[32,24,512]{2,1,0:T(8,128)(2,1)} %bitcast.73), custom_call_target="tpu_custom_call" | custom-call | tf_op jit(solution)/shard_map/pallas_call | solution.py:92
  314.1 4.8 edge_forward.5
  318.9 23.5 %shard_map.169 = bf16[32,24,512]{2,1,0:T(8,128)(2,1)} custom-call(bf16[32,24,512]{2,1,0:T(8,128)(2,1)} %bitcast.71), custom_call_target="tpu_custom_call" | custom-call | tf_op jit(solution)/shard_map/pallas_call | solution.py:92
  343.1 17.0 %node_forward.5 = (f32[2048,512]{1,0:T(8,128)}, bf16[2048,512]{1,0:T(8,128)(2,1)}, bf16[2048,512]{1,0:T(8,128)(2,1)}, f32[2048,512]{1,0:T(8,128)}, f32[2048,512]...) custom-call(s32[1,768]{1,0:T(1,128)} %broadcast_in_dim_reshape_squeeze.6.served, ...), custom_call_target="tpu_custom_call" | custom-call | tf_op jit(solution)/shard_map/node_forward/pallas_call | solution.py:522
  360.2 0.8 slice.342
  363.8 2.8 copy.79.target
  366.7 1.8 copy.80.level
  368.5 1.3 copy.81.land
  369.8 15.4 %decode.1 = (f32[51160,128]{1,0:T(8,128)}, f32[2048,512]{1,0:T(8,128)}, f32[512,256]{1,0:T(8,128)}, f32[8,512]{1,0:T(8,128)}, f32[1,256]{1,0:T(1,128)}) custom-call(bf16[2048,227]{1,0:T(8,128)(2,1)} %copy-done.1, f32[2048,227]{1,0:T(8,128)} %copy.79.target, s32[2048,227]{1,0:T(8,128)} %copy.80.level, s32[2048,1]{1,0:T(8,128)} %copy.81.land, ...), custom_call_target="tpu_custom_call" | custom-call | tf_op jit(solution)/shard_map/decode/pallas_call | solution.py:602
  385.2 1.6 reshape.284
  388.2 0.8 fusion.3.extra
  389.0 21.7 %node_backward.3 = (f32[51160,128]{1,0:T(8,128)}, f32[2048,512]{1,0:T(8,128)}, bf16[768,512]{1,0:T(8,128)(2,1)}) custom-call(s32[1,768]{1,0:T(1,128)} %broadcast_in_dim_reshape_squeeze.6.served, s32[768,1]{1,0:T(8,128)} %broadcast_in_dim_reshape_squeeze.8.want, f32[2048,512]{1,0:T(8,128)} %get-tuple-element.127.g_node, ...), custom_call_target="tpu_custom_call", output_to_operand_aliasing={{0}: (11, {})} | custom-call | tf_op jit(solution)/shard_map/node_backward/pallas_call | solution.py:652
  410.7 23.5 %shard_map.170 = bf16[32,24,512]{2,1,0:T(8,128)(2,1)} custom-call(bf16[32,24,512]{2,1,0:T(8,128)(2,1)} %bitcast.66), custom_call_target="tpu_custom_call" | custom-call | tf_op jit(solution)/shard_map/pallas_call | solution.py:92
  434.3 7.2 edge_backward.3
  441.5 23.5 %shard_map.171 = bf16[32,24,512]{2,1,0:T(8,128)(2,1)} custom-call(bf16[32,24,512]{2,1,0:T(8,128)(2,1)} %bitcast.67), custom_call_target="tpu_custom_call" | custom-call | tf_op jit(solution)/shard_map/pallas_call | solution.py:92
  465.0 24.1 %node_backward.4 = (f32[51160,128]{1,0:T(8,128)}, f32[2048,512]{1,0:T(8,128)}, bf16[768,512]{1,0:T(8,128)(2,1)}) custom-call(s32[1,768]{1,0:T(1,128)} %broadcast_in_dim_reshape_squeeze.6.served, s32[768,1]{1,0:T(8,128)} %broadcast_in_dim_reshape_squeeze.8.want, f32[2048,512]{1,0:T(8,128)} %get-tuple-element.135.g_node, ...), custom_call_target="tpu_custom_call", output_to_operand_aliasing={{0}: (11, {})} | custom-call | tf_op jit(solution)/shard_map/node_backward/pallas_call | solution.py:652
  489.1 23.5 %shard_map.172 = bf16[32,24,512]{2,1,0:T(8,128)(2,1)} custom-call(bf16[32,24,512]{2,1,0:T(8,128)(2,1)} %bitcast.68), custom_call_target="tpu_custom_call" | custom-call | tf_op jit(solution)/shard_map/pallas_call | solution.py:92
  512.6 7.4 edge_backward.4
  520.0 23.5 %shard_map.173 = bf16[32,24,512]{2,1,0:T(8,128)(2,1)} custom-call(bf16[32,24,512]{2,1,0:T(8,128)(2,1)} %bitcast.64), custom_call_target="tpu_custom_call" | custom-call | tf_op jit(solution)/shard_map/pallas_call | solution.py:92
  543.5 24.0 %node_backward.5 = (f32[51160,128]{1,0:T(8,128)}, f32[2048,512]{1,0:T(8,128)}, bf16[768,512]{1,0:T(8,128)(2,1)}) custom-call(s32[1,768]{1,0:T(1,128)} %broadcast_in_dim_reshape_squeeze.6.served, s32[768,1]{1,0:T(8,128)} %broadcast_in_dim_reshape_squeeze.8.want, f32[2048,512]{1,0:T(8,128)} %get-tuple-element.150.g_node, ...), custom_call_target="tpu_custom_call", output_to_operand_aliasing={{0}: (11, {})} | custom-call | tf_op jit(solution)/shard_map/node_backward/pallas_call | solution.py:652
  567.6 23.5 %shard_map.174 = bf16[32,24,512]{2,1,0:T(8,128)(2,1)} custom-call(bf16[32,24,512]{2,1,0:T(8,128)(2,1)} %bitcast.65), custom_call_target="tpu_custom_call" | custom-call | tf_op jit(solution)/shard_map/pallas_call | solution.py:92
  591.1 8.3 %edge_backward.5 = (f32[51160,128]{1,0:T(8,128)}, f32[256,512]{1,0:T(8,128)}, bf16[768,512]{1,0:T(8,128)(2,1)}) custom-call(s32[256,2]{1,0:T(8,128)} %copy-done, s32[1,256]{1,0:T(1,128)} %bitcast.87, s32[1,256]{1,0:T(1,128)} %bitcast.83, bf16[768,512]{1,0:T(8,128)(2,1)} %bitcast.57, ...), custom_call_target="tpu_custom_call", output_to_operand_aliasing={{0}: (13, {})} | custom-call | tf_op jit(solution)/shard_map/edge_backward/pallas_call | solution.py:712
  599.4 23.5 %shard_map.175 = bf16[32,24,512]{2,1,0:T(8,128)(2,1)} custom-call(bf16[32,24,512]{2,1,0:T(8,128)(2,1)} %bitcast.63), custom_call_target="tpu_custom_call" | custom-call | tf_op jit(solution)/shard_map/pallas_call | solution.py:92
  622.9 14.6 %encode_backward.1.g_ref = f32[51160,128]{1,0:T(8,128)} custom-call(s32[1,768]{1,0:T(1,128)} %broadcast_in_dim_reshape_squeeze.6.served, bf16[768,512]{1,0:T(8,128)(2,1)} %bitcast.51, f32[2048,512]{1,0:T(8,128)} %get-tuple-element.179.g_node, bf16[2048,256]{1,0:T(8,128)(2,1)} %pad.49.x, ...), custom_call_target="tpu_custom_call", output_to_operand_aliasing={{}: (9, {})} | custom-call | tf_op jit(solution)/shard_map/encode_backward/pallas_call | solution.py:745
  638.8 149.2 %shard_map.176 = (f32[1616,128]{1,0:T(8,128)S(1)}, f32[32,8,128]{2,1,0:T(8,128)S(1)}, f32[32,8,128]{2,1,0:T(8,128)S(1)}) custom-call(f32[51160,128]{1,0:T(8,128)} %encode_backward.1.g_ref, f32[8,128]{1,0:T(8,128)S(1)} %scatter.9.err_ref), custom_call_target="tpu_custom_call" | custom-call | tf_op jit(solution)/shard_map/pallas_call | solution.py:336
  792.0 3.4 multiply_add_fusion
  (119 shorter events, 21.0 us)
Async XLA Ops:
  116.0 4.7 copy-start.9
  116.0 5.7 copy-start.13
  116.0 7.5 copy-start.4
  123.5 37.5 %copy-start.10 = (s32[256,2]{0,1:T(2,128)S(1)}, s32[256,2]{0,1:T(2,128)}, u32[]{:S(2)}) copy-start(s32[256,2]{0,1:T(2,128)} %param.21) | copy-start | bytes 6148
  124.0 43.1 %copy-start.1 = (bf16[2048,227]{1,0:T(8,128)(2,1)}, bf16[2048,227]{1,0:T(8,128)(2,1)S(1)}, u32[]{:S(2)}) copy-start(bf16[2048,227]{1,0:T(8,128)(2,1)S(1)} %copy.78.x) | copy-start | bytes 2789380
  161.1 6.0 copy-start
  161.9 6.6 copy-start.11
  343.1 18.7 %slice-start = ((bf16[6545408]{0:T(1024)(128)(2,1)}), bf16[116224]{0:T(1024)(128)(2,1)S(1)}, s32[]{:S(2)}) async-start(bf16[6545408]{0:T(1024)(128)(2,1)} %reshape.270), calls=%async_computation | async-start | bytes 466944 | tf_op jit(solution)/shard_map/slice | solution.py:56
  343.1 20.1 %copy-start.7 = (f32[32,8,128]{2,1,0:T(8,128)S(1)}, f32[32,8,128]{2,1,0:T(8,128)}, u32[]{:S(2)}) copy-start(f32[32,8,128]{2,1,0:T(8,128)} %get-tuple-element.110) | copy-start | bytes 393220
  360.2 6.5 copy-start.2
  363.2 5.3 copy-start.8
  622.9 14.6 %copy-start.12 = (f32[1,256]{1,0:T(1,128)S(1)}, f32[1,256]{1,0:T(1,128)}, u32[]{:S(2)}) copy-start(f32[1,256]{1,0:T(1,128)} %get-tuple-element.184) | copy-start | bytes 3076
  638.8 153.3 %copy-start.3 = (f32[204544]{0:T(1024)S(1)}, f32[204544]{0:T(1024)}, u32[]{:S(2)}) copy-start(f32[204544]{0:T(1024)} %param.24) | copy-start | bytes 2454532
  638.8 153.2 %copy-start.5 = (f32[204544]{0:T(1024)S(1)}, f32[204544]{0:T(1024)}, u32[]{:S(2)}) copy-start(f32[204544]{0:T(1024)} %param.27) | copy-start | bytes 2454532
  638.8 153.2 %copy-start.6 = (f32[204544]{0:T(1024)S(1)}, f32[204544]{0:T(1024)}, u32[]{:S(2)}) copy-start(f32[204544]{0:T(1024)} %param.26) | copy-start | bytes 2454532

commit v2 on v1

--- a/solution.py
+++ b/solution.py
@@ -345,6 +345,8 @@
 
 F32, BF16 = jnp.float32, jnp.bfloat16
 VMEM_LIMIT = 56 << 20
+ANY = pl.BlockSpec(memory_space=pl.ANY)
+DMA = pltpu.SemaphoreType.DMA
 
 
 def mm(a, b):
@@ -373,68 +375,75 @@
     return jnp.where(slots == r, 1.0, 0.0).astype(BF16)
 
 
-def activate(pre):
-    sigma = jax.nn.sigmoid(pre)
-    return sigma, (pre * sigma).astype(BF16)
-
-
-def normalize(post):
-    centred = post - jnp.mean(post, axis=-1, keepdims=True)
-    inv = lax.rsqrt(jnp.mean(centred * centred, axis=-1, keepdims=True) + norm_eps)
-    return centred * inv, inv
-
-
-def forward(us, w_in, w_out, vec):
+def first_half(us, w_in, vec):
     pre = vec[0:1, :]
     at = 0
     for u in us:
         pre = pre + mm(u, w_in[at : at + u.shape[1], :])
         at += u.shape[1]
-    _, act = activate(pre)
-    post = mm(act, w_out[...]) + vec[1:2, :]
-    hat, inv = normalize(post)
-    return hat * vec[2:3, :] + vec[3:4, :], pre, hat, inv
-
-
-def norm_back(g, hat, inv, gain):
-    s = g * gain
-    return inv * (
+    return pre
+
+
+def activate(pre):
+    sigma = jax.nn.sigmoid(pre)
+    return sigma, (pre * sigma).astype(BF16)
+
+
+def normalize(post):
+    centred = post - jnp.mean(post, axis=-1, keepdims=True)
+    inv = lax.rsqrt(jnp.mean(centred * centred, axis=-1, keepdims=True) + norm_eps)
+    return centred * inv, inv
+
+
+def second_half(act, w_out, vec):
+    return normalize(mm(act, w_out[...]) + vec[1:2, :])
+
+
+def scale_shift(hat, vec):
+    return hat * vec[2:3, :] + vec[3:4, :]
+
+
+def norm_back(g, hat, inv, vec, d_vec):
+    d_vec[2:3, :] += col(g * hat)
+    d_vec[3:4, :] += col(g)
+    s = g * vec[2:3, :]
+    post = inv * (
         s - jnp.mean(s, axis=-1, keepdims=True) - hat * jnp.mean(s * hat, axis=-1, keepdims=True)
     )
-
-
-def back(us, g_post, pre, w_out, d_in, d_out, d_vec):
-    low = g_post.astype(BF16)
-    sigma, act = activate(pre)
+    return post.astype(BF16)
+
+
+def act_back(low, pre, sigma, w_out):
+    g_act = mm_nt(low, w_out[...])
+    return (g_act * sigma * (1.0 + pre * (1.0 - sigma))).astype(BF16)
+
+
+def weight_sums(us, act, low, g_pre, d_in, d_out, d_vec):
     d_out[...] += mm_tn(act, low)
     d_vec[1:2, : low.shape[1]] += col(low.astype(F32))
-    g_act = mm_nt(low, w_out[...])
-    g_pre = (g_act * sigma * (1.0 + pre * (1.0 - sigma))).astype(BF16)
     d_vec[0:1, :] += col(g_pre.astype(F32))
     at = 0
     for u in us:
         d_in[at : at + u.shape[1], :] += mm_tn(u, g_pre)
         at += u.shape[1]
-    return g_pre
+
+
+def pack_matrix(packed, ref, rows, at):
+    for j in range(4):
+        packed[pl.ds(at + j, rows, stride=4), :] = ref[:rows, 128 * j : 128 * (j + 1)]
+    return at + 4 * rows
 
 
 def pack(packed, lead, rows_in, d_in, d_out, d_vec):
-    at = lead
-    def matrix(ref, rows, at):
-        for j in range(4):
-            packed[pl.ds(at + j, rows, stride=4), :] = ref[:rows, 128 * j : 128 * (j + 1)]
-        return at + 4 * rows
     def vector(i, at):
         for j in range(4):
             packed[at + j : at + j + 1, :] = d_vec[i : i + 1, 128 * j : 128 * (j + 1)]
         return at + 4
-    at = matrix(d_in, rows_in, at)
+    at = pack_matrix(packed, d_in, rows_in, lead)
     at = vector(0, at)
-    if d_out is not None:
-        at = matrix(d_out, d_out.shape[0], at)
-        for i in (1, 2, 3):
-            at = vector(i, at)
-    return at
+    at = pack_matrix(packed, d_out, d_out.shape[0], at)
+    for i in (1, 2, 3):
+        at = vector(i, at)
 
 
 def clear(*refs):
@@ -454,18 +463,6 @@
 
 def shaped(*shape, dtype=F32):
     return jax.ShapeDtypeStruct(shape, dtype)
-
-
-ANY = pl.BlockSpec(memory_space=pl.ANY)
-
-
-def encode_kernel(bm, x, w_in, w_out, vec, want, node, low, pre, hat, inv, out, acc):
-    i = pl.program_id(0)
-    r, p, h, v = forward([x[...]], w_in, w_out, vec)
-    node[...] = r
-    low[...] = r.astype(BF16)
-    pre[...], hat[...], inv[...] = p, h, v
-    send_rows(i, bm, low[...], want, out, acc)
 
 
 def send_rows(i, bm, low, want, out, acc):
@@ -478,43 +475,62 @@
         out[...] = acc[...].astype(BF16)
 
 
-def kept_shapes(rows):
-    return (shaped(rows, LATENT), shaped(rows, LATENT), shaped(rows, 1))
-
-
-def kept_specs(bm):
-    return (spec((bm, LATENT), False), spec((bm, LATENT), False), spec((bm, 1), False))
-
-
-def encode(x, block, want, bm=256):
+def store_flat(packed, flat, at, sem):
+    copy = pltpu.make_async_copy(packed, flat.at[pl.ds(at, packed.shape[0])], sem)
+    copy.start()
+    return copy
+
+
+def mlp_sums(rows_in, wide=LATENT):
+    return [pltpu.VMEM((rows_in, LATENT), F32), pltpu.VMEM((LATENT, wide), F32), pltpu.VMEM((8, LATENT), F32)]
+
+
+def packed_rows(rows_in, lead=0):
+    return pltpu.VMEM((lead + 4 * rows_in + 4 * LATENT + 16, 128), F32)
+
+
+def encode_kernel(bm, x, w_in, w_out, vec, want, node, low, out, acc):
+    i = pl.program_id(0)
+    _, act = activate(first_half([x[...]], w_in, vec))
+    hat, _ = second_half(act, w_out, vec)
+    r = scale_shift(hat, vec)
+    node[...] = r
+    rounded = r.astype(BF16)
+    low[...] = rounded
+    send_rows(i, bm, rounded, want, out, acc)
+
+
+def encode(x, block, want, bm=512):
     rows, k = x.shape
     slots = want.shape[0]
     w_in, w_out, vec = block
     return pl.pallas_call(
         functools.partial(encode_kernel, bm),
         grid=(rows // bm,),
-        out_shape=(shaped(rows, LATENT), shaped(rows, LATENT, dtype=BF16)) + kept_shapes(rows) + (shaped(slots, LATENT, dtype=BF16),),
+        out_shape=(shaped(rows, LATENT), shaped(rows, LATENT, dtype=BF16), shaped(slots, LATENT, dtype=BF16)),
         in_specs=[spec((bm, k), False), spec(w_in.shape), spec(w_out.shape), spec(vec.shape), spec((slots, 1))],
-        out_specs=(spec((bm, LATENT), False), spec((bm, LATENT), False)) + kept_specs(bm) + (spec((slots, LATENT)),),
+        out_specs=(spec((bm, LATENT), False), spec((bm, LATENT), False), spec((slots, LATENT))),
         scratch_shapes=[pltpu.VMEM((slots, LATENT), F32)],
         compiler_params=params(),
         name="encode",
     )(x, w_in, w_out, vec, want)
 
 
-def node_kernel(bm, served, want, landed, node, low, w_in, w_out, vec, node_new, low_new, sums, pre, hat, inv, out, acc):
+def node_kernel(bm, served, want, landed, node, w_in, w_out, vec, node_new, low_new, sums, out, acc):
     i = pl.program_id(0)
     got = mm(place(served[...], i * bm, bm), landed[...]).astype(BF16)
     sums[...] = got
-    r, p, h, v = forward([low[...], got], w_in, w_out, vec)
-    r = node[...] + r
+    old = node[...]
+    _, act = activate(first_half([old.astype(BF16), got], w_in, vec))
+    hat, _ = second_half(act, w_out, vec)
+    r = old + scale_shift(hat, vec)
     node_new[...] = r
-    low_new[...] = r.astype(BF16)
-    pre[...], hat[...], inv[...] = p, h, v
-    send_rows(i, bm, low_new[...], want, out, acc)
-
-
-def node_forward(served, want, landed, node, low, block, bm=256):
+    rounded = r.astype(BF16)
+    low_new[...] = rounded
+    send_rows(i, bm, rounded, want, out, acc)
+
+
+def node_forward(served, want, landed, node, block, bm=512):
     rows = node.shape[0]
     slots = want.shape[0]
     w_in, w_out, vec = block
@@ -522,237 +538,427 @@
     return pl.pallas_call(
         functools.partial(node_kernel, bm),
         grid=(rows // bm,),
-        out_shape=(shaped(rows, LATENT), shaped(rows, LATENT, dtype=BF16), shaped(rows, LATENT, dtype=BF16)) + kept_shapes(rows) + (shaped(slots, LATENT, dtype=BF16),),
-        in_specs=[spec((1, slots)), spec((slots, 1)), spec((slots, LATENT)), b(), b(), spec(w_in.shape), spec(w_out.shape), spec(vec.shape)],
-        out_specs=(b(), b(), b()) + kept_specs(bm) + (spec((slots, LATENT)),),
+        out_shape=(shaped(rows, LATENT), shaped(rows, LATENT, dtype=BF16), shaped(rows, LATENT, dtype=BF16), shaped(slots, LATENT, dtype=BF16)),
+        in_specs=[spec((1, slots)), spec((slots, 1)), spec((slots, LATENT)), b(), spec(w_in.shape), spec(w_out.shape), spec(vec.shape)],
+        out_specs=(b(), b(), b(), spec((slots, LATENT))),
         scratch_shapes=[pltpu.VMEM((slots, LATENT), F32)],
         compiler_params=params(),
         name="node_forward",
-    )(served, want, landed, node, low, w_in, w_out, vec)
-
-
-def edge_kernel(first, pos, pos_r, arrived, source, w_in, w_out, vec, *rest):
+    )(served, want, landed, node, w_in, w_out, vec)
+
+
+def swap_start(n, me, src, dst, own, ssem, rsem):
+    pltpu.make_async_copy(src.at[me], dst.at[me], own).start()
+    def go(j, c):
+        t = lax.rem(me + j, n)
+        remote(src.at[t], dst.at[me], ssem.at[j], rsem.at[j], t).start()
+        return c
+    lax.fori_loop(1, n, go, 0)
+
+
+def swap_wait(n, me, src, dst, own, ssem, rsem):
+    def end(j, c):
+        t = lax.rem(me + j, n)
+        remote(src.at[t], dst.at[me], ssem.at[j], rsem.at[j], t).wait()
+        return c
+    lax.fori_loop(1, n, end, 0)
+    pltpu.make_async_copy(src.at[me], dst.at[me], own).wait()
+
+
+def flat_rows_of(ref):
+    return ref[...].reshape(ref.shape[0] * ref.shape[1], ref.shape[2])
+
+
+def edge_kernel(n, first, outgoing, source, pos, pos_r, *rest):
+    rest = list(rest)
+    blocks = rest[:3]
+    geo_blocks = rest[3:6] if first else []
+    rest = rest[6 if first else 3 :]
+    edge_new, edge_low, sent, recv, landed, arrived, buffer, w_in, w_out, vec, own, s1, r1, s2, r2, wsem = rest[:16]
+    held = [w_in, w_out, vec] + rest[16:]
+    loads = [pltpu.make_async_copy(a, b, wsem.at[i]) for i, (a, b) in enumerate(zip(blocks + geo_blocks, held))]
+    for load in loads:
+        load.start()
+    me = lax.axis_index("dev")
+    greet(n, me)
+    swap_start(n, me, outgoing, arrived, own.at[0], s1, r1)
+    for load in loads:
+        load.wait()
     if first:
-        g_in, g_out, g_vec, edge_new, buffer, edge_low, sent, recv, pre, hat, inv, g_pre, g_hat, g_inv = rest
-        edge, p, h, v = forward([source[...]], g_in, g_out, g_vec)
-        g_pre[...], g_hat[...], g_inv[...] = p, h, v
+        g_in, g_out, g_vec = held[3:]
+        _, act = activate(first_half([source[...]], g_in, g_vec))
+        hat, _ = second_half(act, g_out, g_vec)
+        edge = scale_shift(hat, g_vec)
     else:
-        edge_new, buffer, edge_low, sent, recv, pre, hat, inv = rest
         edge = source[...]
-    slots = arrived.shape[0]
     e = edge.astype(BF16)
-    s = mm(pick(pos[:, 0:1], 0, slots), arrived[...]).astype(BF16)
-    r = mm(pick(pos[:, 1:2], 0, slots), arrived[...]).astype(BF16)
-    edge_low[...], sent[...], recv[...] = e, s, r
-    out, p, h, v = forward([e, s, r], w_in, w_out, vec)
-    new = edge + out
+    edge_low[...] = e
+    slots = n * arrived.shape[1]
+    pre = first_half([e], w_in, vec)
+    pick_s, pick_r = pick(pos[:, 0:1], 0, slots), pick(pos[:, 1:2], 0, slots)
+    put_r = place(pos_r[...], 0, slots)
+    swap_wait(n, me, outgoing, arrived, own.at[0], s1, r1)
+    rows = flat_rows_of(arrived)
+    s = mm(pick_s, rows).astype(BF16)
+    r = mm(pick_r, rows).astype(BF16)
+    pre = pre + mm(s, w_in[LATENT : 2 * LATENT, :]) + mm(r, w_in[2 * LATENT :, :])
+    _, act = activate(pre)
+    hat, _ = second_half(act, w_out, vec)
+    new = edge + scale_shift(hat, vec)
+    buffer[...] = mm(put_r, new.astype(BF16)).astype(BF16).reshape(buffer.shape)
+    swap_start(n, me, buffer, landed, own.at[1], s2, r2)
     edge_new[...] = new
-    pre[...], hat[...], inv[...] = p, h, v
-    buffer[...] = mm(place(pos_r[...], 0, slots), new.astype(BF16)).astype(BF16)
-
-
-def edge_forward(pos, pos_r, arrived, source, block, geo=None):
+    sent[...], recv[...] = s, r
+    swap_wait(n, me, buffer, landed, own.at[1], s2, r2)
+
+
+def held_scratch(block):
+    return [pltpu.VMEM(a.shape, a.dtype) for a in block]
+
+
+def edge_forward(n, outgoing, source, pos, pos_r, block, cid, geo=None):
     rows = source.shape[0]
-    slots = arrived.shape[0]
-    kept = kept_shapes(rows)
+    slots = outgoing.shape[0]
+    outgoing = outgoing.reshape(n, slots // n, LATENT)
+    V = pl.BlockSpec(memory_space=pltpu.VMEM)
+    weights = list(block) + list(geo or ())
+    low = lambda r: shaped(r, LATENT, dtype=BF16)
     return pl.pallas_call(
-        functools.partial(edge_kernel, geo is not None),
-        out_shape=(shaped(rows, LATENT), shaped(slots, LATENT, dtype=BF16)) + (shaped(rows, LATENT, dtype=BF16),) * 3 + kept + (kept if geo is not None else ()),
-        compiler_params=params(),
+        functools.partial(edge_kernel, n, geo is not None),
+        out_shape=(shaped(rows, LATENT), low(rows), low(rows), low(rows), shaped(*outgoing.shape, dtype=BF16)),
+        in_specs=[ANY, V, V, V] + [ANY] * len(weights),
+        out_specs=(V, V, V, V, ANY),
+        scratch_shapes=[pltpu.VMEM(outgoing.shape, BF16), pltpu.VMEM(outgoing.shape, BF16)]
+        + held_scratch(block)
+        + [DMA((2,)), DMA((n,)), DMA((n,)), DMA((n,)), DMA((n,)), DMA((6,))]
+        + held_scratch(geo or ()),
+        compiler_params=params(collective_id=cid, has_side_effects=True),
         name="edge_forward",
-    )(pos, pos_r, arrived, source, *block, *(geo or ()))
-
-
-def decode_kernel(bm, at, x, target, level, land, count, low, w_in, w_out, vec, flat, g_node, d_out_o, d_vec_o, err_o, packed, d_in, d_out, d_vec, err, sem):
+    )(outgoing, source, pos, pos_r, *weights)
+
+
+def turn_kernel(bm, at, dec_at, served, want, landed, node, x, target, level, land, count, w_in, w_out, vec, c_in, c_out, c_vec, flat, g_prev, out, d_out_o, d_vec_o, err_o, packed, packed2, d_in, d_out, d_vec, e_in, e_out, e_vec, err, acc, sem):
     i = pl.program_id(0)
     @pl.when(i == 0)
     def _():
-        clear(d_in, d_out, d_vec, err)
-    u = low[...]
-    pre = vec[0:1, :] + mm(u, w_in[...])
-    _, act = activate(pre)
-    wide = w_out.shape[1]
-    post = mm(act, w_out[...]) + vec[1:2, :wide]
+        clear(d_in, d_out, d_vec, e_in, e_out, e_vec, err)
+    got = mm(place(served[...], i * bm, bm), landed[...]).astype(BF16)
+    old = node[...]
+    low = old.astype(BF16)
+    pre = first_half([low, got], w_in, vec)
+    sigma, act = activate(pre)
+    hat, inv = second_half(act, w_out, vec)
+    u = (old + scale_shift(hat, vec)).astype(BF16)
+    c_pre = first_half([u], c_in, c_vec)
+    c_sigma, c_act = activate(c_pre)
+    wide = c_out.shape[1]
+    post = mm(c_act, c_out[...]) + c_vec[1:2, :wide]
     sea = (lax.broadcasted_iota(jnp.int32, (1, VARS), 1) < SEA_VARS).astype(F32)
     mask = level[...].astype(F32) * (1.0 - land[...].astype(F32) * sea)
     residual = x[...].astype(F32) + post[:, :VARS] - target[...]
     divisor = jnp.maximum(count[...], 1.0)
     err[:, :VARS] += col(mask * residual * residual)
     g = 2.0 * mask * residual / divisor
-    g_low = jnp.concatenate([g, jnp.zeros((bm, wide - VARS), F32)], axis=1)
-    g_pre = back([u], g_low, pre, w_out, d_in, d_out, d_vec)
-    g_node[...] = mm_nt(g_pre, w_in[...])
+    g_low = jnp.concatenate([g, jnp.zeros((bm, wide - VARS), F32)], axis=1).astype(BF16)
+    c_g = act_back(g_low, c_pre, c_sigma, c_out)
+    weight_sums([u], c_act, g_low, c_g, e_in, e_out, e_vec)
+    g_node = mm_nt(c_g, c_in[...])
+    g_post = norm_back(g_node, hat, inv, vec, d_vec)
+    g_pre = act_back(g_post, pre, sigma, w_out)
+    weight_sums([low, got], act, g_post, g_pre, d_in, d_out, d_vec)
+    g_prev[...] = g_node + mm_nt(g_pre, w_in[:LATENT, :])
+    send_rows(i, bm, mm_nt(g_pre, w_in[LATENT:, :]).astype(BF16), want, out, acc)
     @pl.when(i == pl.num_programs(0) - 1)
     def _():
-        d_out_o[...] = d_out[...]
-        d_vec_o[...] = d_vec[...]
+        d_out_o[...] = e_out[...]
+        d_vec_o[...] = e_vec[...]
         err_o[...] = err[...]
-        for j in range(4):
-            packed[pl.ds(j, LATENT, stride=4), :] = d_in[:, 128 * j : 128 * (j + 1)]
-        cp = pltpu.make_async_copy(packed, flat.at[pl.ds(at, 4 * LATENT)], sem)
-        cp.start()
-        cp.wait()
-
-
-def decode(x, target, level, land, count, low, block, flat_rows, at, bm=256):
-    rows = low.shape[0]
-    w_in, w_out, vec = block
-    wide = w_out.shape[1]
+        pack_matrix(packed2, e_in, LATENT, 0)
+        one = store_flat(packed2, flat, dec_at, sem.at[0])
+        pack(packed, 0, 2 * LATENT, d_in, d_out, d_vec)
+        two = store_flat(packed, flat, at, sem.at[1])
+        one.wait()
+        two.wait()
+
+
+def turn(served, want, landed, node, x, target, level, land, count, block, dec, flat_rows, at, dec_at, bm=512):
+    rows = node.shape[0]
+    slots = want.shape[0]
+    wide = dec[1].shape[1]
     v = lambda: spec((bm, VARS), False)
     return pl.pallas_call(
-        functools.partial(decode_kernel, bm, at),
+        functools.partial(turn_kernel, bm, at, dec_at),
         grid=(rows // bm,),
-        out_shape=(shaped(flat_rows, 128), shaped(rows, LATENT), shaped(LATENT, wide), shaped(8, LATENT), shaped(1, wide)),
-        in_specs=[v(), v(), v(), spec((bm, 1), False), spec((1, 1)), spec((bm, LATENT), False), spec(w_in.shape), spec(w_out.shape), spec(vec.shape)],
-        out_specs=(ANY, spec((bm, LATENT), False), spec((LATENT, wide)), spec((8, LATENT)), spec((1, wide))),
-        scratch_shapes=[pltpu.VMEM((4 * LATENT, 128), F32), pltpu.VMEM((LATENT, LATENT), F32), pltpu.VMEM((LATENT, wide), F32), pltpu.VMEM((8, LATENT), F32), pltpu.VMEM((1, wide), F32), pltpu.SemaphoreType.DMA],
+        out_shape=(shaped(flat_rows, 128), shaped(rows, LATENT), shaped(slots, LATENT, dtype=BF16), shaped(LATENT, wide), shaped(8, LATENT), shaped(1, wide)),
+        in_specs=[spec((1, slots)), spec((slots, 1)), spec((slots, LATENT)), spec((bm, LATENT), False), v(), v(), v(), spec((bm, 1), False), spec((1, 1))] + [spec(a.shape) for a in (*block, *dec)],
+        out_specs=(ANY, spec((bm, LATENT), False), spec((slots, LATENT)), spec((LATENT, wide)), spec((8, LATENT)), spec((1, wide))),
+        scratch_shapes=[packed_rows(2 * LATENT), pltpu.VMEM((4 * LATENT, 128), F32)] + mlp_sums(2 * LATENT) + mlp_sums(LATENT, wide) + [pltpu.VMEM((1, wide), F32), pltpu.VMEM((slots, LATENT), F32), DMA((2,))],
         compiler_params=params(),
-        name="decode",
-    )(x, target, level, land, count, low, w_in, w_out, vec)
-
-
-def layer_norm_back(g, hat, inv, vec, d_vec):
-    d_vec[2:3, :] += col(g * hat)
-    d_vec[3:4, :] += col(g)
-    return norm_back(g, hat, inv, vec[2:3, :])
-
-
-def node_back_kernel(bm, at, landed_given, tail_at, served, want, g_node, low, sums, pre, hat, inv, w_in, w_out, vec, flat_in, extra, flat, g_prev, out, packed, d_in, d_out, d_vec, acc, sem):
-    i = pl.program_id(0)
-    @pl.when(i == 0)
-    def _():
-        clear(d_in, d_out, d_vec, acc)
-        if tail_at is not None:
-            pltpu.make_async_copy(extra, flat.at[pl.ds(tail_at, extra.shape[0])], sem.at[0]).start()
-    g = g_node[...]
-    if landed_given:
-        g = g + mm(place(served[...], i * bm, bm), extra[...])
-    g_post = layer_norm_back(g, hat[...], inv[...], vec, d_vec)
-    u, s = low[...], sums[...]
-    g_pre = back([u, s], g_post, pre[...], w_out, d_in, d_out, d_vec)
-    g_prev[...] = g + mm_nt(g_pre, w_in[:LATENT, :])
-    g_sum = mm_nt(g_pre, w_in[LATENT:, :]).astype(BF16)
-    send_rows(i, bm, g_sum, want, out, acc)
-    @pl.when(i == pl.num_programs(0) - 1)
-    def _():
-        pack(packed, 0, 2 * LATENT, d_in, d_out, d_vec)
-        cp = pltpu.make_async_copy(packed, flat.at[pl.ds(at, packed.shape[0])], sem.at[1])
-        cp.start()
-        if tail_at is not None:
-            pltpu.make_async_copy(extra, flat.at[pl.ds(tail_at, extra.shape[0])], sem.at[0]).wait()
-        cp.wait()
-
-
-def node_backward(served, want, g_node, low, sums, kept, block, flat, at, landed=None, tail=None, tail_at=None, bm=256):
-    rows = low.shape[0]
-    slots = want.shape[0]
-    w_in, w_out, vec = block
-    b = lambda: spec((bm, LATENT), False)
-    extra = landed if landed is not None else tail
-    return pl.pallas_call(
-        functools.partial(node_back_kernel, bm, at, landed is not None, tail_at),
-        grid=(rows // bm,),
-        out_shape=(shaped(*flat.shape), shaped(rows, LATENT), shaped(slots, LATENT, dtype=BF16)),
-        in_specs=[spec((1, slots)), spec((slots, 1)), b(), b(), b()] + list(kept_specs(bm)) + [spec(w_in.shape), spec(w_out.shape), spec(vec.shape), ANY, spec(extra.shape)],
-        out_specs=(ANY, b(), spec((slots, LATENT))),
-        scratch_shapes=[pltpu.VMEM((8 * LATENT + 4 * LATENT + 16, 128), F32), pltpu.VMEM((2 * LATENT, LATENT), F32), pltpu.VMEM((LATENT, LATENT), F32), pltpu.VMEM((8, LATENT), F32), pltpu.VMEM((slots, LATENT), F32), pltpu.SemaphoreType.DMA((2,))],
-        input_output_aliases={11: 0},
-        compiler_params=params(),
-        name="node_backward",
-    )(served, want, g_node, low, sums, *kept, w_in, w_out, vec, flat, extra)
-
-
-def edge_back_kernel(at, has_edge, geo_at, pos, pos_s, pos_r, returned, edge_low, sent, recv, pre, hat, inv, w_in, w_out, vec, flat_in, *rest):
+        name="turn",
+    )(served, want, landed, node, x, target, level, land, count, *block, *dec)
+
+
+def edge_back_kernel(n, at, has_edge, geo_at, tail_at, outgoing, edge_low, sent, recv, pos, pos_s, pos_r, *rest):
     rest = list(rest)
+    blocks = [rest.pop(0) for _ in range(3)]
+    geo_blocks = [rest.pop(0) for _ in range(3)] if geo_at is not None else []
+    rest.pop(0)
     g_edge = rest.pop(0) if has_edge else None
-    if geo_at is not None:
-        geo, g_pre, g_hat, g_inv, g_out, g_vec = rest[:6]
-        rest = rest[6:]
-    flat, edge_prev, buffer, packed, d_in, d_out, d_vec, sem = rest[:8]
-    slots = returned.shape[0]
+    geo = rest.pop(0) if geo_at is not None else None
+    tail = rest.pop(0) if tail_at is not None else None
+    flat, edge_prev, landed, returned, buffer, packed, d_in, d_out, d_vec, own, s1, r1, s2, r2, wsem, fsem, w_in, w_out, vec = rest[:19]
+    rest = rest[19:]
+    held = [w_in, w_out, vec] + rest[:3]
+    loads = [pltpu.make_async_copy(a, b, wsem.at[i]) for i, (a, b) in enumerate(zip(blocks + geo_blocks, held))]
+    for load in loads:
+        load.start()
+    stores = []
+    if tail is not None:
+        stores.append(store_flat(tail, flat, tail_at, fsem.at[2]))
+    me = lax.axis_index("dev")
+    greet(n, me)
+    swap_start(n, me, outgoing, returned, own.at[0], s1, r1)
+    for load in loads:
+        load.wait()
     clear(d_in, d_out, d_vec)
-    g = mm(pick(pos[:, 1:2], 0, slots), returned[...])
+    us = [edge_low[...], sent[...], recv[...]]
+    slots = n * returned.shape[1]
+    pre = first_half(us, w_in, vec)
+    sigma, act = activate(pre)
+    hat, inv = second_half(act, w_out, vec)
+    pick_r = pick(pos[:, 1:2], 0, slots)
+    put_s, put_r = place(pos_s[...], 0, slots), place(pos_r[...], 0, slots)
+    if geo is not None:
+        g_in, g_out, g_vec = rest[:3]
+        c_pre = first_half([geo[...]], g_in, g_vec)
+        c_sigma, c_act = activate(c_pre)
+        c_hat, c_inv = second_half(c_act, g_out, g_vec)
+    swap_wait(n, me, outgoing, returned, own.at[0], s1, r1)
+    g = mm(pick_r, flat_rows_of(returned))
     if has_edge:
         g = g_edge[...] + g
-    g_post = layer_norm_back(g, hat[...], inv[...], vec, d_vec)
-    p = back([edge_low[...], sent[...], recv[...]], g_post, pre[...], w_out, d_in, d_out, d_vec)
-    prev = g + mm_nt(p, w_in[:LATENT, :])
+    low = norm_back(g, hat, inv, vec, d_vec)
+    g_pre = act_back(low, pre, sigma, w_out)
+    s = mm_nt(g_pre, w_in[LATENT : 2 * LATENT, :]).astype(BF16)
+    r = mm_nt(g_pre, w_in[2 * LATENT :, :]).astype(BF16)
+    buffer[...] = (mm(put_s, s) + mm(put_r, r)).astype(BF16).reshape(buffer.shape)
+    swap_start(n, me, buffer, landed, own.at[1], s2, r2)
+    prev = g + mm_nt(g_pre, w_in[:LATENT, :])
     edge_prev[...] = prev
-    s = mm_nt(p, w_in[LATENT : 2 * LATENT, :]).astype(BF16)
-    r = mm_nt(p, w_in[2 * LATENT :, :]).astype(BF16)
-    buffer[...] = (mm(place(pos_s[...], 0, slots), s) + mm(place(pos_r[...], 0, slots), r)).astype(BF16)
+    weight_sums(us, act, low, g_pre, d_in, d_out, d_vec)
     pack(packed, 0, 3 * LATENT, d_in, d_out, d_vec)
-    cp = pltpu.make_async_copy(packed, flat.at[pl.ds(at, packed.shape[0])], sem.at[0])
-    cp.start()
-    if geo_at is not None:
-        packed2, c_in, c_out, c_vec = rest[8:]
-        clear(c_in, c_out, c_vec)
-        g_post = layer_norm_back(prev, g_hat[...], g_inv[...], g_vec, c_vec)
-        back([geo[...]], g_post, g_pre[...], g_out, c_in, c_out, c_vec)
-        pack(packed2, 0, GEO, c_in, c_out, c_vec)
-        cp2 = pltpu.make_async_copy(packed2, flat.at[pl.ds(geo_at, packed2.shape[0])], sem.at[1])
-        cp2.start()
-        cp2.wait()
-    cp.wait()
-
-
-def edge_backward(pos, pos_s, pos_r, returned, ins, kept, block, flat, at, g_edge=None, geo=None, geo_at=None):
+    stores.append(store_flat(packed, flat, at, fsem.at[0]))
+    if geo is not None:
+        packed2, e_in, e_out, e_vec = rest[3:]
+        clear(e_in, e_out, e_vec)
+        c_low = norm_back(prev, c_hat, c_inv, g_vec, e_vec)
+        c_g = act_back(c_low, c_pre, c_sigma, g_out)
+        weight_sums([geo[...]], c_act, c_low, c_g, e_in, e_out, e_vec)
+        pack(packed2, 0, GEO, e_in, e_out, e_vec)
+        stores.append(store_flat(packed2, flat, geo_at, fsem.at[1]))
+    swap_wait(n, me, buffer, landed, own.at[1], s2, r2)
+    for store in stores:
+        store.wait()
+
+
+def edge_backward(n, outgoing, ins, pos, pos_s, pos_r, block, flat, at, cid, g_edge=None, geo=None, geo_at=None, tail=None, tail_at=None):
     rows = pos.shape[0]
-    slots = returned.shape[0]
+    slots = outgoing.shape[0]
+    outgoing = outgoing.reshape(n, slots // n, LATENT)
     V = pl.BlockSpec(memory_space=pltpu.VMEM)
-    args = [pos, pos_s, pos_r, returned, *ins, *kept, *block, flat]
+    geo_block = geo[1] if geo is not None else ()
+    args = [outgoing, *ins, pos, pos_s, pos_r, *block, *geo_block, flat]
+    specs = [ANY] + [V] * 6 + [ANY] * (4 + len(geo_block))
     which = len(args) - 1
-    if g_edge is not None:
-        args.append(g_edge)
-    scratch = [pltpu.VMEM((12 * LATENT + 4 * LATENT + 16, 128), F32), pltpu.VMEM((3 * LATENT, LATENT), F32), pltpu.VMEM((LATENT, LATENT), F32), pltpu.VMEM((8, LATENT), F32), pltpu.SemaphoreType.DMA((2,))]
+    scratch = [pltpu.VMEM(outgoing.shape, BF16), pltpu.VMEM(outgoing.shape, BF16), packed_rows(3 * LATENT)] + mlp_sums(3 * LATENT)
+    scratch += [DMA((2,)), DMA((n,)), DMA((n,)), DMA((n,)), DMA((n,)), DMA((6,)), DMA((3,))] + held_scratch(block)
+    for more in (g_edge, geo[0] if geo is not None else None, tail):
+        if more is not None:
+            args.append(more)
+            specs.append(V)
     if geo is not None:
-        args += geo
-        wide = geo[0].shape[1]
-        scratch += [pltpu.VMEM((4 * GEO + 4 * LATENT + 16, 128), F32), pltpu.VMEM((wide, LATENT), F32), pltpu.VMEM((LATENT, LATENT), F32), pltpu.VMEM((8, LATENT), F32)]
+        scratch += held_scratch(geo_block) + [packed_rows(GEO)] + mlp_sums(geo[0].shape[1])
     return pl.pallas_call(
-        functools.partial(edge_back_kernel, at, g_edge is not None, geo_at),
-        out_shape=(shaped(*flat.shape), shaped(rows, LATENT), shaped(slots, LATENT, dtype=BF16)),
-        in_specs=[ANY if i == which else V for i in range(len(args))],
-        out_specs=(ANY, V, V),
+        functools.partial(edge_back_kernel, n, at, g_edge is not None, geo_at, tail_at),
+        out_shape=(shaped(*flat.shape), shaped(rows, LATENT), shaped(*outgoing.shape, dtype=BF16)),
+        in_specs=specs,
+        out_specs=(ANY, V, ANY),
         scratch_shapes=scratch,
         input_output_aliases={which: 0},
-        compiler_params=params(),
+        compiler_params=params(collective_id=cid, has_side_effects=True),
         name="edge_backward",
     )(*args)
 
 
-def encode_back_kernel(bm, served, landed, g_node, x, pre, hat, inv, w_out, vec, flat_in, flat, packed, d_in, d_out, d_vec, sem):
+def node_back_kernel(bm, at, served, want, landed, g_node, low, sums, w_in, w_out, vec, flat_in, flat, g_prev, out, packed, d_in, d_out, d_vec, acc, sem):
     i = pl.program_id(0)
     @pl.when(i == 0)
     def _():
         clear(d_in, d_out, d_vec)
+    us = [low[...], sums[...]]
+    pre = first_half(us, w_in, vec)
+    sigma, act = activate(pre)
+    hat, inv = second_half(act, w_out, vec)
     g = g_node[...] + mm(place(served[...], i * bm, bm), landed[...])
-    g_post = layer_norm_back(g, hat[...], inv[...], vec, d_vec)
-    back([x[...]], g_post, pre[...], w_out, d_in, d_out, d_vec)
+    g_post = norm_back(g, hat, inv, vec, d_vec)
+    g_pre = act_back(g_post, pre, sigma, w_out)
+    weight_sums(us, act, g_post, g_pre, d_in, d_out, d_vec)
+    g_prev[...] = g + mm_nt(g_pre, w_in[:LATENT, :])
+    send_rows(i, bm, mm_nt(g_pre, w_in[LATENT:, :]).astype(BF16), want, out, acc)
+    @pl.when(i == pl.num_programs(0) - 1)
+    def _():
+        pack(packed, 0, 2 * LATENT, d_in, d_out, d_vec)
+        store_flat(packed, flat, at, sem).wait()
+
+
+def node_backward(served, want, landed, g_node, low, sums, block, flat, at, bm=512):
+    rows = low.shape[0]
+    slots = want.shape[0]
+    b = lambda: spec((bm, LATENT), False)
+    return pl.pallas_call(
+        functools.partial(node_back_kernel, bm, at),
+        grid=(rows // bm,),
+        out_shape=(shaped(*flat.shape), shaped(rows, LATENT), shaped(slots, LATENT, dtype=BF16)),
+        in_specs=[spec((1, slots)), spec((slots, 1)), spec((slots, LATENT)), b(), b(), b()] + [spec(a.shape) for a in block] + [ANY],
+        out_specs=(ANY, b(), spec((slots, LATENT))),
+        scratch_shapes=[packed_rows(2 * LATENT)] + mlp_sums(2 * LATENT) + [pltpu.VMEM((slots, LATENT), F32), DMA],
+        input_output_aliases={9: 0},
+        compiler_params=params(),
+        name="node_backward",
+    )(served, want, landed, g_node, low, sums, *block, flat)
+
+
+def encode_back_kernel(bm, served, landed, g_node, x, w_in, w_out, vec, flat_in, flat, packed, d_in, d_out, d_vec, sem):
+    i = pl.program_id(0)
+    @pl.when(i == 0)
+    def _():
+        clear(d_in, d_out, d_vec)
+    us = [x[...]]
+    pre = first_half(us, w_in, vec)
+    sigma, act = activate(pre)
+    hat, inv = second_half(act, w_out, vec)
+    g = g_node[...] + mm(place(served[...], i * bm, bm), landed[...])
+    g_post = norm_back(g, hat, inv, vec, d_vec)
+    g_pre = act_back(g_post, pre, sigma, w_out)
+    weight_sums(us, act, g_post, g_pre, d_in, d_out, d_vec)
     @pl.when(i == pl.num_programs(0) - 1)
     def _():
         packed[0:4, :] = jnp.zeros((4, 128), F32)
         pack(packed, 4, VARS, d_in, d_out, d_vec)
-        cp = pltpu.make_async_copy(packed, flat.at[pl.ds(0, packed.shape[0])], sem)
-        cp.start()
-        cp.wait()
-
-
-def encode_backward(served, landed, g_node, x, kept, block, flat, bm=256):
+        store_flat(packed, flat, 0, sem).wait()
+
+
+def encode_backward(served, landed, g_node, x, block, flat, bm=512):
     rows, k = x.shape
     slots = landed.shape[0]
-    w_in, w_out, vec = block
     return pl.pallas_call(
         functools.partial(encode_back_kernel, bm),
         grid=(rows // bm,),
         out_shape=shaped(*flat.shape),
-        in_specs=[spec((1, slots)), spec((slots, LATENT)), spec((bm, LATENT), False), spec((bm, k), False)] + list(kept_specs(bm)) + [spec(w_out.shape), spec(vec.shape), ANY],
+        in_specs=[spec((1, slots)), spec((slots, LATENT)), spec((bm, LATENT), False), spec((bm, k), False)] + [spec(a.shape) for a in block] + [ANY],
         out_specs=ANY,
-        scratch_shapes=[pltpu.VMEM((4 + 4 * VARS + 4 * LATENT + 16, 128), F32), pltpu.VMEM((k, LATENT), F32), pltpu.VMEM((LATENT, LATENT), F32), pltpu.VMEM((8, LATENT), F32), pltpu.SemaphoreType.DMA],
-        input_output_aliases={9: 0},
+        scratch_shapes=[packed_rows(VARS, 4)] + mlp_sums(k) + [DMA],
+        input_output_aliases={7: 0},
         compiler_params=params(),
         name="encode_backward",
-    )(served, landed, g_node, x, *kept, w_out, vec, flat)
+    )(served, landed, g_node, x, *block, flat)
+
+
+def relay_plan(segments, share_rows):
+    jobs = []
+    for block_id, part_name, part_shape, offset, entries in segments:
+        if part_name not in ("w_in", "w_out") or part_shape[1] != LATENT:
+            continue
+        for first in range(0, part_shape[0], LATENT):
+            rows = min(LATENT, part_shape[0] - first)
+            follow = 0
+            if first + rows == part_shape[0]:
+                follow = 1 if part_name == "w_in" else 3
+            begin = offset // 128 + 4 * first
+            end = begin + 4 * (rows + follow)
+            parts = []
+            at = begin
+            while at < end:
+                owner, low = divmod(at, share_rows)
+                size = min(end - at, share_rows - low)
+                base = low // 16 * 16
+                span = (low + size - base + 15) // 16 * 16
+                parts.append((owner, base, span, low - base, at - begin))
+                at += size
+            jobs.append((block_id, part_name, first, rows, follow, parts))
+    return jobs
+
+
+def relay_kernel(jobs, shapes, shares, *rest):
+    count = sum(len(s) for s in shapes)
+    outs = rest[:count]
+    stage, lines, made, vecs, isem, osem, vsem = rest[count:]
+    index = {}
+    for b, s in enumerate(shapes):
+        for name, _ in s:
+            index[b, name] = len(index)
+    loads, at = [], 0
+    for number, (b, name, first, rows, follow, parts) in enumerate(jobs):
+        mine = []
+        for owner, base, span, skip, to in parts:
+            copy = pltpu.make_async_copy(shares.at[owner, pl.ds(base, span)], stage.at[pl.ds(at, span)], isem.at[len(loads) * 0 + number * 4 + len(mine)])
+            copy.start()
+            mine.append((copy, at, span, skip, to))
+            at += span
+        loads.append(mine)
+    vecs[...] = jnp.zeros_like(vecs)
+    stores = []
+    for number, ((b, name, first, rows, follow, parts), mine) in enumerate(zip(jobs, loads)):
+        for copy, where, span, skip, to in mine:
+            copy.wait()
+            lines[pl.ds(16 + to - skip, span), :] = stage[pl.ds(where, span), :].astype(F32)
+        full = (rows + 15) // 16 * 16
+        for j in range(4):
+            made[number, :rows, 128 * j : 128 * (j + 1)] = lines[pl.ds(16 + j, rows, stride=4), :].astype(BF16)
+        if rows < LATENT:
+            made[number, rows:, :] = jnp.zeros((LATENT - rows, LATENT), BF16)
+        for i in range(follow):
+            row = i if name == "w_in" else i + 1
+            for j in range(4):
+                p = 16 + 4 * (rows + i) + j
+                vecs[b, row : row + 1, 128 * j : 128 * (j + 1)] = lines[p : p + 1, :]
+        out = outs[index[b, name]]
+        size = min(LATENT, out.shape[0] - first)
+        store = pltpu.make_async_copy(made.at[number, pl.ds(0, size)], out.at[pl.ds(first, size)], osem.at[number])
+        store.start()
+        stores.append(store)
+    for b in range(len(shapes)):
+        store = pltpu.make_async_copy(vecs.at[b], outs[index[b, "vec"]], vsem.at[b])
+        store.start()
+        stores.append(store)
+    for store in stores:
+        store.wait()
+
+
+def relay(shares, segments, share_rows):
+    jobs = relay_plan(segments, share_rows)
+    blocks = segments[-1][0] + 1
+    shapes = [[] for _ in range(blocks)]
+    for b, name, shape, _, _ in segments:
+        if name in ("w_in", "w_out") and shape[1] == LATENT:
+            shapes[b].append((name, (-(-shape[0] // 128) * 128, LATENT)))
+    for s in shapes:
+        s.append(("vec", (8, LATENT)))
+    stage = sum(span for job in jobs for _, _, span, _, _ in job[5])
+    out_shape = [shaped(*shape, dtype=F32 if name == "vec" else BF16) for s in shapes for name, shape in s]
+    outs = pl.pallas_call(
+        functools.partial(relay_kernel, jobs, shapes),
+        out_shape=out_shape,
+        in_specs=[ANY],
+        out_specs=[ANY] * len(out_shape),
+        scratch_shapes=[pltpu.VMEM((stage, 128), BF16), pltpu.VMEM((16 + 4 * LATENT + 64, 128), F32), pltpu.VMEM((len(jobs), LATENT, LATENT), BF16), pltpu.VMEM((blocks, 8, LATENT), F32), DMA((4 * len(jobs),)), DMA((len(jobs),)), DMA((blocks,))],
+        compiler_params=params(),
+        name="relay",
+    )(shares)
+    made = [{} for _ in shapes]
+    for (b, name), value in zip([(b, name) for b, s in enumerate(shapes) for name, _ in s], outs):
+        made[b][name] = value
+    return made
 
 
 def make_asks(edge_owners, edge_local, devices):
@@ -782,6 +988,25 @@
     vectors = [widen(params[name][None], LATENT) for name in names]
     vectors.append(jnp.zeros((8 - len(vectors), LATENT), jnp.bfloat16))
     return (w_in, w_out, jnp.concatenate(vectors).astype(jnp.float32))
+
+
+def relaid_blocks(shares, segments, share_rows):
+    def rows_of(first, last):
+        parts = []
+        while first < last:
+            owner, low = divmod(first, share_rows)
+            size = min(last - first, share_rows - low)
+            parts.append(shares[owner, low : low + size])
+            first += size
+        return jnp.concatenate(parts) if len(parts) > 1 else parts[0]
+    made = relay(shares, segments, share_rows)
+    [(shape, begin, size)] = [(s, o, e) for _, name, s, o, e in segments if name == "w_out" and s[1] != LATENT]
+    wide = shape[1]
+    lines = rows_of(begin // 128, -(-(begin + size + wide) // 128)).reshape(-1)
+    made[-1]["w_out"] = widen(lines[:size].reshape(shape), (wide + 127) // 128 * 128)
+    bias = lines[size : size + wide].astype(jnp.float32)
+    made[-1]["vec"] = made[-1]["vec"].at[1, :wide].set(bias)
+    return [(m["w_in"], m["w_out"], m["vec"]) for m in made]
 
 
 def local(
@@ -813,61 +1038,67 @@
         ask = jnp.pad(asking.reshape(devices, 1, capacity), ((0, 0), (0, 0), (0, 128 - capacity)))
         number = jnp.zeros((8, 128), jnp.float32).at[0, 0].set(counted)
         gathered, served, numbers = gather_weights(low, ask, number, 1)
-        full_weights = gathered[:, :share_rows].reshape(-1)
+        blocks = relaid_blocks(gathered, segments, share_rows)
         served = served[:, 0, :capacity].reshape(-1)
         count = jnp.sum(numbers)
     else:
         full_weights = lax.all_gather(master.astype(jnp.bfloat16), "dev", axis=0, tiled=True)
+        blocks = [make_block(b) for b in unpack(full_weights, segments)]
         served = lax.all_to_all(asking.reshape(devices, capacity), "dev", 0, 0, tiled=True).reshape(-1)
         count = lax.psum(counted, "dev")
-    blocks = [make_block(b) for b in unpack(full_weights, segments)]
     want = served[:, None]
     served = served[None, :]
     pos = position.reshape(-1, 2)
     pos_s, pos_r = pos[:, 0][None, :], pos[:, 1][None, :]
-
-    def exchange(rows):
-        return a2a(rows.reshape(devices, capacity, LATENT), 0).reshape(slots, LATENT)
-
     x = widen(inputs, 256)
     geo = widen(geometry, 128)
-    node, low, *enc_kept, outgoing = encode(x, blocks[0], want)
+    land = land_sea[:, None]
+    node, low, outgoing = encode(x, blocks[0], want)
     node_kept, edge_kept = [], []
     edge = geo
     for k in range(LAYERS):
-        arrived = exchange(outgoing)
-        edge, buffer, *kept = edge_forward(pos, pos_r, arrived, edge, blocks[2 + 2 * k], blocks[1] if k == 0 else None)
-        edge_kept.append((kept[:3], kept[3:6]))
-        if k == 0:
-            geo_kept = kept[6:]
-        landed = exchange(buffer)
-        before = low
-        node, low, sums, *kept, outgoing = node_forward(served, want, landed, node, low, blocks[3 + 2 * k])
-        node_kept.append((before, sums, kept))
+        edge, *kept, landed = edge_forward(
+            devices, outgoing, edge, pos, pos_r, blocks[2 + 2 * k], 3 + min(k, 1), blocks[1] if k == 0 else None
+        )
+        edge_kept.append(kept)
+        landed = landed.reshape(slots, LATENT)
+        if k < LAYERS - 1:
+            before = low
+            node, low, sums, outgoing = node_forward(served, want, landed, node, blocks[3 + 2 * k])
+            node_kept.append((before, sums))
     pieces = [4 * s for s in (VARS + LATENT + 4, GEO + LATENT + 4) + (3 * LATENT + LATENT + 4, 2 * LATENT + LATENT + 4) * LAYERS]
     lead = 4
     places = [0] + [lead + sum(pieces[: i + 1]) for i in range(len(pieces))]
     flat_rows = (lead + PARAMS // 128 + 15) // 16 * 16 + 8
     dec_at = places[-1]
     tail_at = dec_at + 4 * LATENT
-    flat, g_node, d_out, d_vec, errors = decode(
-        inputs, targets, level_mask, land_sea[:, None], count.reshape(1, 1), low, blocks[-1], flat_rows, dec_at
+    k = LAYERS - 1
+    flat, g_node, outgoing, d_out, d_vec, errors = turn(
+        served, want, landed, node, inputs, targets, level_mask, land, count.reshape(1, 1),
+        blocks[3 + 2 * k], blocks[-1], flat_rows, places[3 + 2 * k], dec_at,
     )
     error_here = jnp.sum(errors)
     tail = jnp.concatenate([d_vec[0], d_out[:, :VARS].reshape(-1), d_vec[1, :VARS]])
     tail_rows = flat_rows - tail_at
     tail = jnp.pad(tail, (0, tail_rows * 128 - tail.shape[0])).reshape(tail_rows, 128)
-    landed, g_edge = None, None
+    g_edge = None
     for k in reversed(range(LAYERS)):
-        before, sums, kept = node_kept[k]
-        more = dict(landed=landed) if landed is not None else dict(tail=tail, tail_at=tail_at)
-        flat, g_node, outgoing = node_backward(served, want, g_node, before, sums, kept, blocks[3 + 2 * k], flat, places[3 + 2 * k], **more)
-        returned = exchange(outgoing)
-        ins, kept = edge_kept[k]
-        more = dict(geo=[geo, *geo_kept, blocks[1][1], blocks[1][2]], geo_at=places[1]) if k == 0 else {}
-        flat, g_edge, buffer = edge_backward(pos, pos_s, pos_r, returned, ins, kept, blocks[2 + 2 * k], flat, places[2 + 2 * k], g_edge=g_edge, **more)
-        landed = exchange(buffer)
-    flat = encode_backward(served, landed, g_node, x, enc_kept, blocks[0], flat)
+        more = {}
+        if k == LAYERS - 1:
+            more = dict(tail=tail, tail_at=tail_at)
+        if k == 0:
+            more = dict(geo=(geo, blocks[1]), geo_at=places[1])
+        flat, g_edge, landed = edge_backward(
+            devices, outgoing, edge_kept[k], pos, pos_s, pos_r, blocks[2 + 2 * k], flat, places[2 + 2 * k],
+            5 + (LAYERS - 1 - k), g_edge=g_edge, **more,
+        )
+        landed = landed.reshape(slots, LATENT)
+        if k > 0:
+            before, sums = node_kept[k - 1]
+            flat, g_node, outgoing = node_backward(
+                served, want, landed, g_node, before, sums, blocks[1 + 2 * k], flat, places[1 + 2 * k]
+            )
+    flat = encode_backward(served, landed, g_node, x, blocks[0], flat)
     if mine:
         rows = (share_rows + 6 + 15) // 16 * 16
         error = jnp.zeros((8, 128), jnp.float32).at[0, 0].set(error_here)

time: 810 us -> 690 us (0.85)
  Pallas kernels: 701 us -> 636 us
  local copies, waits for them, and re-layouts: 70.3 us -> 24.1 us
  other arithmetic: 19.1 us -> 10.3 us
    slice x10 -> x1, local copies, waits for them, and re-layouts: 36.6 us -> 1 us  [relaid_blocks(): lines[:size].reshape(shape)]
    pallas_call x22 -> x10, Pallas kernels: 403 us -> 367 us  [the longest x3 139 us: edge_backward(): pl.pallas_call(functools.partial(edge_back_kernel, n, at, g_edge is not N...]
    pallas_call x3 -> x2, Pallas kernels: 50.3 us -> 27 us  [node_forward(): pl.pallas_call(functools.partial(node_kernel, bm), grid=(rows // bm,), ou...]
    reshape x2 -> x1, local copies, waits for them, and re-layouts: 13.4 us -> 0.65 us  [relaid_blocks(): lines[:size].reshape(shape)]
where the time goes in v2:
time: 690 us; the launch traced here: 678 us
  Pallas kernels  636 us (92%)
  local copies, waits for them, and re-layouts  24.1 us (3%)
  other arithmetic  10.3 us (1%)
  between operations  7.16 us (1%)
    pallas_call x1, Pallas kernels, reduce_gradient(): pl.pallas_call(functools.partial(reduce_kernel, share_rows, lead), out_sh...  148 us
    pallas_call x3, Pallas kernels, edge_backward(): pl.pallas_call(functools.partial(edge_back_kernel, n, at, g_edge is not N...  139 us
    pallas_call x3, Pallas kernels, edge_forward(): pl.pallas_call(functools.partial(edge_kernel, n, geo is not None), out_sh...  138 us
    pallas_call x1, Pallas kernels, gather_weights(): pl.pallas_call(gather_kernel, out_shape=(jax.ShapeDtypeStruct((n, rows, 1...  72.3 us
    pallas_call x2, Pallas kernels, node_backward(): pl.pallas_call(functools.partial(node_back_kernel, bm, at), grid=(rows //...  46.9 us
    pallas_call x1, Pallas kernels, turn(): pl.pallas_call(functools.partial(turn_kernel, bm, at, dec_at), grid=(rows...  32.7 us
    pallas_call x2, Pallas kernels, node_forward(): pl.pallas_call(functools.partial(node_kernel, bm), grid=(rows // bm,), ou...  27 us

profile of v2, /device:TPU:27, one launch (start us, length us, event | category | flops | bytes accessed | tf_op | source)
XLA Modules:
  0.0 677.8 jit_solution(10014794208551710619)
XLA Ops:
  0.7 0.9 copy.65
  1.8 0.3 convert_reduce_fusion
  2.0 0.7 broadcast_add_fusion.1
  3.3 0.6 pad.39.ask_ref
  4.0 1.2 convert_bitcast_fusion
  5.1 0.8 pad.38.w_ref
  5.9 1.2 multiply_reduce_fusion
  7.8 0.6 scatter.10.num_ref
  8.4 72.3 %shard_map.163 = (bf16[32,1600,128]{2,1,0:T(8,128)(2,1)}, s32[32,1,128]{2,1,0:T(1,128)}, f32[32,8,128]{2,1,0:T(8,128)}) custom-call(bf16[1600,128]{1,0:T(8,128)(2,1)} %pad.38.w_ref, s32[32,1,128]{2,1,0:T(1,128)} %pad.39.ask_ref, f32[8,128]{1,0:T(8,128)} %scatter.10.num_ref), custom_call_target="tpu_custom_call" | custom-call | tf_op jit(solution)/shard_map/pallas_call | solution.py:207
  80.7 10.8 %relay.1 = (bf16[256,512]{1,0:T(8,128)(2,1)}, bf16[512,512]{1,0:T(8,128)(2,1)}, f32[8,512]{1,0:T(8,128)}, bf16[128,512]{1,0:T(8,128)(2,1)}, bf16[512,512]{1,0:T(...) custom-call(bf16[32,1600,128]{2,1,0:T(8,128)(2,1)} %get-tuple-elemen, ...), custom_call_target="tpu_custom_call" | custom-call | tf_op jit(solution)/shard_map/relay/pallas_call | solution.py:949
  91.6 0.9 broadcast_in_dim_reshape_squeeze.8.want
  92.5 1.5 copy.68.x
  94.0 1.3 pad.40.x
  95.3 8.9 %encode.1 = (f32[2048,512]{1,0:T(8,128)}, bf16[2048,512]{1,0:T(8,128)(2,1)}, bf16[768,512]{1,0:T(8,128)(2,1)}) custom-call(bf16[2048,256]{1,0:T(8,128)(2,1)} %pad.40.x, bf16[256,512]{1,0:T(8,128)(2,1)} %get-tuple-element.120.w_in, bf16[512,512]{1,0:T(8,128)(2,1)} %get-tuple-element.121.w_out, f32[8,512]{1,0:T(8,128)} %get-tuple-element.122.vec, ...), custom_call_target="tpu_custom_call" | custom-call | tf_op jit(solution)/shard_map/encode/pallas_call | solution.py:507
  104.6 0.8 slice_reduce_fusion
  105.5 0.6 pad.41.source.rest_8_
  106.1 44.8 %edge_forward.3 = (f32[256,512]{1,0:T(8,128)}, bf16[256,512]{1,0:T(8,128)(2,1)}, bf16[256,512]{1,0:T(8,128)(2,1)}, bf16[256,512]{1,0:T(8,128)(2,1)}, bf16[32,24,512]{2,1,0:T(8,128)(2,1)}) custom-call(bf16[32,24,512]{2,1,0:T(8,128)(2,1)} %bitcast.41, bf16[256,128]{1,0:T(8,128)(2,1)} %pad.41.source.rest_8_, s32[256,2]{1,0:T(8,128)} %copy-done, ...), custom_call_target="tpu_custom_call" | custom-call | tf_op jit(solution)/shard_map/edge_forward/pallas_call | solution.py:626
  151.0 0.7 broadcast_in_dim_reshape_squeeze.6.served
  151.6 13.7 %node_forward.2 = (f32[2048,512]{1,0:T(8,128)}, bf16[2048,512]{1,0:T(8,128)(2,1)}, bf16[2048,512]{1,0:T(8,128)(2,1)}, bf16[768,512]{1,0:T(8,128)(2,1)}) custom-call(s32[1,768]{1,0:T(1,128)} %broadcast_in_dim_reshape_squeeze.6.served, s32[768,1]{1,0:T(8,128)} %broadcast_in_dim_reshape_squeeze.8.want, bf16[768,512]{1,0:T(8,128)(2,1)} %bitcast.42, ...), custom_call_target="tpu_custom_call" | custom-call | tf_op jit(solution)/shard_map/node_forward/pallas_call | solution.py:538
  165.3 46.4 %edge_forward.4 = (f32[256,512]{1,0:T(8,128)}, bf16[256,512]{1,0:T(8,128)(2,1)}, bf16[256,512]{1,0:T(8,128)(2,1)}, bf16[256,512]{1,0:T(8,128)(2,1)}, bf16[32,24,512]{2,1,0:T(8,128)(2,1)}) custom-call(bf16[32,24,512]{2,1,0:T(8,128)(2,1)} %bitcast.43, f32[256,512]{1,0:T(8,128)} %get-tuple-element.136.source, s32[256,2]{1,0:T(8,128)} %copy-done, ...), custom_call_target="tpu_custom_call" | custom-call | tf_op jit(solution)/shard_map/edge_forward/pallas_call | solution.py:626
  211.8 13.3 %node_forward.3 = (f32[2048,512]{1,0:T(8,128)}, bf16[2048,512]{1,0:T(8,128)(2,1)}, bf16[2048,512]{1,0:T(8,128)(2,1)}, bf16[768,512]{1,0:T(8,128)(2,1)}) custom-call(s32[1,768]{1,0:T(1,128)} %broadcast_in_dim_reshape_squeeze.6.served, s32[768,1]{1,0:T(8,128)} %broadcast_in_dim_reshape_squeeze.8.want, bf16[768,512]{1,0:T(8,128)(2,1)} %bitcast.44, ...), custom_call_target="tpu_custom_call" | custom-call | tf_op jit(solution)/shard_map/node_forward/pallas_call | solution.py:538
  225.1 46.4 %edge_forward.5 = (f32[256,512]{1,0:T(8,128)}, bf16[256,512]{1,0:T(8,128)(2,1)}, bf16[256,512]{1,0:T(8,128)(2,1)}, bf16[256,512]{1,0:T(8,128)(2,1)}, bf16[32,24,512]{2,1,0:T(8,128)(2,1)}) custom-call(bf16[32,24,512]{2,1,0:T(8,128)(2,1)} %bitcast.45, f32[256,512]{1,0:T(8,128)} %get-tuple-element.146.source, s32[256,2]{1,0:T(8,128)} %copy-done, ...), custom_call_target="tpu_custom_call" | custom-call | tf_op jit(solution)/shard_map/edge_forward/pallas_call | solution.py:626
  271.4 1.0 slice_bitcast_fusion
  272.5 1.4 scatter.11.c_vec
  273.8 1.0 slice.82
  274.8 0.7 reshape.218
  275.5 0.7 pad.42.c_out
  276.2 0.6 reduce_sum.69
  276.9 2.9 copy.76.target
  279.7 1.8 copy.77.level
  281.6 1.3 copy.78.land
  282.9 32.7 %turn.1 = (f32[51160,128]{1,0:T(8,128)}, f32[2048,512]{1,0:T(8,128)}, bf16[768,512]{1,0:T(8,128)(2,1)}, f32[512,256]{1,0:T(8,128)}, f32[8,512]{1,0:T(8,128)}, /*index=5*/f32[1,256]{1,0:T(1,128)}) custom-call(s32[1,768]{1,0:T(1,128)} %broadcast_in_dim_reshape_squeeze.6.served, s32[768,1]{1,0:T(8,128)} %broadcast_in_dim_reshape_squeeze.8.want, ...), custom_call_target="tpu_custom_call" | custom-call | tf_op jit(solution)/shard_map/turn/pallas_call | solution.py:689
  315.7 1.6 reshape.221
  317.3 0.7 slice.86
  318.0 0.7 slice.88
  318.7 0.8 fusion.3.rest_4_
  319.5 46.4 %edge_backward.3 = (f32[51160,128]{1,0:T(8,128)}, f32[256,512]{1,0:T(8,128)}, bf16[32,24,512]{2,1,0:T(8,128)(2,1)}) custom-call(bf16[32,24,512]{2,1,0:T(8,128)(2,1)} %bitcast.46, bf16[256,512]{1,0:T(8,128)(2,1)} %get-tuple-element.159.edge_low, bf16[256,512]{1,0:T(8,128)(2,1)} %get-tuple-element.160.sent, ...), custom_call_target="tpu_custom_call", output_to_operand_aliasing={{0}: (10, {})} | custom-call | tf_op jit(solution)/shard_map/edge_backward/pallas_call | solution.py:781
  365.9 23.4 %node_backward.2 = (f32[51160,128]{1,0:T(8,128)}, f32[2048,512]{1,0:T(8,128)}, bf16[768,512]{1,0:T(8,128)(2,1)}) custom-call(s32[1,768]{1,0:T(1,128)} %broadcast_in_dim_reshape_squeeze.6.served, s32[768,1]{1,0:T(8,128)} %broadcast_in_dim_reshape_squeeze.8.want, bf16[768,512]{1,0:T(8,128)(2,1)} %bitcast.50, ...), custom_call_target="tpu_custom_call", output_to_operand_aliasing={{0}: (9, {})} | custom-call | tf_op jit(solution)/shard_map/node_backward/pallas_call | solution.py:818
  389.3 46.4 %edge_backward.4 = (f32[51160,128]{1,0:T(8,128)}, f32[256,512]{1,0:T(8,128)}, bf16[32,24,512]{2,1,0:T(8,128)(2,1)}) custom-call(bf16[32,24,512]{2,1,0:T(8,128)(2,1)} %bitcast.48, bf16[256,512]{1,0:T(8,128)(2,1)} %get-tuple-element.171.edge_low, bf16[256,512]{1,0:T(8,128)(2,1)} %get-tuple-element.172.sent, ...), custom_call_target="tpu_custom_call", output_to_operand_aliasing={{0}: (10, {})} | custom-call | tf_op jit(solution)/shard_map/edge_backward/pallas_call | solution.py:781
  435.7 23.5 %node_backward.3 = (f32[51160,128]{1,0:T(8,128)}, f32[2048,512]{1,0:T(8,128)}, bf16[768,512]{1,0:T(8,128)(2,1)}) custom-call(s32[1,768]{1,0:T(1,128)} %broadcast_in_dim_reshape_squeeze.6.served, s32[768,1]{1,0:T(8,128)} %broadcast_in_dim_reshape_squeeze.8.want, bf16[768,512]{1,0:T(8,128)(2,1)} %bitcast.49, ...), custom_call_target="tpu_custom_call", output_to_operand_aliasing={{0}: (9, {})} | custom-call | tf_op jit(solution)/shard_map/node_backward/pallas_call | solution.py:818
  459.2 46.6 %edge_backward.5 = (f32[51160,128]{1,0:T(8,128)}, f32[256,512]{1,0:T(8,128)}, bf16[32,24,512]{2,1,0:T(8,128)(2,1)}) custom-call(bf16[32,24,512]{2,1,0:T(8,128)(2,1)} %bitcast.47, bf16[256,512]{1,0:T(8,128)(2,1)} %get-tuple-element.182.edge_low, bf16[256,512]{1,0:T(8,128)(2,1)} %get-tuple-element.183.sent, ...), custom_call_target="tpu_custom_call", output_to_operand_aliasing={{0}: (13, {})} | custom-call | tf_op jit(solution)/shard_map/edge_backward/pallas_call | solution.py:781
  505.8 12.4 %encode_backward.1.g_ref = f32[51160,128]{1,0:T(8,128)} custom-call(s32[1,768]{1,0:T(1,128)} %broadcast_in_dim_reshape_squeeze.6.served, bf16[768,512]{1,0:T(8,128)(2,1)} %bitcast.39, f32[2048,512]{1,0:T(8,128)} %get-tuple-element.188.g_node, bf16[2048,256]{1,0:T(8,128)(2,1)} %pad.40.x, ...), custom_call_target="tpu_custom_call", output_to_operand_aliasing={{}: (7, {})} | custom-call | tf_op jit(solution)/shard_map/encode_backward/pallas_call | solution.py:854
  518.2 0.6 reduce_sum.70
  518.8 0.6 scatter.14.err_ref
  519.5 148.2 %shard_map.164 = (f32[1616,128]{1,0:T(8,128)S(1)}, f32[32,8,128]{2,1,0:T(8,128)S(1)}, f32[32,8,128]{2,1,0:T(8,128)S(1)}) custom-call(f32[51160,128]{1,0:T(8,128)} %encode_backward.1.g_ref, f32[8,128]{1,0:T(8,128)S(1)} %scatter.14.err_ref), custom_call_target="tpu_custom_call" | custom-call | tf_op jit(solution)/shard_map/pallas_call | solution.py:336
  667.6 0.6 reduce_sum.72
  669.6 0.6 reduce_sum.71
  671.7 3.4 multiply_add_fusion
  (39 shorter events, 1.3 us)
Async XLA Ops:
  0.6 5.3 copy-start.7
  0.6 5.3 copy-start.2
  80.7 10.8 %copy-start.8 = (s32[32,1,128]{2,1,0:T(1,128)S(1)}, s32[32,1,128]{2,1,0:T(1,128)}, u32[]{:S(2)}) copy-start(s32[32,1,128]{2,1,0:T(1,128)} %get-tuple-element.118) | copy-start | bytes 49156
  94.0 10.3 %copy-start.1 = (bf16[2048,227]{1,0:T(8,128)(2,1)}, bf16[2048,227]{1,0:T(8,128)(2,1)S(1)}, u32[]{:S(2)}) copy-start(bf16[2048,227]{1,0:T(8,128)(2,1)S(1)} %copy.68.x) | copy-start | bytes 2789380
  94.0 10.4 %copy-start.9 = (s32[256,2]{0,1:T(2,128)S(1)}, s32[256,2]{0,1:T(2,128)}, u32[]{:S(2)}) copy-start(s32[256,2]{0,1:T(2,128)} %param.23) | copy-start | bytes 6148
  95.3 10.1 %copy-start.10 = (bf16[256,4]{0,1:T(4,128)(2,1)S(1)}, bf16[256,4]{0,1:T(4,128)(2,1)}, u32[]{:S(2)}) copy-start(bf16[256,4]{0,1:T(4,128)(2,1)} %param.20) | copy-start | bytes 6148
  104.6 1.5 copy-start
  225.0 51.2 %copy-start.6 = (f32[32,8,128]{2,1,0:T(8,128)S(1)}, f32[32,8,128]{2,1,0:T(8,128)}, u32[]{:S(2)}) copy-start(f32[32,8,128]{2,1,0:T(8,128)} %get-tuple-element.152) | copy-start | bytes 393220
  505.8 12.4 %copy-start.11 = (f32[1,256]{1,0:T(1,128)S(1)}, f32[1,256]{1,0:T(1,128)}, u32[]{:S(2)}) copy-start(f32[1,256]{1,0:T(1,128)} %get-tuple-element.190) | copy-start | bytes 3076
  519.4 152.3 %copy-start.3 = (f32[204544]{0:T(1024)S(1)}, f32[204544]{0:T(1024)}, u32[]{:S(2)}) copy-start(f32[204544]{0:T(1024)} %param.26) | copy-start | bytes 2454532
  519.5 152.3 %copy-start.4 = (f32[204544]{0:T(1024)S(1)}, f32[204544]{0:T(1024)}, u32[]{:S(2)}) copy-start(f32[204544]{0:T(1024)} %param.29) | copy-start | bytes 2454532
  519.5 152.3 %copy-start.5 = (f32[204544]{0:T(1024)S(1)}, f32[204544]{0:T(1024)}, u32[]{:S(2)}) copy-start(f32[204544]{0:T(1024)} %param.28) | copy-start | bytes 2454532

commit v3 on v2

--- a/solution.py
+++ b/solution.py
@@ -1,4 +1,5 @@
 import functools
+import types
 
 import jax
 import jax.numpy as jnp
@@ -109,15 +110,31 @@
         return ((z * 2 + y) * 2 + x) * 2 + c
     greet(n, me)
     tx, ty, tc = dev(z, y, 1 - x, c), dev(z, 1 - y, x, c), dev(z, y, x, 1 - c)
+    up, down = dev(lax.rem(z + 1, 4), y, x, c), dev(lax.rem(z + 3, 4), y, x, c)
     pend = []
     def start(cp):
         cp.start(); pend.append(cp)
     mine = pltpu.make_async_copy(w_ref, o_ref.at[me], own.at[0])
     mine.start()
+    planes = [z, z + 1 - 2 * lax.rem(z, 2), 2 - z // 2, 3 - 3 * (z // 2)]
+    def on_up(i, wait):
+        src = w_ref if i == 0 else o_ref.at[dev(planes[i], y, x, c)]
+        slot = dev(planes[i], y, x, c)
+        @pl.when((planes[i] <= z) & (z < 3))
+        def _():
+            cp = remote(src, o_ref.at[slot], zs.at[0, i], zr.at[planes[i]], up)
+            cp.wait_send() if wait else cp.start()
+    def on_down(i, wait):
+        src = w_ref if i == 0 else o_ref.at[dev(planes[i], y, x, c)]
+        slot = dev(planes[i], y, x, c)
+        @pl.when((planes[i] >= z) & (z > 0))
+        def _():
+            cp = remote(src, o_ref.at[slot], zs.at[1, i], zr.at[planes[i]], down)
+            cp.wait_send() if wait else cp.start()
     start(remote(w_ref.at[A], o_ref.at[me, A], hs.at[0, 0], hr.at[0, 0], tx))
     start(remote(w_ref.at[B], o_ref.at[me, B], hs.at[0, 1], hr.at[0, 1], ty))
-    for j in (1, 3, 2):
-        start(remote(w_ref, o_ref.at[me], zs.at[j], zr.at[4 - j], dev(lax.rem(z + j, 4), y, x, c)))
+    on_up(0, False)
+    on_down(0, False)
     start(remote(w_ref, o_ref.at[me], bs.at[0], br.at[0], tc))
     mine2 = pltpu.make_async_copy(ask_ref.at[me], served_ref.at[me], own.at[1])
     mine2.start()
@@ -134,20 +151,30 @@
         i = nb[0]; nb[0] += 1
         ref = o_ref.at[slot] if part is None else o_ref.at[slot, part]
         start(remote(ref, ref, bs.at[i], br.at[i], tc))
-    def second(k, zz):
+    def first(k):
+        s = dev(planes[k], y, x, c)
+        remote(w_ref, o_ref.at[s], zs.at[0, k], zr.at[planes[k]], tc).wait_recv()
+        start(remote(o_ref.at[s, A], o_ref.at[s, A], hs.at[k, 0], hr.at[k, 0], tx))
+        start(remote(o_ref.at[s, B], o_ref.at[s, B], hs.at[k, 1], hr.at[k, 1], ty))
+        on_up(k, False)
+        on_down(k, False)
+        sib(s, None)
+    def second(k):
+        zz = planes[k]
         s = dev(zz, y, x, c)
         sx, sy = dev(zz, y, 1 - x, c), dev(zz, 1 - y, x, c)
         own_a = w_ref.at[A] if k == 0 else o_ref.at[s, A]
         own_b = w_ref.at[B] if k == 0 else o_ref.at[s, B]
+        start(remote(own_a, o_ref.at[s, A], cs.at[k, 0], cr.at[k, 0], ty))
+        start(remote(own_b, o_ref.at[s, B], ds.at[k, 0], dr.at[k, 0], tx))
         remote(own_a, o_ref.at[sx, A], hs.at[k, 0], hr.at[k, 0], tx).wait_recv()
-        start(remote(own_a, o_ref.at[s, A], cs.at[k, 0], cr.at[k, 0], ty))
         start(remote(o_ref.at[sx, A], o_ref.at[sx, A], cs.at[k, 1], cr.at[k, 1], ty))
         remote(own_b, o_ref.at[sy, B], hs.at[k, 1], hr.at[k, 1], ty).wait_recv()
-        start(remote(own_b, o_ref.at[s, B], ds.at[k, 0], dr.at[k, 0], tx))
         start(remote(o_ref.at[sy, B], o_ref.at[sy, B], ds.at[k, 1], dr.at[k, 1], tx))
         sib(sx, A)
         sib(sy, B)
-    def third(k, zz):
+    def third(k):
+        zz = planes[k]
         sx, sy, sd = dev(zz, y, 1 - x, c), dev(zz, 1 - y, x, c), dev(zz, 1 - y, 1 - x, c)
         w = w_ref.at[A]
         remote(w, o_ref.at[sy, A], cs.at[k, 0], cr.at[k, 0], ty).wait_recv()
@@ -158,45 +185,40 @@
         sib(sd, A)
         remote(w, o_ref.at[sd, B], ds.at[k, 1], dr.at[k, 1], tx).wait_recv()
         sib(sd, B)
-    def first(k, zz):
-        s = dev(zz, y, x, c)
-        remote(w_ref, o_ref.at[s], zs.at[k], zr.at[k], tc).wait_recv()
-        start(remote(o_ref.at[s, A], o_ref.at[s, A], hs.at[k, 0], hr.at[k, 0], tx))
-        start(remote(o_ref.at[s, B], o_ref.at[s, B], hs.at[k, 1], hr.at[k, 1], ty))
-        sib(s, None)
-    order = [0, 1, 3, 2]
-    zz = [lax.rem(z + k, 4) for k in range(4)]
-    second(0, zz[0])
-    first(1, zz[1])
-    second(1, zz[1])
-    first(3, zz[3])
-    third(0, zz[0])
-    second(3, zz[3])
-    first(2, zz[2])
-    third(1, zz[1])
-    second(2, zz[2])
-    third(3, zz[3])
-    third(2, zz[2])
+    second(0)
+    first(1)
+    third(0)
+    second(1)
+    first(2)
+    third(1)
+    second(2)
+    first(3)
+    third(2)
+    second(3)
+    third(3)
     nb2 = [0]
-    def got(part):
-        i = nb2[0]; nb2[0] += 1
-        ref = w_ref if part is None else w_ref.at[part]
-        o = o_ref.at[me] if part is None else o_ref.at[me, part]
-        remote(ref, o, bs.at[i], br.at[i], tc).wait_recv()
-    got(None)
-    def g2(): got(A); got(B)
-    def g3(): got(A); got(B); got(A); got(B)
-    def g1(): got(None)
-    g2(); g1(); g2(); g1(); g3(); g2(); g1(); g3(); g2(); g3(); g3()
+    def got(*parts):
+        for part in parts:
+            i = nb2[0]; nb2[0] += 1
+            ref = w_ref if part is None else w_ref.at[part]
+            o = o_ref.at[me] if part is None else o_ref.at[me, part]
+            remote(ref, o, bs.at[i], br.at[i], tc).wait_recv()
+    g1, g2, g3 = (None,), (A, B), (A, B, A, B)
+    for g in (g1, g2, g1, g3, g2, g1, g3, g2, g1, g3, g2, g3):
+        got(*g)
     def end(j, carry):
         t = lax.rem(me + j, n)
         remote(ask_ref.at[t], served_ref.at[me], small_s.at[0, j], small_r.at[0, j], t).wait()
         remote(num_ref, nums_ref.at[me], small_s.at[1, j], small_r.at[1, j], t).wait()
         return carry
     lax.fori_loop(1, n, end, 0)
+    for i in range(4):
+        on_up(i, True)
+        on_down(i, True)
     for cp in pend:
         cp.wait_send()
     mine.wait(); mine2.wait(); mine3.wait()
+
 
 def gather_weights(w, ask, num, cid):
     n = 32
@@ -208,7 +230,7 @@
         gather_kernel,
         out_shape=(jax.ShapeDtypeStruct((n, rows, 128), w.dtype), jax.ShapeDtypeStruct(ask.shape, ask.dtype), jax.ShapeDtypeStruct((n,) + num.shape, num.dtype)),
         in_specs=[anyspec] * 3, out_specs=(anyspec,) * 3,
-        scratch_shapes=[D((3,)), D((2, n)), D((2, n)), D((4,)), D((4,)), D((4, 2)), D((4, 2)), D((4, 2)), D((4, 2)), D((4, 2)), D((4, 2)), D((sib,)), D((sib,))],
+        scratch_shapes=[D((3,)), D((2, n)), D((2, n)), D((2, 4)), D((4,)), D((4, 2)), D((4, 2)), D((4, 2)), D((4, 2)), D((4, 2)), D((4, 2)), D((sib,)), D((sib,))],
         compiler_params=pltpu.CompilerParams(collective_id=cid, has_side_effects=True),
     )(w, ask, num)
 
@@ -224,6 +246,9 @@
     if rows % step:
         at = pl.ds(whole * step, rows % step)
         dst[at] = dst[at] + src[at]
+
+SCHEDULE = ['g0', 'g1', 's0', 'm0', 'g2', 's1', 'f0', 'm1', 'g3', 's2', 'f1', 'm2', 's3', 'f2', 'm3', 'f3']
+
 
 def reduce_kernel(share_rows, lead, g_ref, err_ref, o_ref, sq_ref, errs_ref, L, R, YA, XA, XB, YB, Z, sq, own, ls, rs0_s, rs0_r, as1, ar1, as2, ar2, bs1, br1, bs2, br2, zs, zr, es, er, qs, qr):
     n = 32
@@ -241,9 +266,9 @@
     pend = []
     def start(cp):
         cp.start(); pend.append(cp)
-    order = [1, 2, 3, 0]
+    order = [2, 1, 3, 0]
     zz = [lax.rem(z + k, 4) for k in range(4)]
-    for k in order:
+    def fetch(k):
         for i in range(4):
             ys, xs = i // 2, i % 2
             start(remote(g_ref.at[pl.ds(begin(dev(zz[k], ys, xs, 1 - c)), rows)], R.at[k, i], rs0_s.at[k, i], rs0_r.at[k, i], tc))
@@ -280,34 +305,29 @@
         accumulate(L.at[k, i_own, B], YB.at[k], half)
         if k:
             start(remote(L.at[k, i_own], Z.at[k - 1], zs.at[k - 1], zr.at[k - 1], dev(zz[k], y, x, c)))
-    s0(1)
-    s0(2)
-    mid(1)
-    s0(3)
-    mid(2)
-    fin(1)
-    s0(0)
-    mid(3)
-    fin(2)
-    mid(0)
-    fin(3)
-    fin(0)
+    for step in SCHEDULE:
+        {"g": fetch, "s": s0, "m": mid, "f": fin}[step[0]](order[int(step[1])])
     for k in range(3):
         remote(L.at[0, 0], Z.at[k], zs.at[k], zr.at[k], tc).wait_recv()
     first = lax.rem(lead + share_rows * me, 8)
     sq[...] = jnp.zeros_like(sq)
     mine = L.at[0, i_own]
-    def total(i, carry):
-        r = pl.multiple_of(i * 8, 8)
-        at = pl.ds(r, 8)
+    def total(r, size):
+        at = pl.ds(r, size)
         v = mine[at] + Z[0, at] + (Z[1, at] + Z[2, at])
         o_ref[at] = v
-        row = r + lax.broadcasted_iota(jnp.int32, (8, 128), 0)
+        row = r + lax.broadcasted_iota(jnp.int32, (size, 128), 0)
         inside = (row >= first) & (row < first + share_rows)
         v = jnp.where(inside, v, 0.0)
-        sq[...] += v * v
+        v = v * v
+        sq[...] += jnp.sum(v.reshape(size // 8, 8, 128), axis=0)
+    step = 80
+    def several(i, carry):
+        total(pl.multiple_of(i * step, 8), step)
         return carry
-    lax.fori_loop(0, rows // 8, total, 0)
+    lax.fori_loop(0, rows // step, several, 0)
+    if rows % step:
+        total(rows // step * step, rows % step)
     q_own = pltpu.make_async_copy(sq, sq_ref.at[me], own.at[1])
     q_own.start()
     def go2(j, carry):
@@ -404,8 +424,9 @@
 
 
 def norm_back(g, hat, inv, vec, d_vec):
-    d_vec[2:3, :] += col(g * hat)
-    d_vec[3:4, :] += col(g)
+    if d_vec is not None:
+        d_vec[2:3, :] += col(g * hat)
+        d_vec[3:4, :] += col(g)
     s = g * vec[2:3, :]
     post = inv * (
         s - jnp.mean(s, axis=-1, keepdims=True) - hat * jnp.mean(s * hat, axis=-1, keepdims=True)
@@ -465,16 +486,6 @@
     return jax.ShapeDtypeStruct(shape, dtype)
 
 
-def send_rows(i, bm, low, want, out, acc):
-    @pl.when(i == 0)
-    def _():
-        clear(acc)
-    acc[...] += mm(pick(want[...], i * bm, bm), low)
-    @pl.when(i == pl.num_programs(0) - 1)
-    def _():
-        out[...] = acc[...].astype(BF16)
-
-
 def store_flat(packed, flat, at, sem):
     copy = pltpu.make_async_copy(packed, flat.at[pl.ds(at, packed.shape[0])], sem)
     copy.start()
@@ -489,62 +500,23 @@
     return pltpu.VMEM((lead + 4 * rows_in + 4 * LATENT + 16, 128), F32)
 
 
-def encode_kernel(bm, x, w_in, w_out, vec, want, node, low, out, acc):
-    i = pl.program_id(0)
-    _, act = activate(first_half([x[...]], w_in, vec))
-    hat, _ = second_half(act, w_out, vec)
-    r = scale_shift(hat, vec)
-    node[...] = r
-    rounded = r.astype(BF16)
-    low[...] = rounded
-    send_rows(i, bm, rounded, want, out, acc)
-
-
-def encode(x, block, want, bm=512):
-    rows, k = x.shape
-    slots = want.shape[0]
-    w_in, w_out, vec = block
-    return pl.pallas_call(
-        functools.partial(encode_kernel, bm),
-        grid=(rows // bm,),
-        out_shape=(shaped(rows, LATENT), shaped(rows, LATENT, dtype=BF16), shaped(slots, LATENT, dtype=BF16)),
-        in_specs=[spec((bm, k), False), spec(w_in.shape), spec(w_out.shape), spec(vec.shape), spec((slots, 1))],
-        out_specs=(spec((bm, LATENT), False), spec((bm, LATENT), False), spec((slots, LATENT))),
-        scratch_shapes=[pltpu.VMEM((slots, LATENT), F32)],
-        compiler_params=params(),
-        name="encode",
-    )(x, w_in, w_out, vec, want)
-
-
-def node_kernel(bm, served, want, landed, node, w_in, w_out, vec, node_new, low_new, sums, out, acc):
-    i = pl.program_id(0)
-    got = mm(place(served[...], i * bm, bm), landed[...]).astype(BF16)
-    sums[...] = got
-    old = node[...]
-    _, act = activate(first_half([old.astype(BF16), got], w_in, vec))
-    hat, _ = second_half(act, w_out, vec)
-    r = old + scale_shift(hat, vec)
-    node_new[...] = r
-    rounded = r.astype(BF16)
-    low_new[...] = rounded
-    send_rows(i, bm, rounded, want, out, acc)
-
-
-def node_forward(served, want, landed, node, block, bm=512):
-    rows = node.shape[0]
-    slots = want.shape[0]
-    w_in, w_out, vec = block
-    b = lambda: spec((bm, LATENT), False)
-    return pl.pallas_call(
-        functools.partial(node_kernel, bm),
-        grid=(rows // bm,),
-        out_shape=(shaped(rows, LATENT), shaped(rows, LATENT, dtype=BF16), shaped(rows, LATENT, dtype=BF16), shaped(slots, LATENT, dtype=BF16)),
-        in_specs=[spec((1, slots)), spec((slots, 1)), spec((slots, LATENT)), b(), spec(w_in.shape), spec(w_out.shape), spec(vec.shape)],
-        out_specs=(b(), b(), b(), spec((slots, LATENT))),
-        scratch_shapes=[pltpu.VMEM((slots, LATENT), F32)],
-        compiler_params=params(),
-        name="node_forward",
-    )(served, want, landed, node, w_in, w_out, vec)
+def named_call(body, name, inputs, outputs, scratch, aliases=None, cid=None):
+    names = [*inputs, *outputs, *scratch]
+    aliases = {list(inputs).index(i): list(outputs).index(o) for i, o in (aliases or {}).items()}
+    def kernel(*refs):
+        body(types.SimpleNamespace(**dict(zip(names, refs))))
+    more = {} if cid is None else dict(collective_id=cid, has_side_effects=True)
+    values = pl.pallas_call(
+        kernel,
+        out_shape=tuple(shape for shape, _ in outputs.values()),
+        in_specs=[s for _, s in inputs.values()],
+        out_specs=tuple(s for _, s in outputs.values()),
+        scratch_shapes=list(scratch.values()),
+        input_output_aliases=aliases,
+        compiler_params=params(**more),
+        name=name,
+    )(*[v for v, _ in inputs.values()])
+    return types.SimpleNamespace(**dict(zip(outputs, values)))
 
 
 def swap_start(n, me, src, dst, own, ssem, rsem):
@@ -569,79 +541,170 @@
     return ref[...].reshape(ref.shape[0] * ref.shape[1], ref.shape[2])
 
 
-def edge_kernel(n, first, outgoing, source, pos, pos_r, *rest):
-    rest = list(rest)
-    blocks = rest[:3]
-    geo_blocks = rest[3:6] if first else []
-    rest = rest[6 if first else 3 :]
-    edge_new, edge_low, sent, recv, landed, arrived, buffer, w_in, w_out, vec, own, s1, r1, s2, r2, wsem = rest[:16]
-    held = [w_in, w_out, vec] + rest[16:]
-    loads = [pltpu.make_async_copy(a, b, wsem.at[i]) for i, (a, b) in enumerate(zip(blocks + geo_blocks, held))]
-    for load in loads:
-        load.start()
+def greet_start(n, me):
+    barrier = pltpu.get_barrier_semaphore()
+    def hello(j, c):
+        pl.semaphore_signal(barrier, inc=1, device_id=(lax.rem(me + j, n),), device_id_type=MESH)
+        return c
+    lax.fori_loop(1, n, hello, 0)
+
+
+def greet_wait(n):
+    pl.semaphore_wait(pltpu.get_barrier_semaphore(), n - 1)
+
+
+class Loads:
+    def __init__(self, r, sem):
+        self.r, self.sem, self.copies = r, sem, {}
+
+    def start(self, *names):
+        for name in names:
+            copy = pltpu.make_async_copy(getattr(self.r, name), getattr(self.r, "_" + name), self.sem.at[len(self.copies)])
+            copy.start()
+            self.copies[name] = copy
+
+    def wait(self, *names):
+        for name in names:
+            self.copies[name].wait()
+
+
+def store_all(r, sem, *names):
+    copies = [pltpu.make_async_copy(getattr(r, "_" + name), getattr(r, name), sem.at[i]) for i, name in enumerate(names)]
+    for copy in copies:
+        copy.start()
+    return copies
+
+
+def same_rows(want, served):
+    return jnp.where((want[...] == served[...]) & (want[...] >= 0), 1.0, 0.0).astype(BF16)
+
+
+def swap_scratch(shape, n):
+    return dict(away=pltpu.VMEM(shape, BF16), here=pltpu.VMEM(shape, BF16), back=pltpu.VMEM(shape, BF16), own=DMA((2,)), s1=DMA((n,)), r1=DMA((n,)), s2=DMA((n,)), r2=DMA((n,)))
+
+
+def held(prefix, block):
+    return {prefix + part: pltpu.VMEM(a.shape, a.dtype) for part, a in zip(("_in", "_out", "_vec"), block)}
+
+
+def weights(prefix, block):
+    return {prefix + part: (a, ANY) for part, a in zip(("_in", "_out", "_vec"), block)}
+
+
+def rows_block(bm, width=LATENT):
+    return pl.BlockSpec((bm, width), lambda i: (i, 0))
+
+
+def edge_kernel(n, first, bm, r):
     me = lax.axis_index("dev")
-    greet(n, me)
-    swap_start(n, me, outgoing, arrived, own.at[0], s1, r1)
-    for load in loads:
-        load.wait()
+    greet_start(n, me)
+    loads = Loads(r, r.lsem)
+    node_weights = ["p_in", "p_out", "p_vec"]
+    early = node_weights + ([] if first else ["landed_in", "slots_in"])
+    late = ["e_in", "e_out", "e_vec"] + (["g_in", "g_out", "g_vec"] if first else [])
+    loads.start(*early)
+    loads.start(*late)
+    loads.wait(*early)
+    count = r.want.shape[0]
     if first:
-        g_in, g_out, g_vec = held[3:]
-        _, act = activate(first_half([source[...]], g_in, g_vec))
-        hat, _ = second_half(act, g_out, g_vec)
-        edge = scale_shift(hat, g_vec)
+        rows = r.x.shape[0]
+        us = [mm(pick(r.want[...], 0, rows), r.x[...]).astype(BF16)]
     else:
-        edge = source[...]
-    e = edge.astype(BF16)
-    edge_low[...] = e
-    slots = n * arrived.shape[1]
-    pre = first_half([e], w_in, vec)
-    pick_s, pick_r = pick(pos[:, 0:1], 0, slots), pick(pos[:, 1:2], 0, slots)
-    put_r = place(pos_r[...], 0, slots)
-    swap_wait(n, me, outgoing, arrived, own.at[0], s1, r1)
-    rows = flat_rows_of(arrived)
+        landed = flat_rows_of(r._landed_in)
+        got = mm(same_rows(r.want, r.served), landed).astype(BF16)
+        r._sums_s[...] = got
+        old = r._slots_in[...]
+        us = [old.astype(BF16), got]
+    _, act = activate(first_half(us, r._p_in, r._p_vec))
+    hat, _ = second_half(act, r._p_out, r._p_vec)
+    slots = scale_shift(hat, r._p_vec)
+    if not first:
+        slots = old + slots
+    r._slots[...] = slots
+    r.away[...] = slots.astype(BF16).reshape(r.away.shape)
+    greet_wait(n)
+    swap_start(n, me, r.away, r.here, r.own.at[0], r.s1, r.r1)
+    stores = store_all(r, r.ssem, *(["slots"] if first else ["slots", "sums_s"]))
+    loads.wait(*late)
+    if first:
+        _, act = activate(first_half([r.source[...]], r._g_in, r._g_vec))
+        hat, _ = second_half(act, r._g_out, r._g_vec)
+        r._edge[...] = scale_shift(hat, r._g_vec)
+    else:
+        r._edge[...] = r.source[...]
+    e = r._edge[...].astype(BF16)
+    r.edge_low[...] = e
+    r._pre[...] = first_half([e], r._e_in, r._e_vec)
+    if first:
+        def body(node, low):
+            i = pl.program_id(0)
+            u = r.x[pl.ds(pl.multiple_of(i * bm, bm), bm), :]
+            _, act = activate(first_half([u], r._p_in, r._p_vec))
+            hat, _ = second_half(act, r._p_out, r._p_vec)
+            new = scale_shift(hat, r._p_vec)
+            node[...] = new
+            low[...] = new.astype(BF16)
+        pltpu.emit_pipeline(body, grid=(r.node.shape[0] // bm,), in_specs=[], out_specs=[rows_block(bm)] * 2)(r.node, r.low)
+    else:
+        def body(node_in, node, low, sums):
+            i = pl.program_id(0)
+            got = mm(place(r.served[...], i * bm, bm), flat_rows_of(r._landed_in)).astype(BF16)
+            sums[...] = got
+            old = node_in[...]
+            _, act = activate(first_half([old.astype(BF16), got], r._p_in, r._p_vec))
+            hat, _ = second_half(act, r._p_out, r._p_vec)
+            new = old + scale_shift(hat, r._p_vec)
+            node[...] = new
+            low[...] = new.astype(BF16)
+        pltpu.emit_pipeline(body, grid=(r.node.shape[0] // bm,), in_specs=[rows_block(bm)], out_specs=[rows_block(bm)] * 3)(r.node_in, r.node, r.low, r.sums)
+    pick_s, pick_r = pick(r.pos[:, 0:1], 0, count), pick(r.pos[:, 1:2], 0, count)
+    put_r = place(r.pos_r[...], 0, count)
+    swap_wait(n, me, r.away, r.here, r.own.at[0], r.s1, r.r1)
+    rows = flat_rows_of(r.here)
     s = mm(pick_s, rows).astype(BF16)
-    r = mm(pick_r, rows).astype(BF16)
-    pre = pre + mm(s, w_in[LATENT : 2 * LATENT, :]) + mm(r, w_in[2 * LATENT :, :])
+    v = mm(pick_r, rows).astype(BF16)
+    pre = r._pre[...] + mm(s, r._e_in[LATENT : 2 * LATENT, :]) + mm(v, r._e_in[2 * LATENT :, :])
     _, act = activate(pre)
-    hat, _ = second_half(act, w_out, vec)
-    new = edge + scale_shift(hat, vec)
-    buffer[...] = mm(put_r, new.astype(BF16)).astype(BF16).reshape(buffer.shape)
-    swap_start(n, me, buffer, landed, own.at[1], s2, r2)
-    edge_new[...] = new
-    sent[...], recv[...] = s, r
-    swap_wait(n, me, buffer, landed, own.at[1], s2, r2)
-
-
-def held_scratch(block):
-    return [pltpu.VMEM(a.shape, a.dtype) for a in block]
-
-
-def edge_forward(n, outgoing, source, pos, pos_r, block, cid, geo=None):
-    rows = source.shape[0]
-    slots = outgoing.shape[0]
-    outgoing = outgoing.reshape(n, slots // n, LATENT)
+    hat, _ = second_half(act, r._e_out, r._e_vec)
+    new = r._edge[...] + scale_shift(hat, r._e_vec)
+    r.back[...] = mm(put_r, new.astype(BF16)).astype(BF16).reshape(r.back.shape)
+    swap_start(n, me, r.back, r.landed, r.own.at[1], r.s2, r.r2)
+    r.edge[...] = new
+    r.sent[...], r.recv[...] = s, v
+    for store in stores:
+        store.wait()
+    swap_wait(n, me, r.back, r.landed, r.own.at[1], r.s2, r.r2)
+
+
+def edge_forward(n, cid, source, routes, edge_block, node_block, rows, x=None, geo_block=None, landed=None, node=None, slots=None, bm=512):
+    first = x is not None
+    want, served, pos, pos_s, pos_r = routes
+    count = want.shape[0]
+    edges = source.shape[0]
+    shape = (n, count // n, LATENT)
     V = pl.BlockSpec(memory_space=pltpu.VMEM)
-    weights = list(block) + list(geo or ())
+    inputs = dict(source=(source, V), want=(want, V), served=(served, V), pos=(pos, V), pos_r=(pos_r, V))
+    inputs |= weights("p", node_block) | weights("e", edge_block)
+    scratch = held("_p", node_block) | held("_e", edge_block) | swap_scratch(shape, n)
+    scratch |= dict(_slots=pltpu.VMEM((count, LATENT), F32), _edge=pltpu.VMEM((edges, LATENT), F32), _pre=pltpu.VMEM((edges, LATENT), F32), lsem=DMA((12,)), ssem=DMA((2,)))
     low = lambda r: shaped(r, LATENT, dtype=BF16)
-    return pl.pallas_call(
-        functools.partial(edge_kernel, n, geo is not None),
-        out_shape=(shaped(rows, LATENT), low(rows), low(rows), low(rows), shaped(*outgoing.shape, dtype=BF16)),
-        in_specs=[ANY, V, V, V] + [ANY] * len(weights),
-        out_specs=(V, V, V, V, ANY),
-        scratch_shapes=[pltpu.VMEM(outgoing.shape, BF16), pltpu.VMEM(outgoing.shape, BF16)]
-        + held_scratch(block)
-        + [DMA((2,)), DMA((n,)), DMA((n,)), DMA((n,)), DMA((n,)), DMA((6,))]
-        + held_scratch(geo or ()),
-        compiler_params=params(collective_id=cid, has_side_effects=True),
-        name="edge_forward",
-    )(outgoing, source, pos, pos_r, *weights)
-
-
-def turn_kernel(bm, at, dec_at, served, want, landed, node, x, target, level, land, count, w_in, w_out, vec, c_in, c_out, c_vec, flat, g_prev, out, d_out_o, d_vec_o, err_o, packed, packed2, d_in, d_out, d_vec, e_in, e_out, e_vec, err, acc, sem):
+    outputs = dict(edge=(shaped(edges, LATENT), V), edge_low=(low(edges), V), sent=(low(edges), V), recv=(low(edges), V), landed=(shaped(*shape, dtype=BF16), ANY))
+    outputs |= dict(node=(shaped(rows, LATENT), ANY), low=(low(rows), ANY), slots=(shaped(count, LATENT), ANY))
+    if first:
+        inputs |= dict(x=(x, V)) | weights("g", geo_block)
+        scratch |= held("_g", geo_block)
+    else:
+        inputs |= dict(landed_in=(landed, ANY), node_in=(node, ANY), slots_in=(slots, ANY))
+        scratch |= dict(_landed_in=pltpu.VMEM(shape, BF16), _slots_in=pltpu.VMEM((count, LATENT), F32), _sums_s=pltpu.VMEM((count, LATENT), BF16))
+        outputs |= dict(sums=(low(rows), ANY), sums_s=(low(count), ANY))
+    return named_call(functools.partial(edge_kernel, n, first, bm), "edge_forward", inputs, outputs, scratch, cid=cid)
+
+
+def turn_kernel(bm, at, dec_at, served, want, landed, node, x, target, level, land, count, w_in, w_out, vec, c_in, c_out, c_vec, flat, g_prev, g_slots, out, d_out_o, d_vec_o, err_o, packed, packed2, d_in, d_out, d_vec, e_in, e_out, e_vec, err, acc, sem):
     i = pl.program_id(0)
     @pl.when(i == 0)
     def _():
-        clear(d_in, d_out, d_vec, e_in, e_out, e_vec, err)
+        clear(d_in, d_out, d_vec, e_in, e_out, e_vec, err, acc, g_slots)
     got = mm(place(served[...], i * bm, bm), landed[...]).astype(BF16)
     old = node[...]
     low = old.astype(BF16)
@@ -666,10 +729,18 @@
     g_post = norm_back(g_node, hat, inv, vec, d_vec)
     g_pre = act_back(g_post, pre, sigma, w_out)
     weight_sums([low, got], act, g_post, g_pre, d_in, d_out, d_vec)
-    g_prev[...] = g_node + mm_nt(g_pre, w_in[:LATENT, :])
-    send_rows(i, bm, mm_nt(g_pre, w_in[LATENT:, :]).astype(BF16), want, out, acc)
+    g = g_node + mm_nt(g_pre, w_in[:LATENT, :])
+    g_prev[...] = g
+    chosen = pick(want[...], i * bm, bm)
+    acc[...] += mm(chosen, mm_nt(g_pre, w_in[LATENT:, :]).astype(BF16))
+    high = g.astype(BF16)
+    rest = g - high.astype(F32)
+    middle = rest.astype(BF16)
+    small = (rest - middle.astype(F32)).astype(BF16)
+    g_slots[...] += mm(chosen, high) + (mm(chosen, middle) + mm(chosen, small))
     @pl.when(i == pl.num_programs(0) - 1)
     def _():
+        out[...] = acc[...].astype(BF16)
         d_out_o[...] = e_out[...]
         d_vec_o[...] = e_vec[...]
         err_o[...] = err[...]
@@ -689,143 +760,143 @@
     return pl.pallas_call(
         functools.partial(turn_kernel, bm, at, dec_at),
         grid=(rows // bm,),
-        out_shape=(shaped(flat_rows, 128), shaped(rows, LATENT), shaped(slots, LATENT, dtype=BF16), shaped(LATENT, wide), shaped(8, LATENT), shaped(1, wide)),
+        out_shape=(shaped(flat_rows, 128), shaped(rows, LATENT), shaped(slots, LATENT), shaped(slots, LATENT, dtype=BF16), shaped(LATENT, wide), shaped(8, LATENT), shaped(1, wide)),
         in_specs=[spec((1, slots)), spec((slots, 1)), spec((slots, LATENT)), spec((bm, LATENT), False), v(), v(), v(), spec((bm, 1), False), spec((1, 1))] + [spec(a.shape) for a in (*block, *dec)],
-        out_specs=(ANY, spec((bm, LATENT), False), spec((slots, LATENT)), spec((LATENT, wide)), spec((8, LATENT)), spec((1, wide))),
+        out_specs=(ANY, spec((bm, LATENT), False), spec((slots, LATENT)), spec((slots, LATENT)), spec((LATENT, wide)), spec((8, LATENT)), spec((1, wide))),
         scratch_shapes=[packed_rows(2 * LATENT), pltpu.VMEM((4 * LATENT, 128), F32)] + mlp_sums(2 * LATENT) + mlp_sums(LATENT, wide) + [pltpu.VMEM((1, wide), F32), pltpu.VMEM((slots, LATENT), F32), DMA((2,))],
         compiler_params=params(),
         name="turn",
     )(served, want, landed, node, x, target, level, land, count, *block, *dec)
 
 
-def edge_back_kernel(n, at, has_edge, geo_at, tail_at, outgoing, edge_low, sent, recv, pos, pos_s, pos_r, *rest):
-    rest = list(rest)
-    blocks = [rest.pop(0) for _ in range(3)]
-    geo_blocks = [rest.pop(0) for _ in range(3)] if geo_at is not None else []
-    rest.pop(0)
-    g_edge = rest.pop(0) if has_edge else None
-    geo = rest.pop(0) if geo_at is not None else None
-    tail = rest.pop(0) if tail_at is not None else None
-    flat, edge_prev, landed, returned, buffer, packed, d_in, d_out, d_vec, own, s1, r1, s2, r2, wsem, fsem, w_in, w_out, vec = rest[:19]
-    rest = rest[19:]
-    held = [w_in, w_out, vec] + rest[:3]
-    loads = [pltpu.make_async_copy(a, b, wsem.at[i]) for i, (a, b) in enumerate(zip(blocks + geo_blocks, held))]
-    for load in loads:
-        load.start()
+def edge_back_kernel(n, at, node_at, geo_at, tail_at, bm, r):
+    me = lax.axis_index("dev")
+    greet_start(n, me)
+    loads = Loads(r, r.lsem)
+    nodes = node_at is not None
+    early = ["p_in", "p_out", "p_vec", "landed_in", "g_slots_in", "slots_in", "sums_s"] if nodes else []
+    late = ["e_in", "e_out", "e_vec"] + (["g_in", "g_out", "g_vec"] if geo_at is not None else [])
+    loads.start(*early)
+    loads.start(*late)
     stores = []
-    if tail is not None:
-        stores.append(store_flat(tail, flat, tail_at, fsem.at[2]))
-    me = lax.axis_index("dev")
-    greet(n, me)
-    swap_start(n, me, outgoing, returned, own.at[0], s1, r1)
-    for load in loads:
-        load.wait()
-    clear(d_in, d_out, d_vec)
-    us = [edge_low[...], sent[...], recv[...]]
-    slots = n * returned.shape[1]
-    pre = first_half(us, w_in, vec)
+    if tail_at is not None:
+        stores.append(store_flat(r.tail, r.flat, tail_at, r.fsem.at[2]))
+    count = r.want.shape[0]
+    if nodes:
+        loads.wait(*early)
+        us = [r._slots_in[...].astype(BF16), r._sums_s[...]]
+        pre = first_half(us, r._p_in, r._p_vec)
+        sigma, act = activate(pre)
+        hat, inv = second_half(act, r._p_out, r._p_vec)
+        g = r._g_slots_in[...] + mm(same_rows(r.want, r.served), flat_rows_of(r._landed_in))
+        low = norm_back(g, hat, inv, r._p_vec, None)
+        g_pre = act_back(low, pre, sigma, r._p_out)
+        r.away[...] = mm_nt(g_pre, r._p_in[LATENT:, :]).astype(BF16).reshape(r.away.shape)
+        source = r.away
+    else:
+        source = r.outgoing
+    greet_wait(n)
+    swap_start(n, me, source, r.here, r.own.at[0], r.s1, r.r1)
+    if nodes:
+        r._g_slots[...] = g + mm_nt(g_pre, r._p_in[:LATENT, :])
+        stores += store_all(r, r.ssem, "g_slots")
+        clear(r.n_in, r.n_out, r.n_vec)
+    clear(r.d_in, r.d_out, r.d_vec)
+    def node_rows(first, last):
+        if not nodes:
+            return
+        def body(g_node, low_in, sums_in, g_prev):
+            i = first + pl.program_id(0)
+            us = [low_in[...], sums_in[...]]
+            pre = first_half(us, r._p_in, r._p_vec)
+            sigma, act = activate(pre)
+            hat, inv = second_half(act, r._p_out, r._p_vec)
+            g = g_node[...] + mm(place(r.served[...], i * bm, bm), flat_rows_of(r._landed_in))
+            low = norm_back(g, hat, inv, r._p_vec, r.n_vec)
+            g_pre = act_back(low, pre, sigma, r._p_out)
+            weight_sums(us, act, low, g_pre, r.n_in, r.n_out, r.n_vec)
+            g_prev[...] = g + mm_nt(g_pre, r._p_in[:LATENT, :])
+        block = pl.BlockSpec((bm, LATENT), lambda i: (first + i, 0))
+        pltpu.emit_pipeline(body, grid=(last - first,), in_specs=[block] * 3, out_specs=[block])(r.g_node, r.low, r.sums, r.g_prev)
+    blocks = r.g_node.shape[0] // bm if nodes else 0
+    node_rows(0, blocks // 2)
+    loads.wait(*late)
+    us = [r.edge_low[...], r.sent[...], r.recv[...]]
+    pre = first_half(us, r._e_in, r._e_vec)
     sigma, act = activate(pre)
-    hat, inv = second_half(act, w_out, vec)
-    pick_r = pick(pos[:, 1:2], 0, slots)
-    put_s, put_r = place(pos_s[...], 0, slots), place(pos_r[...], 0, slots)
-    if geo is not None:
-        g_in, g_out, g_vec = rest[:3]
-        c_pre = first_half([geo[...]], g_in, g_vec)
+    hat, inv = second_half(act, r._e_out, r._e_vec)
+    pick_r = pick(r.pos[:, 1:2], 0, count)
+    put_s, put_r = place(r.pos_s[...], 0, count), place(r.pos_r[...], 0, count)
+    swap_wait(n, me, source, r.here, r.own.at[0], r.s1, r.r1)
+    g = mm(pick_r, flat_rows_of(r.here))
+    if hasattr(r, "g_edge"):
+        g = r.g_edge[...] + g
+    low = norm_back(g, hat, inv, r._e_vec, r.d_vec)
+    g_pre = act_back(low, pre, sigma, r._e_out)
+    s = mm_nt(g_pre, r._e_in[LATENT : 2 * LATENT, :]).astype(BF16)
+    v = mm_nt(g_pre, r._e_in[2 * LATENT :, :]).astype(BF16)
+    r.back[...] = (mm(put_s, s) + mm(put_r, v)).astype(BF16).reshape(r.back.shape)
+    swap_start(n, me, r.back, r.landed, r.own.at[1], r.s2, r.r2)
+    prev = g + mm_nt(g_pre, r._e_in[:LATENT, :])
+    r.edge_prev[...] = prev
+    weight_sums(us, act, low, g_pre, r.d_in, r.d_out, r.d_vec)
+    pack(r.packed, 0, 3 * LATENT, r.d_in, r.d_out, r.d_vec)
+    stores.append(store_flat(r.packed, r.flat, at, r.fsem.at[0]))
+    if geo_at is not None:
+        c_us = [r.geo[...]]
+        c_pre = first_half(c_us, r._g_in, r._g_vec)
         c_sigma, c_act = activate(c_pre)
-        c_hat, c_inv = second_half(c_act, g_out, g_vec)
-    swap_wait(n, me, outgoing, returned, own.at[0], s1, r1)
-    g = mm(pick_r, flat_rows_of(returned))
-    if has_edge:
-        g = g_edge[...] + g
-    low = norm_back(g, hat, inv, vec, d_vec)
-    g_pre = act_back(low, pre, sigma, w_out)
-    s = mm_nt(g_pre, w_in[LATENT : 2 * LATENT, :]).astype(BF16)
-    r = mm_nt(g_pre, w_in[2 * LATENT :, :]).astype(BF16)
-    buffer[...] = (mm(put_s, s) + mm(put_r, r)).astype(BF16).reshape(buffer.shape)
-    swap_start(n, me, buffer, landed, own.at[1], s2, r2)
-    prev = g + mm_nt(g_pre, w_in[:LATENT, :])
-    edge_prev[...] = prev
-    weight_sums(us, act, low, g_pre, d_in, d_out, d_vec)
-    pack(packed, 0, 3 * LATENT, d_in, d_out, d_vec)
-    stores.append(store_flat(packed, flat, at, fsem.at[0]))
-    if geo is not None:
-        packed2, e_in, e_out, e_vec = rest[3:]
-        clear(e_in, e_out, e_vec)
-        c_low = norm_back(prev, c_hat, c_inv, g_vec, e_vec)
-        c_g = act_back(c_low, c_pre, c_sigma, g_out)
-        weight_sums([geo[...]], c_act, c_low, c_g, e_in, e_out, e_vec)
-        pack(packed2, 0, GEO, e_in, e_out, e_vec)
-        stores.append(store_flat(packed2, flat, geo_at, fsem.at[1]))
-    swap_wait(n, me, buffer, landed, own.at[1], s2, r2)
+        c_hat, c_inv = second_half(c_act, r._g_out, r._g_vec)
+        clear(r.c_in, r.c_out, r.c_vec)
+        c_low = norm_back(prev, c_hat, c_inv, r._g_vec, r.c_vec)
+        c_g = act_back(c_low, c_pre, c_sigma, r._g_out)
+        weight_sums(c_us, c_act, c_low, c_g, r.c_in, r.c_out, r.c_vec)
+        pack(r.c_packed, 0, GEO, r.c_in, r.c_out, r.c_vec)
+        stores.append(store_flat(r.c_packed, r.flat, geo_at, r.fsem.at[1]))
+    node_rows(blocks // 2, blocks)
+    if nodes:
+        pack(r.n_packed, 0, 2 * LATENT, r.n_in, r.n_out, r.n_vec)
+        stores.append(store_flat(r.n_packed, r.flat, node_at, r.fsem.at[3]))
+    swap_wait(n, me, r.back, r.landed, r.own.at[1], r.s2, r.r2)
     for store in stores:
         store.wait()
 
 
-def edge_backward(n, outgoing, ins, pos, pos_s, pos_r, block, flat, at, cid, g_edge=None, geo=None, geo_at=None, tail=None, tail_at=None):
-    rows = pos.shape[0]
-    slots = outgoing.shape[0]
-    outgoing = outgoing.reshape(n, slots // n, LATENT)
+def sums_scratch(prefix, rows_in):
+    return dict(zip((prefix + "_in", prefix + "_out", prefix + "_vec"), mlp_sums(rows_in)))
+
+
+def edge_backward(n, cid, ins, routes, edge_block, flat, at, g_edge=None, outgoing=None, tail=None, tail_at=None, node=None, node_at=None, geo=None, geo_at=None, bm=512):
+    want, served, pos, pos_s, pos_r = routes
+    count = want.shape[0]
+    edges = pos.shape[0]
+    shape = (n, count // n, LATENT)
     V = pl.BlockSpec(memory_space=pltpu.VMEM)
-    geo_block = geo[1] if geo is not None else ()
-    args = [outgoing, *ins, pos, pos_s, pos_r, *block, *geo_block, flat]
-    specs = [ANY] + [V] * 6 + [ANY] * (4 + len(geo_block))
-    which = len(args) - 1
-    scratch = [pltpu.VMEM(outgoing.shape, BF16), pltpu.VMEM(outgoing.shape, BF16), packed_rows(3 * LATENT)] + mlp_sums(3 * LATENT)
-    scratch += [DMA((2,)), DMA((n,)), DMA((n,)), DMA((n,)), DMA((n,)), DMA((6,)), DMA((3,))] + held_scratch(block)
-    for more in (g_edge, geo[0] if geo is not None else None, tail):
-        if more is not None:
-            args.append(more)
-            specs.append(V)
+    inputs = dict(want=(want, V), served=(served, V), pos=(pos, V), pos_s=(pos_s, V), pos_r=(pos_r, V), flat_in=(flat, ANY))
+    inputs |= {name: (value, V) for name, value in zip(("edge_low", "sent", "recv"), ins)} | weights("e", edge_block)
+    scratch = held("_e", edge_block) | swap_scratch(shape, n) | sums_scratch("d", 3 * LATENT)
+    scratch |= dict(packed=packed_rows(3 * LATENT), lsem=DMA((16,)), ssem=DMA((1,)), fsem=DMA((4,)))
+    outputs = dict(flat=(shaped(*flat.shape), ANY), edge_prev=(shaped(edges, LATENT), V), landed=(shaped(*shape, dtype=BF16), ANY))
+    if g_edge is not None:
+        inputs |= dict(g_edge=(g_edge, V))
+    if outgoing is not None:
+        inputs |= dict(outgoing=(outgoing.reshape(shape), ANY))
+    if tail is not None:
+        inputs |= dict(tail=(tail, V))
+    if node is not None:
+        for name, value in zip(("landed_in", "g_slots_in", "slots_in", "sums_s", "g_node", "low", "sums"), node):
+            inputs[name] = (value, ANY)
+        inputs |= weights("p", node[7])
+        scratch |= held("_p", node[7]) | sums_scratch("n", 2 * LATENT)
+        f = pltpu.VMEM((count, LATENT), F32)
+        scratch |= dict(n_packed=packed_rows(2 * LATENT), _landed_in=pltpu.VMEM(shape, BF16), _g_slots_in=f, _slots_in=f, _g_slots=f, _sums_s=pltpu.VMEM((count, LATENT), BF16))
+        rows = node[4].shape[0]
+        outputs |= dict(g_prev=(shaped(rows, LATENT), ANY), g_slots=(shaped(count, LATENT), ANY))
     if geo is not None:
-        scratch += held_scratch(geo_block) + [packed_rows(GEO)] + mlp_sums(geo[0].shape[1])
-    return pl.pallas_call(
-        functools.partial(edge_back_kernel, n, at, g_edge is not None, geo_at, tail_at),
-        out_shape=(shaped(*flat.shape), shaped(rows, LATENT), shaped(*outgoing.shape, dtype=BF16)),
-        in_specs=specs,
-        out_specs=(ANY, V, ANY),
-        scratch_shapes=scratch,
-        input_output_aliases={which: 0},
-        compiler_params=params(collective_id=cid, has_side_effects=True),
-        name="edge_backward",
-    )(*args)
-
-
-def node_back_kernel(bm, at, served, want, landed, g_node, low, sums, w_in, w_out, vec, flat_in, flat, g_prev, out, packed, d_in, d_out, d_vec, acc, sem):
-    i = pl.program_id(0)
-    @pl.when(i == 0)
-    def _():
-        clear(d_in, d_out, d_vec)
-    us = [low[...], sums[...]]
-    pre = first_half(us, w_in, vec)
-    sigma, act = activate(pre)
-    hat, inv = second_half(act, w_out, vec)
-    g = g_node[...] + mm(place(served[...], i * bm, bm), landed[...])
-    g_post = norm_back(g, hat, inv, vec, d_vec)
-    g_pre = act_back(g_post, pre, sigma, w_out)
-    weight_sums(us, act, g_post, g_pre, d_in, d_out, d_vec)
-    g_prev[...] = g + mm_nt(g_pre, w_in[:LATENT, :])
-    send_rows(i, bm, mm_nt(g_pre, w_in[LATENT:, :]).astype(BF16), want, out, acc)
-    @pl.when(i == pl.num_programs(0) - 1)
-    def _():
-        pack(packed, 0, 2 * LATENT, d_in, d_out, d_vec)
-        store_flat(packed, flat, at, sem).wait()
-
-
-def node_backward(served, want, landed, g_node, low, sums, block, flat, at, bm=512):
-    rows = low.shape[0]
-    slots = want.shape[0]
-    b = lambda: spec((bm, LATENT), False)
-    return pl.pallas_call(
-        functools.partial(node_back_kernel, bm, at),
-        grid=(rows // bm,),
-        out_shape=(shaped(*flat.shape), shaped(rows, LATENT), shaped(slots, LATENT, dtype=BF16)),
-        in_specs=[spec((1, slots)), spec((slots, 1)), spec((slots, LATENT)), b(), b(), b()] + [spec(a.shape) for a in block] + [ANY],
-        out_specs=(ANY, b(), spec((slots, LATENT))),
-        scratch_shapes=[packed_rows(2 * LATENT)] + mlp_sums(2 * LATENT) + [pltpu.VMEM((slots, LATENT), F32), DMA],
-        input_output_aliases={9: 0},
-        compiler_params=params(),
-        name="node_backward",
-    )(served, want, landed, g_node, low, sums, *block, flat)
+        inputs |= dict(geo=(geo[0], V)) | weights("g", geo[1])
+        scratch |= held("_g", geo[1]) | sums_scratch("c", geo[0].shape[1]) | dict(c_packed=packed_rows(GEO))
+    body = functools.partial(edge_back_kernel, n, at, node_at, geo_at, tail_at, bm)
+    return named_call(body, "edge_backward", inputs, outputs, scratch, aliases=dict(flat_in="flat"), cid=cid)
 
 
 def encode_back_kernel(bm, served, landed, g_node, x, w_in, w_out, vec, flat_in, flat, packed, d_in, d_out, d_vec, sem):
@@ -1053,19 +1124,16 @@
     x = widen(inputs, 256)
     geo = widen(geometry, 128)
     land = land_sea[:, None]
-    node, low, outgoing = encode(x, blocks[0], want)
-    node_kept, edge_kept = [], []
-    edge = geo
-    for k in range(LAYERS):
-        edge, *kept, landed = edge_forward(
-            devices, outgoing, edge, pos, pos_r, blocks[2 + 2 * k], 3 + min(k, 1), blocks[1] if k == 0 else None
+    routes = (want, served, pos, pos_s, pos_r)
+    done = [edge_forward(devices, 3, geo, routes, blocks[2], blocks[0], inputs.shape[0], x=x, geo_block=blocks[1])]
+    for k in range(1, LAYERS):
+        f = done[-1]
+        done.append(
+            edge_forward(
+                devices, 4, f.edge, routes, blocks[2 + 2 * k], blocks[1 + 2 * k], inputs.shape[0],
+                landed=f.landed, node=f.node, slots=f.slots,
+            )
         )
-        edge_kept.append(kept)
-        landed = landed.reshape(slots, LATENT)
-        if k < LAYERS - 1:
-            before = low
-            node, low, sums, outgoing = node_forward(served, want, landed, node, blocks[3 + 2 * k])
-            node_kept.append((before, sums))
     pieces = [4 * s for s in (VARS + LATENT + 4, GEO + LATENT + 4) + (3 * LATENT + LATENT + 4, 2 * LATENT + LATENT + 4) * LAYERS]
     lead = 4
     places = [0] + [lead + sum(pieces[: i + 1]) for i in range(len(pieces))]
@@ -1073,32 +1141,35 @@
     dec_at = places[-1]
     tail_at = dec_at + 4 * LATENT
     k = LAYERS - 1
-    flat, g_node, outgoing, d_out, d_vec, errors = turn(
-        served, want, landed, node, inputs, targets, level_mask, land, count.reshape(1, 1),
+    flat, g_node, g_slots, outgoing, d_out, d_vec, errors = turn(
+        served, want, done[k].landed.reshape(slots, LATENT), done[k].node, inputs, targets, level_mask, land, count.reshape(1, 1),
         blocks[3 + 2 * k], blocks[-1], flat_rows, places[3 + 2 * k], dec_at,
     )
     error_here = jnp.sum(errors)
     tail = jnp.concatenate([d_vec[0], d_out[:, :VARS].reshape(-1), d_vec[1, :VARS]])
     tail_rows = flat_rows - tail_at
     tail = jnp.pad(tail, (0, tail_rows * 128 - tail.shape[0])).reshape(tail_rows, 128)
-    g_edge = None
+    g_edge, landed = None, None
     for k in reversed(range(LAYERS)):
         more = {}
         if k == LAYERS - 1:
-            more = dict(tail=tail, tail_at=tail_at)
+            more |= dict(outgoing=outgoing, tail=tail, tail_at=tail_at)
+        else:
+            more |= dict(
+                node=(landed, g_slots, done[k].slots, done[k + 1].sums_s, g_node, done[k].low, done[k + 1].sums, blocks[3 + 2 * k]),
+                node_at=places[3 + 2 * k],
+            )
         if k == 0:
-            more = dict(geo=(geo, blocks[1]), geo_at=places[1])
-        flat, g_edge, landed = edge_backward(
-            devices, outgoing, edge_kept[k], pos, pos_s, pos_r, blocks[2 + 2 * k], flat, places[2 + 2 * k],
-            5 + (LAYERS - 1 - k), g_edge=g_edge, **more,
+            more |= dict(geo=(geo, blocks[1]), geo_at=places[1])
+        f = done[k]
+        b = edge_backward(
+            devices, 5 + (LAYERS - 1 - k), (f.edge_low, f.sent, f.recv), routes, blocks[2 + 2 * k], flat, places[2 + 2 * k],
+            g_edge=g_edge, **more,
         )
-        landed = landed.reshape(slots, LATENT)
-        if k > 0:
-            before, sums = node_kept[k - 1]
-            flat, g_node, outgoing = node_backward(
-                served, want, landed, g_node, before, sums, blocks[1 + 2 * k], flat, places[1 + 2 * k]
-            )
-    flat = encode_backward(served, landed, g_node, x, blocks[0], flat)
+        flat, g_edge, landed = b.flat, b.edge_prev, b.landed
+        if k < LAYERS - 1:
+            g_node, g_slots = b.g_prev, b.g_slots
+    flat = encode_backward(served, landed.reshape(slots, LATENT), g_node, x, blocks[0], flat)
     if mine:
         rows = (share_rows + 6 + 15) // 16 * 16
         error = jnp.zeros((8, 128), jnp.float32).at[0, 0].set(error_here)

time: 690 us -> 593 us (0.86)
  the two profiles are of different devices: /device:TPU:27 before, /device:TPU:0 now
where the time goes in v3:
time: 593 us; the launch traced here: 583 us
  Pallas kernels  541 us (91%)
  local copies, waits for them, and re-layouts  24.3 us (4%)
  other arithmetic  10.3 us (2%)
  between operations  7.12 us (1%)
    pallas_call x6, Pallas kernels, named_call(): pl.pallas_call(kernel, out_shape=tuple((shape for shape, _ in outputs.val...  273 us
    pallas_call x1, Pallas kernels, reduce_gradient(): pl.pallas_call(functools.partial(reduce_kernel, share_rows, lead), out_sh...  137 us
    pallas_call x1, Pallas kernels, gather_weights(): pl.pallas_call(gather_kernel, out_shape=(jax.ShapeDtypeStruct((n, rows, 1...  69.5 us
    pallas_call x1, Pallas kernels, turn(): pl.pallas_call(functools.partial(turn_kernel, bm, at, dec_at), grid=(rows...  38 us
    pallas_call x1, Pallas kernels, encode_backward(): pl.pallas_call(functools.partial(encode_back_kernel, bm), grid=(rows // b...  12.6 us

profile of v3, /device:TPU:0, one launch (start us, length us, event | category | flops | bytes accessed | tf_op | source)
XLA Modules:
  0.0 582.8 jit_solution(2858710777357767778)
XLA Ops:
  0.7 0.9 copy.65
  1.6 0.1 reshape.182
  1.8 0.3 convert_reduce_fusion
  2.0 0.7 broadcast_add_fusion.1
  2.9 0.1 add.82
  3.0 0.2 select_reduce_fusion
  3.3 0.6 pad.39.ask_ref
  4.0 1.2 convert_bitcast_fusion
  5.1 0.8 pad.38.w_ref
  5.9 1.2 multiply_reduce_fusion
  7.8 0.6 scatter.10.num_ref
  8.4 69.5 %shard_map.163 = (bf16[32,1600,128]{2,1,0:T(8,128)(2,1)}, s32[32,1,128]{2,1,0:T(1,128)}, f32[32,8,128]{2,1,0:T(8,128)}) custom-call(bf16[1600,128]{1,0:T(8,128)(2,1)} %pad.38.w_ref, s32[32,1,128]{2,1,0:T(1,128)} %pad.39.ask_ref, f32[8,128]{1,0:T(8,128)} %scatter.10.num_ref), custom_call_target="tpu_custom_call" | custom-call | tf_op jit(solution)/shard_map/pallas_call | solution.py:229
  78.0 10.8 %relay.1 = (bf16[256,512]{1,0:T(8,128)(2,1)}, bf16[512,512]{1,0:T(8,128)(2,1)}, f32[8,512]{1,0:T(8,128)}, bf16[128,512]{1,0:T(8,128)(2,1)}, bf16[512,512]{1,0:T(...) custom-call(bf16[32,1600,128]{2,1,0:T(8,128)(2,1)} %get-tuple-elemen, ...), custom_call_target="tpu_custom_call" | custom-call | tf_op jit(solution)/shard_map/relay/pallas_call | solution.py:1020
  88.7 0.1 reduce_sum.68
  89.1 0.8 slice_reduce_fusion
  89.9 0.7 broadcast_in_dim_reshape_squeeze.6.refs_2_.served.refs_1_
  90.6 0.9 broadcast_in_dim_reshape_squeeze.8.refs_1_.want.refs_0_
  91.5 1.5 copy.70.x
  93.0 1.3 pad.41.refs_11_.x
  94.4 0.1 copy.69
  94.5 0.6 pad.40.refs_0_.refs_23_
  95.1 38.1 %edge_forward.3 = (f32[256,512]{1,0:T(8,128)}, bf16[256,512]{1,0:T(8,128)(2,1)}, bf16[256,512]{1,0:T(8,128)(2,1)}, bf16[256,512]{1,0:T(8,128)(2,1)}, bf16[32,24,...) custom-call(bf16[256,128]{1,0:T(8,128)(2,1)} %pad.40.refs_0_.refs_23_, ...), custom_call_target="tpu_custom_call" | custom-call | tf_op jit(solution)/shard_map/edge_forward/pallas_call | solution.py:509
  133.3 45.7 %edge_forward.4 = (f32[256,512]{1,0:T(8,128)}, bf16[256,512]{1,0:T(8,128)(2,1)}, bf16[256,512]{1,0:T(8,128)(2,1)}, bf16[256,512]{1,0:T(8,128)(2,1)}, bf16[32,24,...) custom-call(f32[256,512]{1,0:T(8,128)} %get-tuple-element.128.refs_0, ...), custom_call_target="tpu_custom_call" | custom-call | tf_op jit(solution)/shard_map/edge_forward/pallas_call | solution.py:509
  179.0 46.4 %edge_forward.5 = (f32[256,512]{1,0:T(8,128)}, bf16[256,512]{1,0:T(8,128)(2,1)}, bf16[256,512]{1,0:T(8,128)(2,1)}, bf16[256,512]{1,0:T(8,128)(2,1)}, bf16[32,24,...) custom-call(f32[256,512]{1,0:T(8,128)} %get-tuple-element.138.refs_0, ...), custom_call_target="tpu_custom_call" | custom-call | tf_op jit(solution)/shard_map/edge_forward/pallas_call | solution.py:509
  225.4 1.0 slice_bitcast_fusion
  226.5 1.4 scatter.11.c_vec
  227.8 1.0 slice.83
  228.8 0.7 reshape.186
  229.5 0.7 pad.42.c_out
  230.2 0.6 reduce_sum.69
  230.9 2.9 copy.76.target
  233.8 1.8 copy.77.level
  235.6 1.3 copy.78.land
  236.9 38.0 %turn.1 = (f32[51160,128]{1,0:T(8,128)}, f32[2048,512]{1,0:T(8,128)}, f32[768,512]{1,0:T(8,128)}, bf16[768,512]{1,0:T(8,128)(2,1)}, f32[512,256]{1,0:T(8,128)}, /*index=5*/f32[8,512]{1,0:T(8,128)}, f32[1,256]{1,0:T(1,128)}) custom-call(s32[1,768]{1,0:T(1,128)} %broadcast_in_dim_reshape_squeeze.6.refs_2_.served.refs_1_, ...), custom_call_target="tpu_custom_call" | custom-call | tf_op jit(solution)/shard_map/turn/pallas_call | solution.py:760
  274.9 1.6 reshape.189
  276.5 0.7 slice.86
  277.2 0.7 slice.88
  277.9 0.8 fusion.3.refs_13_
  278.7 47.2 %edge_backward.3 = (f32[51160,128]{1,0:T(8,128)}, f32[256,512]{1,0:T(8,128)}, bf16[32,24,512]{2,1,0:T(8,128)(2,1)}) custom-call(s32[768,1]{1,0:T(8,128)} %broadcast_in_dim_reshape_squeeze.8.refs_1_.want.refs_0_, s32[1,768]{1,0:T(1,128)} %broadcast_in_dim_reshape_squeeze.6.refs_2_.served.refs_1_, s32[256,2]{1,0:T(8,128)} %copy-done, ...), custom_call_target="tpu_custom_call", output_to_operand_aliasing={{0}: (5, {})} | custom-call | tf_op jit(solution)/shard_map/edge_backward/pallas_call | solution.py:509
  325.9 48.4 %edge_backward.4 = (f32[51160,128]{1,0:T(8,128)}, f32[256,512]{1,0:T(8,128)}, bf16[32,24,512]{2,1,0:T(8,128)(2,1)}, f32[2048,512]{1,0:T(8,128)}, f32[768,512]{1,0:T(8,128)}) custom-call(s32[768,1]{1,0:T(8,128)} %broadcast_in_dim_reshape_squeeze.8.refs_1_.want.refs_0_, ...), custom_call_target="tpu_custom_call", output_to_operand_aliasing={{0}: (5, {})} | custom-call | tf_op jit(solution)/shard_map/edge_backward/pallas_call | solution.py:509
  374.4 46.8 %edge_backward.5 = (f32[51160,128]{1,0:T(8,128)}, f32[256,512]{1,0:T(8,128)}, bf16[32,24,512]{2,1,0:T(8,128)(2,1)}, f32[2048,512]{1,0:T(8,128)}, f32[768,512]{1,0:T(8,128)}) custom-call(s32[768,1]{1,0:T(8,128)} %broadcast_in_dim_reshape_squeeze.8.refs_1_.want.refs_0_, ...), custom_call_target="tpu_custom_call", output_to_operand_aliasing={{0}: (5, {})} | custom-call | tf_op jit(solution)/shard_map/edge_backward/pallas_call | solution.py:509
  421.2 12.6 %encode_backward.1.g_ref = f32[51160,128]{1,0:T(8,128)} custom-call(s32[1,768]{1,0:T(1,128)} %broadcast_in_dim_reshape_squeeze.6.refs_2_.served.refs_1_, bf16[768,512]{1,0:T(8,128)(2,1)} %bitcast.30, f32[2048,512]{1,0:T(8,128)} %get-tuple-element.186.g_node, bf16[2048,256]{1,0:T(8,128)(2,1)} %pad.41.refs_11_.x, ...), custom_call_target="tpu_custom_call", output_to_operand_aliasing={{}: (7, {})} | custom-call | tf_op jit(solution)/shard_map/encode_backward/pallas_call | solution.py:925
  433.9 0.6 reduce_sum.70
  434.5 0.6 scatter.14.err_ref
  435.2 137.4 %shard_map.164 = (f32[1616,128]{1,0:T(8,128)S(1)}, f32[32,8,128]{2,1,0:T(8,128)S(1)}, f32[32,8,128]{2,1,0:T(8,128)S(1)}) custom-call(f32[51160,128]{1,0:T(8,128)} %encode_backward.1.g_ref, f32[8,128]{1,0:T(8,128)S(1)} %scatter.14.err_ref), custom_call_target="tpu_custom_call" | custom-call | tf_op jit(solution)/shard_map/pallas_call | solution.py:356
  572.6 0.6 reduce_sum.72
  574.5 0.6 reduce_sum.71
  576.7 3.4 multiply_add_fusion
  (34 shorter events, 0.5 us)
Async XLA Ops:
  0.6 5.3 copy-start.7
  0.6 5.3 copy-start.2
  77.9 10.9 %copy-start.9 = (s32[256,2]{0,1:T(2,128)S(1)}, s32[256,2]{0,1:T(2,128)}, u32[]{:S(2)}) copy-start(s32[256,2]{0,1:T(2,128)} %param.23) | copy-start | bytes 6148
  78.0 11.9 %copy-start.8 = (s32[32,1,128]{2,1,0:T(1,128)S(1)}, s32[32,1,128]{2,1,0:T(1,128)}, u32[]{:S(2)}) copy-start(s32[32,1,128]{2,1,0:T(1,128)} %get-tuple-element.117) | copy-start | bytes 49156
  89.1 5.3 copy-start
  91.5 2.8 copy-start.10
  93.0 40.3 %copy-start.1 = (bf16[2048,227]{1,0:T(8,128)(2,1)}, bf16[2048,227]{1,0:T(8,128)(2,1)S(1)}, u32[]{:S(2)}) copy-start(bf16[2048,227]{1,0:T(8,128)(2,1)S(1)} %copy.70.x) | copy-start | bytes 2789380
  225.4 4.8 copy-start.6
  421.2 12.6 %copy-start.11 = (f32[1,256]{1,0:T(1,128)S(1)}, f32[1,256]{1,0:T(1,128)}, u32[]{:S(2)}) copy-start(f32[1,256]{1,0:T(1,128)} %get-tuple-element.188) | copy-start | bytes 3076
  435.1 141.5 %copy-start.3 = (f32[204544]{0:T(1024)S(1)}, f32[204544]{0:T(1024)}, u32[]{:S(2)}) copy-start(f32[204544]{0:T(1024)} %param.26) | copy-start | bytes 2454532
  435.1 141.5 %copy-start.4 = (f32[204544]{0:T(1024)S(1)}, f32[204544]{0:T(1024)}, u32[]{:S(2)}) copy-start(f32[204544]{0:T(1024)} %param.29) | copy-start | bytes 2454532
  435.1 141.5 %copy-start.5 = (f32[204544]{0:T(1024)S(1)}, f32[204544]{0:T(1024)}, u32[]{:S(2)}) copy-start(f32[204544]{0:T(1024)} %param.28) | copy-start | bytes 2454532

commit v4 on v3

--- a/solution.py
+++ b/solution.py
@@ -235,136 +235,8 @@
     )(w, ask, num)
 
 
-def accumulate(dst, src, rows):
-    step = 80
-    whole = rows // step
-    def body(i, carry):
-        at = pl.ds(pl.multiple_of(i * step, 8), step)
-        dst[at] = dst[at] + src[at]
-        return carry
-    lax.fori_loop(0, whole, body, 0)
-    if rows % step:
-        at = pl.ds(whole * step, rows % step)
-        dst[at] = dst[at] + src[at]
-
-SCHEDULE = ['g0', 'g1', 's0', 'm0', 'g2', 's1', 'f0', 'm1', 'g3', 's2', 'f1', 'm2', 's3', 'f2', 'm3', 'f3']
-
-
-def reduce_kernel(share_rows, lead, g_ref, err_ref, o_ref, sq_ref, errs_ref, L, R, YA, XA, XB, YB, Z, sq, own, ls, rs0_s, rs0_r, as1, ar1, as2, ar2, bs1, br1, bs2, br2, zs, zr, es, er, qs, qr):
-    n = 32
-    me = lax.axis_index('dev')
-    c, x, y, z = lax.rem(me, 2), lax.rem(me // 2, 2), lax.rem(me // 4, 2), me // 8
-    rows = L.shape[2]
-    half = rows // 2
-    A, B = pl.ds(0, half), pl.ds(half, half)
-    def dev(z, y, x, c):
-        return ((z * 2 + y) * 2 + x) * 2 + c
-    def begin(d):
-        return pl.multiple_of((lead + share_rows * d) // 8 * 8, 8)
-    greet(n, me)
-    tx, ty, tc = dev(z, y, 1 - x, c), dev(z, 1 - y, x, c), dev(z, y, x, 1 - c)
-    pend = []
-    def start(cp):
-        cp.start(); pend.append(cp)
-    order = [2, 1, 3, 0]
-    zz = [lax.rem(z + k, 4) for k in range(4)]
-    def fetch(k):
-        for i in range(4):
-            ys, xs = i // 2, i % 2
-            start(remote(g_ref.at[pl.ds(begin(dev(zz[k], ys, xs, 1 - c)), rows)], R.at[k, i], rs0_s.at[k, i], rs0_r.at[k, i], tc))
-            pltpu.make_async_copy(g_ref.at[pl.ds(begin(dev(zz[k], ys, xs, c)), rows)], L.at[k, i], ls.at[k, i]).start()
-    e_own = pltpu.make_async_copy(err_ref, errs_ref.at[me], own.at[0])
-    e_own.start()
-    def go(j, carry):
-        t = lax.rem(me + j, n)
-        remote(err_ref, errs_ref.at[me], es.at[j], er.at[j], t).start()
-        return carry
-    lax.fori_loop(1, n, go, 0)
-    i_own, i_x, i_y = y * 2 + x, y * 2 + 1 - x, (1 - y) * 2 + x
-    def s0(k):
-        for i in range(4):
-            pltpu.make_async_copy(g_ref.at[pl.ds(0, rows)], L.at[k, i], ls.at[k, i]).wait()
-            remote(L.at[k, i], R.at[k, i], rs0_s.at[k, i], rs0_r.at[k, i], tc).wait_recv()
-            accumulate(L.at[k, i], R.at[k, i], rows)
-        for j in range(2):
-            start(remote(L.at[k, (1 - y) * 2 + j, A], YA.at[k, j], as1.at[k, j], ar1.at[k, j], ty))
-            start(remote(L.at[k, j * 2 + 1 - x, B], XB.at[k, j], bs1.at[k, j], br1.at[k, j], tx))
-    def mid(k):
-        for j in range(2):
-            remote(L.at[k, 0, A], YA.at[k, j], as1.at[k, j], ar1.at[k, j], ty).wait_recv()
-            accumulate(L.at[k, y * 2 + j, A], YA.at[k, j], half)
-        start(remote(L.at[k, i_x, A], XA.at[k], as2.at[k], ar2.at[k], tx))
-        for j in range(2):
-            remote(L.at[k, 0, B], XB.at[k, j], bs1.at[k, j], br1.at[k, j], tx).wait_recv()
-            accumulate(L.at[k, j * 2 + x, B], XB.at[k, j], half)
-        start(remote(L.at[k, i_y, B], YB.at[k], bs2.at[k], br2.at[k], ty))
-    def fin(k):
-        remote(L.at[k, 0, A], XA.at[k], as2.at[k], ar2.at[k], tx).wait_recv()
-        accumulate(L.at[k, i_own, A], XA.at[k], half)
-        remote(L.at[k, 0, B], YB.at[k], bs2.at[k], br2.at[k], ty).wait_recv()
-        accumulate(L.at[k, i_own, B], YB.at[k], half)
-        if k:
-            start(remote(L.at[k, i_own], Z.at[k - 1], zs.at[k - 1], zr.at[k - 1], dev(zz[k], y, x, c)))
-    for step in SCHEDULE:
-        {"g": fetch, "s": s0, "m": mid, "f": fin}[step[0]](order[int(step[1])])
-    for k in range(3):
-        remote(L.at[0, 0], Z.at[k], zs.at[k], zr.at[k], tc).wait_recv()
-    first = lax.rem(lead + share_rows * me, 8)
-    sq[...] = jnp.zeros_like(sq)
-    mine = L.at[0, i_own]
-    def total(r, size):
-        at = pl.ds(r, size)
-        v = mine[at] + Z[0, at] + (Z[1, at] + Z[2, at])
-        o_ref[at] = v
-        row = r + lax.broadcasted_iota(jnp.int32, (size, 128), 0)
-        inside = (row >= first) & (row < first + share_rows)
-        v = jnp.where(inside, v, 0.0)
-        v = v * v
-        sq[...] += jnp.sum(v.reshape(size // 8, 8, 128), axis=0)
-    step = 80
-    def several(i, carry):
-        total(pl.multiple_of(i * step, 8), step)
-        return carry
-    lax.fori_loop(0, rows // step, several, 0)
-    if rows % step:
-        total(rows // step * step, rows % step)
-    q_own = pltpu.make_async_copy(sq, sq_ref.at[me], own.at[1])
-    q_own.start()
-    def go2(j, carry):
-        t = lax.rem(me + j, n)
-        remote(sq, sq_ref.at[me], qs.at[j], qr.at[j], t).start()
-        return carry
-    lax.fori_loop(1, n, go2, 0)
-    for cp in pend:
-        cp.wait_send()
-    def end(j, carry):
-        t = lax.rem(me + j, n)
-        remote(err_ref, errs_ref.at[me], es.at[j], er.at[j], t).wait()
-        remote(sq, sq_ref.at[me], qs.at[j], qr.at[j], t).wait()
-        return carry
-    lax.fori_loop(1, n, end, 0)
-    e_own.wait()
-    q_own.wait()
-
-def reduce_gradient(g, err, share_rows, lead, rows, cid):
-    n = 32
-    D = pltpu.SemaphoreType.DMA
-    anyspec = pl.BlockSpec(memory_space=pl.ANY)
-    vm = pl.BlockSpec(memory_space=pltpu.VMEM)
-    half = rows // 2
-    F = lambda *s: pltpu.VMEM(s + (128,), jnp.float32)
-    return pl.pallas_call(
-        functools.partial(reduce_kernel, share_rows, lead),
-        out_shape=(jax.ShapeDtypeStruct((rows, 128), jnp.float32), jax.ShapeDtypeStruct((n, 8, 128), jnp.float32), jax.ShapeDtypeStruct((n, 8, 128), jnp.float32)),
-        in_specs=[anyspec, vm], out_specs=(vm, vm, vm),
-        scratch_shapes=[F(4, 4, rows), F(4, 4, rows), F(4, 2, half), F(4, half), F(4, 2, half), F(4, half), F(3, rows), F(8),
-            D((2,)), D((4, 4)), D((4, 4)), D((4, 4)), D((4, 2)), D((4, 2)), D((4,)), D((4,)), D((4, 2)), D((4, 2)), D((4,)), D((4,)), D((3,)), D((3,)), D((n,)), D((n,)), D((n,)), D((n,))],
-        compiler_params=pltpu.CompilerParams(collective_id=cid, has_side_effects=True, vmem_limit_bytes=48 << 20),
-    )(g, err)
-
-
 F32, BF16 = jnp.float32, jnp.bfloat16
-VMEM_LIMIT = 56 << 20
+VMEM_LIMIT = 60 << 20
 ANY = pl.BlockSpec(memory_space=pl.ANY)
 DMA = pltpu.SemaphoreType.DMA
 
@@ -379,6 +251,10 @@
 
 def mm_tn(a, b):
     return lax.dot_general(a, b, (((0,), (0,)), ((), ())), preferred_element_type=F32)
+
+
+def contract(a, b, left, right):
+    return lax.dot_general(a, b, (((left,), (right,)), ((), ())), preferred_element_type=F32)
 
 
 def col(v):
@@ -486,10 +362,48 @@
     return jax.ShapeDtypeStruct(shape, dtype)
 
 
-def store_flat(packed, flat, at, sem):
-    copy = pltpu.make_async_copy(packed, flat.at[pl.ds(at, packed.shape[0])], sem)
-    copy.start()
-    return copy
+class Chunks:
+    def __init__(self, begins, rows, cuts):
+        self.begins, self.rows, self.cuts = begins, rows, cuts
+
+    def shape(self, group):
+        return (self.cuts[group + 1] - self.cuts[group], self.rows, 128)
+
+    def pieces(self, at, size):
+        found = []
+        for group in range(len(self.cuts) - 1):
+            for owner in range(self.cuts[group], self.cuts[group + 1]):
+                begin = self.begins[owner]
+                low, high = max(at, begin), min(at + size, begin + self.rows)
+                if low < high:
+                    found.append((group, owner - self.cuts[group], low - begin, low - at, high - low))
+        return found
+
+    def groups(self, *places):
+        return sorted({p[0] for at, size in places for p in self.pieces(at, size)})
+
+
+class Stores:
+    def __init__(self, refs, chunks, sem):
+        self.refs, self.chunks, self.sem, self.copies = refs, chunks, sem, []
+
+    def put(self, packed, at):
+        for group, owner, row, skip, size in self.chunks.pieces(at, packed.shape[0]):
+            source = packed.at[pl.ds(skip, size)]
+            copy = pltpu.make_async_copy(source, self.refs[group].at[owner, pl.ds(row, size)], self.sem.at[len(self.copies)])
+            copy.start()
+            self.copies.append(copy)
+
+    def wait(self):
+        for copy in self.copies:
+            copy.wait()
+
+
+STORES = 48
+
+
+def flat_refs(r, groups):
+    return {group: getattr(r, f"flat{group}") for group in groups}
 
 
 def mlp_sums(rows_in, wide=LATENT):
@@ -519,26 +433,47 @@
     return types.SimpleNamespace(**dict(zip(outputs, values)))
 
 
-def swap_start(n, me, src, dst, own, ssem, rsem):
-    pltpu.make_async_copy(src.at[me], dst.at[me], own).start()
+def swap_start(n, me, srcs, dsts, own, ssem, rsem):
+    for i, (src, dst) in enumerate(zip(srcs, dsts)):
+        pltpu.make_async_copy(src.at[me], dst.at[me], own.at[i]).start()
     def go(j, c):
         t = lax.rem(me + j, n)
-        remote(src.at[t], dst.at[me], ssem.at[j], rsem.at[j], t).start()
+        for i, (src, dst) in enumerate(zip(srcs, dsts)):
+            remote(src.at[t], dst.at[me], ssem.at[i, j], rsem.at[i, j], t).start()
         return c
     lax.fori_loop(1, n, go, 0)
 
 
-def swap_wait(n, me, src, dst, own, ssem, rsem):
+def swap_wait(n, me, srcs, dsts, own, ssem, rsem):
     def end(j, c):
         t = lax.rem(me + j, n)
-        remote(src.at[t], dst.at[me], ssem.at[j], rsem.at[j], t).wait()
+        for i, (src, dst) in enumerate(zip(srcs, dsts)):
+            remote(src.at[t], dst.at[me], ssem.at[i, j], rsem.at[i, j], t).wait()
         return c
     lax.fori_loop(1, n, end, 0)
-    pltpu.make_async_copy(src.at[me], dst.at[me], own).wait()
-
-
-def flat_rows_of(ref):
-    return ref[...].reshape(ref.shape[0] * ref.shape[1], ref.shape[2])
+    for i, (src, dst) in enumerate(zip(srcs, dsts)):
+        pltpu.make_async_copy(src.at[me], dst.at[me], own.at[i]).wait()
+
+
+def several(r, name):
+    return [getattr(r, f"{name}{i}") for i in range(4) if hasattr(r, f"{name}{i}")]
+
+
+def numbered(name, values):
+    return {f"{name}{i}": value for i, value in enumerate(values)}
+
+
+def slot_rows(refs):
+    rows = [ref[...].reshape(ref.shape[0] * ref.shape[1], ref.shape[2]) for ref in refs]
+    return rows[0] if len(rows) == 1 else jnp.concatenate(rows, axis=0)
+
+
+def put_slot_rows(refs, rows):
+    at = 0
+    for ref in refs:
+        size = ref.shape[0] * ref.shape[1]
+        ref[...] = rows[at : at + size, :].reshape(ref.shape)
+        at += size
 
 
 def greet_start(n, me):
@@ -579,8 +514,12 @@
     return jnp.where((want[...] == served[...]) & (want[...] >= 0), 1.0, 0.0).astype(BF16)
 
 
-def swap_scratch(shape, n):
-    return dict(away=pltpu.VMEM(shape, BF16), here=pltpu.VMEM(shape, BF16), back=pltpu.VMEM(shape, BF16), own=DMA((2,)), s1=DMA((n,)), r1=DMA((n,)), s2=DMA((n,)), r2=DMA((n,)))
+def swap_scratch(shapes, n):
+    parts = len(shapes)
+    scratch = dict(own=DMA((2, parts)), s1=DMA((parts, n)), r1=DMA((parts, n)), s2=DMA((parts, n)), r2=DMA((parts, n)))
+    for name in ("away", "here", "back"):
+        scratch |= numbered(name, [pltpu.VMEM(shape, BF16) for shape in shapes])
+    return scratch
 
 
 def held(prefix, block):
@@ -600,30 +539,32 @@
     greet_start(n, me)
     loads = Loads(r, r.lsem)
     node_weights = ["p_in", "p_out", "p_vec"]
-    early = node_weights + ([] if first else ["landed_in", "slots_in"])
+    landing = [name for name in vars(r) if name.startswith("landed_in")]
+    early = node_weights + ([] if first else [*landing, "slots_in"])
     late = ["e_in", "e_out", "e_vec"] + (["g_in", "g_out", "g_vec"] if first else [])
     loads.start(*early)
     loads.start(*late)
     loads.wait(*early)
     count = r.want.shape[0]
     if first:
-        rows = r.x.shape[0]
-        us = [mm(pick(r.want[...], 0, rows), r.x[...]).astype(BF16)]
+        asked = contract(pick(r.want[...], 0, r.x.shape[1]), r.x[...], 1, 1).astype(BF16)
+        pre = contract(asked, r._p_in[:VARS, :], 1, 0) + r._p_vec[0:1, :]
     else:
-        landed = flat_rows_of(r._landed_in)
+        landed = slot_rows(several(r, "_landed_in"))
         got = mm(same_rows(r.want, r.served), landed).astype(BF16)
         r._sums_s[...] = got
         old = r._slots_in[...]
-        us = [old.astype(BF16), got]
-    _, act = activate(first_half(us, r._p_in, r._p_vec))
+        pre = first_half([old.astype(BF16), got], r._p_in, r._p_vec)
+    _, act = activate(pre)
     hat, _ = second_half(act, r._p_out, r._p_vec)
     slots = scale_shift(hat, r._p_vec)
     if not first:
         slots = old + slots
     r._slots[...] = slots
-    r.away[...] = slots.astype(BF16).reshape(r.away.shape)
+    away, here, back, out = (several(r, name) for name in ("away", "here", "back", "landed"))
+    put_slot_rows(away, slots.astype(BF16))
     greet_wait(n)
-    swap_start(n, me, r.away, r.here, r.own.at[0], r.s1, r.r1)
+    swap_start(n, me, away, here, r.own.at[0], r.s1, r.r1)
     stores = store_all(r, r.ssem, *(["slots"] if first else ["slots", "sums_s"]))
     loads.wait(*late)
     if first:
@@ -638,8 +579,8 @@
     if first:
         def body(node, low):
             i = pl.program_id(0)
-            u = r.x[pl.ds(pl.multiple_of(i * bm, bm), bm), :]
-            _, act = activate(first_half([u], r._p_in, r._p_vec))
+            u = r.x[:, pl.ds(pl.multiple_of(i * bm, bm), bm)]
+            _, act = activate(contract(u, r._p_in[:VARS, :], 0, 0) + r._p_vec[0:1, :])
             hat, _ = second_half(act, r._p_out, r._p_vec)
             new = scale_shift(hat, r._p_vec)
             node[...] = new
@@ -648,7 +589,7 @@
     else:
         def body(node_in, node, low, sums):
             i = pl.program_id(0)
-            got = mm(place(r.served[...], i * bm, bm), flat_rows_of(r._landed_in)).astype(BF16)
+            got = mm(place(r.served[...], i * bm, bm), slot_rows(several(r, "_landed_in"))).astype(BF16)
             sums[...] = got
             old = node_in[...]
             _, act = activate(first_half([old.astype(BF16), got], r._p_in, r._p_vec))
@@ -659,53 +600,57 @@
         pltpu.emit_pipeline(body, grid=(r.node.shape[0] // bm,), in_specs=[rows_block(bm)], out_specs=[rows_block(bm)] * 3)(r.node_in, r.node, r.low, r.sums)
     pick_s, pick_r = pick(r.pos[:, 0:1], 0, count), pick(r.pos[:, 1:2], 0, count)
     put_r = place(r.pos_r[...], 0, count)
-    swap_wait(n, me, r.away, r.here, r.own.at[0], r.s1, r.r1)
-    rows = flat_rows_of(r.here)
+    swap_wait(n, me, away, here, r.own.at[0], r.s1, r.r1)
+    rows = slot_rows(here)
     s = mm(pick_s, rows).astype(BF16)
     v = mm(pick_r, rows).astype(BF16)
     pre = r._pre[...] + mm(s, r._e_in[LATENT : 2 * LATENT, :]) + mm(v, r._e_in[2 * LATENT :, :])
     _, act = activate(pre)
     hat, _ = second_half(act, r._e_out, r._e_vec)
     new = r._edge[...] + scale_shift(hat, r._e_vec)
-    r.back[...] = mm(put_r, new.astype(BF16)).astype(BF16).reshape(r.back.shape)
-    swap_start(n, me, r.back, r.landed, r.own.at[1], r.s2, r.r2)
+    put_slot_rows(back, mm(put_r, new.astype(BF16)).astype(BF16))
+    swap_start(n, me, back, out, r.own.at[1], r.s2, r.r2)
     r.edge[...] = new
     r.sent[...], r.recv[...] = s, v
     for store in stores:
         store.wait()
-    swap_wait(n, me, r.back, r.landed, r.own.at[1], r.s2, r.r2)
-
-
-def edge_forward(n, cid, source, routes, edge_block, node_block, rows, x=None, geo_block=None, landed=None, node=None, slots=None, bm=512):
+    swap_wait(n, me, back, out, r.own.at[1], r.s2, r.r2)
+
+
+def edge_forward(n, parts, cid, source, routes, edge_block, node_block, rows, x=None, geo_block=None, landed=None, node=None, slots=None, bm=512):
     first = x is not None
     want, served, pos, pos_s, pos_r = routes
     count = want.shape[0]
     edges = source.shape[0]
-    shape = (n, count // n, LATENT)
+    shapes = [(n, p, LATENT) for p in parts]
     V = pl.BlockSpec(memory_space=pltpu.VMEM)
     inputs = dict(source=(source, V), want=(want, V), served=(served, V), pos=(pos, V), pos_r=(pos_r, V))
     inputs |= weights("p", node_block) | weights("e", edge_block)
-    scratch = held("_p", node_block) | held("_e", edge_block) | swap_scratch(shape, n)
+    scratch = held("_p", node_block) | held("_e", edge_block) | swap_scratch(shapes, n)
     scratch |= dict(_slots=pltpu.VMEM((count, LATENT), F32), _edge=pltpu.VMEM((edges, LATENT), F32), _pre=pltpu.VMEM((edges, LATENT), F32), lsem=DMA((12,)), ssem=DMA((2,)))
     low = lambda r: shaped(r, LATENT, dtype=BF16)
-    outputs = dict(edge=(shaped(edges, LATENT), V), edge_low=(low(edges), V), sent=(low(edges), V), recv=(low(edges), V), landed=(shaped(*shape, dtype=BF16), ANY))
+    outputs = dict(edge=(shaped(edges, LATENT), V), edge_low=(low(edges), V), sent=(low(edges), V), recv=(low(edges), V)) | numbered("landed", [(shaped(*s, dtype=BF16), ANY) for s in shapes])
     outputs |= dict(node=(shaped(rows, LATENT), ANY), low=(low(rows), ANY), slots=(shaped(count, LATENT), ANY))
     if first:
         inputs |= dict(x=(x, V)) | weights("g", geo_block)
         scratch |= held("_g", geo_block)
     else:
-        inputs |= dict(landed_in=(landed, ANY), node_in=(node, ANY), slots_in=(slots, ANY))
-        scratch |= dict(_landed_in=pltpu.VMEM(shape, BF16), _slots_in=pltpu.VMEM((count, LATENT), F32), _sums_s=pltpu.VMEM((count, LATENT), BF16))
+        inputs |= numbered("landed_in", [(v, ANY) for v in landed]) | dict(node_in=(node, ANY), slots_in=(slots, ANY))
+        scratch |= numbered("_landed_in", [pltpu.VMEM(s, BF16) for s in shapes]) | dict(_slots_in=pltpu.VMEM((count, LATENT), F32), _sums_s=pltpu.VMEM((count, LATENT), BF16))
         outputs |= dict(sums=(low(rows), ANY), sums_s=(low(count), ANY))
     return named_call(functools.partial(edge_kernel, n, first, bm), "edge_forward", inputs, outputs, scratch, cid=cid)
 
 
-def turn_kernel(bm, at, dec_at, served, want, landed, node, x, target, level, land, count, w_in, w_out, vec, c_in, c_out, c_vec, flat, g_prev, g_slots, out, d_out_o, d_vec_o, err_o, packed, packed2, d_in, d_out, d_vec, e_in, e_out, e_vec, err, acc, sem):
+def turn_kernel(parts, bm, chunks, group, at, dec_at, served, want, *refs):
+    landed, refs = refs[:parts], refs[parts:]
+    flat, g_prev, *outs = refs[13 : 15 + parts]
+    node, x, target, level, land, count, w_in, w_out, vec, c_in, c_out, c_vec, c_bias = refs[:13]
+    d_out_o, d_first_o, d_bias_o, err_o, packed, packed2, d_in, d_out, d_vec, e_in, e_out, e_vec, e_bias, err, acc, sem = refs[13 + 2 + parts:]
     i = pl.program_id(0)
     @pl.when(i == 0)
     def _():
-        clear(d_in, d_out, d_vec, e_in, e_out, e_vec, err, acc, g_slots)
-    got = mm(place(served[...], i * bm, bm), landed[...]).astype(BF16)
+        clear(d_in, d_out, d_vec, e_in, e_out, e_vec, e_bias, err, acc)
+    got = mm(place(served[...], i * bm, bm), slot_rows(landed)).astype(BF16)
     old = node[...]
     low = old.astype(BF16)
     pre = first_half([low, got], w_in, vec)
@@ -715,88 +660,104 @@
     c_pre = first_half([u], c_in, c_vec)
     c_sigma, c_act = activate(c_pre)
     wide = c_out.shape[1]
-    post = mm(c_act, c_out[...]) + c_vec[1:2, :wide]
-    sea = (lax.broadcasted_iota(jnp.int32, (1, VARS), 1) < SEA_VARS).astype(F32)
-    mask = level[...].astype(F32) * (1.0 - land[...].astype(F32) * sea)
-    residual = x[...].astype(F32) + post[:, :VARS] - target[...]
+    post = contract(c_out[...], c_act, 0, 1)
+    sea = (lax.broadcasted_iota(jnp.int32, (VARS, 1), 0) < SEA_VARS).astype(F32)
+    mask = level[...].astype(F32) * (1.0 - sea * land[...].astype(F32))
+    residual = x[...].astype(F32) + (post[:VARS, :] + c_bias[...]) - target[...]
     divisor = jnp.maximum(count[...], 1.0)
-    err[:, :VARS] += col(mask * residual * residual)
+    err[...] += jnp.sum(mask * residual * residual, axis=0, keepdims=True)
     g = 2.0 * mask * residual / divisor
-    g_low = jnp.concatenate([g, jnp.zeros((bm, wide - VARS), F32)], axis=1).astype(BF16)
-    c_g = act_back(g_low, c_pre, c_sigma, c_out)
-    weight_sums([u], c_act, g_low, c_g, e_in, e_out, e_vec)
+    g_low = jnp.concatenate([g, jnp.zeros((wide - VARS, bm), F32)], axis=0).astype(BF16)
+    e_bias[...] += jnp.sum(g_low.astype(F32), axis=1, keepdims=True)
+    e_out[...] += contract(c_act, g_low, 0, 1)
+    g_act = contract(g_low, c_out[...], 0, 1)
+    c_g = (g_act * c_sigma * (1.0 + c_pre * (1.0 - c_sigma))).astype(BF16)
+    e_vec[0:1, :] += col(c_g.astype(F32))
+    e_in[...] += mm_tn(u, c_g)
     g_node = mm_nt(c_g, c_in[...])
     g_post = norm_back(g_node, hat, inv, vec, d_vec)
     g_pre = act_back(g_post, pre, sigma, w_out)
     weight_sums([low, got], act, g_post, g_pre, d_in, d_out, d_vec)
-    g = g_node + mm_nt(g_pre, w_in[:LATENT, :])
-    g_prev[...] = g
-    chosen = pick(want[...], i * bm, bm)
-    acc[...] += mm(chosen, mm_nt(g_pre, w_in[LATENT:, :]).astype(BF16))
-    high = g.astype(BF16)
-    rest = g - high.astype(F32)
-    middle = rest.astype(BF16)
-    small = (rest - middle.astype(F32)).astype(BF16)
-    g_slots[...] += mm(chosen, high) + (mm(chosen, middle) + mm(chosen, small))
+    g_prev[...] = g_node + mm_nt(g_pre, w_in[:LATENT, :])
+    acc[...] += mm(pick(want[...], i * bm, bm), mm_nt(g_pre, w_in[LATENT:, :]).astype(BF16))
     @pl.when(i == pl.num_programs(0) - 1)
     def _():
-        out[...] = acc[...].astype(BF16)
+        put_slot_rows(outs, acc[...].astype(BF16))
         d_out_o[...] = e_out[...]
-        d_vec_o[...] = e_vec[...]
+        d_first_o[...] = e_vec[0:1, :]
+        d_bias_o[...] = e_bias[...]
         err_o[...] = err[...]
+        stores = Stores({group: flat}, chunks, sem)
         pack_matrix(packed2, e_in, LATENT, 0)
-        one = store_flat(packed2, flat, dec_at, sem.at[0])
+        stores.put(packed2, dec_at)
         pack(packed, 0, 2 * LATENT, d_in, d_out, d_vec)
-        two = store_flat(packed, flat, at, sem.at[1])
-        one.wait()
-        two.wait()
-
-
-def turn(served, want, landed, node, x, target, level, land, count, block, dec, flat_rows, at, dec_at, bm=512):
+        stores.put(packed, at)
+        stores.wait()
+
+
+def turn(served, want, landed, node, x, target, level, land, count, block, dec, bias, chunks, at, dec_at, bm=512):
     rows = node.shape[0]
     slots = want.shape[0]
     wide = dec[1].shape[1]
-    v = lambda: spec((bm, VARS), False)
+    [group] = chunks.groups((at, dec_at + 4 * LATENT - at))
+    v = lambda height: pl.BlockSpec((height, bm), lambda i: (0, i))
+    part = [spec(p.shape) for p in landed]
     return pl.pallas_call(
-        functools.partial(turn_kernel, bm, at, dec_at),
+        functools.partial(turn_kernel, len(landed), bm, chunks, group, at, dec_at),
         grid=(rows // bm,),
-        out_shape=(shaped(flat_rows, 128), shaped(rows, LATENT), shaped(slots, LATENT), shaped(slots, LATENT, dtype=BF16), shaped(LATENT, wide), shaped(8, LATENT), shaped(1, wide)),
-        in_specs=[spec((1, slots)), spec((slots, 1)), spec((slots, LATENT)), spec((bm, LATENT), False), v(), v(), v(), spec((bm, 1), False), spec((1, 1))] + [spec(a.shape) for a in (*block, *dec)],
-        out_specs=(ANY, spec((bm, LATENT), False), spec((slots, LATENT)), spec((slots, LATENT)), spec((LATENT, wide)), spec((8, LATENT)), spec((1, wide))),
-        scratch_shapes=[packed_rows(2 * LATENT), pltpu.VMEM((4 * LATENT, 128), F32)] + mlp_sums(2 * LATENT) + mlp_sums(LATENT, wide) + [pltpu.VMEM((1, wide), F32), pltpu.VMEM((slots, LATENT), F32), DMA((2,))],
+        out_shape=(shaped(*chunks.shape(group)), shaped(rows, LATENT), *(shaped(*p.shape, dtype=BF16) for p in landed), shaped(LATENT, wide), shaped(1, LATENT), shaped(wide, 1), shaped(1, bm)),
+        in_specs=[spec((1, slots)), spec((slots, 1)), *part, spec((bm, LATENT), False), v(VARS), v(VARS), v(VARS), v(1), spec((1, 1))] + [spec(a.shape) for a in (*block, *dec, bias)],
+        out_specs=(ANY, spec((bm, LATENT), False), *part, spec((LATENT, wide)), spec((1, LATENT)), spec((wide, 1)), spec((1, bm))),
+        scratch_shapes=[packed_rows(2 * LATENT), pltpu.VMEM((4 * LATENT, 128), F32)] + mlp_sums(2 * LATENT) + mlp_sums(LATENT, wide) + [pltpu.VMEM((wide, 1), F32), pltpu.VMEM((1, bm), F32), pltpu.VMEM((slots, LATENT), F32), DMA((STORES,))],
         compiler_params=params(),
         name="turn",
-    )(served, want, landed, node, x, target, level, land, count, *block, *dec)
-
-
-def edge_back_kernel(n, at, node_at, geo_at, tail_at, bm, r):
+    )(served, want, *landed, node, x, target, level, land, count, *block, *dec, bias)
+
+
+def gather_slots(r, bm):
+    clear(r._g_slots)
+    def body(g_node):
+        chosen = pick(r.want[...], pl.program_id(0) * bm, bm)
+        g = g_node[...]
+        high = g.astype(BF16)
+        rest = g - high.astype(F32)
+        middle = rest.astype(BF16)
+        small = (rest - middle.astype(F32)).astype(BF16)
+        r._g_slots[...] += mm(chosen, high) + (mm(chosen, middle) + mm(chosen, small))
+    pltpu.emit_pipeline(body, grid=(r.g_node.shape[0] // bm,), in_specs=[rows_block(bm)], out_specs=[])(r.g_node)
+
+
+def edge_back_kernel(n, chunks, groups, at, node_at, geo_at, tail_at, bm, r):
     me = lax.axis_index("dev")
     greet_start(n, me)
     loads = Loads(r, r.lsem)
     nodes = node_at is not None
-    early = ["p_in", "p_out", "p_vec", "landed_in", "g_slots_in", "slots_in", "sums_s"] if nodes else []
+    landing = [name for name in vars(r) if name.startswith("landed_in")]
+    early = ["p_in", "p_out", "p_vec", *landing, "g_slots_in", "slots_in", "sums_s"] if nodes else []
     late = ["e_in", "e_out", "e_vec"] + (["g_in", "g_out", "g_vec"] if geo_at is not None else [])
     loads.start(*early)
     loads.start(*late)
-    stores = []
+    flats = Stores(flat_refs(r, groups), chunks, r.fsem)
+    stores = [flats]
     if tail_at is not None:
-        stores.append(store_flat(r.tail, r.flat, tail_at, r.fsem.at[2]))
+        flats.put(r.tail, tail_at)
     count = r.want.shape[0]
+    here, back, out = (several(r, name) for name in ("here", "back", "landed"))
     if nodes:
         loads.wait(*early)
         us = [r._slots_in[...].astype(BF16), r._sums_s[...]]
         pre = first_half(us, r._p_in, r._p_vec)
         sigma, act = activate(pre)
         hat, inv = second_half(act, r._p_out, r._p_vec)
-        g = r._g_slots_in[...] + mm(same_rows(r.want, r.served), flat_rows_of(r._landed_in))
+        g = r._g_slots_in[...] + mm(same_rows(r.want, r.served), slot_rows(several(r, "_landed_in")))
         low = norm_back(g, hat, inv, r._p_vec, None)
         g_pre = act_back(low, pre, sigma, r._p_out)
-        r.away[...] = mm_nt(g_pre, r._p_in[LATENT:, :]).astype(BF16).reshape(r.away.shape)
-        source = r.away
+        source = several(r, "away")
+        put_slot_rows(source, mm_nt(g_pre, r._p_in[LATENT:, :]).astype(BF16))
     else:
-        source = r.outgoing
+        source = several(r, "outgoing")
     greet_wait(n)
-    swap_start(n, me, source, r.here, r.own.at[0], r.s1, r.r1)
+    swap_start(n, me, source, here, r.own.at[0], r.s1, r.r1)
     if nodes:
         r._g_slots[...] = g + mm_nt(g_pre, r._p_in[:LATENT, :])
         stores += store_all(r, r.ssem, "g_slots")
@@ -811,7 +772,7 @@
             pre = first_half(us, r._p_in, r._p_vec)
             sigma, act = activate(pre)
             hat, inv = second_half(act, r._p_out, r._p_vec)
-            g = g_node[...] + mm(place(r.served[...], i * bm, bm), flat_rows_of(r._landed_in))
+            g = g_node[...] + mm(place(r.served[...], i * bm, bm), slot_rows(several(r, "_landed_in")))
             low = norm_back(g, hat, inv, r._p_vec, r.n_vec)
             g_pre = act_back(low, pre, sigma, r._p_out)
             weight_sums(us, act, low, g_pre, r.n_in, r.n_out, r.n_vec)
@@ -820,6 +781,8 @@
         pltpu.emit_pipeline(body, grid=(last - first,), in_specs=[block] * 3, out_specs=[block])(r.g_node, r.low, r.sums, r.g_prev)
     blocks = r.g_node.shape[0] // bm if nodes else 0
     node_rows(0, blocks // 2)
+    if not nodes:
+        gather_slots(r, bm)
     loads.wait(*late)
     us = [r.edge_low[...], r.sent[...], r.recv[...]]
     pre = first_half(us, r._e_in, r._e_vec)
@@ -827,21 +790,21 @@
     hat, inv = second_half(act, r._e_out, r._e_vec)
     pick_r = pick(r.pos[:, 1:2], 0, count)
     put_s, put_r = place(r.pos_s[...], 0, count), place(r.pos_r[...], 0, count)
-    swap_wait(n, me, source, r.here, r.own.at[0], r.s1, r.r1)
-    g = mm(pick_r, flat_rows_of(r.here))
+    swap_wait(n, me, source, here, r.own.at[0], r.s1, r.r1)
+    g = mm(pick_r, slot_rows(here))
     if hasattr(r, "g_edge"):
         g = r.g_edge[...] + g
     low = norm_back(g, hat, inv, r._e_vec, r.d_vec)
     g_pre = act_back(low, pre, sigma, r._e_out)
     s = mm_nt(g_pre, r._e_in[LATENT : 2 * LATENT, :]).astype(BF16)
     v = mm_nt(g_pre, r._e_in[2 * LATENT :, :]).astype(BF16)
-    r.back[...] = (mm(put_s, s) + mm(put_r, v)).astype(BF16).reshape(r.back.shape)
-    swap_start(n, me, r.back, r.landed, r.own.at[1], r.s2, r.r2)
+    put_slot_rows(back, (mm(put_s, s) + mm(put_r, v)).astype(BF16))
+    swap_start(n, me, back, out, r.own.at[1], r.s2, r.r2)
     prev = g + mm_nt(g_pre, r._e_in[:LATENT, :])
     r.edge_prev[...] = prev
     weight_sums(us, act, low, g_pre, r.d_in, r.d_out, r.d_vec)
     pack(r.packed, 0, 3 * LATENT, r.d_in, r.d_out, r.d_vec)
-    stores.append(store_flat(r.packed, r.flat, at, r.fsem.at[0]))
+    flats.put(r.packed, at)
     if geo_at is not None:
         c_us = [r.geo[...]]
         c_pre = first_half(c_us, r._g_in, r._g_vec)
@@ -852,12 +815,14 @@
         c_g = act_back(c_low, c_pre, c_sigma, r._g_out)
         weight_sums(c_us, c_act, c_low, c_g, r.c_in, r.c_out, r.c_vec)
         pack(r.c_packed, 0, GEO, r.c_in, r.c_out, r.c_vec)
-        stores.append(store_flat(r.c_packed, r.flat, geo_at, r.fsem.at[1]))
+        flats.put(r.c_packed, geo_at)
     node_rows(blocks // 2, blocks)
     if nodes:
         pack(r.n_packed, 0, 2 * LATENT, r.n_in, r.n_out, r.n_vec)
-        stores.append(store_flat(r.n_packed, r.flat, node_at, r.fsem.at[3]))
-    swap_wait(n, me, r.back, r.landed, r.own.at[1], r.s2, r.r2)
+        flats.put(r.n_packed, node_at)
+    if not nodes:
+        stores += store_all(r, r.ssem, "g_slots")
+    swap_wait(n, me, back, out, r.own.at[1], r.s2, r.r2)
     for store in stores:
         store.wait()
 
@@ -866,73 +831,93 @@
     return dict(zip((prefix + "_in", prefix + "_out", prefix + "_vec"), mlp_sums(rows_in)))
 
 
-def edge_backward(n, cid, ins, routes, edge_block, flat, at, g_edge=None, outgoing=None, tail=None, tail_at=None, node=None, node_at=None, geo=None, geo_at=None, bm=512):
+def edge_backward(n, parts, cid, ins, routes, edge_block, chunks, flats, at, g_edge=None, outgoing=None, g_node=None, tail=None, tail_at=None, node=None, node_at=None, geo=None, geo_at=None, bm=512):
     want, served, pos, pos_s, pos_r = routes
     count = want.shape[0]
     edges = pos.shape[0]
-    shape = (n, count // n, LATENT)
+    shapes = [(n, p, LATENT) for p in parts]
     V = pl.BlockSpec(memory_space=pltpu.VMEM)
-    inputs = dict(want=(want, V), served=(served, V), pos=(pos, V), pos_s=(pos_s, V), pos_r=(pos_r, V), flat_in=(flat, ANY))
+    inputs = dict(want=(want, V), served=(served, V), pos=(pos, V), pos_s=(pos_s, V), pos_r=(pos_r, V))
     inputs |= {name: (value, V) for name, value in zip(("edge_low", "sent", "recv"), ins)} | weights("e", edge_block)
-    scratch = held("_e", edge_block) | swap_scratch(shape, n) | sums_scratch("d", 3 * LATENT)
-    scratch |= dict(packed=packed_rows(3 * LATENT), lsem=DMA((16,)), ssem=DMA((1,)), fsem=DMA((4,)))
-    outputs = dict(flat=(shaped(*flat.shape), ANY), edge_prev=(shaped(edges, LATENT), V), landed=(shaped(*shape, dtype=BF16), ANY))
+    scratch = held("_e", edge_block) | swap_scratch(shapes, n) | sums_scratch("d", 3 * LATENT)
+    scratch |= dict(packed=packed_rows(3 * LATENT), lsem=DMA((16,)), ssem=DMA((2,)), fsem=DMA((STORES,)))
+    outputs = dict(edge_prev=(shaped(edges, LATENT), V)) | numbered("landed", [(shaped(*s, dtype=BF16), ANY) for s in shapes])
+    places = [(at, scratch["packed"].shape[0])]
     if g_edge is not None:
         inputs |= dict(g_edge=(g_edge, V))
     if outgoing is not None:
-        inputs |= dict(outgoing=(outgoing.reshape(shape), ANY))
+        inputs |= numbered("outgoing", [(v, ANY) for v in outgoing]) | dict(g_node=(g_node, ANY))
+        outputs |= dict(g_slots=(shaped(count, LATENT), ANY))
+        scratch |= dict(_g_slots=pltpu.VMEM((count, LATENT), F32))
     if tail is not None:
         inputs |= dict(tail=(tail, V))
+        places.append((tail_at, tail.shape[0]))
     if node is not None:
-        for name, value in zip(("landed_in", "g_slots_in", "slots_in", "sums_s", "g_node", "low", "sums"), node):
+        inputs |= numbered("landed_in", [(v, ANY) for v in node[0]])
+        for name, value in zip(("g_slots_in", "slots_in", "sums_s", "g_node", "low", "sums"), node[1:]):
             inputs[name] = (value, ANY)
         inputs |= weights("p", node[7])
         scratch |= held("_p", node[7]) | sums_scratch("n", 2 * LATENT)
         f = pltpu.VMEM((count, LATENT), F32)
-        scratch |= dict(n_packed=packed_rows(2 * LATENT), _landed_in=pltpu.VMEM(shape, BF16), _g_slots_in=f, _slots_in=f, _g_slots=f, _sums_s=pltpu.VMEM((count, LATENT), BF16))
+        scratch |= numbered("_landed_in", [pltpu.VMEM(s, BF16) for s in shapes]) | dict(n_packed=packed_rows(2 * LATENT), _g_slots_in=f, _slots_in=f, _g_slots=f, _sums_s=pltpu.VMEM((count, LATENT), BF16))
         rows = node[4].shape[0]
+        places.append((node_at, scratch["n_packed"].shape[0]))
         outputs |= dict(g_prev=(shaped(rows, LATENT), ANY), g_slots=(shaped(count, LATENT), ANY))
     if geo is not None:
         inputs |= dict(geo=(geo[0], V)) | weights("g", geo[1])
         scratch |= held("_g", geo[1]) | sums_scratch("c", geo[0].shape[1]) | dict(c_packed=packed_rows(GEO))
-    body = functools.partial(edge_back_kernel, n, at, node_at, geo_at, tail_at, bm)
-    return named_call(body, "edge_backward", inputs, outputs, scratch, aliases=dict(flat_in="flat"), cid=cid)
-
-
-def encode_back_kernel(bm, served, landed, g_node, x, w_in, w_out, vec, flat_in, flat, packed, d_in, d_out, d_vec, sem):
+        places.append((geo_at, scratch["c_packed"].shape[0]))
+    groups = chunks.groups(*places)
+    aliases = {}
+    for group in groups:
+        outputs[f"flat{group}"] = (shaped(*chunks.shape(group)), ANY)
+        if group in flats:
+            inputs[f"flat{group}_in"] = (flats[group], ANY)
+            aliases[f"flat{group}_in"] = f"flat{group}"
+    body = functools.partial(edge_back_kernel, n, chunks, groups, at, node_at, geo_at, tail_at, bm)
+    made = named_call(body, "edge_backward", inputs, outputs, scratch, aliases=aliases, cid=cid)
+    flats.update(flat_refs(made, groups))
+    return made
+
+
+def encode_back_kernel(parts, bm, chunks, served, *refs):
+    landed, refs = refs[:parts], refs[parts:]
+    g_node, x, w_in, w_out, vec, flat_in, flat, packed, d_in, d_out, d_vec, sem = refs
     i = pl.program_id(0)
     @pl.when(i == 0)
     def _():
         clear(d_in, d_out, d_vec)
-    us = [x[...]]
-    pre = first_half(us, w_in, vec)
+    pre = contract(x[...], w_in[:VARS, :], 0, 0) + vec[0:1, :]
     sigma, act = activate(pre)
     hat, inv = second_half(act, w_out, vec)
-    g = g_node[...] + mm(place(served[...], i * bm, bm), landed[...])
+    g = g_node[...] + mm(place(served[...], i * bm, bm), slot_rows(landed))
     g_post = norm_back(g, hat, inv, vec, d_vec)
     g_pre = act_back(g_post, pre, sigma, w_out)
-    weight_sums(us, act, g_post, g_pre, d_in, d_out, d_vec)
+    weight_sums([], act, g_post, g_pre, d_in, d_out, d_vec)
+    d_in[:VARS, :] += mm(x[...], g_pre)
     @pl.when(i == pl.num_programs(0) - 1)
     def _():
         packed[0:4, :] = jnp.zeros((4, 128), F32)
         pack(packed, 4, VARS, d_in, d_out, d_vec)
-        store_flat(packed, flat, 0, sem).wait()
-
-
-def encode_backward(served, landed, g_node, x, block, flat, bm=512):
-    rows, k = x.shape
-    slots = landed.shape[0]
+        stores = Stores({0: flat}, chunks, sem)
+        stores.put(packed, 0)
+        stores.wait()
+
+
+def encode_backward(served, landed, g_node, x, block, chunks, flat, bm=512):
+    k, rows = block[0].shape[0], x.shape[1]
+    slots = served.shape[1]
     return pl.pallas_call(
-        functools.partial(encode_back_kernel, bm),
+        functools.partial(encode_back_kernel, len(landed), bm, chunks),
         grid=(rows // bm,),
         out_shape=shaped(*flat.shape),
-        in_specs=[spec((1, slots)), spec((slots, LATENT)), spec((bm, LATENT), False), spec((bm, k), False)] + [spec(a.shape) for a in block] + [ANY],
+        in_specs=[spec((1, slots)), *(spec(p.shape) for p in landed), spec((bm, LATENT), False), pl.BlockSpec((VARS, bm), lambda i: (0, i))] + [spec(a.shape) for a in block] + [ANY],
         out_specs=ANY,
-        scratch_shapes=[packed_rows(VARS, 4)] + mlp_sums(k) + [DMA],
-        input_output_aliases={7: 0},
+        scratch_shapes=[packed_rows(VARS, 4)] + mlp_sums(k) + [DMA((STORES,))],
+        input_output_aliases={6 + len(landed): 0},
         compiler_params=params(),
         name="encode_backward",
-    )(served, landed, g_node, x, *block, flat)
+    )(served, *landed, g_node, x, *block, flat)
 
 
 def relay_plan(segments, share_rows):
@@ -1032,19 +1017,220 @@
     return made
 
 
-def make_asks(edge_owners, edge_local, devices):
-    edges_here = edge_owners.shape[0]
-    capacity = (5 * edges_here // (2 * devices) + 7) // 8 * 8
+def accumulate(dst, src, rows):
+    step = 80
+    whole = rows // step
+    def body(i, carry):
+        at = pl.ds(pl.multiple_of(i * step, 8), step)
+        dst[at] = dst[at] + src[at]
+        return carry
+    lax.fori_loop(0, whole, body, 0)
+    if rows % step:
+        at = pl.ds(whole * step, rows % step)
+        dst[at] = dst[at] + src[at]
+
+
+def where_am_i():
+    me = lax.axis_index("dev")
+    return me, me // 8, lax.rem(me // 4, 2), lax.rem(me // 2, 2), lax.rem(me, 2)
+
+
+def device_at(z, y, x, c):
+    return ((z * 2 + y) * 2 + x) * 2 + c
+
+
+def plane_scratch(units, rows):
+    upper = rows // 16 * 8
+    lower = rows - upper
+    F = lambda *s: pltpu.VMEM((units,) + s + (128,), F32)
+    refs = dict(pL=F(4, rows), pR=F(4, rows), pYA=F(2, upper), pXA=F(upper), pXB=F(2, lower), pYB=F(lower))
+    sems = {}
+    for name, count in (("c", 4), ("a1", 2), ("a2", 1), ("b1", 2), ("b2", 1)):
+        sems["p" + name + "s"] = DMA((units, count))
+        sems["p" + name + "r"] = DMA((units, count))
+    return refs | sems | dict(pl=DMA((units, 4)))
+
+
+class PlaneSum:
+    def __init__(self, r, rows):
+        self.r, self.rows = r, rows
+        self.upper = rows // 16 * 8
+        self.A, self.B = pl.ds(0, self.upper), pl.ds(self.upper, rows - self.upper)
+        _, z, y, x, c = where_am_i()
+        self.y, self.x, self.c = y, x, c
+        self.tx, self.ty, self.tc = device_at(z, y, 1 - x, c), device_at(z, 1 - y, x, c), device_at(z, y, x, 1 - c)
+        self.own = y * 2 + x
+        self.sends = []
+
+    def send(self, *args):
+        copy = remote(*args)
+        copy.start()
+        self.sends.append(copy)
+
+    def fetch(self, u, source):
+        r = self.r
+        self.example = source(0, 0)
+        for i in range(4):
+            self.send(source(i, 1 - self.c), r.pR.at[u, i], r.pcs.at[u, i], r.pcr.at[u, i], self.tc)
+            pltpu.make_async_copy(source(i, self.c), r.pL.at[u, i], r.pl.at[u, i]).start()
+
+    def pair(self, u):
+        r, L = self.r, self.r.pL
+        for i in range(4):
+            pltpu.make_async_copy(self.example, L.at[u, i], r.pl.at[u, i]).wait()
+            remote(L.at[u, i], r.pR.at[u, i], r.pcs.at[u, i], r.pcr.at[u, i], self.tc).wait_recv()
+            accumulate(L.at[u, i], r.pR.at[u, i], self.rows)
+        for j in range(2):
+            self.send(L.at[u, (1 - self.y) * 2 + j, self.A], r.pYA.at[u, j], r.pa1s.at[u, j], r.pa1r.at[u, j], self.ty)
+            self.send(L.at[u, j * 2 + 1 - self.x, self.B], r.pXB.at[u, j], r.pb1s.at[u, j], r.pb1r.at[u, j], self.tx)
+
+    def middle(self, u):
+        r, L = self.r, self.r.pL
+        up, low = self.upper, self.rows - self.upper
+        for j in range(2):
+            remote(L.at[u, 0, self.A], r.pYA.at[u, j], r.pa1s.at[u, j], r.pa1r.at[u, j], self.ty).wait_recv()
+            accumulate(L.at[u, self.y * 2 + j, self.A], r.pYA.at[u, j], up)
+        self.send(L.at[u, self.y * 2 + 1 - self.x, self.A], r.pXA.at[u], r.pa2s.at[u, 0], r.pa2r.at[u, 0], self.tx)
+        for j in range(2):
+            remote(L.at[u, 0, self.B], r.pXB.at[u, j], r.pb1s.at[u, j], r.pb1r.at[u, j], self.tx).wait_recv()
+            accumulate(L.at[u, j * 2 + self.x, self.B], r.pXB.at[u, j], low)
+        self.send(L.at[u, (1 - self.y) * 2 + self.x, self.B], r.pYB.at[u], r.pb2s.at[u, 0], r.pb2r.at[u, 0], self.ty)
+
+    def last(self, u):
+        r, L = self.r, self.r.pL
+        remote(L.at[u, 0, self.A], r.pXA.at[u], r.pa2s.at[u, 0], r.pa2r.at[u, 0], self.tx).wait_recv()
+        accumulate(L.at[u, self.own, self.A], r.pXA.at[u], self.upper)
+        remote(L.at[u, 0, self.B], r.pYB.at[u], r.pb2s.at[u, 0], r.pb2r.at[u, 0], self.ty).wait_recv()
+        accumulate(L.at[u, self.own, self.B], r.pYB.at[u], self.rows - self.upper)
+
+    def result(self, u):
+        return self.r.pL.at[u, self.own]
+
+    def finish(self):
+        for copy in self.sends:
+            copy.wait_send()
+
+
+PARTS = 1
+
+
+def reduce_kernel(n, share_rows, lead, rows, r):
+    me, z, y, x, c = where_am_i()
+    greet(n, me)
+    size = rows // PARTS
+    plane = PlaneSum(r, size)
+    units = [(away, part) for away in (2, 1, 3, 0) for part in range(PARTS)]
+    goal = [lax.rem(z + away, 4) for away, _ in units]
+    rows_of = [pl.ds(part * size, size) for _, part in units]
+
+    def fetch(u):
+        if u < len(units):
+            plane.fetch(u, lambda i, core: r.flat.at[goal[u] * 8 + i * 2 + core, rows_of[u]])
+
+    def along(u):
+        away, part = units[u]
+        at = 3 - away
+        return remote(plane.result(u), r.zq.at[at, rows_of[u]], r.zqs.at[at, part], r.zqr.at[at, part], device_at(goal[u], y, x, c))
+
+    def last(u):
+        plane.last(u)
+        if units[u][0]:
+            along(u).start()
+
+    fetch(0)
+    fetch(1)
+    e_own = pltpu.make_async_copy(r.err, r.errs.at[me], r.own.at[0])
+    e_own.start()
+    def go(j, carry):
+        t = lax.rem(me + j, n)
+        remote(r.err, r.errs.at[me], r.es.at[j], r.er.at[j], t).start()
+        return carry
+    lax.fori_loop(1, n, go, 0)
+    plane.pair(0)
+    plane.middle(0)
+    for u in range(1, len(units)):
+        fetch(u + 1)
+        plane.pair(u)
+        last(u - 1)
+        plane.middle(u)
+    last(len(units) - 1)
+    first = lax.rem(lead + share_rows * me, 8)
+    r.sq[...] = jnp.zeros_like(r.sq)
+
+    def piece(ref, base, at, count):
+        here, there = pl.ds(at, count), pl.ds(base + at, count)
+        v = ref[here] + r.zq[0, there] + (r.zq[1, there] + r.zq[2, there])
+        r.out[there] = v
+        row = base + at + lax.broadcasted_iota(jnp.int32, v.shape, 0)
+        v = jnp.where((row >= first) & (row < first + share_rows), v, 0.0)
+        v = v * v
+        r.sq[...] += jnp.sum(v.reshape(count // 8, 8, 128), axis=0)
+
+    for u in range(len(units) - PARTS, len(units)):
+        part = units[u][1]
+        for at in range(3):
+            remote(plane.result(u), r.zq.at[at, rows_of[u]], r.zqs.at[at, part], r.zqr.at[at, part], plane.tc).wait_recv()
+        step = 80
+        def several(i, carry):
+            piece(plane.result(u), part * size, pl.multiple_of(i * step, 8), step)
+            return carry
+        lax.fori_loop(0, size // step, several, 0)
+        if size % step:
+            piece(plane.result(u), part * size, size // step * step, size % step)
+    q_own = pltpu.make_async_copy(r.sq, r.squares.at[me], r.own.at[1])
+    q_own.start()
+    def go2(j, carry):
+        t = lax.rem(me + j, n)
+        remote(r.sq, r.squares.at[me], r.qs.at[j], r.qr.at[j], t).start()
+        return carry
+    lax.fori_loop(1, n, go2, 0)
+    plane.finish()
+    for u in range(len(units)):
+        if units[u][0]:
+            along(u).wait_send()
+    def end(j, carry):
+        t = lax.rem(me + j, n)
+        remote(r.err, r.errs.at[me], r.es.at[j], r.er.at[j], t).wait()
+        remote(r.sq, r.squares.at[me], r.qs.at[j], r.qr.at[j], t).wait()
+        return carry
+    lax.fori_loop(1, n, end, 0)
+    e_own.wait()
+    q_own.wait()
+
+
+def reduce_gradient(n, flat, err, share_rows, lead, rows, cid):
+    V = pl.BlockSpec(memory_space=pltpu.VMEM)
+    F = lambda *s: pltpu.VMEM(s + (128,), F32)
+    inputs = dict(flat=(flat, ANY), err=(err, V))
+    small = (shaped(n, 8, 128), V)
+    outputs = dict(out=(shaped(rows, 128), V), squares=small, errs=small)
+    scratch = plane_scratch(4 * PARTS, rows // PARTS) | dict(zq=F(3, rows), sq=F(8), zqs=DMA((3, PARTS)), zqr=DMA((3, PARTS)))
+    scratch |= dict(own=DMA((2,)), es=DMA((n,)), er=DMA((n,)), qs=DMA((n,)), qr=DMA((n,)))
+    out = named_call(functools.partial(reduce_kernel, n, share_rows, lead, rows), "reduce_gradient", inputs, outputs, scratch, cid=cid)
+    return out.out, out.squares, out.errs
+
+
+def make_parts(capacity):
+    whole = capacity // 16 * 16
+    rest = (capacity - whole + 3) // 4 * 4
+    return [rows for rows in (whole, rest) if rows]
+
+
+def make_asks(edge_owners, edge_local, devices, parts):
     owner = edge_owners.reshape(-1)
     local = edge_local.reshape(-1)
     wants = owner.shape[0]
     order = jnp.arange(wants, dtype=jnp.int32)
     before = (owner[:, None] == owner[None, :]) & (order[None, :] < order[:, None])
     ranking = jnp.sum(before.astype(jnp.int32), axis=1)
-    position = owner * capacity + ranking
+    capacity = sum(parts)
     slots = jnp.arange(devices * capacity, dtype=jnp.int32)
-    asking = jnp.sum(jnp.where(slots[:, None] == position[None, :], local[None, :] + 1, 0), axis=1) - 1
-    return (position, asking, capacity)
+    place = owner * capacity + ranking
+    asking = jnp.sum(jnp.where(slots[:, None] == place[None, :], local[None, :] + 1, 0), axis=1) - 1
+    position = owner * parts[0] + ranking
+    if len(parts) > 1:
+        position = jnp.where(ranking < parts[0], position, devices * parts[0] + owner * parts[1] + ranking - parts[0])
+    return (position, asking.reshape(devices, capacity))
 
 
 def widen(values, width):
@@ -1073,11 +1259,10 @@
     made = relay(shares, segments, share_rows)
     [(shape, begin, size)] = [(s, o, e) for _, name, s, o, e in segments if name == "w_out" and s[1] != LATENT]
     wide = shape[1]
-    lines = rows_of(begin // 128, -(-(begin + size + wide) // 128)).reshape(-1)
-    made[-1]["w_out"] = widen(lines[:size].reshape(shape), (wide + 127) // 128 * 128)
-    bias = lines[size : size + wide].astype(jnp.float32)
-    made[-1]["vec"] = made[-1]["vec"].at[1, :wide].set(bias)
-    return [(m["w_in"], m["w_out"], m["vec"]) for m in made]
+    first, end = begin // 128, (begin + size) // 128
+    made[-1]["w_out"] = widen(rows_of(first, end).reshape(shape), (wide + 127) // 128 * 128)
+    bias = rows_of(end, end + (wide + 127) // 128).reshape(-1)[:wide, None].astype(jnp.float32)
+    return [(m["w_in"], m["w_out"], m["vec"]) for m in made], bias
 
 
 def local(
@@ -1099,8 +1284,9 @@
     share = master.shape[0]
     mine = devices == 32 and share % 128 == 0
     ocean = (jnp.arange(VARS) < SEA_VARS).astype(jnp.float32)
-    position, asking, capacity = make_asks(edge_owners, edge_local, devices)
-    slots = devices * capacity
+    parts = make_parts(5 * edge_owners.shape[0] // (2 * devices))
+    capacity = sum(parts)
+    position, asking = make_asks(edge_owners, edge_local, devices, parts)
     counted = jnp.sum(level_mask * (1 - land_sea[:, None] * ocean.astype(jnp.int32)[None, :])).astype(jnp.float32)
     if mine:
         share_rows = share // 128
@@ -1109,51 +1295,60 @@
         ask = jnp.pad(asking.reshape(devices, 1, capacity), ((0, 0), (0, 0), (0, 128 - capacity)))
         number = jnp.zeros((8, 128), jnp.float32).at[0, 0].set(counted)
         gathered, served, numbers = gather_weights(low, ask, number, 1)
-        blocks = relaid_blocks(gathered, segments, share_rows)
-        served = served[:, 0, :capacity].reshape(-1)
+        blocks, bias = relaid_blocks(gathered, segments, share_rows)
+        served = served[:, 0, :capacity]
         count = jnp.sum(numbers)
     else:
         full_weights = lax.all_gather(master.astype(jnp.bfloat16), "dev", axis=0, tiled=True)
-        blocks = [make_block(b) for b in unpack(full_weights, segments)]
-        served = lax.all_to_all(asking.reshape(devices, capacity), "dev", 0, 0, tiled=True).reshape(-1)
+        whole = unpack(full_weights, segments)
+        blocks = [make_block(b) for b in whole]
+        bias = whole[-1]["b_out"][:, None].astype(jnp.float32)
+        served = lax.all_to_all(asking, "dev", 0, 0, tiled=True)
         count = lax.psum(counted, "dev")
+    served = jnp.concatenate([served[:, sum(parts[:i]) : sum(parts[: i + 1])].reshape(-1) for i in range(len(parts))])
     want = served[:, None]
     served = served[None, :]
     pos = position.reshape(-1, 2)
     pos_s, pos_r = pos[:, 0][None, :], pos[:, 1][None, :]
-    x = widen(inputs, 256)
+    x = inputs.T
     geo = widen(geometry, 128)
-    land = land_sea[:, None]
+    land = land_sea[None, :]
     routes = (want, served, pos, pos_s, pos_r)
-    done = [edge_forward(devices, 3, geo, routes, blocks[2], blocks[0], inputs.shape[0], x=x, geo_block=blocks[1])]
+    done = [edge_forward(devices, parts, 3, geo, routes, blocks[2], blocks[0], inputs.shape[0], x=x, geo_block=blocks[1])]
     for k in range(1, LAYERS):
         f = done[-1]
         done.append(
             edge_forward(
-                devices, 4, f.edge, routes, blocks[2 + 2 * k], blocks[1 + 2 * k], inputs.shape[0],
-                landed=f.landed, node=f.node, slots=f.slots,
+                devices, parts, 4, f.edge, routes, blocks[2 + 2 * k], blocks[1 + 2 * k], inputs.shape[0],
+                landed=several(f, "landed"), node=f.node, slots=f.slots,
             )
         )
     pieces = [4 * s for s in (VARS + LATENT + 4, GEO + LATENT + 4) + (3 * LATENT + LATENT + 4, 2 * LATENT + LATENT + 4) * LAYERS]
     lead = 4
     places = [0] + [lead + sum(pieces[: i + 1]) for i in range(len(pieces))]
     flat_rows = (lead + PARAMS // 128 + 15) // 16 * 16 + 8
+    if mine:
+        begins = [(lead + share_rows * d) // 8 * 8 for d in range(devices)]
+        chunks = Chunks(begins, (share_rows + 6 + 15) // 16 * 16, [0, 32])
+    else:
+        chunks = Chunks([0], flat_rows, [0, 1])
     dec_at = places[-1]
     tail_at = dec_at + 4 * LATENT
     k = LAYERS - 1
-    flat, g_node, g_slots, outgoing, d_out, d_vec, errors = turn(
-        served, want, done[k].landed.reshape(slots, LATENT), done[k].node, inputs, targets, level_mask, land, count.reshape(1, 1),
-        blocks[3 + 2 * k], blocks[-1], flat_rows, places[3 + 2 * k], dec_at,
+    flat, g_node, *outgoing, d_out, d_first, d_bias, errors = turn(
+        served, want, several(done[k], "landed"), done[k].node, x, targets.T, level_mask.T, land, count.reshape(1, 1),
+        blocks[3 + 2 * k], blocks[-1], bias, chunks, places[3 + 2 * k], dec_at,
     )
+    flats = {len(chunks.cuts) - 2: flat}
     error_here = jnp.sum(errors)
-    tail = jnp.concatenate([d_vec[0], d_out[:, :VARS].reshape(-1), d_vec[1, :VARS]])
+    tail = jnp.concatenate([d_first[0], d_out[:, :VARS].reshape(-1), d_bias[:VARS, 0]])
     tail_rows = flat_rows - tail_at
     tail = jnp.pad(tail, (0, tail_rows * 128 - tail.shape[0])).reshape(tail_rows, 128)
     g_edge, landed = None, None
     for k in reversed(range(LAYERS)):
         more = {}
         if k == LAYERS - 1:
-            more |= dict(outgoing=outgoing, tail=tail, tail_at=tail_at)
+            more |= dict(outgoing=outgoing, g_node=g_node, tail=tail, tail_at=tail_at)
         else:
             more |= dict(
                 node=(landed, g_slots, done[k].slots, done[k + 1].sums_s, g_node, done[k].low, done[k + 1].sums, blocks[3 + 2 * k]),
@@ -1163,23 +1358,23 @@
             more |= dict(geo=(geo, blocks[1]), geo_at=places[1])
         f = done[k]
         b = edge_backward(
-            devices, 5 + (LAYERS - 1 - k), (f.edge_low, f.sent, f.recv), routes, blocks[2 + 2 * k], flat, places[2 + 2 * k],
+            devices, parts, 5 + (LAYERS - 1 - k), (f.edge_low, f.sent, f.recv), routes, blocks[2 + 2 * k], chunks, flats, places[2 + 2 * k],
             g_edge=g_edge, **more,
         )
-        flat, g_edge, landed = b.flat, b.edge_prev, b.landed
+        g_edge, landed = b.edge_prev, several(b, "landed")
+        g_slots = b.g_slots
         if k < LAYERS - 1:
-            g_node, g_slots = b.g_prev, b.g_slots
-    flat = encode_backward(served, landed.reshape(slots, LATENT), g_node, x, blocks[0], flat)
+            g_node = b.g_prev
+    flat = encode_backward(served, landed, g_node, x, blocks[0], chunks, flats[0])
     if mine:
-        rows = (share_rows + 6 + 15) // 16 * 16
         error = jnp.zeros((8, 128), jnp.float32).at[0, 0].set(error_here)
-        summed, squares, errors = reduce_gradient(flat, error, share_rows, lead, rows, 2)
+        summed, squares, errors = reduce_gradient(devices, flat, error, share_rows, lead, chunks.rows, 2)
         skip = lax.rem(lead + share_rows * lax.axis_index("dev"), 8)
         own_grad = lax.dynamic_slice_in_dim(summed, skip, share_rows).reshape(-1)
         grad_norm = jnp.sqrt(jnp.sum(squares))
         error_sum = jnp.sum(errors)
     else:
-        own_grad = lax.psum_scatter(flat[lead : lead + PARAMS // 128].reshape(-1), "dev", scatter_dimension=0, tiled=True)
+        own_grad = lax.psum_scatter(flat[0, lead : lead + PARAMS // 128].reshape(-1), "dev", scatter_dimension=0, tiled=True)
         error_sum, squares = lax.psum((error_here, jnp.sum(own_grad * own_grad)), "dev")
         grad_norm = jnp.sqrt(squares)
     loss = error_sum / jnp.maximum(count, 1.0)

time: 593 us -> 555 us (0.936)
  Pallas kernels: 541 us -> 510 us
  local copies, waits for them, and re-layouts: 24.3 us -> 14.9 us
    pallas_call x3 -> x2, Pallas kernels: 188 us -> 44.9 us  [the longest x1 32.1 us: turn(): pl.pallas_call(functools.partial(turn_kernel, len(landed), bm, chunks, gr...]
    pallas_call x6 -> x7, Pallas kernels: 273 us -> 385 us  [named_call(): pl.pallas_call(kernel, out_shape=tuple((shape for shape, _ in outputs.val...]
    unnamed x29 -> x27, local copies, waits for them, and re-layouts: 7.33 us -> 1.15 us
where the time goes in v4:
time: 555 us; the launch traced here: 545 us
  Pallas kernels  510 us (92%)
  local copies, waits for them, and re-layouts  14.9 us (3%)
  other arithmetic  12.8 us (2%)
  between operations  7.1 us (1%)
    pallas_call x7, Pallas kernels, named_call(): pl.pallas_call(kernel, out_shape=tuple((shape for shape, _ in outputs.val...  385 us
    pallas_call x1, Pallas kernels, gather_weights(): pl.pallas_call(gather_kernel, out_shape=(jax.ShapeDtypeStruct((n, rows, 1...  69.5 us
    pallas_call x1, Pallas kernels, turn(): pl.pallas_call(functools.partial(turn_kernel, len(landed), bm, chunks, gr...  32.1 us
    pallas_call x1, Pallas kernels, encode_backward(): pl.pallas_call(functools.partial(encode_back_kernel, len(landed), bm, chu...  12.8 us

profile of v4, /device:TPU:0, one launch (start us, length us, event | category | flops | bytes accessed | tf_op | source)
XLA Modules:
  0.0 545.2 jit_solution(8600863021753091438)
XLA Ops:
  0.7 0.9 copy.62
  1.6 0.1 reshape.145
  1.8 0.3 convert_reduce_fusion
  2.0 0.7 broadcast_add_fusion.1
  2.7 0.1 copy.63
  2.9 0.1 add.92
  3.0 0.2 select_reduce_fusion
  3.2 0.1 sub.31
  3.3 0.6 pad.32.ask_ref
  4.0 1.2 convert_bitcast_fusion
  5.1 0.8 pad.31.w_ref
  5.9 1.2 multiply_reduce_fusion
  7.8 0.6 scatter.6.num_ref
  8.4 69.5 %shard_map.163 = (bf16[32,1600,128]{2,1,0:T(8,128)(2,1)}, s32[32,1,128]{2,1,0:T(1,128)}, f32[32,8,128]{2,1,0:T(8,128)}) custom-call(bf16[1600,128]{1,0:T(8,128)(2,1)} %pad.31.w_ref, s32[32,1,128]{2,1,0:T(1,128)} %pad.32.ask_ref, f32[8,128]{1,0:T(8,128)} %scatter.6.num_ref), custom_call_target="tpu_custom_call" | custom-call | tf_op jit(solution)/shard_map/pallas_call | solution.py:229
  78.0 10.7 %relay.1 = (bf16[256,512]{1,0:T(8,128)(2,1)}, bf16[512,512]{1,0:T(8,128)(2,1)}, f32[8,512]{1,0:T(8,128)}, bf16[128,512]{1,0:T(8,128)(2,1)}, bf16[512,512]{1,0:T(...) custom-call(bf16[32,1600,128]{2,1,0:T(8,128)(2,1)} %get-tuple-elemen, ...), custom_call_target="tpu_custom_call" | custom-call | tf_op jit(solution)/shard_map/relay/pallas_call | solution.py:1005
  88.8 0.1 reshape.148
  88.9 0.1 reshape.147
  89.0 0.6 broadcast_in_dim.30.refs_2_.served.refs_1_
  89.6 0.9 broadcast_in_dim.33.refs_1_.want.refs_0_
  90.5 0.1 reduce_sum.68
  90.7 0.1 copy.66
  90.8 0.1 copy.67
  91.0 0.8 slice_reduce_fusion
  91.8 0.1 copy.68
  91.9 0.6 pad.33.refs_0_.refs_23_
  92.6 35.2 %edge_forward.3 = (f32[256,512]{1,0:T(8,128)}, bf16[256,512]{1,0:T(8,128)(2,1)}, bf16[256,512]{1,0:T(8,128)(2,1)}, bf16[256,512]{1,0:T(8,128)(2,1)}, bf16[32,16,...) custom-call(bf16[256,128]{1,0:T(8,128)(2,1)} %pad.33.refs_0_.refs_23, ...), custom_call_target="tpu_custom_call" | custom-call | tf_op jit(solution)/shard_map/edge_forward/pallas_call | solution.py:423
  127.7 41.6 %edge_forward.4 = (f32[256,512]{1,0:T(8,128)}, bf16[256,512]{1,0:T(8,128)(2,1)}, bf16[256,512]{1,0:T(8,128)(2,1)}, bf16[256,512]{1,0:T(8,128)(2,1)}, bf16[32,16,...) custom-call(f32[256,512]{1,0:T(8,128)} %get-tuple-element.127.refs_0, ...), custom_call_target="tpu_custom_call" | custom-call | tf_op jit(solution)/shard_map/edge_forward/pallas_call | solution.py:423
  169.4 42.3 %edge_forward.5 = (f32[256,512]{1,0:T(8,128)}, bf16[256,512]{1,0:T(8,128)(2,1)}, bf16[256,512]{1,0:T(8,128)(2,1)}, bf16[256,512]{1,0:T(8,128)(2,1)}, bf16[32,16,...) custom-call(f32[256,512]{1,0:T(8,128)} %get-tuple-element.141.refs_0, ...), custom_call_target="tpu_custom_call" | custom-call | tf_op jit(solution)/shard_map/edge_forward/pallas_call | solution.py:423
  211.7 1.0 slice.67
  212.7 0.7 reshape_squeeze.6
  213.3 0.8 pad.34.refs_12_
  214.1 0.6 slice_bitcast_fusion
  214.7 0.8 copy.73.refs_14_
  215.5 0.6 reduce_sum.69
  216.2 32.1 %turn.1 = (f32[32,1616,128]{2,1,0:T(8,128)}, f32[2048,512]{1,0:T(8,128)}, bf16[32,16,512]{2,1,0:T(8,128)(2,1)}, bf16[32,4,512]{2,1,0:T(4,128)(2,1)}, f32[512,256...) custom-call(s32[1,640]{1,0:T(1,128)} %broadcast_in_dim.30.refs_2_.served.refs_1_, ...), custom_call_target="tpu_custom_call" | custom-call | tf_op jit(solution)/shard_map/turn/pallas_call | solution.py:705
  248.3 1.6 reshape.150
  249.8 1.0 slice_reduce_fusion.2
  250.8 1.6 fusion.3.refs_14_
  252.4 41.6 %edge_backward.3 = (f32[256,512]{1,0:T(8,128)}, bf16[32,16,512]{2,1,0:T(8,128)(2,1)}, bf16[32,4,512]{2,1,0:T(4,128)(2,1)}, f32[640,512]{1,0:T(8,128)}, f32[32,1616,128]{2,1,0:T(8,128)}) custom-call(s32[640,1]{1,0:T(8,128)} %broadcast_in_dim.33.refs_1_.want.refs_0_, ...), custom_call_target="tpu_custom_call", output_to_operand_aliasing={{4}: (15, {})} | custom-call | tf_op jit(solution)/shard_map/edge_backward/pallas_call | solution.py:423
  294.0 45.1 %edge_backward.4 = (f32[256,512]{1,0:T(8,128)}, bf16[32,16,512]{2,1,0:T(8,128)(2,1)}, bf16[32,4,512]{2,1,0:T(4,128)(2,1)}, f32[2048,512]{1,0:T(8,128)}, f32[640,512]{1,0:T(8,128)}, /*index=5*/f32[32,1616,128]{2,1,0:T(8,128)}) custom-call(s32[640,1]{1,0:T(8,128)} %broadcast_in_dim.33.refs_1_.want.refs_0_, ...), custom_call_target="tpu_custom_call", output_to_operand_aliasing={{5}: (23, {})} | custom-call | tf_op jit(solution)/shard_map/edge_backward/pallas_call | solution.py:423
  339.1 44.1 %edge_backward.5 = (f32[256,512]{1,0:T(8,128)}, bf16[32,16,512]{2,1,0:T(8,128)(2,1)}, bf16[32,4,512]{2,1,0:T(4,128)(2,1)}, f32[2048,512]{1,0:T(8,128)}, f32[640,512]{1,0:T(8,128)}, /*index=5*/f32[32,1616,128]{2,1,0:T(8,128)}) custom-call(s32[640,1]{1,0:T(8,128)} %broadcast_in_dim.33.refs_1_.want.refs_0_, ...), custom_call_target="tpu_custom_call", output_to_operand_aliasing={{5}: (27, {})} | custom-call | tf_op jit(solution)/shard_map/edge_backward/pallas_call | solution.py:423
  383.1 12.8 %encode_backward.1.refs_0_ = f32[32,1616,128]{2,1,0:T(8,128)} custom-call(s32[1,640]{1,0:T(1,128)} %broadcast_in_dim.30.refs_2_.served.refs_1_, bf16[32,16,512]{2,1,0:T(8,128)(2,1)} %get-tuple-element.188.refs_0_, bf16[32,4,512]{2,1,0:T(4,128)(2,1)} %get-tuple-element.189.refs_1_, ...), custom_call_target="tpu_custom_call", output_to_operand_aliasing={{}: (8, {})} | custom-call | tf_op jit(solution)/shard_map/encode_backward/pallas_call | solution.py:910
  396.0 0.6 reduce_sum.70
  396.6 1.2 scatter.9.refs_1_
  397.8 135.4 %reduce_gradient.1 = (f32[1616,128]{1,0:T(8,128)}, f32[32,8,128]{2,1,0:T(8,128)}, f32[32,8,128]{2,1,0:T(8,128)}) custom-call(f32[32,1616,128]{2,1,0:T(8,128)} %encode_backward.1.refs_0_, f32[8,128]{1,0:T(8,128)} %scatter.9.refs_1_), custom_call_target="tpu_custom_call" | custom-call | tf_op jit(solution)/shard_map/reduce_gradient/pallas_call | solution.py:423
  533.2 1.5 reduce_sum.72
  536.1 1.5 reduce_sum.71
  539.2 3.4 multiply_add_fusion
  (34 shorter events, 0.2 us)
Async XLA Ops:
  0.6 5.3 copy-start.8
  0.6 5.3 copy-start.1
  77.9 10.8 %copy-start.7 = (s32[32,1,128]{2,1,0:T(1,128)S(1)}, s32[32,1,128]{2,1,0:T(1,128)}, u32[]{:S(2)}) copy-start(s32[32,1,128]{2,1,0:T(1,128)} %get-tuple-element.113) | copy-start | bytes 49156
  78.0 12.7 %copy-start.9 = (s32[256,2]{0,1:T(2,128)S(1)}, s32[256,2]{0,1:T(2,128)}, u32[]{:S(2)}) copy-start(s32[256,2]{0,1:T(2,128)} %param.21) | copy-start | bytes 6148
  78.0 13.8 %copy-start.10 = (bf16[256,4]{0,1:T(4,128)(2,1)S(1)}, bf16[256,4]{0,1:T(4,128)(2,1)}, u32[]{:S(2)}) copy-start(bf16[256,4]{0,1:T(4,128)(2,1)} %param.18) | copy-start | bytes 6148
  91.0 1.6 copy-start
  169.4 46.1 %copy-start.6 = (f32[32,8,128]{2,1,0:T(8,128)S(1)}, f32[32,8,128]{2,1,0:T(8,128)}, u32[]{:S(2)}) copy-start(f32[32,8,128]{2,1,0:T(8,128)} %get-tuple-element.158) | copy-start | bytes 393220
  383.1 12.8 %copy-start.11 = (f32[1,512]{1,0:T(1,128)S(1)}, f32[1,512]{1,0:T(1,128)}, u32[]{:S(2)}) copy-start(f32[1,512]{1,0:T(1,128)} %get-tuple-element.192) | copy-start | bytes 6148
  397.8 141.3 %copy-start.2 = (f32[204544]{0:T(1024)S(1)}, f32[204544]{0:T(1024)}, u32[]{:S(2)}) copy-start(f32[204544]{0:T(1024)} %param.24) | copy-start | bytes 2454532
  397.8 141.3 %copy-start.3 = (f32[204544]{0:T(1024)S(1)}, f32[204544]{0:T(1024)}, u32[]{:S(2)}) copy-start(f32[204544]{0:T(1024)} %param.27) | copy-start | bytes 2454532
  397.8 141.3 %copy-start.4 = (f32[204544]{0:T(1024)S(1)}, f32[204544]{0:T(1024)}, u32[]{:S(2)}) copy-start(f32[204544]{0:T(1024)} %param.26) | copy-start | bytes 2454532
  397.8 141.3 %copy-start.5 = (f32[204544]{0:T(1024)S(1)}, f32[204544]{0:T(1024)}, u32[]{:S(2)}) copy-start(f32[204544]{0:T(1024)} %param.25) | copy-start | bytes 2454532

commit v5 on v4

--- a/solution.py
+++ b/solution.py
@@ -880,6 +880,22 @@
     return made
 
 
+def encode_back_rows(first, bm, served, landed, g_node, x, w_in, w_out, vec, d_in, d_out, d_vec):
+    pre = contract(x[...], w_in[:VARS, :], 0, 0) + vec[0:1, :]
+    sigma, act = activate(pre)
+    hat, inv = second_half(act, w_out, vec)
+    g = g_node[...] + mm(place(served[...], first, bm), slot_rows(landed))
+    g_post = norm_back(g, hat, inv, vec, d_vec)
+    g_pre = act_back(g_post, pre, sigma, w_out)
+    weight_sums([], act, g_post, g_pre, d_in, d_out, d_vec)
+    d_in[:VARS, :] += mm(x[...], g_pre)
+
+
+def encode_pack(packed, d_in, d_out, d_vec):
+    packed[0:4, :] = jnp.zeros((4, 128), F32)
+    pack(packed, 4, VARS, d_in, d_out, d_vec)
+
+
 def encode_back_kernel(parts, bm, chunks, served, *refs):
     landed, refs = refs[:parts], refs[parts:]
     g_node, x, w_in, w_out, vec, flat_in, flat, packed, d_in, d_out, d_vec, sem = refs
@@ -887,18 +903,10 @@
     @pl.when(i == 0)
     def _():
         clear(d_in, d_out, d_vec)
-    pre = contract(x[...], w_in[:VARS, :], 0, 0) + vec[0:1, :]
-    sigma, act = activate(pre)
-    hat, inv = second_half(act, w_out, vec)
-    g = g_node[...] + mm(place(served[...], i * bm, bm), slot_rows(landed))
-    g_post = norm_back(g, hat, inv, vec, d_vec)
-    g_pre = act_back(g_post, pre, sigma, w_out)
-    weight_sums([], act, g_post, g_pre, d_in, d_out, d_vec)
-    d_in[:VARS, :] += mm(x[...], g_pre)
+    encode_back_rows(i * bm, bm, served, landed, g_node, x, w_in, w_out, vec, d_in, d_out, d_vec)
     @pl.when(i == pl.num_programs(0) - 1)
     def _():
-        packed[0:4, :] = jnp.zeros((4, 128), F32)
-        pack(packed, 4, VARS, d_in, d_out, d_vec)
+        encode_pack(packed, d_in, d_out, d_vec)
         stores = Stores({0: flat}, chunks, sem)
         stores.put(packed, 0)
         stores.wait()
@@ -1111,103 +1119,101 @@
             copy.wait_send()
 
 
-PARTS = 1
-
-
-def reduce_kernel(n, share_rows, lead, rows, r):
+def reduce_kernel(n, chunks, share_rows, lead, bm, r):
     me, z, y, x, c = where_am_i()
     greet(n, me)
-    size = rows // PARTS
-    plane = PlaneSum(r, size)
-    units = [(away, part) for away in (2, 1, 3, 0) for part in range(PARTS)]
-    goal = [lax.rem(z + away, 4) for away, _ in units]
-    rows_of = [pl.ds(part * size, size) for _, part in units]
+    rows = chunks.rows
+    plane = PlaneSum(r, rows)
+    def by_plane(*goals):
+        return jnp.where(z == 0, goals[0], jnp.where(z == 1, goals[1], jnp.where(z == 2, goals[2], goals[3])))
+    goal = [by_plane(2, 3, 3, 1), by_plane(1, 2, 0, 0), by_plane(3, 0, 1, 2), z]
 
     def fetch(u):
-        if u < len(units):
-            plane.fetch(u, lambda i, core: r.flat.at[goal[u] * 8 + i * 2 + core, rows_of[u]])
+        if u < 4:
+            plane.fetch(u, lambda i, core: r.flat0.at[goal[u] * 8 + i * 2 + core])
 
     def along(u):
-        away, part = units[u]
-        at = 3 - away
-        return remote(plane.result(u), r.zq.at[at, rows_of[u]], r.zqs.at[at, part], r.zqr.at[at, part], device_at(goal[u], y, x, c))
-
-    def last(u):
-        plane.last(u)
-        if units[u][0]:
-            along(u).start()
+        at = lax.rem(z - goal[u] + 4, 4) - 1
+        return remote(plane.result(u), r.zq.at[at], r.zqs.at[u], r.zqr.at[at], device_at(goal[u], y, x, c))
 
     fetch(0)
+    clear(r.d_in, r.d_out, r.d_vec)
+    plane.pair(0)
+    def body(g_node, x_rows):
+        encode_back_rows(pl.program_id(0) * bm, bm, r.served, several(r, "landed"), g_node, x_rows, r.p_in, r.p_out, r.p_vec, r.d_in, r.d_out, r.d_vec)
+    pltpu.emit_pipeline(body, grid=(r.g_node.shape[0] // bm,), in_specs=[rows_block(bm), pl.BlockSpec((VARS, bm), lambda i: (0, i))], out_specs=[])(r.g_node, r.x)
+    encode_pack(r.packed, r.d_in, r.d_out, r.d_vec)
+    stores = Stores({0: r.flat0}, chunks, r.fsem)
+    stores.put(r.packed, 0)
+    stores.wait()
     fetch(1)
-    e_own = pltpu.make_async_copy(r.err, r.errs.at[me], r.own.at[0])
-    e_own.start()
+    plane.middle(0)
+    for u in (1, 2, 3):
+        fetch(u + 1)
+        plane.pair(u)
+        plane.last(u - 1)
+        along(u - 1).start()
+        plane.middle(u)
+    plane.last(3)
+    first = lax.rem(lead + share_rows * me, 8)
+    r.both[0:8, :] = jnp.zeros((8, 128), F32)
+    width = r.err.shape[1] // 128
+    for j in range(8):
+        r.both[8 + j : 9 + j, :] = r.err[:, 128 * j : 128 * (j + 1)] if j < width else jnp.zeros((1, 128), F32)
+    own = plane.result(3)
+
+    def piece(at, count):
+        rows_here = pl.ds(at, count)
+        v = own[rows_here] + r.zq[0, rows_here] + (r.zq[1, rows_here] + r.zq[2, rows_here])
+        r.out[rows_here] = v
+        row = at + lax.broadcasted_iota(jnp.int32, v.shape, 0)
+        v = jnp.where((row >= first) & (row < first + share_rows), v, 0.0)
+        v = v * v
+        r.both[0:8, :] += jnp.sum(v.reshape(count // 8, 8, 128), axis=0)
+
+    for at in range(3):
+        remote(own, r.zq.at[at], r.zqs.at[at], r.zqr.at[at], plane.tc).wait_recv()
+    step = 80
+    def several_tiles(i, carry):
+        piece(pl.multiple_of(i * step, 8), step)
+        return carry
+    lax.fori_loop(0, rows // step, several_tiles, 0)
+    if rows % step:
+        piece(rows // step * step, rows % step)
+    q_own = pltpu.make_async_copy(r.both, r.all.at[me], r.own)
+    q_own.start()
     def go(j, carry):
         t = lax.rem(me + j, n)
-        remote(r.err, r.errs.at[me], r.es.at[j], r.er.at[j], t).start()
+        remote(r.both, r.all.at[me], r.qs.at[j], r.qr.at[j], t).start()
         return carry
     lax.fori_loop(1, n, go, 0)
-    plane.pair(0)
-    plane.middle(0)
-    for u in range(1, len(units)):
-        fetch(u + 1)
-        plane.pair(u)
-        last(u - 1)
-        plane.middle(u)
-    last(len(units) - 1)
-    first = lax.rem(lead + share_rows * me, 8)
-    r.sq[...] = jnp.zeros_like(r.sq)
-
-    def piece(ref, base, at, count):
-        here, there = pl.ds(at, count), pl.ds(base + at, count)
-        v = ref[here] + r.zq[0, there] + (r.zq[1, there] + r.zq[2, there])
-        r.out[there] = v
-        row = base + at + lax.broadcasted_iota(jnp.int32, v.shape, 0)
-        v = jnp.where((row >= first) & (row < first + share_rows), v, 0.0)
-        v = v * v
-        r.sq[...] += jnp.sum(v.reshape(count // 8, 8, 128), axis=0)
-
-    for u in range(len(units) - PARTS, len(units)):
-        part = units[u][1]
-        for at in range(3):
-            remote(plane.result(u), r.zq.at[at, rows_of[u]], r.zqs.at[at, part], r.zqr.at[at, part], plane.tc).wait_recv()
-        step = 80
-        def several(i, carry):
-            piece(plane.result(u), part * size, pl.multiple_of(i * step, 8), step)
-            return carry
-        lax.fori_loop(0, size // step, several, 0)
-        if size % step:
-            piece(plane.result(u), part * size, size // step * step, size % step)
-    q_own = pltpu.make_async_copy(r.sq, r.squares.at[me], r.own.at[1])
-    q_own.start()
-    def go2(j, carry):
-        t = lax.rem(me + j, n)
-        remote(r.sq, r.squares.at[me], r.qs.at[j], r.qr.at[j], t).start()
-        return carry
-    lax.fori_loop(1, n, go2, 0)
     plane.finish()
-    for u in range(len(units)):
-        if units[u][0]:
-            along(u).wait_send()
+    for u in range(3):
+        along(u).wait_send()
     def end(j, carry):
         t = lax.rem(me + j, n)
-        remote(r.err, r.errs.at[me], r.es.at[j], r.er.at[j], t).wait()
-        remote(r.sq, r.squares.at[me], r.qs.at[j], r.qr.at[j], t).wait()
+        remote(r.both, r.all.at[me], r.qs.at[j], r.qr.at[j], t).wait()
         return carry
     lax.fori_loop(1, n, end, 0)
-    e_own.wait()
     q_own.wait()
-
-
-def reduce_gradient(n, flat, err, share_rows, lead, rows, cid):
+    r.sums[...] = jnp.sum(r.all[...], axis=0)
+
+
+def reduce_gradient(n, chunks, flat, errors, share_rows, lead, encoder, cid, bm=512):
+    served, landed, g_node, x, block = encoder
     V = pl.BlockSpec(memory_space=pltpu.VMEM)
     F = lambda *s: pltpu.VMEM(s + (128,), F32)
-    inputs = dict(flat=(flat, ANY), err=(err, V))
-    small = (shaped(n, 8, 128), V)
-    outputs = dict(out=(shaped(rows, 128), V), squares=small, errs=small)
-    scratch = plane_scratch(4 * PARTS, rows // PARTS) | dict(zq=F(3, rows), sq=F(8), zqs=DMA((3, PARTS)), zqr=DMA((3, PARTS)))
-    scratch |= dict(own=DMA((2,)), es=DMA((n,)), er=DMA((n,)), qs=DMA((n,)), qr=DMA((n,)))
-    out = named_call(functools.partial(reduce_kernel, n, share_rows, lead, rows), "reduce_gradient", inputs, outputs, scratch, cid=cid)
-    return out.out, out.squares, out.errs
+    rows = chunks.rows
+    inputs = dict(flat_in=(flat, ANY), err=(errors, V), served=(served, V), g_node=(g_node, ANY), x=(x, ANY))
+    inputs |= numbered("landed", [(v, V) for v in landed])
+    inputs |= {name: (v, V) for name, v in zip(("p_in", "p_out", "p_vec"), block)}
+    outputs = dict(flat0=(shaped(*flat.shape), ANY), out=(shaped(rows, 128), V), sums=(shaped(16, 128), V))
+    scratch = plane_scratch(4, rows) | dict(zq=F(3, rows), zqs=DMA((3,)), zqr=DMA((3,)))
+    scratch |= dict(both=F(16), all=F(n, 16), own=DMA, qs=DMA((n,)), qr=DMA((n,)), packed=packed_rows(VARS, 4), fsem=DMA((STORES,)))
+    scratch |= sums_scratch("d", block[0].shape[0])
+    body = functools.partial(reduce_kernel, n, chunks, share_rows, lead, bm)
+    made = named_call(body, "reduce_gradient", inputs, outputs, scratch, aliases=dict(flat_in="flat0"), cid=cid)
+    return made.out, jnp.sum(made.sums[:8]), jnp.sum(made.sums[8:])
 
 
 def make_parts(capacity):
@@ -1340,7 +1346,6 @@
         blocks[3 + 2 * k], blocks[-1], bias, chunks, places[3 + 2 * k], dec_at,
     )
     flats = {len(chunks.cuts) - 2: flat}
-    error_here = jnp.sum(errors)
     tail = jnp.concatenate([d_first[0], d_out[:, :VARS].reshape(-1), d_bias[:VARS, 0]])
     tail_rows = flat_rows - tail_at
     tail = jnp.pad(tail, (0, tail_rows * 128 - tail.shape[0])).reshape(tail_rows, 128)
@@ -1365,18 +1370,16 @@
         g_slots = b.g_slots
         if k < LAYERS - 1:
             g_node = b.g_prev
-    flat = encode_backward(served, landed, g_node, x, blocks[0], chunks, flats[0])
     if mine:
-        error = jnp.zeros((8, 128), jnp.float32).at[0, 0].set(error_here)
-        summed, squares, errors = reduce_gradient(devices, flat, error, share_rows, lead, chunks.rows, 2)
+        encoder = (served, landed, g_node, x, blocks[0])
+        summed, squares, error_sum = reduce_gradient(devices, chunks, flats[0], errors, share_rows, lead, encoder, 2)
         skip = lax.rem(lead + share_rows * lax.axis_index("dev"), 8)
         own_grad = lax.dynamic_slice_in_dim(summed, skip, share_rows).reshape(-1)
-        grad_norm = jnp.sqrt(jnp.sum(squares))
-        error_sum = jnp.sum(errors)
     else:
+        flat = encode_backward(served, landed, g_node, x, blocks[0], chunks, flats[0])
         own_grad = lax.psum_scatter(flat[0, lead : lead + PARAMS // 128].reshape(-1), "dev", scatter_dimension=0, tiled=True)
-        error_sum, squares = lax.psum((error_here, jnp.sum(own_grad * own_grad)), "dev")
-        grad_norm = jnp.sqrt(squares)
+        error_sum, squares = lax.psum((jnp.sum(errors), jnp.sum(own_grad * own_grad)), "dev")
+    grad_norm = jnp.sqrt(squares)
     loss = error_sum / jnp.maximum(count, 1.0)
     clipped = own_grad * jnp.minimum(1.0, clip_limit / grad_norm)
     step = step_count[0].astype(jnp.float32)

time: 555 us -> 541 us (0.975)
  the two profiles are of different devices: /device:TPU:0 before, /device:TPU:27 now
where the time goes in v5:
time: 541 us; the launch traced here: 531 us
  Pallas kernels  500 us (92%)
  local copies, waits for them, and re-layouts  13.7 us (3%)
  other arithmetic  10.4 us (2%)
  between operations  7.09 us (1%)
    pallas_call x7, Pallas kernels, named_call(): pl.pallas_call(kernel, out_shape=tuple((shape for shape, _ in outputs.val...  391 us
    pallas_call x1, Pallas kernels, gather_weights(): pl.pallas_call(gather_kernel, out_shape=(jax.ShapeDtypeStruct((n, rows, 1...  66 us
    pallas_call x1, Pallas kernels, turn(): pl.pallas_call(functools.partial(turn_kernel, len(landed), bm, chunks, gr...  32.1 us

profile of v5, /device:TPU:27, one launch (start us, length us, event | category | flops | bytes accessed | tf_op | source)
XLA Modules:
  0.0 530.7 jit_solution(7523889285073329987)
XLA Ops:
  0.6 0.0 copy-start.8
  0.7 0.9 copy.62
  1.6 0.1 reshape.120
  1.8 0.3 convert_reduce_fusion
  2.0 0.7 broadcast_add_fusion.1
  2.7 0.1 copy.63
  2.9 0.1 add.88
  3.0 0.2 select_reduce_fusion
  3.2 0.1 sub.31
  3.3 0.6 pad.27.ask_ref
  4.0 1.2 convert_bitcast_fusion
  5.1 0.8 pad.26.w_ref
  5.9 1.2 multiply_reduce_fusion
  7.8 0.6 scatter.4.num_ref
  8.4 66.0 %shard_map.163 = (bf16[32,1600,128]{2,1,0:T(8,128)(2,1)}, s32[32,1,128]{2,1,0:T(1,128)}, f32[32,8,128]{2,1,0:T(8,128)}) custom-call(bf16[1600,128]{1,0:T(8,128)(2,1)} %pad.26.w_ref, s32[32,1,128]{2,1,0:T(1,128)} %pad.27.ask_ref, f32[8,128]{1,0:T(8,128)} %scatter.4.num_ref), custom_call_target="tpu_custom_call" | custom-call | tf_op jit(solution)/shard_map/pallas_call | solution.py:229
  74.4 0.0 copy-start.10
  74.4 10.7 %relay.1 = (bf16[256,512]{1,0:T(8,128)(2,1)}, bf16[512,512]{1,0:T(8,128)(2,1)}, f32[8,512]{1,0:T(8,128)}, bf16[128,512]{1,0:T(8,128)(2,1)}, bf16[512,512]{1,0:T(...) custom-call(bf16[32,1600,128]{2,1,0:T(8,128)(2,1)} %get-tuple-elemen, ...), custom_call_target="tpu_custom_call" | custom-call | tf_op jit(solution)/shard_map/relay/pallas_call | solution.py:1013
  85.2 0.1 slice.65
  85.3 0.1 reshape.123
  85.4 0.1 reshape.122
  85.5 0.6 broadcast_in_dim.32.refs_2_.served.refs_1_
  86.1 0.9 broadcast_in_dim.34.refs_1_.want.refs_0_
  87.0 0.1 reduce_sum.59
  87.1 0.1 copy.66
  87.3 0.1 copy.67
  87.5 0.8 slice_reduce_fusion
  88.2 0.1 copy.68
  88.4 0.6 pad.28.refs_0_.refs_23_
  89.0 42.2 %edge_forward.3 = (f32[256,512]{1,0:T(8,128)}, bf16[256,512]{1,0:T(8,128)(2,1)}, bf16[256,512]{1,0:T(8,128)(2,1)}, bf16[256,512]{1,0:T(8,128)(2,1)}, bf16[32,16,...) custom-call(bf16[256,128]{1,0:T(8,128)(2,1)} %pad.28.refs_0_.refs_23, ...), custom_call_target="tpu_custom_call" | custom-call | tf_op jit(solution)/shard_map/edge_forward/pallas_call | solution.py:423
  131.3 41.9 %edge_forward.4 = (f32[256,512]{1,0:T(8,128)}, bf16[256,512]{1,0:T(8,128)(2,1)}, bf16[256,512]{1,0:T(8,128)(2,1)}, bf16[256,512]{1,0:T(8,128)(2,1)}, bf16[32,16,...) custom-call(f32[256,512]{1,0:T(8,128)} %get-tuple-element.114.refs_0, ...), custom_call_target="tpu_custom_call" | custom-call | tf_op jit(solution)/shard_map/edge_forward/pallas_call | solution.py:423
  173.2 42.3 %edge_forward.5 = (f32[256,512]{1,0:T(8,128)}, bf16[256,512]{1,0:T(8,128)(2,1)}, bf16[256,512]{1,0:T(8,128)(2,1)}, bf16[256,512]{1,0:T(8,128)(2,1)}, bf16[32,16,...) custom-call(f32[256,512]{1,0:T(8,128)} %get-tuple-element.128.refs_0, ...), custom_call_target="tpu_custom_call" | custom-call | tf_op jit(solution)/shard_map/edge_forward/pallas_call | solution.py:423
  215.4 1.0 slice.57
  216.4 0.7 reshape_squeeze.6
  217.1 0.8 pad.29.refs_12_
  217.9 0.6 slice_bitcast_fusion
  218.5 0.8 copy.73.refs_14_
  219.3 0.6 reduce_sum.60
  219.9 32.1 %turn.1 = (f32[32,1616,128]{2,1,0:T(8,128)}, f32[2048,512]{1,0:T(8,128)}, bf16[32,16,512]{2,1,0:T(8,128)(2,1)}, bf16[32,4,512]{2,1,0:T(4,128)(2,1)}, f32[512,256...) custom-call(s32[1,640]{1,0:T(1,128)} %broadcast_in_dim.32.refs_2_.served.refs_1_, ...), custom_call_target="tpu_custom_call" | custom-call | tf_op jit(solution)/shard_map/turn/pallas_call | solution.py:705
  252.0 1.6 reshape.125
  253.6 1.0 slice_reduce_fusion.2
  254.6 1.6 fusion.3.refs_14_
  256.2 42.4 %edge_backward.3 = (f32[256,512]{1,0:T(8,128)}, bf16[32,16,512]{2,1,0:T(8,128)(2,1)}, bf16[32,4,512]{2,1,0:T(4,128)(2,1)}, f32[640,512]{1,0:T(8,128)}, f32[32,1616,128]{2,1,0:T(8,128)}) custom-call(s32[640,1]{1,0:T(8,128)} %broadcast_in_dim.34.refs_1_.want.refs_0_, ...), custom_call_target="tpu_custom_call", output_to_operand_aliasing={{4}: (15, {})} | custom-call | tf_op jit(solution)/shard_map/edge_backward/pallas_call | solution.py:423
  298.6 42.5 %edge_backward.4 = (f32[256,512]{1,0:T(8,128)}, bf16[32,16,512]{2,1,0:T(8,128)(2,1)}, bf16[32,4,512]{2,1,0:T(4,128)(2,1)}, f32[2048,512]{1,0:T(8,128)}, f32[640,512]{1,0:T(8,128)}, /*index=5*/f32[32,1616,128]{2,1,0:T(8,128)}) custom-call(s32[640,1]{1,0:T(8,128)} %broadcast_in_dim.34.refs_1_.want.refs_0_, ...), custom_call_target="tpu_custom_call", output_to_operand_aliasing={{5}: (23, {})} | custom-call | tf_op jit(solution)/shard_map/edge_backward/pallas_call | solution.py:423
  341.1 43.6 %edge_backward.5 = (f32[256,512]{1,0:T(8,128)}, bf16[32,16,512]{2,1,0:T(8,128)(2,1)}, bf16[32,4,512]{2,1,0:T(4,128)(2,1)}, f32[2048,512]{1,0:T(8,128)}, f32[640,512]{1,0:T(8,128)}, /*index=5*/f32[32,1616,128]{2,1,0:T(8,128)}) custom-call(s32[640,1]{1,0:T(8,128)} %broadcast_in_dim.34.refs_1_.want.refs_0_, ...), custom_call_target="tpu_custom_call", output_to_operand_aliasing={{5}: (27, {})} | custom-call | tf_op jit(solution)/shard_map/edge_backward/pallas_call | solution.py:423
  384.8 0.0 copy-start.2
  384.8 135.7 %reduce_gradient.1 = (f32[32,1616,128]{2,1,0:T(8,128)}, f32[1616,128]{1,0:T(8,128)}, f32[16,128]{1,0:T(8,128)}) custom-call(f32[32,1616,128]{2,1,0:T(8,128)} %get-tuple-element.175.refs_0_, f32[1,512]{1,0:T(1,128)} %get-tuple-element.176.refs_1_, s32[1,640]{1,0:T(1,128)} %broadcast_in_dim.32.refs_2_.served.refs_1_, ...), custom_call_target="tpu_custom_call", output_to_operand_aliasing={{0}: (0, {})} | custom-call | tf_op jit(solution)/shard_map/reduce_gradient/pallas_call | solution.py:423
  520.6 1.3 slice_reduce_fusion.3
  524.7 3.4 multiply_add_fusion
  (28 shorter events, 0.1 us)
Async XLA Ops:
  0.6 5.3 copy-start.8
  0.6 5.3 copy-start.1
  74.4 10.8 %copy-start.7 = (s32[32,1,128]{2,1,0:T(1,128)S(1)}, s32[32,1,128]{2,1,0:T(1,128)}, u32[]{:S(2)}) copy-start(s32[32,1,128]{2,1,0:T(1,128)} %get-tuple-element.100) | copy-start | bytes 49156
  74.4 12.7 %copy-start.9 = (s32[256,2]{0,1:T(2,128)S(1)}, s32[256,2]{0,1:T(2,128)}, u32[]{:S(2)}) copy-start(s32[256,2]{0,1:T(2,128)} %param.19) | copy-start | bytes 6148
  74.4 13.8 %copy-start.10 = (bf16[256,4]{0,1:T(4,128)(2,1)S(1)}, bf16[256,4]{0,1:T(4,128)(2,1)}, u32[]{:S(2)}) copy-start(bf16[256,4]{0,1:T(4,128)(2,1)} %param.16) | copy-start | bytes 6148
  87.4 1.6 copy-start
  173.1 46.1 %copy-start.6 = (f32[32,8,128]{2,1,0:T(8,128)S(1)}, f32[32,8,128]{2,1,0:T(8,128)}, u32[]{:S(2)}) copy-start(f32[32,8,128]{2,1,0:T(8,128)} %get-tuple-element.145) | copy-start | bytes 393220
  384.8 139.9 %copy-start.2 = (f32[204544]{0:T(1024)S(1)}, f32[204544]{0:T(1024)}, u32[]{:S(2)}) copy-start(f32[204544]{0:T(1024)} %param.22) | copy-start | bytes 2454532
  384.8 139.9 %copy-start.3 = (f32[204544]{0:T(1024)S(1)}, f32[204544]{0:T(1024)}, u32[]{:S(2)}) copy-start(f32[204544]{0:T(1024)} %param.25) | copy-start | bytes 2454532
  384.8 139.9 %copy-start.4 = (f32[204544]{0:T(1024)S(1)}, f32[204544]{0:T(1024)}, u32[]{:S(2)}) copy-start(f32[204544]{0:T(1024)} %param.24) | copy-start | bytes 2454532
  384.8 139.9 %copy-start.5 = (f32[204544]{0:T(1024)S(1)}, f32[204544]{0:T(1024)}, u32[]{:S(2)}) copy-start(f32[204544]{0:T(1024)} %param.23) | copy-start | bytes 2454532

commit v6 on v5

--- a/solution.py
+++ b/solution.py
@@ -70,169 +70,6 @@
         return c
     lax.fori_loop(1, n, hello, 0)
     pl.semaphore_wait(barrier, n - 1)
-
-def a2a_kernel(n, a_ref, o_ref, own, ssem, rsem):
-    me = lax.axis_index('dev')
-    greet(n, me)
-    here = pltpu.make_async_copy(a_ref.at[me], o_ref.at[me], own)
-    here.start()
-    def go(j, c):
-        t = lax.rem(me + j, n)
-        remote(a_ref.at[t], o_ref.at[me], ssem.at[j], rsem.at[j], t).start()
-        return c
-    lax.fori_loop(1, n, go, 0)
-    def end(j, c):
-        t = lax.rem(me + j, n)
-        remote(a_ref.at[t], o_ref.at[me], ssem.at[j], rsem.at[j], t).wait()
-        return c
-    lax.fori_loop(1, n, end, 0)
-    here.wait()
-
-def a2a(x, cid, space=pl.ANY):
-    n = x.shape[0]
-    return pl.pallas_call(
-        functools.partial(a2a_kernel, n),
-        out_shape=jax.ShapeDtypeStruct(x.shape, x.dtype),
-        in_specs=[pl.BlockSpec(memory_space=space)],
-        out_specs=pl.BlockSpec(memory_space=space),
-        scratch_shapes=[pltpu.SemaphoreType.DMA, pltpu.SemaphoreType.DMA((n,)), pltpu.SemaphoreType.DMA((n,))],
-        compiler_params=pltpu.CompilerParams(collective_id=cid, has_side_effects=True),
-    )(x)
-
-def gather_kernel(w_ref, ask_ref, num_ref, o_ref, served_ref, nums_ref, own, small_s, small_r, zs, zr, hs, hr, cs, cr, ds, dr, bs, br):
-    n = 32
-    me = lax.axis_index('dev')
-    c, x, y, z = lax.rem(me, 2), lax.rem(me // 2, 2), lax.rem(me // 4, 2), me // 8
-    rows = w_ref.shape[0]
-    half = rows // 2
-    A, B = pl.ds(0, half), pl.ds(half, half)
-    def dev(z, y, x, c):
-        return ((z * 2 + y) * 2 + x) * 2 + c
-    greet(n, me)
-    tx, ty, tc = dev(z, y, 1 - x, c), dev(z, 1 - y, x, c), dev(z, y, x, 1 - c)
-    up, down = dev(lax.rem(z + 1, 4), y, x, c), dev(lax.rem(z + 3, 4), y, x, c)
-    pend = []
-    def start(cp):
-        cp.start(); pend.append(cp)
-    mine = pltpu.make_async_copy(w_ref, o_ref.at[me], own.at[0])
-    mine.start()
-    planes = [z, z + 1 - 2 * lax.rem(z, 2), 2 - z // 2, 3 - 3 * (z // 2)]
-    def on_up(i, wait):
-        src = w_ref if i == 0 else o_ref.at[dev(planes[i], y, x, c)]
-        slot = dev(planes[i], y, x, c)
-        @pl.when((planes[i] <= z) & (z < 3))
-        def _():
-            cp = remote(src, o_ref.at[slot], zs.at[0, i], zr.at[planes[i]], up)
-            cp.wait_send() if wait else cp.start()
-    def on_down(i, wait):
-        src = w_ref if i == 0 else o_ref.at[dev(planes[i], y, x, c)]
-        slot = dev(planes[i], y, x, c)
-        @pl.when((planes[i] >= z) & (z > 0))
-        def _():
-            cp = remote(src, o_ref.at[slot], zs.at[1, i], zr.at[planes[i]], down)
-            cp.wait_send() if wait else cp.start()
-    start(remote(w_ref.at[A], o_ref.at[me, A], hs.at[0, 0], hr.at[0, 0], tx))
-    start(remote(w_ref.at[B], o_ref.at[me, B], hs.at[0, 1], hr.at[0, 1], ty))
-    on_up(0, False)
-    on_down(0, False)
-    start(remote(w_ref, o_ref.at[me], bs.at[0], br.at[0], tc))
-    mine2 = pltpu.make_async_copy(ask_ref.at[me], served_ref.at[me], own.at[1])
-    mine2.start()
-    mine3 = pltpu.make_async_copy(num_ref, nums_ref.at[me], own.at[2])
-    mine3.start()
-    def go(j, carry):
-        t = lax.rem(me + j, n)
-        remote(ask_ref.at[t], served_ref.at[me], small_s.at[0, j], small_r.at[0, j], t).start()
-        remote(num_ref, nums_ref.at[me], small_s.at[1, j], small_r.at[1, j], t).start()
-        return carry
-    lax.fori_loop(1, n, go, 0)
-    nb = [1]
-    def sib(slot, part):
-        i = nb[0]; nb[0] += 1
-        ref = o_ref.at[slot] if part is None else o_ref.at[slot, part]
-        start(remote(ref, ref, bs.at[i], br.at[i], tc))
-    def first(k):
-        s = dev(planes[k], y, x, c)
-        remote(w_ref, o_ref.at[s], zs.at[0, k], zr.at[planes[k]], tc).wait_recv()
-        start(remote(o_ref.at[s, A], o_ref.at[s, A], hs.at[k, 0], hr.at[k, 0], tx))
-        start(remote(o_ref.at[s, B], o_ref.at[s, B], hs.at[k, 1], hr.at[k, 1], ty))
-        on_up(k, False)
-        on_down(k, False)
-        sib(s, None)
-    def second(k):
-        zz = planes[k]
-        s = dev(zz, y, x, c)
-        sx, sy = dev(zz, y, 1 - x, c), dev(zz, 1 - y, x, c)
-        own_a = w_ref.at[A] if k == 0 else o_ref.at[s, A]
-        own_b = w_ref.at[B] if k == 0 else o_ref.at[s, B]
-        start(remote(own_a, o_ref.at[s, A], cs.at[k, 0], cr.at[k, 0], ty))
-        start(remote(own_b, o_ref.at[s, B], ds.at[k, 0], dr.at[k, 0], tx))
-        remote(own_a, o_ref.at[sx, A], hs.at[k, 0], hr.at[k, 0], tx).wait_recv()
-        start(remote(o_ref.at[sx, A], o_ref.at[sx, A], cs.at[k, 1], cr.at[k, 1], ty))
-        remote(own_b, o_ref.at[sy, B], hs.at[k, 1], hr.at[k, 1], ty).wait_recv()
-        start(remote(o_ref.at[sy, B], o_ref.at[sy, B], ds.at[k, 1], dr.at[k, 1], tx))
-        sib(sx, A)
-        sib(sy, B)
-    def third(k):
-        zz = planes[k]
-        sx, sy, sd = dev(zz, y, 1 - x, c), dev(zz, 1 - y, x, c), dev(zz, 1 - y, 1 - x, c)
-        w = w_ref.at[A]
-        remote(w, o_ref.at[sy, A], cs.at[k, 0], cr.at[k, 0], ty).wait_recv()
-        sib(sy, A)
-        remote(w, o_ref.at[sx, B], ds.at[k, 0], dr.at[k, 0], tx).wait_recv()
-        sib(sx, B)
-        remote(w, o_ref.at[sd, A], cs.at[k, 1], cr.at[k, 1], ty).wait_recv()
-        sib(sd, A)
-        remote(w, o_ref.at[sd, B], ds.at[k, 1], dr.at[k, 1], tx).wait_recv()
-        sib(sd, B)
-    second(0)
-    first(1)
-    third(0)
-    second(1)
-    first(2)
-    third(1)
-    second(2)
-    first(3)
-    third(2)
-    second(3)
-    third(3)
-    nb2 = [0]
-    def got(*parts):
-        for part in parts:
-            i = nb2[0]; nb2[0] += 1
-            ref = w_ref if part is None else w_ref.at[part]
-            o = o_ref.at[me] if part is None else o_ref.at[me, part]
-            remote(ref, o, bs.at[i], br.at[i], tc).wait_recv()
-    g1, g2, g3 = (None,), (A, B), (A, B, A, B)
-    for g in (g1, g2, g1, g3, g2, g1, g3, g2, g1, g3, g2, g3):
-        got(*g)
-    def end(j, carry):
-        t = lax.rem(me + j, n)
-        remote(ask_ref.at[t], served_ref.at[me], small_s.at[0, j], small_r.at[0, j], t).wait()
-        remote(num_ref, nums_ref.at[me], small_s.at[1, j], small_r.at[1, j], t).wait()
-        return carry
-    lax.fori_loop(1, n, end, 0)
-    for i in range(4):
-        on_up(i, True)
-        on_down(i, True)
-    for cp in pend:
-        cp.wait_send()
-    mine.wait(); mine2.wait(); mine3.wait()
-
-
-def gather_weights(w, ask, num, cid):
-    n = 32
-    rows = w.shape[0]
-    D = pltpu.SemaphoreType.DMA
-    sib = 1 + 4 * 2 + 3 + 4 * 4
-    anyspec = pl.BlockSpec(memory_space=pl.ANY)
-    return pl.pallas_call(
-        gather_kernel,
-        out_shape=(jax.ShapeDtypeStruct((n, rows, 128), w.dtype), jax.ShapeDtypeStruct(ask.shape, ask.dtype), jax.ShapeDtypeStruct((n,) + num.shape, num.dtype)),
-        in_specs=[anyspec] * 3, out_specs=(anyspec,) * 3,
-        scratch_shapes=[D((3,)), D((2, n)), D((2, n)), D((2, 4)), D((4,)), D((4, 2)), D((4, 2)), D((4, 2)), D((4, 2)), D((4, 2)), D((4, 2)), D((sib,)), D((sib,))],
-        compiler_params=pltpu.CompilerParams(collective_id=cid, has_side_effects=True),
-    )(w, ask, num)
 
 
 F32, BF16 = jnp.float32, jnp.bfloat16
@@ -953,76 +790,297 @@
     return jobs
 
 
-def relay_kernel(jobs, shapes, shares, *rest):
-    count = sum(len(s) for s in shapes)
-    outs = rest[:count]
-    stage, lines, made, vecs, isem, osem, vsem = rest[count:]
-    index = {}
-    for b, s in enumerate(shapes):
-        for name, _ in s:
-            index[b, name] = len(index)
-    loads, at = [], 0
-    for number, (b, name, first, rows, follow, parts) in enumerate(jobs):
-        mine = []
-        for owner, base, span, skip, to in parts:
-            copy = pltpu.make_async_copy(shares.at[owner, pl.ds(base, span)], stage.at[pl.ds(at, span)], isem.at[len(loads) * 0 + number * 4 + len(mine)])
+class Relay:
+    def __init__(self, r, shares):
+        self.r, self.shares, self.loads, self.at, self.count = r, shares, {}, 0, 0
+
+    def load(self, job):
+        r, mine = self.r, []
+        for owner, base, span, skip, to in job[5]:
+            place = pl.ds(self.at, span)
+            copy = pltpu.make_async_copy(self.shares.at[owner, pl.ds(base, span)], r.stage.at[place], r.isem.at[self.count])
             copy.start()
-            mine.append((copy, at, span, skip, to))
-            at += span
-        loads.append(mine)
-    vecs[...] = jnp.zeros_like(vecs)
-    stores = []
-    for number, ((b, name, first, rows, follow, parts), mine) in enumerate(zip(jobs, loads)):
-        for copy, where, span, skip, to in mine:
+            mine.append((copy, place, span, skip, to))
+            self.at += span
+            self.count += 1
+        self.loads[job[:3]] = mine
+
+    def run(self, job, target, vec):
+        _, name, _, rows, follow, _ = job
+        lines = self.r.lines
+        for copy, place, span, skip, to in self.loads[job[:3]]:
             copy.wait()
-            lines[pl.ds(16 + to - skip, span), :] = stage[pl.ds(where, span), :].astype(F32)
-        full = (rows + 15) // 16 * 16
+            lines[pl.ds(16 + to - skip, span), :] = self.r.stage[place, :].astype(F32)
         for j in range(4):
-            made[number, :rows, 128 * j : 128 * (j + 1)] = lines[pl.ds(16 + j, rows, stride=4), :].astype(BF16)
-        if rows < LATENT:
-            made[number, rows:, :] = jnp.zeros((LATENT - rows, LATENT), BF16)
+            target[:rows, 128 * j : 128 * (j + 1)] = lines[pl.ds(16 + j, rows, stride=4), :].astype(BF16)
+        if rows < target.shape[0]:
+            target[rows:, :] = jnp.zeros((target.shape[0] - rows, LATENT), BF16)
         for i in range(follow):
             row = i if name == "w_in" else i + 1
             for j in range(4):
                 p = 16 + 4 * (rows + i) + j
-                vecs[b, row : row + 1, 128 * j : 128 * (j + 1)] = lines[p : p + 1, :]
-        out = outs[index[b, name]]
-        size = min(LATENT, out.shape[0] - first)
-        store = pltpu.make_async_copy(made.at[number, pl.ds(0, size)], out.at[pl.ds(first, size)], osem.at[number])
-        store.start()
-        stores.append(store)
-    for b in range(len(shapes)):
-        store = pltpu.make_async_copy(vecs.at[b], outs[index[b, "vec"]], vsem.at[b])
-        store.start()
-        stores.append(store)
+                vec[row : row + 1, 128 * j : 128 * (j + 1)] = lines[p : p + 1, :]
+
+
+class Gather:
+    def __init__(self, r, w, o):
+        self.r, self.w, self.o = r, w, o
+        self.me, z, y, x, c = where_am_i()
+        self.z = z
+        half = w.shape[0] // 2
+        self.A, self.B = pl.ds(0, half), pl.ds(half, half)
+        self.dev = lambda zz, fy=0, fx=0: device_at(zz, y + fy * (1 - 2 * y), x + fx * (1 - 2 * x), c)
+        self.tx, self.ty, self.tc = self.dev(z, 0, 1), self.dev(z, 1, 0), device_at(z, y, x, 1 - c)
+        self.up, self.down = self.dev(jnp.minimum(z + 1, 3)), self.dev(jnp.maximum(z - 1, 0))
+        def by_plane(*v):
+            return jnp.where(z == 0, v[0], jnp.where(z == 1, v[1], jnp.where(z == 2, v[2], v[3])))
+        self.come = [z, by_plane(1, 0, 1, 2), by_plane(2, 2, 3, 1), by_plane(3, 3, 0, 0)]
+        self.go = [z, by_plane(1, 0, 1, 2), by_plane(2, 2, 0, 0), by_plane(3, 3, 3, 1)]
+        self.sends, self.sibling, self.seen = [], [], 0
+
+    def send(self, *args):
+        copy = remote(*args)
+        copy.start()
+        self.sends.append(copy)
+
+    def share(self, k, part=None):
+        ref = self.w if k == 0 else self.o.at[self.dev(self.go[k])]
+        return ref if part is None else ref.at[part]
+
+    def to_sibling(self, slot, part=None, source=None):
+        r, i = self.r, len(self.sibling)
+        ref = self.o.at[slot] if part is None else self.o.at[slot, part]
+        self.send(ref if source is None else source, ref, r.bs.at[i], r.br.at[i], self.tc)
+        self.sibling.append(part)
+
+    def from_sibling(self, count):
+        r = self.r
+        for i in range(self.seen, count):
+            part = self.sibling[i]
+            ref = self.o.at[self.me] if part is None else self.o.at[self.me, part]
+            remote(ref, ref, r.bs.at[i], r.br.at[i], self.tc).wait_recv()
+        self.seen = count
+
+    def onward(self, i, wait=False):
+        r, z, plane = self.r, self.z, self.come[i]
+        slot = self.dev(plane)
+        source = self.w if i == 0 else self.o.at[slot]
+        for d, target, here in ((0, self.up, (plane <= z) & (z < 3)), (1, self.down, (plane >= z) & (z > 0))):
+            @pl.when(here)
+            def _():
+                copy = remote(source, self.o.at[slot], r.zs.at[d, i], r.zr.at[plane], target)
+                if wait:
+                    copy.wait_send()
+                else:
+                    copy.start()
+
+    def begin(self):
+        r = self.r
+        self.mine = pltpu.make_async_copy(self.w, self.o.at[self.me], r.gown.at[0])
+        self.mine.start()
+        self.spread(0)
+        self.onward(0)
+        self.to_sibling(self.me, None, self.w)
+
+    def arrive(self, i):
+        slot = self.dev(self.come[i])
+        remote(self.w, self.o.at[slot], self.r.zs.at[0, i], self.r.zr.at[self.come[i]], self.tc).wait_recv()
+        self.onward(i)
+        self.to_sibling(slot)
+
+    def spread(self, k):
+        r, slot = self.r, self.dev(self.go[k])
+        self.send(self.share(k, self.A), self.o.at[slot, self.A], r.hs.at[k, 0], r.hr.at[k, 0], self.tx)
+        self.send(self.share(k, self.B), self.o.at[slot, self.B], r.hs.at[k, 1], r.hr.at[k, 1], self.ty)
+
+    def second(self, k):
+        r, o, zz = self.r, self.o, self.go[k]
+        s, sx, sy = self.dev(zz), self.dev(zz, 0, 1), self.dev(zz, 1, 0)
+        self.send(self.share(k, self.A), o.at[s, self.A], r.cs.at[k, 0], r.cr.at[k, 0], self.ty)
+        self.send(self.share(k, self.B), o.at[s, self.B], r.ds.at[k, 0], r.dr.at[k, 0], self.tx)
+        remote(o.at[sx, self.A], o.at[sx, self.A], r.hs.at[k, 0], r.hr.at[k, 0], self.tx).wait_recv()
+        self.send(o.at[sx, self.A], o.at[sx, self.A], r.cs.at[k, 1], r.cr.at[k, 1], self.ty)
+        remote(o.at[sy, self.B], o.at[sy, self.B], r.hs.at[k, 1], r.hr.at[k, 1], self.ty).wait_recv()
+        self.send(o.at[sy, self.B], o.at[sy, self.B], r.ds.at[k, 1], r.dr.at[k, 1], self.tx)
+        self.to_sibling(sx, self.A)
+        self.to_sibling(sy, self.B)
+
+    def third(self, k):
+        r, o, zz = self.r, self.o, self.go[k]
+        for slot, part, ss, rr, i, target in (
+            (self.dev(zz, 1, 0), self.A, r.cs, r.cr, 0, self.ty),
+            (self.dev(zz, 0, 1), self.B, r.ds, r.dr, 0, self.tx),
+            (self.dev(zz, 1, 1), self.A, r.cs, r.cr, 1, self.ty),
+            (self.dev(zz, 1, 1), self.B, r.ds, r.dr, 1, self.tx),
+        ):
+            remote(o.at[slot, part], o.at[slot, part], ss.at[k, i], rr.at[k, i], target).wait_recv()
+            self.to_sibling(slot, part)
+
+    def finish(self):
+        for i in range(4):
+            self.onward(i, True)
+        for copy in self.sends:
+            copy.wait_send()
+
+
+def start_kernel(n, jobs, bm, r):
+    me = lax.axis_index("dev")
+    gather = Gather(r, r.w, r.shares)
+    greet(n, me)
+    gather.begin()
+    asks, asked = several(r, "ask"), several(r, "asked")
+    swap_start(n, me, asks, asked, r.aown, r.a1, r.b1)
+    number = pltpu.make_async_copy(r.number, r.numbers.at[me], r.gown.at[1])
+    number.start()
+    def go(j, carry):
+        t = lax.rem(me + j, n)
+        remote(r.number, r.numbers.at[me], r.ns.at[j], r.nr.at[j], t).start()
+        return carry
+    lax.fori_loop(1, n, go, 0)
+    gather.second(0)
+    gather.arrive(1)
+    gather.spread(1)
+    gather.third(0)
+    gather.second(1)
+    gather.arrive(2)
+    gather.arrive(3)
+    gather.spread(2)
+    gather.third(1)
+    gather.second(2)
+    swap_wait(n, me, asks, asked, r.aown, r.a1, r.b1)
+    columns = slot_rows(asked)
+    r.want[...] = columns[:, 0:1]
+    r.served[...] = jnp.transpose(columns)[0:1, :]
+    chosen = pick(r.want[...], 0, r.x.shape[1])
+    rows = contract(chosen, r.x[...], 1, 1).astype(BF16)
+    gather.spread(3)
+    gather.third(2)
+    plane_0 = len(gather.sibling)
+    gather.second(3)
+    gather.from_sibling(plane_0)
+    gather.mine.wait()
+    relay = Relay(r, r.shares)
+    block = [[job for job in jobs if job[0] == b] for b in range(jobs[-1][0] + 1)]
+    names = ["p", "g", "e"]
+    def into(b):
+        for job in block[b]:
+            target = getattr(r, "_" + names[b] + job[1][1:])
+            relay.run(job, target.at[pl.ds(job[2], min(LATENT, target.shape[0] - job[2]))], getattr(r, "_" + names[b] + "_vec"))
+    for vec in (r._p_vec, r._g_vec, r._e_vec, r.vecs):
+        vec[...] = jnp.zeros_like(vec)
+    for job in block[0]:
+        relay.load(job)
+    into(0)
+    for job in block[1]:
+        relay.load(job)
+    _, act = activate(contract(rows, r._p_in[:VARS, :], 1, 0) + r._p_vec[0:1, :])
+    hat, _ = second_half(act, r._p_out, r._p_vec)
+    r._slots[...] = scale_shift(hat, r._p_vec)
+    away, here, back, out = (several(r, name) for name in ("away", "here", "back", "landed"))
+    put_slot_rows(away, r._slots[...].astype(BF16))
+    swap_start(n, me, away, here, r.own.at[0], r.s1, r.r1)
+    stores = store_all(r, r.ssem, "slots")
+    def body(node, low):
+        i = pl.program_id(0)
+        u = r.x[:, pl.ds(pl.multiple_of(i * bm, bm), bm)]
+        _, act = activate(contract(u, r._p_in[:VARS, :], 0, 0) + r._p_vec[0:1, :])
+        hat, _ = second_half(act, r._p_out, r._p_vec)
+        new = scale_shift(hat, r._p_vec)
+        node[...] = new
+        low[...] = new.astype(BF16)
+    pltpu.emit_pipeline(body, grid=(r.node.shape[0] // bm,), in_specs=[], out_specs=[rows_block(bm)] * 2)(r.node, r.low)
+    gather.third(3)
+    gather.from_sibling(len(gather.sibling))
+    for b in range(2, len(block)):
+        for job in block[b]:
+            relay.load(job)
+    into(1)
+    into(2)
+    _, act = activate(first_half([r.source[...]], r._g_in, r._g_vec))
+    hat, _ = second_half(act, r._g_out, r._g_vec)
+    r._edge[...] = scale_shift(hat, r._g_vec)
+    e = r._edge[...].astype(BF16)
+    r.edge_low[...] = e
+    count = r.want.shape[0]
+    pre = first_half([e], r._e_in, r._e_vec)
+    pick_s, pick_r = pick(r.pos[:, 0:1], 0, count), pick(r.pos[:, 1:2], 0, count)
+    put_r = place(r.pos_r[...], 0, count)
+    kept = [f"m{b}{part}" for b in range(3) for part in ("_in", "_out", "_vec")]
+    for i, name in enumerate(kept):
+        b, part = int(name[1]), name[2:]
+        copy = pltpu.make_async_copy(getattr(r, "_" + names[b] + part), getattr(r, name), r.osem.at[i])
+        copy.start()
+        stores.append(copy)
+    swap_wait(n, me, away, here, r.own.at[0], r.s1, r.r1)
+    rows = slot_rows(here)
+    s = mm(pick_s, rows).astype(BF16)
+    v = mm(pick_r, rows).astype(BF16)
+    pre = pre + mm(s, r._e_in[LATENT : 2 * LATENT, :]) + mm(v, r._e_in[2 * LATENT :, :])
+    _, act = activate(pre)
+    hat, _ = second_half(act, r._e_out, r._e_vec)
+    new = r._edge[...] + scale_shift(hat, r._e_vec)
+    put_slot_rows(back, mm(put_r, new.astype(BF16)).astype(BF16))
+    swap_start(n, me, back, out, r.own.at[1], r.s2, r.r2)
+    r.edge[...] = new
+    r.sent[...], r.recv[...] = s, v
+    at = len(kept)
+    late = [job for b in range(3, len(block)) for job in block[b]]
+    for i, job in enumerate(late):
+        b, name, first = job[:3]
+        relay.run(job, r.made.at[i], r.vecs.at[b])
+        copy = pltpu.make_async_copy(r.made.at[i], getattr(r, f"m{b}{name[1:]}").at[pl.ds(first, LATENT)], r.osem.at[at + i])
+        copy.start()
+        stores.append(copy)
+    at += len(late)
+    for b in range(3, len(block)):
+        copy = pltpu.make_async_copy(r.vecs.at[b], getattr(r, f"m{b}_vec"), r.osem.at[at + b])
+        copy.start()
+        stores.append(copy)
+    gather.finish()
+    def end(j, carry):
+        t = lax.rem(me + j, n)
+        remote(r.number, r.numbers.at[me], r.ns.at[j], r.nr.at[j], t).wait()
+        return carry
+    lax.fori_loop(1, n, end, 0)
+    number.wait()
     for store in stores:
         store.wait()
-
-
-def relay(shares, segments, share_rows):
+    swap_wait(n, me, back, out, r.own.at[1], r.s2, r.r2)
+
+
+def start(n, parts, cid, w, number, asks, source, pos, pos_r, x, segments, share_rows, bm=512):
     jobs = relay_plan(segments, share_rows)
     blocks = segments[-1][0] + 1
-    shapes = [[] for _ in range(blocks)]
+    count, edges, rows = n * sum(parts), source.shape[0], x.shape[1]
+    V = pl.BlockSpec(memory_space=pltpu.VMEM)
+    tables = [(n, p, 128) for p in parts]
+    shapes = [(n, p, LATENT) for p in parts]
+    inputs = dict(w=(w, ANY), number=(number, V), source=(source, V), pos=(pos, V), pos_r=(pos_r, V), x=(x, V)) | numbered("ask", [(a, V) for a in asks])
+    low = lambda r: shaped(r, LATENT, dtype=BF16)
+    outputs = dict(shares=(shaped(n, *w.shape, dtype=BF16), ANY), numbers=(shaped(n, *number.shape), ANY))
+    outputs |= dict(want=(shaped(count, 1, dtype=jnp.int32), V), served=(shaped(1, count, dtype=jnp.int32), V))
+    outputs |= dict(edge=(shaped(edges, LATENT), V), edge_low=(low(edges), V), sent=(low(edges), V), recv=(low(edges), V))
+    outputs |= numbered("landed", [(shaped(*s, dtype=BF16), ANY) for s in shapes])
+    outputs |= dict(node=(shaped(rows, LATENT), ANY), low=(low(rows), ANY), slots=(shaped(count, LATENT), ANY))
+    made = {}
     for b, name, shape, _, _ in segments:
         if name in ("w_in", "w_out") and shape[1] == LATENT:
-            shapes[b].append((name, (-(-shape[0] // 128) * 128, LATENT)))
-    for s in shapes:
-        s.append(("vec", (8, LATENT)))
-    stage = sum(span for job in jobs for _, _, span, _, _ in job[5])
-    out_shape = [shaped(*shape, dtype=F32 if name == "vec" else BF16) for s in shapes for name, shape in s]
-    outs = pl.pallas_call(
-        functools.partial(relay_kernel, jobs, shapes),
-        out_shape=out_shape,
-        in_specs=[ANY],
-        out_specs=[ANY] * len(out_shape),
-        scratch_shapes=[pltpu.VMEM((stage, 128), BF16), pltpu.VMEM((16 + 4 * LATENT + 64, 128), F32), pltpu.VMEM((len(jobs), LATENT, LATENT), BF16), pltpu.VMEM((blocks, 8, LATENT), F32), DMA((4 * len(jobs),)), DMA((len(jobs),)), DMA((blocks,))],
-        compiler_params=params(),
-        name="relay",
-    )(shares)
-    made = [{} for _ in shapes]
-    for (b, name), value in zip([(b, name) for b, s in enumerate(shapes) for name, _ in s], outs):
-        made[b][name] = value
-    return made
+            made[f"m{b}{name[1:]}"] = (-(-shape[0] // 128) * 128, LATENT)
+    outputs |= {name: (shaped(*shape, dtype=BF16), ANY) for name, shape in made.items()}
+    outputs |= {f"m{b}_vec": (shaped(8, LATENT), ANY) for b in range(blocks)}
+    scratch = swap_scratch(shapes, n) | numbered("asked", [pltpu.VMEM(s, jnp.int32) for s in tables])
+    scratch |= dict(aown=DMA((len(parts),)), a1=DMA((len(parts), n)), b1=DMA((len(parts), n)), ns=DMA((n,)), nr=DMA((n,)), gown=DMA((2,)))
+    for b, name in enumerate(("_p", "_g", "_e")):
+        scratch |= {name + "_in": pltpu.VMEM(made[f"m{b}_in"], BF16), name + "_out": pltpu.VMEM(made[f"m{b}_out"], BF16), name + "_vec": pltpu.VMEM((8, LATENT), F32)}
+    stage = sum(part[2] for job in jobs for part in job[5])
+    late = sum(1 for job in jobs if job[0] > 2)
+    scratch |= dict(_slots=pltpu.VMEM((count, LATENT), F32), _edge=pltpu.VMEM((edges, LATENT), F32), ssem=DMA((1,)))
+    scratch |= dict(stage=pltpu.VMEM((stage, 128), BF16), lines=pltpu.VMEM((16 + 4 * LATENT + 64, 128), F32), made=pltpu.VMEM((late, LATENT, LATENT), BF16))
+    scratch |= dict(vecs=pltpu.VMEM((blocks, 8, LATENT), F32), isem=DMA((sum(len(job[5]) for job in jobs),)), osem=DMA((9 + late + blocks,)))
+    scratch |= dict(zs=DMA((2, 4)), zr=DMA((4,)), bs=DMA((28,)), br=DMA((28,)))
+    for name in ("h", "c", "d"):
+        scratch |= {name + "s": DMA((4, 2)), name + "r": DMA((4, 2))}
+    return named_call(functools.partial(start_kernel, n, jobs, bm), "start", inputs, outputs, scratch, cid=cid)
 
 
 def accumulate(dst, src, rows):
@@ -1253,7 +1311,8 @@
     return (w_in, w_out, jnp.concatenate(vectors).astype(jnp.float32))
 
 
-def relaid_blocks(shares, segments, share_rows):
+def relaid_blocks(made, segments, share_rows):
+    shares = made.shares
     def rows_of(first, last):
         parts = []
         while first < last:
@@ -1262,13 +1321,16 @@
             parts.append(shares[owner, low : low + size])
             first += size
         return jnp.concatenate(parts) if len(parts) > 1 else parts[0]
-    made = relay(shares, segments, share_rows)
     [(shape, begin, size)] = [(s, o, e) for _, name, s, o, e in segments if name == "w_out" and s[1] != LATENT]
     wide = shape[1]
     first, end = begin // 128, (begin + size) // 128
-    made[-1]["w_out"] = widen(rows_of(first, end).reshape(shape), (wide + 127) // 128 * 128)
+    w_out = widen(rows_of(first, end).reshape(shape), (wide + 127) // 128 * 128)
     bias = rows_of(end, end + (wide + 127) // 128).reshape(-1)[:wide, None].astype(jnp.float32)
-    return [(m["w_in"], m["w_out"], m["vec"]) for m in made], bias
+    blocks = []
+    for b in range(segments[-1][0] + 1):
+        get = lambda part: getattr(made, f"m{b}{part}", w_out)
+        blocks.append((get("_in"), get("_out"), get("_vec")))
+    return blocks, bias
 
 
 def local(
@@ -1294,16 +1356,21 @@
     capacity = sum(parts)
     position, asking = make_asks(edge_owners, edge_local, devices, parts)
     counted = jnp.sum(level_mask * (1 - land_sea[:, None] * ocean.astype(jnp.int32)[None, :])).astype(jnp.float32)
+    pos = position.reshape(-1, 2)
+    pos_s, pos_r = pos[:, 0][None, :], pos[:, 1][None, :]
+    x = inputs.T
+    geo = widen(geometry, 128)
     if mine:
         share_rows = share // 128
         pad_rows = (share_rows + 31) // 32 * 32
         low = jnp.pad(master.astype(jnp.bfloat16).reshape(share_rows, 128), ((0, pad_rows - share_rows), (0, 0)))
-        ask = jnp.pad(asking.reshape(devices, 1, capacity), ((0, 0), (0, 0), (0, 128 - capacity)))
         number = jnp.zeros((8, 128), jnp.float32).at[0, 0].set(counted)
-        gathered, served, numbers = gather_weights(low, ask, number, 1)
-        blocks, bias = relaid_blocks(gathered, segments, share_rows)
-        served = served[:, 0, :capacity]
-        count = jnp.sum(numbers)
+        cuts = [sum(parts[:i]) for i in range(len(parts) + 1)]
+        asks = [jnp.broadcast_to(asking[:, a:b, None], (devices, b - a, 128)) for a, b in zip(cuts, cuts[1:])]
+        begun = start(devices, parts, 1, low, number, asks, geo, pos, pos_r, x, segments, share_rows)
+        blocks, bias = relaid_blocks(begun, segments, share_rows)
+        want, served = begun.want, begun.served
+        count = jnp.sum(begun.numbers)
     else:
         full_weights = lax.all_gather(master.astype(jnp.bfloat16), "dev", axis=0, tiled=True)
         whole = unpack(full_weights, segments)
@@ -1311,16 +1378,15 @@
         bias = whole[-1]["b_out"][:, None].astype(jnp.float32)
         served = lax.all_to_all(asking, "dev", 0, 0, tiled=True)
         count = lax.psum(counted, "dev")
-    served = jnp.concatenate([served[:, sum(parts[:i]) : sum(parts[: i + 1])].reshape(-1) for i in range(len(parts))])
-    want = served[:, None]
-    served = served[None, :]
-    pos = position.reshape(-1, 2)
-    pos_s, pos_r = pos[:, 0][None, :], pos[:, 1][None, :]
-    x = inputs.T
-    geo = widen(geometry, 128)
+        served = jnp.concatenate([served[:, sum(parts[:i]) : sum(parts[: i + 1])].reshape(-1) for i in range(len(parts))])
+        want = served[:, None]
+        served = served[None, :]
     land = land_sea[None, :]
     routes = (want, served, pos, pos_s, pos_r)
-    done = [edge_forward(devices, parts, 3, geo, routes, blocks[2], blocks[0], inputs.shape[0], x=x, geo_block=blocks[1])]
+    if mine:
+        done = [begun]
+    else:
+        done = [edge_forward(devices, parts, 3, geo, routes, blocks[2], blocks[0], inputs.shape[0], x=x, geo_block=blocks[1])]
     for k in range(1, LAYERS):
         f = done[-1]
         done.append(

time: 541 us -> 530 us (0.980)
  Pallas kernels: 500 us -> 490 us
    pallas_call x2 -> x0, Pallas kernels: 76.8 us -> none  [the longest x1 66 us: gather_weights(): pl.pallas_call(gather_kernel, out_shape=(jax.ShapeDtypeStruct((n, rows, 1...]
    pallas_call x7, Pallas kernels: 391 us -> 458 us  [named_call(): pl.pallas_call(kernel, out_shape=tuple((shape for shape, _ in outputs.val...]
where the time goes in v6:
time: 530 us; the launch traced here: 520 us
  Pallas kernels  490 us (92%)
  local copies, waits for them, and re-layouts  12.8 us (2%)
  other arithmetic  9.92 us (2%)
  between operations  6.76 us (1%)
    pallas_call x7, Pallas kernels, named_call(): pl.pallas_call(kernel, out_shape=tuple((shape for shape, _ in outputs.val...  458 us
    pallas_call x1, Pallas kernels, turn(): pl.pallas_call(functools.partial(turn_kernel, len(landed), bm, chunks, gr...  32.2 us

profile of v6, /device:TPU:27, one launch (start us, length us, event | category | flops | bytes accessed | tf_op | source)
XLA Modules:
  0.0 519.7 jit_solution(9335232890828822289)
XLA Ops:
  0.6 0.0 copy-start.8
  0.6 0.0 copy-start.2
  0.7 0.9 copy.47
  1.5 0.1 eq.28
  1.7 0.3 convert_reduce_fusion
  1.9 0.1 reduce_sum.58
  2.1 0.7 broadcast_multiply_fusion
  2.8 0.1 copy.49
  2.9 0.1 copy.50
  3.1 0.0 copy-start.1
  3.1 0.0 copy-start.7
  3.1 0.0 copy-start
  3.1 0.7 slice_reduce_fusion
  3.9 0.7 broadcast_add_fusion.1
  4.6 0.1 copy.51
  4.7 0.1 add.84
  4.9 0.2 select_reduce_fusion
  5.1 0.1 sub.34
  5.2 0.8 broadcast_in_dim.20.refs_6_
  6.0 0.1 slice.62
  6.1 0.7 broadcast_in_dim.21.refs_7_
  6.8 0.1 copy.46
  7.0 0.6 pad.23.refs_2_.refs_23_
  7.7 0.8 pad.22.refs_0_
  8.5 1.2 multiply_reduce_fusion
  10.3 0.6 scatter.4.refs_1_
  10.9 107.8 %start.1 = (bf16[32,1600,128]{2,1,0:T(8,128)(2,1)}, f32[32,8,128]{2,1,0:T(8,128)}, s32[640,1]{1,0:T(8,128)}, s32[1,640]{1,0:T(1,128)}, f32[256,512]{1,0:T(8,128)...) custom-call(bf16[1600,128]{1,0:T(8,128)(2,1)} %pad.22.refs_0_, ...), custom_call_target="tpu_custom_call" | custom-call | tf_op jit(solution)/shard_map/start/pallas_call | solution.py:260
  118.7 44.2 %edge_forward.2 = (f32[256,512]{1,0:T(8,128)}, bf16[256,512]{1,0:T(8,128)(2,1)}, bf16[256,512]{1,0:T(8,128)(2,1)}, bf16[256,512]{1,0:T(8,128)(2,1)}, bf16[32,16,...) custom-call(f32[256,512]{1,0:T(8,128)} %get-tuple-element.109.refs_0, ...), custom_call_target="tpu_custom_call" | custom-call | tf_op jit(solution)/shard_map/edge_forward/pallas_call | solution.py:260
  162.9 41.7 %edge_forward.3 = (f32[256,512]{1,0:T(8,128)}, bf16[256,512]{1,0:T(8,128)(2,1)}, bf16[256,512]{1,0:T(8,128)(2,1)}, bf16[256,512]{1,0:T(8,128)(2,1)}, bf16[32,16,...) custom-call(f32[256,512]{1,0:T(8,128)} %get-tuple-element.123.refs_0, ...), custom_call_target="tpu_custom_call" | custom-call | tf_op jit(solution)/shard_map/edge_forward/pallas_call | solution.py:260
  204.7 1.0 slice.53
  205.7 0.7 reshape_squeeze.6
  206.4 0.7 pad.24.refs_12_
  207.1 0.6 slice_bitcast_fusion
  207.7 0.8 copy.52.refs_14_
  208.5 0.6 reduce_sum.60
  209.2 32.2 %turn.1 = (f32[32,1616,128]{2,1,0:T(8,128)}, f32[2048,512]{1,0:T(8,128)}, bf16[32,16,512]{2,1,0:T(8,128)(2,1)}, bf16[32,4,512]{2,1,0:T(4,128)(2,1)}, f32[512,256...) custom-call(s32[1,640]{1,0:T(1,128)} %get-tuple-element.102.refs_2_.served.refs_1_, ...), custom_call_target="tpu_custom_call" | custom-call | tf_op jit(solution)/shard_map/turn/pallas_call | solution.py:542
  241.4 1.6 reshape.108
  243.0 1.0 slice_reduce_fusion.2
  244.0 1.5 fusion.3.refs_14_
  245.5 42.4 %edge_backward.3 = (f32[256,512]{1,0:T(8,128)}, bf16[32,16,512]{2,1,0:T(8,128)(2,1)}, bf16[32,4,512]{2,1,0:T(4,128)(2,1)}, f32[640,512]{1,0:T(8,128)}, f32[32,1616,128]{2,1,0:T(8,128)}) custom-call(s32[640,1]{1,0:T(8,128)} %get-tuple-element.101.refs_1_.want.refs_0_, ...), custom_call_target="tpu_custom_call", output_to_operand_aliasing={{4}: (15, {})} | custom-call | tf_op jit(solution)/shard_map/edge_backward/pallas_call | solution.py:260
  287.9 42.6 %edge_backward.4 = (f32[256,512]{1,0:T(8,128)}, bf16[32,16,512]{2,1,0:T(8,128)(2,1)}, bf16[32,4,512]{2,1,0:T(4,128)(2,1)}, f32[2048,512]{1,0:T(8,128)}, f32[640,512]{1,0:T(8,128)}, /*index=5*/f32[32,1616,128]{2,1,0:T(8,128)}) custom-call(s32[640,1]{1,0:T(8,128)} %get-tuple-element.101.refs_1_.want.refs_0_, ...), custom_call_target="tpu_custom_call", output_to_operand_aliasing={{5}: (23, {})} | custom-call | tf_op jit(solution)/shard_map/edge_backward/pallas_call | solution.py:260
  330.5 43.5 %edge_backward.5 = (f32[256,512]{1,0:T(8,128)}, bf16[32,16,512]{2,1,0:T(8,128)(2,1)}, bf16[32,4,512]{2,1,0:T(4,128)(2,1)}, f32[2048,512]{1,0:T(8,128)}, f32[640,512]{1,0:T(8,128)}, /*index=5*/f32[32,1616,128]{2,1,0:T(8,128)}) custom-call(s32[640,1]{1,0:T(8,128)} %get-tuple-element.101.refs_1_.want.refs_0_, ...), custom_call_target="tpu_custom_call", output_to_operand_aliasing={{5}: (27, {})} | custom-call | tf_op jit(solution)/shard_map/edge_backward/pallas_call | solution.py:260
  374.1 0.0 copy-start.3
  374.1 0.0 copy-start.4
  374.1 0.0 copy-start.5
  374.1 135.7 %reduce_gradient.1 = (f32[32,1616,128]{2,1,0:T(8,128)}, f32[1616,128]{1,0:T(8,128)}, f32[16,128]{1,0:T(8,128)}) custom-call(f32[32,1616,128]{2,1,0:T(8,128)} %get-tuple-element.174.refs_0_, f32[1,512]{1,0:T(1,128)} %get-tuple-element.175.refs_1_, s32[1,640]{1,0:T(1,128)} %get-tuple-element.102.refs_2_.served.refs_1_, ...), custom_call_target="tpu_custom_call", output_to_operand_aliasing={{0}: (0, {})} | custom-call | tf_op jit(solution)/shard_map/reduce_gradient/pallas_call | solution.py:260
  509.8 1.3 slice_reduce_fusion.3
  513.9 3.4 multiply_add_fusion
  (16 shorter events, 0.1 us)
Async XLA Ops:
  0.6 6.2 %copy-start.8 = (bf16[256,4]{0,1:T(4,128)(2,1)S(1)}, bf16[256,4]{0,1:T(4,128)(2,1)}, u32[]{:S(2)}) copy-start(bf16[256,4]{0,1:T(4,128)(2,1)} %param.16) | copy-start | bytes 6148
  0.6 7.0 %copy-start.2 = (f32[204544]{0:T(1024)S(1)}, f32[204544]{0:T(1024)}, u32[]{:S(2)}) copy-start(f32[204544]{0:T(1024)} %param.22) | copy-start | bytes 2454532
  3.1 5.4 %copy-start.1 = (s32[2048,227]{0,1:T(8,128)S(1)}, s32[2048,227]{0,1:T(8,128)}, u32[]{:S(2)}) copy-start(s32[2048,227]{0,1:T(8,128)} %param.18) | copy-start | bytes 5578756
  3.1 5.4 %copy-start.7 = (s32[2048]{0:T(1024)S(1)}, s32[2048]{0:T(1024)}, u32[]{:S(2)}) copy-start(s32[2048]{0:T(1024)} %param.17) | copy-start | bytes 24580
  3.1 6.5 %copy-start = (s32[256,2]{1,0:T(8,128)}, s32[256,2]{1,0:T(8,128)S(1)}, u32[]{:S(2)}) copy-start(s32[256,2]{1,0:T(8,128)S(1)} %add_select_fusion.refs_3_.refs_2_) | copy-start | bytes 6148
  162.9 45.6 %copy-start.6 = (f32[32,8,128]{2,1,0:T(8,128)S(1)}, f32[32,8,128]{2,1,0:T(8,128)}, u32[]{:S(2)}) copy-start(f32[32,8,128]{2,1,0:T(8,128)} %get-tuple-element.140) | copy-start | bytes 393220
  374.1 139.9 %copy-start.3 = (f32[204544]{0:T(1024)S(1)}, f32[204544]{0:T(1024)}, u32[]{:S(2)}) copy-start(f32[204544]{0:T(1024)} %param.25) | copy-start | bytes 2454532
  374.1 139.8 %copy-start.4 = (f32[204544]{0:T(1024)S(1)}, f32[204544]{0:T(1024)}, u32[]{:S(2)}) copy-start(f32[204544]{0:T(1024)} %param.24) | copy-start | bytes 2454532
  374.1 139.8 %copy-start.5 = (f32[204544]{0:T(1024)S(1)}, f32[204544]{0:T(1024)}, u32[]{:S(2)}) copy-start(f32[204544]{0:T(1024)} %param.23) | copy-start | bytes 2454532

commit v7 on v6

--- a/solution.py
+++ b/solution.py
@@ -923,13 +923,55 @@
             copy.wait_send()
 
 
-def start_kernel(n, jobs, bm, r):
+def as_column(row):
+    return jnp.transpose(jnp.broadcast_to(row, (128, row.shape[1])))[:, 0:1]
+
+
+def route(n, parts, r):
+    owner = jnp.concatenate([r.owners[0:1, :], r.owners[1:2, :]], axis=1)
+    local = jnp.concatenate([r.locals[0:1, :], r.locals[1:2, :]], axis=1)
+    wants, edges = owner.shape[1], r.owners.shape[1]
+    earlier = lax.broadcasted_iota(jnp.int32, (wants, wants), 0) < lax.broadcasted_iota(jnp.int32, (wants, wants), 1)
+    same = (as_column(owner) == owner) & earlier
+    rank = jnp.sum(jnp.where(same, 1.0, 0.0), axis=0, keepdims=True).astype(jnp.int32)
+    position = owner * parts[0] + rank
+    if len(parts) > 1:
+        position = jnp.where(rank < parts[0], position, n * parts[0] + owner * parts[1] + rank - parts[0])
+    r.pos_s[...], r.pos_r[...] = position[:, :edges], position[:, edges:]
+    column = as_column(position)
+    r.pos[:, 0:1], r.pos[:, 1:2] = column[:edges, :], column[edges:, :]
+    slots = n * sum(parts)
+    match = lax.broadcasted_iota(jnp.int32, (slots, wants), 0) == position
+    asking = jnp.sum(jnp.where(match, local.astype(F32) + 1.0, 0.0), axis=1, keepdims=True).astype(jnp.int32) - 1
+    put_slot_rows(several(r, "ask"), jnp.broadcast_to(asking, (slots, 128)))
+
+
+def count_mask(r):
+    sea = (lax.broadcasted_iota(jnp.int32, (VARS, 1), 0) < SEA_VARS).astype(jnp.int32)
+    total = jnp.zeros((1, 128), F32)
+    for i in range(r.level.shape[1] // 128):
+        at = slice(128 * i, 128 * (i + 1))
+        total += col((r._level[:, at] * (1 - sea * r.land[:, at])).astype(F32))
+    r.number[...] = jnp.zeros_like(r.number)
+    r.number[0:1, :] = total
+
+
+def start_kernel(n, parts, jobs, bm, r):
     me = lax.axis_index("dev")
     gather = Gather(r, r.w, r.shares)
-    greet(n, me)
+    greet_start(n, me)
+    mask = pltpu.make_async_copy(r.level, r._level, r.gown.at[2])
+    mask.start()
+    rows = r.master.shape[0]
+    r.w[rows // 16 * 16 :, :] = jnp.zeros_like(r.w[rows // 16 * 16 :, :])
+    r.w[:rows, :] = r.master[...].astype(BF16)
+    greet_wait(n)
     gather.begin()
+    route(n, parts, r)
     asks, asked = several(r, "ask"), several(r, "asked")
     swap_start(n, me, asks, asked, r.aown, r.a1, r.b1)
+    mask.wait()
+    count_mask(r)
     number = pltpu.make_async_copy(r.number, r.numbers.at[me], r.gown.at[1])
     number.start()
     def go(j, carry):
@@ -1048,17 +1090,20 @@
     swap_wait(n, me, back, out, r.own.at[1], r.s2, r.r2)
 
 
-def start(n, parts, cid, w, number, asks, source, pos, pos_r, x, segments, share_rows, bm=512):
+def start(n, parts, cid, master, owners, locals_, level, land, source, x, segments, share_rows, bm=512):
+    pad_rows = (share_rows + 31) // 32 * 32
     jobs = relay_plan(segments, share_rows)
     blocks = segments[-1][0] + 1
     count, edges, rows = n * sum(parts), source.shape[0], x.shape[1]
     V = pl.BlockSpec(memory_space=pltpu.VMEM)
     tables = [(n, p, 128) for p in parts]
     shapes = [(n, p, LATENT) for p in parts]
-    inputs = dict(w=(w, ANY), number=(number, V), source=(source, V), pos=(pos, V), pos_r=(pos_r, V), x=(x, V)) | numbered("ask", [(a, V) for a in asks])
+    inputs = dict(master=(master, V), owners=(owners, V), locals=(locals_, V), level=(level, ANY), land=(land, V), source=(source, V), x=(x, V))
+    index = lambda *s: (shaped(*s, dtype=jnp.int32), V)
     low = lambda r: shaped(r, LATENT, dtype=BF16)
-    outputs = dict(shares=(shaped(n, *w.shape, dtype=BF16), ANY), numbers=(shaped(n, *number.shape), ANY))
-    outputs |= dict(want=(shaped(count, 1, dtype=jnp.int32), V), served=(shaped(1, count, dtype=jnp.int32), V))
+    outputs = dict(shares=(shaped(n, pad_rows, 128, dtype=BF16), ANY), numbers=(shaped(n, 8, 128), ANY))
+    outputs |= dict(pos=index(edges, 2), pos_s=index(1, edges), pos_r=index(1, edges))
+    outputs |= dict(want=index(count, 1), served=index(1, count))
     outputs |= dict(edge=(shaped(edges, LATENT), V), edge_low=(low(edges), V), sent=(low(edges), V), recv=(low(edges), V))
     outputs |= numbered("landed", [(shaped(*s, dtype=BF16), ANY) for s in shapes])
     outputs |= dict(node=(shaped(rows, LATENT), ANY), low=(low(rows), ANY), slots=(shaped(count, LATENT), ANY))
@@ -1068,8 +1113,11 @@
             made[f"m{b}{name[1:]}"] = (-(-shape[0] // 128) * 128, LATENT)
     outputs |= {name: (shaped(*shape, dtype=BF16), ANY) for name, shape in made.items()}
     outputs |= {f"m{b}_vec": (shaped(8, LATENT), ANY) for b in range(blocks)}
-    scratch = swap_scratch(shapes, n) | numbered("asked", [pltpu.VMEM(s, jnp.int32) for s in tables])
-    scratch |= dict(aown=DMA((len(parts),)), a1=DMA((len(parts), n)), b1=DMA((len(parts), n)), ns=DMA((n,)), nr=DMA((n,)), gown=DMA((2,)))
+    scratch = swap_scratch(shapes, n)
+    for name in ("ask", "asked"):
+        scratch |= numbered(name, [pltpu.VMEM(s, jnp.int32) for s in tables])
+    scratch |= dict(w=pltpu.VMEM((pad_rows, 128), BF16), number=pltpu.VMEM((8, 128), F32), _level=pltpu.VMEM(level.shape, jnp.int32))
+    scratch |= dict(aown=DMA((len(parts),)), a1=DMA((len(parts), n)), b1=DMA((len(parts), n)), ns=DMA((n,)), nr=DMA((n,)), gown=DMA((3,)))
     for b, name in enumerate(("_p", "_g", "_e")):
         scratch |= {name + "_in": pltpu.VMEM(made[f"m{b}_in"], BF16), name + "_out": pltpu.VMEM(made[f"m{b}_out"], BF16), name + "_vec": pltpu.VMEM((8, LATENT), F32)}
     stage = sum(part[2] for job in jobs for part in job[5])
@@ -1080,7 +1128,7 @@
     scratch |= dict(zs=DMA((2, 4)), zr=DMA((4,)), bs=DMA((28,)), br=DMA((28,)))
     for name in ("h", "c", "d"):
         scratch |= {name + "s": DMA((4, 2)), name + "r": DMA((4, 2))}
-    return named_call(functools.partial(start_kernel, n, jobs, bm), "start", inputs, outputs, scratch, cid=cid)
+    return named_call(functools.partial(start_kernel, n, parts, jobs, bm), "start", inputs, outputs, scratch, cid=cid)
 
 
 def accumulate(dst, src, rows):
@@ -1351,27 +1399,23 @@
     devices = lax.axis_size("dev")
     share = master.shape[0]
     mine = devices == 32 and share % 128 == 0
-    ocean = (jnp.arange(VARS) < SEA_VARS).astype(jnp.float32)
     parts = make_parts(5 * edge_owners.shape[0] // (2 * devices))
     capacity = sum(parts)
-    position, asking = make_asks(edge_owners, edge_local, devices, parts)
-    counted = jnp.sum(level_mask * (1 - land_sea[:, None] * ocean.astype(jnp.int32)[None, :])).astype(jnp.float32)
-    pos = position.reshape(-1, 2)
-    pos_s, pos_r = pos[:, 0][None, :], pos[:, 1][None, :]
     x = inputs.T
     geo = widen(geometry, 128)
+    level, land = level_mask.T, land_sea[None, :]
     if mine:
         share_rows = share // 128
-        pad_rows = (share_rows + 31) // 32 * 32
-        low = jnp.pad(master.astype(jnp.bfloat16).reshape(share_rows, 128), ((0, pad_rows - share_rows), (0, 0)))
-        number = jnp.zeros((8, 128), jnp.float32).at[0, 0].set(counted)
-        cuts = [sum(parts[:i]) for i in range(len(parts) + 1)]
-        asks = [jnp.broadcast_to(asking[:, a:b, None], (devices, b - a, 128)) for a, b in zip(cuts, cuts[1:])]
-        begun = start(devices, parts, 1, low, number, asks, geo, pos, pos_r, x, segments, share_rows)
+        begun = start(devices, parts, 1, master.reshape(share_rows, 128), edge_owners.T, edge_local.T, level, land, geo, x, segments, share_rows)
         blocks, bias = relaid_blocks(begun, segments, share_rows)
-        want, served = begun.want, begun.served
+        want, served, pos, pos_s, pos_r = begun.want, begun.served, begun.pos, begun.pos_s, begun.pos_r
         count = jnp.sum(begun.numbers)
     else:
+        position, asking = make_asks(edge_owners, edge_local, devices, parts)
+        pos = position.reshape(-1, 2)
+        pos_s, pos_r = pos[:, 0][None, :], pos[:, 1][None, :]
+        ocean = (jnp.arange(VARS) < SEA_VARS).astype(jnp.int32)
+        counted = jnp.sum(level_mask * (1 - land_sea[:, None] * ocean[None, :])).astype(jnp.float32)
         full_weights = lax.all_gather(master.astype(jnp.bfloat16), "dev", axis=0, tiled=True)
         whole = unpack(full_weights, segments)
         blocks = [make_block(b) for b in whole]
@@ -1381,7 +1425,6 @@
         served = jnp.concatenate([served[:, sum(parts[:i]) : sum(parts[: i + 1])].reshape(-1) for i in range(len(parts))])
         want = served[:, None]
         served = served[None, :]
-    land = land_sea[None, :]
     routes = (want, served, pos, pos_s, pos_r)
     if mine:
         done = [begun]
@@ -1408,7 +1451,7 @@
     tail_at = dec_at + 4 * LATENT
     k = LAYERS - 1
     flat, g_node, *outgoing, d_out, d_first, d_bias, errors = turn(
-        served, want, several(done[k], "landed"), done[k].node, x, targets.T, level_mask.T, land, count.reshape(1, 1),
+        served, want, several(done[k], "landed"), done[k].node, x, targets.T, level, land, count.reshape(1, 1),
         blocks[3 + 2 * k], blocks[-1], bias, chunks, places[3 + 2 * k], dec_at,
     )
     flats = {len(chunks.cuts) - 2: flat}

time: 530 us -> 521 us (0.983)
  no operation moved by 1% of the time
where the time goes in v7:
time: 521 us; the launch traced here: 511 us
  Pallas kernels  490 us (94%)
  local copies, waits for them, and re-layouts  7.94 us (2%)
  other arithmetic  6.78 us (1%)
  between operations  6.26 us (1%)
    pallas_call x7, Pallas kernels, named_call(): pl.pallas_call(kernel, out_shape=tuple((shape for shape, _ in outputs.val...  458 us
    pallas_call x1, Pallas kernels, turn(): pl.pallas_call(functools.partial(turn_kernel, len(landed), bm, chunks, gr...  32.5 us

profile of v7, /device:TPU:27, one launch (start us, length us, event | category | flops | bytes accessed | tf_op | source)
XLA Modules:
  0.0 511.4 jit_solution(445744790240509109)
XLA Ops:
  0.6 0.8 copy.23
  1.5 0.6 pad.12.refs_5_.refs_23_
  2.1 107.8 %start.1 = (bf16[32,1600,128]{2,1,0:T(8,128)(2,1)}, f32[32,8,128]{2,1,0:T(8,128)}, s32[256,2]{1,0:T(8,128)}, s32[1,256]{1,0:T(1,128)}, s32[1,256]{1,0:T(1,128)},...) custom-call(f32[1598,128]{1,0:T(8,128)} %bitcast.29, ...), custom_call_target="tpu_custom_call" | custom-call | tf_op jit(solution)/shard_map/start/pallas_call | solution.py:260
  109.9 44.1 %edge_forward.2 = (f32[256,512]{1,0:T(8,128)}, bf16[256,512]{1,0:T(8,128)(2,1)}, bf16[256,512]{1,0:T(8,128)(2,1)}, bf16[256,512]{1,0:T(8,128)(2,1)}, bf16[32,16,...) custom-call(f32[256,512]{1,0:T(8,128)} %get-tuple-element.103.refs_0, ...), custom_call_target="tpu_custom_call" | custom-call | tf_op jit(solution)/shard_map/edge_forward/pallas_call | solution.py:260
  153.9 0.0 copy-start.4
  154.0 41.7 %edge_forward.3 = (f32[256,512]{1,0:T(8,128)}, bf16[256,512]{1,0:T(8,128)(2,1)}, bf16[256,512]{1,0:T(8,128)(2,1)}, bf16[256,512]{1,0:T(8,128)(2,1)}, bf16[32,16,...) custom-call(f32[256,512]{1,0:T(8,128)} %get-tuple-element.117.refs_0, ...), custom_call_target="tpu_custom_call" | custom-call | tf_op jit(solution)/shard_map/edge_forward/pallas_call | solution.py:260
  195.7 1.0 slice.21
  196.7 0.7 reshape_squeeze.6
  197.3 0.7 pad.13.refs_12_
  198.1 0.7 slice_bitcast_fusion
  198.8 0.8 copy.24.refs_14_
  199.6 0.0 copy-done.4
  199.6 0.6 reduce_sum.27
  200.2 32.5 %turn.1 = (f32[32,1616,128]{2,1,0:T(8,128)}, f32[2048,512]{1,0:T(8,128)}, bf16[32,16,512]{2,1,0:T(8,128)(2,1)}, bf16[32,4,512]{2,1,0:T(4,128)(2,1)}, f32[512,256...) custom-call(s32[1,640]{1,0:T(1,128)} %get-tuple-element.93.refs_2_.served.refs_1_, ...), custom_call_target="tpu_custom_call" | custom-call | tf_op jit(solution)/shard_map/turn/pallas_call | solution.py:542
  232.7 1.6 reshape.40
  234.2 1.0 slice_reduce_fusion
  235.3 1.5 fusion.2.refs_14_
  236.8 42.4 %edge_backward.3 = (f32[256,512]{1,0:T(8,128)}, bf16[32,16,512]{2,1,0:T(8,128)(2,1)}, bf16[32,4,512]{2,1,0:T(4,128)(2,1)}, f32[640,512]{1,0:T(8,128)}, f32[32,1616,128]{2,1,0:T(8,128)}) custom-call(s32[640,1]{1,0:T(8,128)} %get-tuple-element.92.refs_1_.want.refs_0_, ...), custom_call_target="tpu_custom_call", output_to_operand_aliasing={{4}: (15, {})} | custom-call | tf_op jit(solution)/shard_map/edge_backward/pallas_call | solution.py:260
  279.2 42.6 %edge_backward.4 = (f32[256,512]{1,0:T(8,128)}, bf16[32,16,512]{2,1,0:T(8,128)(2,1)}, bf16[32,4,512]{2,1,0:T(4,128)(2,1)}, f32[2048,512]{1,0:T(8,128)}, f32[640,512]{1,0:T(8,128)}, /*index=5*/f32[32,1616,128]{2,1,0:T(8,128)}) custom-call(s32[640,1]{1,0:T(8,128)} %get-tuple-element.92.refs_1_.want.refs_0_, ...), custom_call_target="tpu_custom_call", output_to_operand_aliasing={{5}: (23, {})} | custom-call | tf_op jit(solution)/shard_map/edge_backward/pallas_call | solution.py:260
  321.8 43.5 %edge_backward.5 = (f32[256,512]{1,0:T(8,128)}, bf16[32,16,512]{2,1,0:T(8,128)(2,1)}, bf16[32,4,512]{2,1,0:T(4,128)(2,1)}, f32[2048,512]{1,0:T(8,128)}, f32[640,512]{1,0:T(8,128)}, /*index=5*/f32[32,1616,128]{2,1,0:T(8,128)}) custom-call(s32[640,1]{1,0:T(8,128)} %get-tuple-element.92.refs_1_.want.refs_0_, ...), custom_call_target="tpu_custom_call", output_to_operand_aliasing={{5}: (27, {})} | custom-call | tf_op jit(solution)/shard_map/edge_backward/pallas_call | solution.py:260
  365.4 0.0 copy-start
  365.4 0.0 copy-start.1
  365.4 0.0 copy-start.2
  365.4 0.0 copy-start.3
  365.4 135.7 %reduce_gradient.1 = (f32[32,1616,128]{2,1,0:T(8,128)}, f32[1616,128]{1,0:T(8,128)}, f32[16,128]{1,0:T(8,128)}) custom-call(f32[32,1616,128]{2,1,0:T(8,128)} %get-tuple-element.168.refs_0_, f32[1,512]{1,0:T(1,128)} %get-tuple-element.169.refs_1_, s32[1,640]{1,0:T(1,128)} %get-tuple-element.93.refs_2_.served.refs_1_, ...), custom_call_target="tpu_custom_call", output_to_operand_aliasing={{0}: (0, {})} | custom-call | tf_op jit(solution)/shard_map/reduce_gradient/pallas_call | solution.py:260
  501.2 1.3 slice_reduce_fusion.1
  505.3 0.0 copy-done
  505.3 0.0 copy-done.1
  505.3 0.0 copy-done.2
  505.3 0.0 copy-done.3
  505.3 3.4 multiply_add_fusion
  (1 shorter events, 0.0 us)
Async XLA Ops:
  153.9 45.6 %copy-start.4 = (f32[32,8,128]{2,1,0:T(8,128)S(1)}, f32[32,8,128]{2,1,0:T(8,128)}, u32[]{:S(2)}) copy-start(f32[32,8,128]{2,1,0:T(8,128)} %get-tuple-element.134) | copy-start | bytes 393220
  365.4 139.9 %copy-start = (f32[204544]{0:T(1024)S(1)}, f32[204544]{0:T(1024)}, u32[]{:S(2)}) copy-start(f32[204544]{0:T(1024)} %param.20) | copy-start | bytes 2454532
  365.4 139.9 %copy-start.1 = (f32[204544]{0:T(1024)S(1)}, f32[204544]{0:T(1024)}, u32[]{:S(2)}) copy-start(f32[204544]{0:T(1024)} %param.23) | copy-start | bytes 2454532
  365.4 139.9 %copy-start.2 = (f32[204544]{0:T(1024)S(1)}, f32[204544]{0:T(1024)}, u32[]{:S(2)}) copy-start(f32[204544]{0:T(1024)} %param.22) | copy-start | bytes 2454532
  365.4 139.9 %copy-start.3 = (f32[204544]{0:T(1024)S(1)}, f32[204544]{0:T(1024)}, u32[]{:S(2)}) copy-start(f32[204544]{0:T(1024)} %param.21) | copy-start | bytes 2454532

commit v8 on v7

--- a/solution.py
+++ b/solution.py
@@ -836,7 +836,7 @@
             return jnp.where(z == 0, v[0], jnp.where(z == 1, v[1], jnp.where(z == 2, v[2], v[3])))
         self.come = [z, by_plane(1, 0, 1, 2), by_plane(2, 2, 3, 1), by_plane(3, 3, 0, 0)]
         self.go = [z, by_plane(1, 0, 1, 2), by_plane(2, 2, 0, 0), by_plane(3, 3, 3, 1)]
-        self.sends, self.sibling, self.seen = [], [], 0
+        self.sends, self.spreads, self.sibling, self.seen = [], {}, [], 0
 
     def send(self, *args):
         copy = remote(*args)
@@ -888,10 +888,21 @@
         self.onward(i)
         self.to_sibling(slot)
 
-    def spread(self, k):
+    def spread(self, k, when=None):
         r, slot = self.r, self.dev(self.go[k])
-        self.send(self.share(k, self.A), self.o.at[slot, self.A], r.hs.at[k, 0], r.hr.at[k, 0], self.tx)
-        self.send(self.share(k, self.B), self.o.at[slot, self.B], r.hs.at[k, 1], r.hr.at[k, 1], self.ty)
+        copies = [
+            remote(self.share(k, self.A), self.o.at[slot, self.A], r.hs.at[k, 0], r.hr.at[k, 0], self.tx),
+            remote(self.share(k, self.B), self.o.at[slot, self.B], r.hs.at[k, 1], r.hr.at[k, 1], self.ty),
+        ]
+        if when is None:
+            for copy in copies:
+                copy.start()
+        else:
+            @pl.when(when)
+            def _():
+                for copy in copies:
+                    copy.start()
+        self.spreads[k] = copies
 
     def second(self, k):
         r, o, zz = self.r, self.o, self.go[k]
@@ -919,7 +930,7 @@
     def finish(self):
         for i in range(4):
             self.onward(i, True)
-        for copy in self.sends:
+        for copy in self.sends + [copy for pair in self.spreads.values() for copy in pair]:
             copy.wait_send()
 
 
@@ -982,11 +993,12 @@
     gather.second(0)
     gather.arrive(1)
     gather.spread(1)
+    gather.arrive(2)
     gather.third(0)
     gather.second(1)
-    gather.arrive(2)
+    gather.spread(2, gather.z < 2)
     gather.arrive(3)
-    gather.spread(2)
+    gather.spread(2, gather.z >= 2)
     gather.third(1)
     gather.second(2)
     swap_wait(n, me, asks, asked, r.aown, r.a1, r.b1)
@@ -1302,7 +1314,12 @@
         return carry
     lax.fori_loop(1, n, end, 0)
     q_own.wait()
-    r.sums[...] = jnp.sum(r.all[...], axis=0)
+    sums = jnp.sum(r.all[...], axis=0)
+    whole = lambda v: jnp.sum(jnp.sum(v, axis=1, keepdims=True), axis=0, keepdims=True)
+    norm = jnp.sqrt(whole(sums[0:8, :]))
+    r.norm[...] = norm
+    r.factor[...] = jnp.minimum(1.0, clip_limit / norm)
+    r.error[...] = whole(sums[8:16, :])
 
 
 def reduce_gradient(n, chunks, flat, errors, share_rows, lead, encoder, cid, bm=512):
@@ -1313,13 +1330,13 @@
     inputs = dict(flat_in=(flat, ANY), err=(errors, V), served=(served, V), g_node=(g_node, ANY), x=(x, ANY))
     inputs |= numbered("landed", [(v, V) for v in landed])
     inputs |= {name: (v, V) for name, v in zip(("p_in", "p_out", "p_vec"), block)}
-    outputs = dict(flat0=(shaped(*flat.shape), ANY), out=(shaped(rows, 128), V), sums=(shaped(16, 128), V))
+    outputs = dict(flat0=(shaped(*flat.shape), ANY), out=(shaped(rows, 128), V)) | {name: (shaped(1, 1), V) for name in ("norm", "factor", "error")}
     scratch = plane_scratch(4, rows) | dict(zq=F(3, rows), zqs=DMA((3,)), zqr=DMA((3,)))
     scratch |= dict(both=F(16), all=F(n, 16), own=DMA, qs=DMA((n,)), qr=DMA((n,)), packed=packed_rows(VARS, 4), fsem=DMA((STORES,)))
     scratch |= sums_scratch("d", block[0].shape[0])
     body = functools.partial(reduce_kernel, n, chunks, share_rows, lead, bm)
     made = named_call(body, "reduce_gradient", inputs, outputs, scratch, aliases=dict(flat_in="flat0"), cid=cid)
-    return made.out, jnp.sum(made.sums[:8]), jnp.sum(made.sums[8:])
+    return made.out, made.norm[0, 0], made.factor[0, 0], made.error[0, 0]
 
 
 def make_parts(capacity):
@@ -1481,16 +1498,17 @@
             g_node = b.g_prev
     if mine:
         encoder = (served, landed, g_node, x, blocks[0])
-        summed, squares, error_sum = reduce_gradient(devices, chunks, flats[0], errors, share_rows, lead, encoder, 2)
+        summed, grad_norm, factor, error_sum = reduce_gradient(devices, chunks, flats[0], errors, share_rows, lead, encoder, 2)
         skip = lax.rem(lead + share_rows * lax.axis_index("dev"), 8)
         own_grad = lax.dynamic_slice_in_dim(summed, skip, share_rows).reshape(-1)
     else:
         flat = encode_backward(served, landed, g_node, x, blocks[0], chunks, flats[0])
         own_grad = lax.psum_scatter(flat[0, lead : lead + PARAMS // 128].reshape(-1), "dev", scatter_dimension=0, tiled=True)
         error_sum, squares = lax.psum((jnp.sum(errors), jnp.sum(own_grad * own_grad)), "dev")
-    grad_norm = jnp.sqrt(squares)
+        grad_norm = jnp.sqrt(squares)
+        factor = jnp.minimum(1.0, clip_limit / grad_norm)
     loss = error_sum / jnp.maximum(count, 1.0)
-    clipped = own_grad * jnp.minimum(1.0, clip_limit / grad_norm)
+    clipped = own_grad * factor
     step = step_count[0].astype(jnp.float32)
     new_first = beta_one * first_moment + (1.0 - beta_one) * clipped
     new_second = beta_two * second_moment + (1.0 - beta_two) * clipped * clipped

time: 521 us -> 515 us (0.988)
  no operation moved by 1% of the time
where the time goes in v8:
time: 515 us; the launch traced here: 506 us
  Pallas kernels  486 us (94%)
  local copies, waits for them, and re-layouts  7.93 us (2%)
  between operations  6.13 us (1%)
  other arithmetic  6.06 us (1%)
    pallas_call x7, Pallas kernels, named_call(): pl.pallas_call(kernel, out_shape=tuple((shape for shape, _ in outputs.val...  453 us
    pallas_call x1, Pallas kernels, turn(): pl.pallas_call(functools.partial(turn_kernel, len(landed), bm, chunks, gr...  32.4 us

profile of v8, /device:TPU:27, one launch (start us, length us, event | category | flops | bytes accessed | tf_op | source)
XLA Modules:
  0.0 505.9 jit_solution(14697178683633104668)
XLA Ops:
  0.6 0.8 copy.23
  1.5 0.6 pad.12.refs_5_.refs_23_
  2.1 103.3 %start.1 = (bf16[32,1600,128]{2,1,0:T(8,128)(2,1)}, f32[32,8,128]{2,1,0:T(8,128)}, s32[256,2]{1,0:T(8,128)}, s32[1,256]{1,0:T(1,128)}, s32[1,256]{1,0:T(1,128)},...) custom-call(f32[1598,128]{1,0:T(8,128)} %bitcast.32, ...), custom_call_target="tpu_custom_call" | custom-call | tf_op jit(solution)/shard_map/start/pallas_call | solution.py:260
  105.4 43.8 %edge_forward.2 = (f32[256,512]{1,0:T(8,128)}, bf16[256,512]{1,0:T(8,128)(2,1)}, bf16[256,512]{1,0:T(8,128)(2,1)}, bf16[256,512]{1,0:T(8,128)(2,1)}, bf16[32,16,...) custom-call(f32[256,512]{1,0:T(8,128)} %get-tuple-element.105.refs_0, ...), custom_call_target="tpu_custom_call" | custom-call | tf_op jit(solution)/shard_map/edge_forward/pallas_call | solution.py:260
  149.2 0.0 copy-start.4
  149.2 41.9 %edge_forward.3 = (f32[256,512]{1,0:T(8,128)}, bf16[256,512]{1,0:T(8,128)(2,1)}, bf16[256,512]{1,0:T(8,128)(2,1)}, bf16[256,512]{1,0:T(8,128)(2,1)}, bf16[32,16,...) custom-call(f32[256,512]{1,0:T(8,128)} %get-tuple-element.119.refs_0, ...), custom_call_target="tpu_custom_call" | custom-call | tf_op jit(solution)/shard_map/edge_forward/pallas_call | solution.py:260
  191.2 1.0 slice.15
  192.2 0.7 reshape_squeeze.6
  192.8 0.7 pad.13.refs_12_
  193.6 0.7 slice_bitcast_fusion
  194.2 0.8 copy.24.refs_14_
  195.0 0.0 copy-done.4
  195.0 0.6 reduce_sum.9
  195.7 32.4 %turn.1 = (f32[32,1616,128]{2,1,0:T(8,128)}, f32[2048,512]{1,0:T(8,128)}, bf16[32,16,512]{2,1,0:T(8,128)(2,1)}, bf16[32,4,512]{2,1,0:T(4,128)(2,1)}, f32[512,256...) custom-call(s32[1,640]{1,0:T(1,128)} %get-tuple-element.95.refs_2_.served.refs_1_, ...), custom_call_target="tpu_custom_call" | custom-call | tf_op jit(solution)/shard_map/turn/pallas_call | solution.py:542
  228.1 1.6 reshape.40
  229.7 1.0 slice_reduce_fusion
  230.7 1.5 fusion.2.refs_14_
  232.2 42.4 %edge_backward.3 = (f32[256,512]{1,0:T(8,128)}, bf16[32,16,512]{2,1,0:T(8,128)(2,1)}, bf16[32,4,512]{2,1,0:T(4,128)(2,1)}, f32[640,512]{1,0:T(8,128)}, f32[32,1616,128]{2,1,0:T(8,128)}) custom-call(s32[640,1]{1,0:T(8,128)} %get-tuple-element.94.refs_1_.want.refs_0_, ...), custom_call_target="tpu_custom_call", output_to_operand_aliasing={{4}: (15, {})} | custom-call | tf_op jit(solution)/shard_map/edge_backward/pallas_call | solution.py:260
  274.6 42.6 %edge_backward.4 = (f32[256,512]{1,0:T(8,128)}, bf16[32,16,512]{2,1,0:T(8,128)(2,1)}, bf16[32,4,512]{2,1,0:T(4,128)(2,1)}, f32[2048,512]{1,0:T(8,128)}, f32[640,512]{1,0:T(8,128)}, /*index=5*/f32[32,1616,128]{2,1,0:T(8,128)}) custom-call(s32[640,1]{1,0:T(8,128)} %get-tuple-element.94.refs_1_.want.refs_0_, ...), custom_call_target="tpu_custom_call", output_to_operand_aliasing={{5}: (23, {})} | custom-call | tf_op jit(solution)/shard_map/edge_backward/pallas_call | solution.py:260
  317.3 43.6 %edge_backward.5 = (f32[256,512]{1,0:T(8,128)}, bf16[32,16,512]{2,1,0:T(8,128)(2,1)}, bf16[32,4,512]{2,1,0:T(4,128)(2,1)}, f32[2048,512]{1,0:T(8,128)}, f32[640,512]{1,0:T(8,128)}, /*index=5*/f32[32,1616,128]{2,1,0:T(8,128)}) custom-call(s32[640,1]{1,0:T(8,128)} %get-tuple-element.94.refs_1_.want.refs_0_, ...), custom_call_target="tpu_custom_call", output_to_operand_aliasing={{5}: (27, {})} | custom-call | tf_op jit(solution)/shard_map/edge_backward/pallas_call | solution.py:260
  360.8 0.0 copy-start
  360.8 0.0 copy-start.1
  360.8 0.0 copy-start.2
  360.9 0.0 copy-start.3
  360.9 135.7 %reduce_gradient.1 = (f32[32,1616,128]{2,1,0:T(8,128)}, f32[1616,128]{1,0:T(8,128)}, f32[1,1]{1,0:T(1,128)}, f32[1,1]{1,0:T(1,128)}, f32[1,1]{1,0:T(1,128)}) custom-call(f32[32,1616,128]{2,1,0:T(8,128)} %get-tuple-element.170.refs_0_, f32[1,512]{1,0:T(1,128)} %get-tuple-element.171.refs_1_, ...), custom_call_target="tpu_custom_call", output_to_operand_aliasing={{0}: (0, {})} | custom-call | tf_op jit(solution)/shard_map/reduce_gradient/pallas_call | solution.py:260
  498.6 0.0 copy-done
  498.7 0.0 copy-done.1
  498.7 0.0 copy-done.2
  498.7 0.0 copy-done.3
  498.7 3.9 multiply_add_fusion
  (1 shorter events, 0.0 us)
Async XLA Ops:
  149.2 45.8 %copy-start.4 = (f32[32,8,128]{2,1,0:T(8,128)S(1)}, f32[32,8,128]{2,1,0:T(8,128)}, u32[]{:S(2)}) copy-start(f32[32,8,128]{2,1,0:T(8,128)} %get-tuple-element.136) | copy-start | bytes 393220
  360.8 137.8 %copy-start = (f32[204544]{0:T(1024)S(1)}, f32[204544]{0:T(1024)}, u32[]{:S(2)}) copy-start(f32[204544]{0:T(1024)} %param.20) | copy-start | bytes 2454532
  360.8 137.8 %copy-start.1 = (f32[204544]{0:T(1024)S(1)}, f32[204544]{0:T(1024)}, u32[]{:S(2)}) copy-start(f32[204544]{0:T(1024)} %param.23) | copy-start | bytes 2454532
  360.8 137.8 %copy-start.2 = (f32[204544]{0:T(1024)S(1)}, f32[204544]{0:T(1024)}, u32[]{:S(2)}) copy-start(f32[204544]{0:T(1024)} %param.22) | copy-start | bytes 2454532
  360.9 137.8 %copy-start.3 = (f32[204544]{0:T(1024)S(1)}, f32[204544]{0:T(1024)}, u32[]{:S(2)}) copy-start(f32[204544]{0:T(1024)} %param.21) | copy-start | bytes 2454532

commit v9 on v8

--- a/solution.py
+++ b/solution.py
@@ -532,7 +532,7 @@
         stores.wait()
 
 
-def turn(served, want, landed, node, x, target, level, land, count, block, dec, bias, chunks, at, dec_at, bm=512):
+def turn(served, want, landed, node, x, target, level, land, count, block, dec, bias, chunks, at, dec_at, bm=1024):
     rows = node.shape[0]
     slots = want.shape[0]
     wide = dec[1].shape[1]

time: 515 us -> 514 us (level)
  no operation moved by 1% of the time
where the time goes in v9:
time: 514 us; the launch traced here: 504 us
  Pallas kernels  484 us (94%)
  local copies, waits for them, and re-layouts  7.93 us (2%)
  between operations  6.13 us (1%)
  other arithmetic  6.06 us (1%)
    pallas_call x7, Pallas kernels, named_call(): pl.pallas_call(kernel, out_shape=tuple((shape for shape, _ in outputs.val...  453 us
    pallas_call x1, Pallas kernels, turn(): pl.pallas_call(functools.partial(turn_kernel, len(landed), bm, chunks, gr...  31.2 us

profile of v9, /device:TPU:27, one launch (start us, length us, event | category | flops | bytes accessed | tf_op | source)
XLA Modules:
  0.0 504.5 jit_solution(5799348125271221004)
XLA Ops:
  0.6 0.8 copy.23
  1.5 0.6 pad.12.refs_5_.refs_23_
  2.1 103.3 %start.1 = (bf16[32,1600,128]{2,1,0:T(8,128)(2,1)}, f32[32,8,128]{2,1,0:T(8,128)}, s32[256,2]{1,0:T(8,128)}, s32[1,256]{1,0:T(1,128)}, s32[1,256]{1,0:T(1,128)},...) custom-call(f32[1598,128]{1,0:T(8,128)} %bitcast.32, ...), custom_call_target="tpu_custom_call" | custom-call | tf_op jit(solution)/shard_map/start/pallas_call | solution.py:260
  105.5 43.7 %edge_forward.2 = (f32[256,512]{1,0:T(8,128)}, bf16[256,512]{1,0:T(8,128)(2,1)}, bf16[256,512]{1,0:T(8,128)(2,1)}, bf16[256,512]{1,0:T(8,128)(2,1)}, bf16[32,16,...) custom-call(f32[256,512]{1,0:T(8,128)} %get-tuple-element.105.refs_0, ...), custom_call_target="tpu_custom_call" | custom-call | tf_op jit(solution)/shard_map/edge_forward/pallas_call | solution.py:260
  149.2 0.0 copy-start.4
  149.2 41.9 %edge_forward.3 = (f32[256,512]{1,0:T(8,128)}, bf16[256,512]{1,0:T(8,128)(2,1)}, bf16[256,512]{1,0:T(8,128)(2,1)}, bf16[256,512]{1,0:T(8,128)(2,1)}, bf16[32,16,...) custom-call(f32[256,512]{1,0:T(8,128)} %get-tuple-element.119.refs_0, ...), custom_call_target="tpu_custom_call" | custom-call | tf_op jit(solution)/shard_map/edge_forward/pallas_call | solution.py:260
  191.1 1.0 slice.15
  192.1 0.7 reshape_squeeze.6
  192.8 0.7 pad.13.refs_12_
  193.5 0.7 slice_bitcast_fusion
  194.2 0.8 copy.24.refs_14_
  195.0 0.0 copy-done.4
  195.0 0.6 reduce_sum.9
  195.6 31.2 %turn.1 = (f32[32,1616,128]{2,1,0:T(8,128)}, f32[2048,512]{1,0:T(8,128)}, bf16[32,16,512]{2,1,0:T(8,128)(2,1)}, bf16[32,4,512]{2,1,0:T(4,128)(2,1)}, f32[512,256...) custom-call(s32[1,640]{1,0:T(1,128)} %get-tuple-element.95.refs_2_.served.refs_1_, ...), custom_call_target="tpu_custom_call" | custom-call | tf_op jit(solution)/shard_map/turn/pallas_call | solution.py:542
  226.8 1.6 reshape.40
  228.4 1.0 slice_reduce_fusion
  229.4 1.5 fusion.2.refs_14_
  230.9 42.4 %edge_backward.3 = (f32[256,512]{1,0:T(8,128)}, bf16[32,16,512]{2,1,0:T(8,128)(2,1)}, bf16[32,4,512]{2,1,0:T(4,128)(2,1)}, f32[640,512]{1,0:T(8,128)}, f32[32,1616,128]{2,1,0:T(8,128)}) custom-call(s32[640,1]{1,0:T(8,128)} %get-tuple-element.94.refs_1_.want.refs_0_, ...), custom_call_target="tpu_custom_call", output_to_operand_aliasing={{4}: (15, {})} | custom-call | tf_op jit(solution)/shard_map/edge_backward/pallas_call | solution.py:260
  273.3 42.8 %edge_backward.4 = (f32[256,512]{1,0:T(8,128)}, bf16[32,16,512]{2,1,0:T(8,128)(2,1)}, bf16[32,4,512]{2,1,0:T(4,128)(2,1)}, f32[2048,512]{1,0:T(8,128)}, f32[640,512]{1,0:T(8,128)}, /*index=5*/f32[32,1616,128]{2,1,0:T(8,128)}) custom-call(s32[640,1]{1,0:T(8,128)} %get-tuple-element.94.refs_1_.want.refs_0_, ...), custom_call_target="tpu_custom_call", output_to_operand_aliasing={{5}: (23, {})} | custom-call | tf_op jit(solution)/shard_map/edge_backward/pallas_call | solution.py:260
  316.1 43.3 %edge_backward.5 = (f32[256,512]{1,0:T(8,128)}, bf16[32,16,512]{2,1,0:T(8,128)(2,1)}, bf16[32,4,512]{2,1,0:T(4,128)(2,1)}, f32[2048,512]{1,0:T(8,128)}, f32[640,512]{1,0:T(8,128)}, /*index=5*/f32[32,1616,128]{2,1,0:T(8,128)}) custom-call(s32[640,1]{1,0:T(8,128)} %get-tuple-element.94.refs_1_.want.refs_0_, ...), custom_call_target="tpu_custom_call", output_to_operand_aliasing={{5}: (27, {})} | custom-call | tf_op jit(solution)/shard_map/edge_backward/pallas_call | solution.py:260
  359.4 0.0 copy-start
  359.4 0.0 copy-start.1
  359.4 0.0 copy-start.2
  359.4 0.0 copy-start.3
  359.5 135.7 %reduce_gradient.1 = (f32[32,1616,128]{2,1,0:T(8,128)}, f32[1616,128]{1,0:T(8,128)}, f32[1,1]{1,0:T(1,128)}, f32[1,1]{1,0:T(1,128)}, f32[1,1]{1,0:T(1,128)}) custom-call(f32[32,1616,128]{2,1,0:T(8,128)} %get-tuple-element.170.refs_0_, f32[1,1024]{1,0:T(1,128)} %get-tuple-element.171.refs_1_, ...), custom_call_target="tpu_custom_call", output_to_operand_aliasing={{0}: (0, {})} | custom-call | tf_op jit(solution)/shard_map/reduce_gradient/pallas_call | solution.py:260
  497.2 0.0 copy-done
  497.2 0.0 copy-done.1
  497.2 0.0 copy-done.2
  497.2 0.0 copy-done.3
  497.3 3.9 multiply_add_fusion
  (1 shorter events, 0.0 us)
Async XLA Ops:
  149.2 45.8 %copy-start.4 = (f32[32,8,128]{2,1,0:T(8,128)S(1)}, f32[32,8,128]{2,1,0:T(8,128)}, u32[]{:S(2)}) copy-start(f32[32,8,128]{2,1,0:T(8,128)} %get-tuple-element.136) | copy-start | bytes 393220
  359.4 137.8 %copy-start = (f32[204544]{0:T(1024)S(1)}, f32[204544]{0:T(1024)}, u32[]{:S(2)}) copy-start(f32[204544]{0:T(1024)} %param.20) | copy-start | bytes 2454532
  359.4 137.8 %copy-start.1 = (f32[204544]{0:T(1024)S(1)}, f32[204544]{0:T(1024)}, u32[]{:S(2)}) copy-start(f32[204544]{0:T(1024)} %param.23) | copy-start | bytes 2454532
  359.4 137.8 %copy-start.2 = (f32[204544]{0:T(1024)S(1)}, f32[204544]{0:T(1024)}, u32[]{:S(2)}) copy-start(f32[204544]{0:T(1024)} %param.22) | copy-start | bytes 2454532
  359.4 137.8 %copy-start.3 = (f32[204544]{0:T(1024)S(1)}, f32[204544]{0:T(1024)}, u32[]{:S(2)}) copy-start(f32[204544]{0:T(1024)} %param.21) | copy-start | bytes 2454532
